TPU v7x, 256 devices: a whole 4x4x8 slice. The times are simulated.
256 devices in a mesh: grp: 4 (over y), dev: 64 (over x, z, core).
Axes of the slice: x: 4, y: 4, z: 8, core: 2. Of those that a mesh axis runs over, the one named last changes fastest.
Arguments:
- stiffness: bfloat16 [4096, 64, 704], P(('grp', 'dev')), may hold values from -6 to 6
- prolongator: bfloat16 [4096, 4096], P(('grp', 'dev')), may hold values from -0.75 to 0.75
- columns: int32 [4096, 11], P(('grp', 'dev')), may hold values from -1 to 271, as said below
- fetch_rows: int32 [16384, 4], P(('grp', 'dev')), may hold values from 0 to 15, as said below
- send_order: int32 [256, 8], P(('grp', 'dev')), may hold values from 0 to 7, each once within a row
- partner_slot: int32 [256, 8], P(('grp', 'dev')), may hold values from 0 to 7, each once within a row
Outputs:
- coarse_blocks: bfloat16 [2048, 64, 1408], P(('grp', 'dev'))
- coarse_columns: int32 [2048, 22], P(('grp', 'dev'))
Inputs may be any that keep to these rules, and one draw needn't show every extreme that they name: `columns`: slot 0 of each row is the row itself; a row's used slots come first and padding (-1) fills the rest of its tile. `fetch_rows`: each row holds 4 distinct rows. `send_order`: each row is a permutation; exactly 2 followers of a device go to each group. `partner_slot`: each row is a permutation.
All inputs are finite; a program needn't handle non-finite values.
Results may differ from a plain program's by a relative error of at most 0.0054.
Values may be sent and summed in bfloat16 or wider, within the bound.
No kernel may reach another device: no remote copies, remote signals or barrier semaphores. Data moves between devices by JAX's collectives and lax.ppermute only.
A program may use at most 64 MiB of HBM per device.

v0:
```python
import jax
import jax.numpy as jnp
from jax import lax
from jax.experimental import pallas as pl
from jax.experimental.pallas import tpu as pltpu
from jax.sharding import Mesh, PartitionSpec as P

BLK = 64
K = 11
C = 4
ROWS = 16
HALF = 8
NG, NX, NZ, NC = 4, 4, 8, 2
N_DEV = NX * NZ * NC
LANES = 128
SLOTS = 12
WIDE = SLOTS * BLK
TABLE = N_DEV * C
CHUNKS = 1
CK = 32 // CHUNKS
AXES = ("grp", "x", "z", "core")

VMEM = pl.BlockSpec(memory_space=pltpu.VMEM)
SMEM = pl.BlockSpec(memory_space=pltpu.SMEM)
LIMIT = pltpu.CompilerParams(vmem_limit_bytes=40 * 1024 * 1024)


def low_lanes(shape):
    return lax.broadcasted_iota(jnp.int32, shape, 1) < BLK


def products_kernel(p_ref, a_ref, perm_ref, y_ref):
    def row(i, carry):
        y = lax.dot_general(
            p_ref[i], a_ref[i], (((0,), (0,)), ((), ())), preferred_element_type=jnp.float32
        )
        y = jnp.concatenate([y, jnp.zeros((BLK, BLK), jnp.float32)], axis=1)
        y = jnp.where(i < HALF, y, pltpu.roll(y, BLK, 1)).astype(jnp.bfloat16)
        for t in range(WIDE // LANES):
            span = slice(t * LANES, (t + 1) * LANES)
            y_ref[i, :, span] = jnp.dot(
                y[:, span], perm_ref[...], preferred_element_type=jnp.float32
            ).astype(jnp.bfloat16)
        return carry

    lax.fori_loop(0, ROWS, row, 0, unroll=4)


def products(blocks, stiffness, perm):
    return pl.pallas_call(
        products_kernel,
        out_shape=jax.ShapeDtypeStruct((ROWS, BLK, WIDE), jnp.bfloat16),
        compiler_params=LIMIT,
        cost_estimate=pl.CostEstimate(
            flops=2 * ROWS * BLK * BLK * WIDE * 3, bytes_accessed=3_200_000, transcendentals=0
        ),
        name="products",
    )(blocks, stiffness, perm)


def select_kernel(wanted_ref, place_ref, *refs):
    held, outs = refs[:NZ], refs[NZ:]
    x, z, c = place_ref[1], place_ref[2], place_ref[3]
    for b in range(NX * NC):
        target = ((x + b // NC) & (NX - 1)) * NC + (c ^ (b % NC))
        for s in range(NZ):
            home = ((z - s) & (NZ - 1)) * C
            for m in range(C):
                outs[b][home + m] = held[s][wanted_ref[target, home + m]]


def select(wanted, place, held):
    shape = jax.ShapeDtypeStruct((NZ * C, CK, LANES), jnp.bfloat16)
    return pl.pallas_call(
        select_kernel,
        out_shape=[shape] * (NX * NC),
        in_specs=[SMEM, SMEM] + [VMEM] * NZ,
        out_specs=[VMEM] * (NX * NC),
        compiler_params=LIMIT,
        name="select",
    )(wanted, place, *held)


def fill(table, own_ref, parts):
    n = NX * NC
    for h in range(CHUNKS):
        for b in range(n):
            table[b * NZ * C:(b + 1) * NZ * C, h * CK:(h + 1) * CK] = parts[h * n + b][...]
    table[TABLE:TABLE + ROWS] = own_ref[...]
    table[TABLE + ROWS] = jnp.zeros((32, LANES), jnp.bfloat16)


def row_tiles(i, table, at_ref, y_ref, emit):
    low = low_lanes((32, LANES))
    zero = jnp.zeros((32, LANES), jnp.bfloat16)
    for t in range(SLOTS // 2):
        a = table[at_ref[i, 2 * t]]
        b = table[at_ref[i, 2 * t + 1]]
        rhs = jnp.concatenate([
            jnp.where(low, a, zero),
            jnp.where(low, pltpu.roll(a, BLK, 1), zero),
            jnp.where(low, zero, pltpu.roll(b, BLK, 1)),
            jnp.where(low, zero, b),
        ], axis=0)
        span = slice(t * LANES, (t + 1) * LANES)
        emit(span, jnp.dot(
            y_ref[i, :, span], rhs, preferred_element_type=jnp.float32
        ).astype(jnp.bfloat16))


def follower_kernel(at_ref, place_ref, send_ref, own_ref, y_ref, *refs):
    n = NX * NC * CHUNKS
    parts, outs, table = refs[:n], refs[n:n + NG], refs[n + NG]
    fill(table, own_ref, parts)
    for s in range(NG):
        target = (place_ref[0] + s) & (NG - 1)
        for q in range(2):
            row = HALF + send_ref[0, target * 2 + q]

            def emit(span, value, s=s, q=q):
                outs[s][q, :, span] = value

            row_tiles(row, table, at_ref, y_ref, emit)


def leader_kernel(at_ref, own_ref, y_ref, *refs):
    n = NX * NC * CHUNKS
    parts, out, table = refs[:n], refs[n], refs[n + 1]
    fill(table, own_ref, parts)

    def row(i, carry):
        def emit(span, value):
            out[i, :, span] = value

        row_tiles(i, table, at_ref, y_ref, emit)
        return carry

    lax.fori_loop(0, HALF, row, 0)


SCRATCH = [pltpu.VMEM((TABLE + ROWS + 1, 32, LANES), jnp.bfloat16)]
ROW_COST = pl.CostEstimate(flops=2 * 8 * 6 * BLK * LANES * LANES, bytes_accessed=5_000_000, transcendentals=0)


def followers(at, place, send, own, y, parts):
    shape = jax.ShapeDtypeStruct((2, BLK, WIDE), jnp.bfloat16)
    return pl.pallas_call(
        follower_kernel,
        out_shape=[shape] * NG,
        in_specs=[SMEM] * 3 + [VMEM] * (2 + len(parts)),
        out_specs=[VMEM] * NG,
        scratch_shapes=SCRATCH,
        compiler_params=LIMIT,
        cost_estimate=ROW_COST,
        name="followers",
    )(at, place, send, own, y, *parts)


def leaders(at, own, y, parts):
    return pl.pallas_call(
        leader_kernel,
        out_shape=jax.ShapeDtypeStruct((HALF, BLK, WIDE), jnp.bfloat16),
        in_specs=[SMEM] + [VMEM] * (2 + len(parts)),
        out_specs=VMEM,
        scratch_shapes=SCRATCH,
        compiler_params=LIMIT,
        cost_estimate=ROW_COST,
        name="leaders",
    )(at, own, y, *parts)


def places_kernel(place_ref, columns_ref, fetch_ref, codes_ref, mine_ref, send_ref, at_ref, lead_ref, follow_ref):
    g, x, z, c = (place_ref[i] for i in range(4))
    device = x * (NZ * NC) + z * NC + c

    def slot(i, k):
        column = columns_ref[i, k]
        ghost = jnp.maximum(column - ROWS, 0)
        peer, m = ghost >> 2, ghost & 3
        px, pz, pc = peer >> 4, (peer >> 1) & (NZ - 1), peer & 1
        way = ((x - px) & (NX - 1)) * NC + (c ^ pc)
        local = column < ROWS
        at = jnp.where(local, TABLE + column, way * (NZ * C) + pz * C + m)
        row = jnp.where(local, jnp.maximum(column, 0), fetch_ref[peer, m])
        late = jnp.maximum(row - HALF, 0)
        code = jnp.where(local, mine_ref[late], codes_ref[px * NC + pc, pz * HALF + late])
        code = jnp.where(row < HALF, g * HALF + row, code)
        owner = jnp.where(local, device, peer)
        label = ((code >> 3) * N_DEV + owner) * HALF + (code & 7)
        present = column >= 0
        return jnp.where(present, at, TABLE + ROWS), jnp.where(present, label, -1)

    def row(i, carry):
        follower = send_ref[0, i] + HALF
        at_ref[i, K] = TABLE + ROWS
        at_ref[follower, 0] = TABLE + ROWS
        for k in range(K):
            at_ref[i, k], lead_ref[i, k] = slot(i, k)
            at_ref[follower, k + 1], follow_ref[i, k] = slot(follower, k)
        return carry

    lax.fori_loop(0, HALF, row, 0)


def places(place, columns, fetch, codes, mine, send):
    labels = jax.ShapeDtypeStruct((HALF, K), jnp.int32)
    return pl.pallas_call(
        places_kernel,
        out_shape=[jax.ShapeDtypeStruct((ROWS, SLOTS), jnp.int32), labels, labels],
        in_specs=[SMEM] * 6,
        out_specs=[SMEM] * 3,
        name="places",
    )(place, columns, fetch, codes, mine, send)


def chains_kernel(slots_ref, lead_ref, arrived_ref, labels_ref, next_ref, work_ref):
    lane = lax.broadcasted_iota(jnp.int32, (HALF, LANES), 1)
    work_ref[...] = jnp.full((HALF, LANES), -1, jnp.int32)
    work_ref[:, 0:K] = lead_ref[...]
    for l in range(HALF):
        work_ref[l:l + 1, K:2 * K] = arrived_ref[pl.ds(slots_ref[0, l], 1), :]
    labels = work_ref[...]
    labels_ref[...] = work_ref[:, 0:2 * K]
    twice = jnp.where(lane < 2 * K, labels, pltpu.roll(labels, 2 * K, 1))
    steps = jnp.full((HALF, LANES), 2 * K, jnp.int32)
    for d in range(2 * K - 1, 0, -1):
        steps = jnp.where(pltpu.roll(twice, LANES - d, 1) == labels, d, steps)
    steps = jnp.where((lane < 2 * K) & (labels >= 0), steps, 2 * K)
    usual = jnp.where((lane == 0) | (lane == K), K, 2 * K)
    odd = jnp.max(jnp.where(steps != usual, 1, 0), axis=1, keepdims=True)
    next_ref[...] = jnp.where(lane == 2 * K, odd, steps)


def chains(slots, lead, arrived):
    return pl.pallas_call(
        chains_kernel,
        out_shape=[
            jax.ShapeDtypeStruct((HALF, 2 * K), jnp.int32),
            jax.ShapeDtypeStruct((HALF, LANES), jnp.int32),
        ],
        in_specs=[SMEM, VMEM, VMEM],
        out_specs=[VMEM, VMEM],
        scratch_shapes=[pltpu.VMEM((HALF, LANES), jnp.int32)],
        name="chains",
    )(slots, lead, arrived)


def merge_kernel(place_ref, slots_ref, next_ref, lead_ref, *refs):
    parts, out, tiles, stage, sems = refs[:NG], refs[NG], refs[NG + 1], refs[NG + 2], refs[NG + 3]
    per = SLOTS // 2
    for t in range(per):
        span = slice(t * LANES, (t + 1) * LANES)
        for n in range(HALF):
            tiles[n * per + t] = lead_ref[n, :, span]
        for s in range(NG):
            for q in range(2):
                tiles[(HALF + 2 * s + q) * per + t] = parts[s][q, :, span]
    low = low_lanes((BLK, LANES))

    def save(n):
        return pltpu.make_async_copy(stage.at[n], out.at[n], sems.at[n])

    for n in range(HALF):
        spot = slots_ref[0, n]
        f = (HALF + ((place_ref[0] - (spot >> 1)) & (NG - 1)) * 2 + (spot & 1)) * per
        l = n * per
        first, second = tiles[l].astype(jnp.float32), tiles[f].astype(jnp.float32)
        stage[n, :, 0:LANES] = (first + pltpu.roll(second, BLK, 1)).astype(jnp.bfloat16)
        middle = tiles[l + per - 1].astype(jnp.float32) + second
        middle = middle + jnp.where(low, 0.0, pltpu.roll(first, BLK, 1))
        stage[n, :, 5 * LANES:6 * LANES] = middle.astype(jnp.bfloat16)
        for t in range(1, per - 1):
            stage[n, :, t * LANES:(t + 1) * LANES] = tiles[l + t]
        for t in range(1, per):
            stage[n, :, (5 + t) * LANES:(6 + t) * LANES] = tiles[f + t]

        @pl.when(next_ref[n, 2 * K] != 0)
        def _(n=n, f=f, l=l):
            plain = (next_ref[n, 0] == K) & (next_ref[n, K] == K)
            for s in range(2 * K):
                step = next_ref[n, s]
                skip = plain if s in (0, K) else step == 2 * K

                @pl.when(jnp.logical_not(skip))
                def _(s=s, step=step):
                    def block(t):
                        spot = jnp.where(t < K, t, t - K + 1)
                        value = tiles[jnp.where(t < K, l, f) + (spot >> 1)].astype(jnp.float32)
                        same = jnp.broadcast_to((spot & 1) == (place & 1), value.shape)
                        return jnp.where(same, value, pltpu.roll(value, BLK, 1))

                    place = s if s < K else s - K + 1

                    def more(carry):
                        return carry[0] != s

                    def add(carry):
                        t, total = carry
                        after = t + next_ref[n, t]
                        after = jnp.where(after >= 2 * K, after - 2 * K, after)
                        return after, total + block(t)

                    after = s + step
                    after = jnp.where(after >= 2 * K, after - 2 * K, after)
                    _, total = lax.while_loop(more, add, (after, block(jnp.int32(s))))
                    span = slice((s // 2) * LANES, (s // 2 + 1) * LANES)
                    keep = low if s % 2 == 0 else jnp.logical_not(low)
                    stage[n, :, span] = jnp.where(
                        keep, total, stage[n, :, span].astype(jnp.float32)
                    ).astype(jnp.bfloat16)

        save(n).start()
    for n in range(HALF):
        save(n).wait()


def merge(place, slots, after, lead, parts):
    return pl.pallas_call(
        merge_kernel,
        out_shape=jax.ShapeDtypeStruct((HALF, BLK, 2 * K * BLK), jnp.bfloat16),
        in_specs=[SMEM] * 3 + [VMEM] * (1 + NG),
        out_specs=pl.BlockSpec(memory_space=pl.ANY),
        scratch_shapes=[
            pltpu.VMEM((2 * HALF * SLOTS // 2, BLK, LANES), jnp.bfloat16),
            pltpu.VMEM((HALF, BLK, 2 * K * BLK), jnp.bfloat16),
            pltpu.SemaphoreType.DMA((HALF,)),
        ],
        compiler_params=LIMIT,
        name="merge",
    )(place, slots, after, lead, *parts)


def shift(value, axis, size, by):
    if by == 0:
        return value
    return lax.ppermute(value, axis, [(i, (i + by) % size) for i in range(size)])


def cross(value, b):
    by, flip = b // NC, b % NC
    pairs = [
        (x * NC + c, ((x + by) % NX) * NC + (c ^ flip)) for x in range(NX) for c in range(NC)
    ]
    return lax.ppermute(value, ("x", "core"), pairs)


def per_device(stiffness, prolongator, columns, fetch_rows, send_order, partner_slot):
    g, x, z, c = (lax.axis_index(name) for name in AXES)
    device = x * (NZ * NC) + z * NC + c
    place = jnp.stack([g, x, z, c]).astype(jnp.int32)
    own = prolongator.reshape(ROWS, 32, LANES)

    held = []
    for h in range(CHUNKS):
        piece = own[:, h * CK:(h + 1) * CK]
        got = {0: piece}
        for s in (4, 2, 6, 1, 7):
            got[s] = shift(piece, "z", NZ, s)
        got[5] = shift(got[4], "z", NZ, 1)
        got[3] = shift(got[4], "z", NZ, NZ - 1)
        held.append([got[s] for s in range(NZ)])

    lists = fetch_rows.reshape(NX, NZ, NC, C).transpose(0, 2, 1, 3).reshape(NX * NC, NZ * C)
    wanted = lax.all_to_all(lists, ("x", "core"), split_axis=0, concat_axis=0, tiled=True)

    sending, slots = send_order[0], partner_slot[0]
    eight = jnp.arange(HALF, dtype=jnp.int32)
    codes = jnp.sum(jnp.where(slots[:, None] == eight[None, :], (g * HALF + eight)[:, None], 0), axis=0)
    returned = lax.all_to_all(codes, "grp", split_axis=0, concat_axis=0, tiled=True)
    mine = jnp.sum(jnp.where(sending[:, None] == eight[None, :], returned[:, None], 0), axis=0)
    line = lax.all_to_all(
        jnp.broadcast_to(mine[None, :], (NZ, HALF)), "z", split_axis=0, concat_axis=0, tiled=True
    )
    plane = lax.all_to_all(
        jnp.broadcast_to(line.reshape(1, NZ * HALF), (NX * NC, NZ * HALF)),
        ("x", "core"), split_axis=0, concat_axis=0, tiled=True,
    )
    at, lead_labels, follower_labels = places(place, columns, fetch_rows, plane, mine, send_order)
    arrived_labels = lax.all_to_all(follower_labels, "grp", split_axis=0, concat_axis=0, tiled=True)
    labels, after = chains(partner_slot, lead_labels, arrived_labels)

    lane = jnp.arange(LANES, dtype=jnp.int32)
    inner = lane & (BLK - 1)
    source = (lane & BLK) + jnp.where(inner < 32, 2 * inner, 2 * (inner - 32) + 1)
    perm = (lane[:, None] == source[None, :]).astype(jnp.bfloat16)
    y = products(prolongator.reshape(ROWS, BLK, BLK), stiffness, perm)

    parts = []
    for h in range(CHUNKS):
        chosen = select(wanted, place, held[h])
        parts.append(chosen[0])
        moved = {b: cross(chosen[b], b) for b in (4, 5, 2, 3, 6, 7, 1)}
        parts += [moved[b] for b in range(1, NX * NC)]

    sent = followers(at, place, send_order, own, y, parts)
    arrived = [sent[0]] + [shift(sent[s], "grp", NG, s) for s in range(1, NG)]
    lead = leaders(at, own, y, parts)
    merged = merge(place, partner_slot, after, lead, arrived)
    return (merged, labels)


def solution(mesh):
    grid = Mesh(mesh.devices.reshape(NG, NX, NZ, NC), AXES)
    return jax.shard_map(
        per_device,
        mesh=grid,
        in_specs=(
            P(AXES, None, None),
            P(AXES, None),
            P(AXES, None),
            P(AXES, None),
            P(AXES, None),
            P(AXES, None),
        ),
        out_specs=(P(AXES, None, None), P(AXES, None)),
        check_vma=False,
    )
```

profile of v0, /device:TPU:2, one launch (start us, length us, event | category | flops | bytes accessed | tf_op | source)
XLA Modules:
  0.0 114.4 jit_solution(6365633862213859506)
XLA Ops:
  0.6 1.0 copy.23
  1.7 7.3 %collective-permute-start.2 = (bf16[16,32,128]{2,1,0:T(8,128)(2,1)S(1)}, bf16[16,32,128]{2,1,0:T(8,128)(2,1)S(1)}, u32[]{:S(2)}, u32[]{:S(2)}) collective-permute-start(bf16[16,32,128]{2,1,0:T(8,128)(2,1)S(1)} %bitcast.20), channel_id=1, source_target_pairs={{0,8},{2,10},{4,12},{6,14},{8,0},{10,2},{12,4},{14,6},{1,9},{3,11}... | collective-permute-start | bytes 393224 | tf_op jit(solution)/shard_map/ppermute | solution.py:336
  9.2 2.8 %collective-permute-start.1 = (bf16[16,32,128]{2,1,0:T(8,128)(2,1)S(1)}, bf16[16,32,128]{2,1,0:T(8,128)(2,1)S(1)}, u32[]{:S(2)}, u32[]{:S(2)}) collective-permute-start(bf16[16,32,128]{2,1,0:T(8,128)(2,1)S(1)} %bitcast.23), channel_id=1, source_target_pairs={{0,4},{2,6},{4,8},{6,10},{8,12},{10,14},{12,0},{14,2},{1,5},{3,7},... | collective-permute-start | bytes 393224 | tf_op jit(solution)/shard_map/ppermute | solution.py:336
  12.0 1.9 %collective-permute-start = (bf16[16,32,128]{2,1,0:T(8,128)(2,1)S(1)}, bf16[16,32,128]{2,1,0:T(8,128)(2,1)S(1)}, u32[]{:S(2)}, u32[]{:S(2)}) collective-permute-start(bf16[16,32,128]{2,1,0:T(8,128)(2,1)S(1)} %bitcast.24), channel_id=1, source_target_pairs={{0,2},{2,4},{4,6},{6,8},{8,10},{10,12},{12,14},{14,0},{1,3},{3,5},... | collective-permute-start | bytes 393224 | tf_op jit(solution)/shard_map/ppermute | solution.py:336
  13.9 2.8 %collective-permute-start.4 = (bf16[16,32,128]{2,1,0:T(8,128)(2,1)S(1)}, bf16[16,32,128]{2,1,0:T(8,128)(2,1)S(1)}, u32[]{:S(2)}, u32[]{:S(2)}) collective-permute-start(bf16[16,32,128]{2,1,0:T(8,128)(2,1)S(1)} %collective-permute-done.2.refs_4_), channel_id=1, source_target_pairs={{0,2},{2,4},{4,6},{6,8},{8,10},{10,12},{12,14},{14,0},{1,3},{3,5},... | collective-permute-start | bytes 393224 | tf_op jit(solution)/shard_map/ppermute | solution.py:336
  16.7 3.9 %collective-permute-done.6.refs_7_ = bf16[16,32,128]{2,1,0:T(8,128)(2,1)S(1)} collective-permute-done((bf16[16,32,128]{2,1,0:T(8,128)(2,1)S(1)}, bf16[16,32,128]{2,1,0:T(8,128)(2,1)S(1)}, u32[]{:S(2)}, u32[]{:S(2)}) %collective-permute-start.6) | collective-permute-done | bytes 131104 | tf_op jit(solution)/shard_map/ppermute | solution.py:336
  20.7 1.7 %collective-permute-start.3 = (bf16[16,32,128]{2,1,0:T(8,128)(2,1)S(1)}, bf16[16,32,128]{2,1,0:T(8,128)(2,1)S(1)}, u32[]{:S(2)}, u32[]{:S(2)}) collective-permute-start(bf16[16,32,128]{2,1,0:T(8,128)(2,1)S(1)} %collective-permute-done.2.refs_4_), channel_id=1, source_target_pairs={{0,14},{2,0},{4,2},{6,4},{8,6},{10,8},{12,10},{14,12},{1,15},{3,1}... | collective-permute-start | bytes 393224 | tf_op jit(solution)/shard_map/ppermute | solution.py:336
  23.9 4.8 %all-to-all-start.4 = ((s32[8,1,32]{2,1,0:T(1,128)}), s32[8,1,32]{2,1,0:T(1,128)S(1)}, u32[]{:S(2)}, u32[]{:S(2)}) async-start(s32[8,1,32]{2,1,0:T(1,128)} %bitcast.12), calls=%async_computation.4 | async-start | bytes 8192 | tf_op jit(solution)/shard_map/all_to_all | solution.py:364
  28.8 3.7 %all-to-all-done.4 = s32[8,1,32]{2,1,0:T(1,128)S(1)} async-done(((s32[8,1,32]{2,1,0:T(1,128)}), s32[8,1,32]{2,1,0:T(1,128)S(1)}, u32[]{:S(2)}, u32[]{:S(2)}) %all-to-all-start.4) | async-done | bytes 1056 | tf_op jit(solution)/shard_map/all_to_all | solution.py:364
  32.5 2.2 %select.1 = (bf16[32,32,128]{2,1,0:T(8,128)(2,1)S(1)}, bf16[32,32,128]{2,1,0:T(8,128)(2,1)S(1)}, bf16[32,32,128]{2,1,0:T(8,128)(2,1)S(1)}, bf16[32,32,128]{2,1,0...) custom-call(s32[8,32]{1,0:T(8,128)S(1)} %bitcast.28, ...), custom_call_target="tpu_custom_call" | custom-call | tf_op jit(solution)/shard_map/select/pallas_call | solution.py:74
  36.7 4.5 %all-to-all-start = ((s32[4,2,1]{1,2,0:T(1,128)}), s32[4,2,1]{1,2,0:T(1,128)S(1)}, u32[]{:S(2)}, u32[]{:S(2)}) async-start(s32[4,2,1]{1,2,0:T(1,128)} %bitcast.6), calls=%async_computation | async-start | bytes 4096 | tf_op jit(solution)/shard_map/all_to_all | solution.py:369
  41.1 5.2 %all-to-all-done = s32[4,2,1]{1,2,0:T(1,128)S(1)} async-done(((s32[4,2,1]{1,2,0:T(1,128)}), s32[4,2,1]{1,2,0:T(1,128)S(1)}, u32[]{:S(2)}, u32[]{:S(2)}) %all-to-all-start) | async-done | bytes 64 | tf_op jit(solution)/shard_map/all_to_all | solution.py:369
  47.7 3.1 %collective-permute-start.10 = (bf16[32,32,128]{2,1,0:T(8,128)(2,1)}, bf16[32,32,128]{2,1,0:T(8,128)(2,1)}, u32[]{:S(2)}, u32[]{:S(2)}) collective-permute-start(bf16[32,32,128]{2,1,0:T(8,128)(2,1)} %get-tuple-element.27), channel_id=1, source_target_pairs={{0,32},{1,33},{16,48},{17,49},{32,0},{33,1},{48,16},{49,17},{2,34}... | collective-permute-start | bytes 786440 | tf_op jit(solution)/shard_map/ppermute | solution.py:344
  50.8 1.4 %collective-permute-start.11 = (bf16[32,32,128]{2,1,0:T(8,128)(2,1)}, bf16[32,32,128]{2,1,0:T(8,128)(2,1)}, u32[]{:S(2)}, u32[]{:S(2)}) collective-permute-start(bf16[32,32,128]{2,1,0:T(8,128)(2,1)} %get-tuple-element.28), channel_id=1, source_target_pairs={{0,33},{1,32},{16,49},{17,48},{32,1},{33,0},{48,17},{49,16},{2,35}... | collective-permute-start | bytes 786440 | tf_op jit(solution)/shard_map/ppermute | solution.py:344
  52.1 0.9 collective-permute-start.12
  53.8 1.9 %collective-permute-start.13 = (bf16[32,32,128]{2,1,0:T(8,128)(2,1)}, bf16[32,32,128]{2,1,0:T(8,128)(2,1)}, u32[]{:S(2)}, u32[]{:S(2)}) collective-permute-start(bf16[32,32,128]{2,1,0:T(8,128)(2,1)} %get-tuple-element.30), channel_id=1, source_target_pairs={{0,49},{1,48},{16,1},{17,0},{32,17},{33,16},{48,33},{49,32},{2,51}... | collective-permute-start | bytes 786440 | tf_op jit(solution)/shard_map/ppermute | solution.py:344
  56.9 4.2 %all-to-all-start.1 = ((s32[8,1,8]{2,1,0:T(1,128)}), s32[8,1,8]{2,1,0:T(1,128)S(1)}, u32[]{:S(2)}, u32[]{:S(2)}) async-start(s32[8,1,8]{2,1,0:T(1,128)} %broadcast_in_dim.43), calls=%async_computation.1 | async-start | bytes 8192 | tf_op jit(solution)/shard_map/all_to_all | solution.py:371
  61.7 1.0 reshape.59.p_ref
  62.7 6.0 %all-to-all-done.1 = s32[8,1,8]{2,1,0:T(1,128)S(1)} async-done(((s32[8,1,8]{2,1,0:T(1,128)}), s32[8,1,8]{2,1,0:T(1,128)S(1)}, u32[]{:S(2)}, u32[]{:S(2)}) %all-to-all-start.1) | async-done | bytes 288 | tf_op jit(solution)/shard_map/all_to_all | solution.py:371
  70.1 3.7 %all-to-all-start.2 = ((s32[8,1,64]{2,1,0:T(1,128)}), s32[8,1,64]{2,1,0:T(1,128)S(1)}, u32[]{:S(2)}, u32[]{:S(2)}) async-start(s32[8,1,64]{2,1,0:T(1,128)} %broadcast_in_dim.45), calls=%async_computation.2 | async-start | bytes 8192 | tf_op jit(solution)/shard_map/all_to_all | solution.py:374
  73.8 0.9 copy-done.5
  75.5 4.8 %products.1.y_ref = bf16[16,64,768]{2,1,0:T(8,128)(2,1)S(1)} custom-call(bf16[16,64,64]{2,1,0:T(8,128)(2,1)S(1)} %copy-done.5, bf16[16,64,704]{2,1,0:T(8,128)(2,1)S(1)} %copy-done, bf16[128,128]{1,0:T(8,128)(2,1)S(1)} %copy-done.6), custom_call_target="tpu_custom_call" | custom-call | flops 301989888 | bytes 3200000 | tf_op jit(solution)/shard_map/products/pallas_call | solution.py:50
  81.0 5.5 %places.1 = (s32[16,12]{1,0:T(8,128)}, s32[8,11]{1,0:T(8,128)}, s32[8,11]{1,0:T(8,128)}) custom-call(s32[4]{0:T(128)} %copy-done.9, s32[16,11]{1,0:T(8,128)} %columns_ref.1, s32[64,4]{1,0:T(8,128)} %copy-done.16, s32[8,64]{1,0:T(8,128)} %bitcast.33, s32[8]{0:T(128)} %copy-done.19, s32[1,8]{1,0:T(1,128)} %send_ref.3), custom_call_target="tpu_custom_call" | custom-call | tf_op jit(solution)/shard_map/places/pallas_call | solution.py:207
  86.6 0.9 copy-done.2
  87.5 0.9 copy-done.4
  89.8 2.6 %followers.1 = (bf16[2,64,768]{2,1,0:T(8,128)(2,1)S(1)}, bf16[2,64,768]{2,1,0:T(8,128)(2,1)}, bf16[2,64,768]{2,1,0:T(8,128)(2,1)}, bf16[2,64,768]{2,1,0:T(8,128)(2,1)S(1)}) custom-call(s32[16,12]{1,0:T(8,128)S(1)} %copy-done.7, s32[4]{0:T(128)S(1)} %copy-done.10, s32[1,8]{1,0:T(1,128)S(1)} %copy-done.13, bf16[16,32,128]{2,1,0:T(8,128)(2,1)S(1)} %bitcast.26, ...), custom_call_target="tpu_custom_call" | custom-call | flops 100663296 | bytes 5000000 | tf_op jit(solution)/shard_map/followers/pallas_call | solution.py:147
  93.0 2.1 %collective-permute-start.15 = (bf16[2,64,768]{2,1,0:T(8,128)(2,1)}, bf16[2,64,768]{2,1,0:T(8,128)(2,1)S(1)}, u32[]{:S(2)}, u32[]{:S(2)}) collective-permute-start(bf16[2,64,768]{2,1,0:T(8,128)(2,1)} %get-tuple-element.33), channel_id=1, source_target_pairs={{0,128},{64,192},{128,0},{192,64},{1,129},{65,193},{129,1},{193,65... | collective-permute-start | bytes 589832 | tf_op jit(solution)/shard_map/ppermute | solution.py:336
  95.0 1.2 %collective-permute-start.16 = (bf16[2,64,768]{2,1,0:T(8,128)(2,1)S(1)}, bf16[2,64,768]{2,1,0:T(8,128)(2,1)S(1)}, u32[]{:S(2)}, u32[]{:S(2)}) collective-permute-start(bf16[2,64,768]{2,1,0:T(8,128)(2,1)S(1)} %get-tuple-element.34), channel_id=1, source_target_pairs={{0,192},{64,0},{128,64},{192,128},{1,193},{65,1},{129,65},{193,129... | collective-permute-start | bytes 589832 | tf_op jit(solution)/shard_map/ppermute | solution.py:336
  96.2 9.5 %all_to_all.45 = s32[4,2,11]{2,1,0:T(2,128)} all-to-all(s32[4,2,11]{2,1,0:T(2,128)S(1)} %bitcast.35), channel_id=1, replica_groups=mesh['grp'=4,'x'=4,'z'=8,'core'=2] {'grp'}, dimensions={0} | all-to-all | bytes 704 | tf_op jit(solution)/shard_map/all_to_all | solution.py:379
  105.8 1.7 %chains.1 = (s32[8,22]{1,0:T(8,128)}, s32[8,128]{1,0:T(8,128)}) custom-call(s32[1,8]{1,0:T(1,128)} %slots_ref.3, s32[8,11]{1,0:T(8,128)} %get-tuple-element.19.lead_ref, s32[8,11]{1,0:T(8,128)} %bitcast.34), custom_call_target="tpu_custom_call" | custom-call | tf_op jit(solution)/shard_map/chains/pallas_call | solution.py:235
  107.5 3.4 %leaders.1.lead_ref = bf16[8,64,768]{2,1,0:T(8,128)(2,1)S(1)} custom-call(s32[16,12]{1,0:T(8,128)S(1)} %copy-done.8, bf16[16,32,128]{2,1,0:T(8,128)(2,1)S(1)} %bitcast.27, bf16[16,64,768]{2,1,0:T(8,128)(2,1)S(1)} %products.1.y_ref, bf16[32,32,128]{2,1,0:T(8,128)(2,1)S(1)} %get-tuple-element.23.refs_0_, bf16[32,32,128]{2,1,0:T(8,128)(2,1)S(1)} %copy-done.2, ...), custom_call_target="tpu_custom_call" | custom-call | flops 100663296 | bytes 5000000 | tf_op jit(solution)/shard_map/leaders/pallas_call | solution.py:160
  111.0 3.2 %merge.1 = bf16[8,64,1408]{2,1,0:T(8,128)(2,1)} custom-call(s32[4]{0:T(128)S(1)} %copy-done.11, s32[1,8]{1,0:T(1,128)S(1)} %copy-done.14, s32[8,128]{1,0:T(8,128)S(1)} %copy-done.12, bf16[8,64,768]{2,1,0:T(8,128)(2,1)S(1)} %leaders.1.lead_ref, bf16[2,64,768]{2,1,0:T(8,128)(2,1)S(1)} %get-tuple-element.31.refs_0_, ...), custom_call_target="tpu_custom_call" | custom-call | tf_op jit(solution)/shard_map/merge/pallas_call | solution.py:318
  (77 shorter events, 12.4 us)
Async XLA Ops:
  0.6 61.1 %copy-start.15 = (bf16[16,4096]{1,0:T(8,128)(2,1)S(1)}, bf16[16,4096]{1,0:T(8,128)(2,1)}, u32[]{:S(2)}) copy-start(bf16[16,4096]{1,0:T(8,128)(2,1)} %param.7) | copy-start | bytes 393220
  0.6 73.2 %copy-start = (bf16[16,64,704]{2,1,0:T(8,128)(2,1)S(1)}, bf16[16,64,704]{2,1,0:T(8,128)(2,1)}, u32[]{:S(2)}) copy-start(bf16[16,64,704]{2,1,0:T(8,128)(2,1)} %a_ref.1) | copy-start | bytes 4325380
  1.7 12.2 %collective-permute-start.2 = (bf16[16,32,128]{2,1,0:T(8,128)(2,1)S(1)}, bf16[16,32,128]{2,1,0:T(8,128)(2,1)S(1)}, u32[]{:S(2)}, u32[]{:S(2)}) collective-permute-start(bf16[16,32,128]{2,1,0:T(8,128)(2,1)S(1)} %bitcast.20), channel_id=1, source_target_pairs={{0,8},{2,10},{4,12},{6,14},{8,0},{10,2},{12,4},{14,6},{1,9},{3,11}... | collective-permute-start | bytes 393224 | tf_op jit(solution)/shard_map/ppermute | solution.py:336
  9.0 11.7 %collective-permute-start.6 = (bf16[16,32,128]{2,1,0:T(8,128)(2,1)S(1)}, bf16[16,32,128]{2,1,0:T(8,128)(2,1)S(1)}, u32[]{:S(2)}, u32[]{:S(2)}) collective-permute-start(bf16[16,32,128]{2,1,0:T(8,128)(2,1)S(1)} %bitcast.21), channel_id=1, source_target_pairs={{0,14},{2,0},{4,2},{6,4},{8,6},{10,8},{12,10},{14,12},{1,15},{3,1}... | collective-permute-start | bytes 393224 | tf_op jit(solution)/shard_map/ppermute | solution.py:336
  9.1 23.3 %collective-permute-start.5 = (bf16[16,32,128]{2,1,0:T(8,128)(2,1)S(1)}, bf16[16,32,128]{2,1,0:T(8,128)(2,1)S(1)}, u32[]{:S(2)}, u32[]{:S(2)}) collective-permute-start(bf16[16,32,128]{2,1,0:T(8,128)(2,1)S(1)} %bitcast.22), channel_id=1, source_target_pairs={{0,12},{2,14},{4,0},{6,2},{8,4},{10,6},{12,8},{14,10},{1,13},{3,15... | collective-permute-start | bytes 393224 | tf_op jit(solution)/shard_map/ppermute | solution.py:336
  9.2 23.2 %collective-permute-start.1 = (bf16[16,32,128]{2,1,0:T(8,128)(2,1)S(1)}, bf16[16,32,128]{2,1,0:T(8,128)(2,1)S(1)}, u32[]{:S(2)}, u32[]{:S(2)}) collective-permute-start(bf16[16,32,128]{2,1,0:T(8,128)(2,1)S(1)} %bitcast.23), channel_id=1, source_target_pairs={{0,4},{2,6},{4,8},{6,10},{8,12},{10,14},{12,0},{14,2},{1,5},{3,7},... | collective-permute-start | bytes 393224 | tf_op jit(solution)/shard_map/ppermute | solution.py:336
  12.0 20.4 %collective-permute-start = (bf16[16,32,128]{2,1,0:T(8,128)(2,1)S(1)}, bf16[16,32,128]{2,1,0:T(8,128)(2,1)S(1)}, u32[]{:S(2)}, u32[]{:S(2)}) collective-permute-start(bf16[16,32,128]{2,1,0:T(8,128)(2,1)S(1)} %bitcast.24), channel_id=1, source_target_pairs={{0,2},{2,4},{4,6},{6,8},{8,10},{10,12},{12,14},{14,0},{1,3},{3,5},... | collective-permute-start | bytes 393224 | tf_op jit(solution)/shard_map/ppermute | solution.py:336
  13.9 18.5 %collective-permute-start.4 = (bf16[16,32,128]{2,1,0:T(8,128)(2,1)S(1)}, bf16[16,32,128]{2,1,0:T(8,128)(2,1)S(1)}, u32[]{:S(2)}, u32[]{:S(2)}) collective-permute-start(bf16[16,32,128]{2,1,0:T(8,128)(2,1)S(1)} %collective-permute-done.2.refs_4_), channel_id=1, source_target_pairs={{0,2},{2,4},{4,6},{6,8},{8,10},{10,12},{12,14},{14,0},{1,3},{3,5},... | collective-permute-start | bytes 393224 | tf_op jit(solution)/shard_map/ppermute | solution.py:336
  20.7 11.8 %collective-permute-start.3 = (bf16[16,32,128]{2,1,0:T(8,128)(2,1)S(1)}, bf16[16,32,128]{2,1,0:T(8,128)(2,1)S(1)}, u32[]{:S(2)}, u32[]{:S(2)}) collective-permute-start(bf16[16,32,128]{2,1,0:T(8,128)(2,1)S(1)} %collective-permute-done.2.refs_4_), channel_id=1, source_target_pairs={{0,14},{2,0},{4,2},{6,4},{8,6},{10,8},{12,10},{14,12},{1,15},{3,1}... | collective-permute-start | bytes 393224 | tf_op jit(solution)/shard_map/ppermute | solution.py:336
  23.2 9.3 %copy-start.16 = (s32[64,4]{1,0:T(8,128)}, s32[64,4]{1,0:T(8,128)S(1)}, u32[]{:S(2)}) copy-start(s32[64,4]{1,0:T(8,128)S(1)} %copy.19.fetch_ref) | copy-start | bytes 3076
  23.9 8.6 %all-to-all-start.4 = ((s32[8,1,32]{2,1,0:T(1,128)}), s32[8,1,32]{2,1,0:T(1,128)S(1)}, u32[]{:S(2)}, u32[]{:S(2)}) async-start(s32[8,1,32]{2,1,0:T(1,128)} %bitcast.12), calls=%async_computation.4 | async-start | bytes 8192 | tf_op jit(solution)/shard_map/all_to_all | solution.py:364
  28.8 51.6 %copy-start.9 = (s32[4]{0:T(128)}, s32[4]{0:T(128)S(1)}, u32[]{:S(2)}) copy-start(s32[4]{0:T(128)S(1)} %pad_add_fusion.place_ref) | copy-start | bytes 52
  34.7 17.4 %collective-permute-start.7 = (bf16[32,32,128]{2,1,0:T(8,128)(2,1)S(1)}, bf16[32,32,128]{2,1,0:T(8,128)(2,1)S(1)}, u32[]{:S(2)}, u32[]{:S(2)}) collective-permute-start(bf16[32,32,128]{2,1,0:T(8,128)(2,1)S(1)} %get-tuple-element.24), channel_id=1, source_target_pairs={{0,1},{1,0},{16,17},{17,16},{32,33},{33,32},{48,49},{49,48},{2,3},... | collective-permute-start | bytes 786440 | tf_op jit(solution)/shard_map/ppermute | solution.py:344
  34.7 18.4 %collective-permute-start.8 = (bf16[32,32,128]{2,1,0:T(8,128)(2,1)S(1)}, bf16[32,32,128]{2,1,0:T(8,128)(2,1)S(1)}, u32[]{:S(2)}, u32[]{:S(2)}) collective-permute-start(bf16[32,32,128]{2,1,0:T(8,128)(2,1)S(1)} %get-tuple-element.25), channel_id=1, source_target_pairs={{0,16},{1,17},{16,32},{17,33},{32,48},{33,49},{48,0},{49,1},{2,18}... | collective-permute-start | bytes 786440 | tf_op jit(solution)/shard_map/ppermute | solution.py:344
  36.7 9.6 %all-to-all-start = ((s32[4,2,1]{1,2,0:T(1,128)}), s32[4,2,1]{1,2,0:T(1,128)S(1)}, u32[]{:S(2)}, u32[]{:S(2)}) async-start(s32[4,2,1]{1,2,0:T(1,128)} %bitcast.6), calls=%async_computation | async-start | bytes 4096 | tf_op jit(solution)/shard_map/all_to_all | solution.py:369
  47.7 38.8 %collective-permute-start.9 = (bf16[32,32,128]{2,1,0:T(8,128)(2,1)}, bf16[32,32,128]{2,1,0:T(8,128)(2,1)}, u32[]{:S(2)}, u32[]{:S(2)}) collective-permute-start(bf16[32,32,128]{2,1,0:T(8,128)(2,1)} %get-tuple-element.26), channel_id=1, source_target_pairs={{0,17},{1,16},{16,33},{17,32},{32,49},{33,48},{48,1},{49,0},{2,19}... | collective-permute-start | bytes 786440 | tf_op jit(solution)/shard_map/ppermute | solution.py:344
  47.7 38.8 %collective-permute-start.10 = (bf16[32,32,128]{2,1,0:T(8,128)(2,1)}, bf16[32,32,128]{2,1,0:T(8,128)(2,1)}, u32[]{:S(2)}, u32[]{:S(2)}) collective-permute-start(bf16[32,32,128]{2,1,0:T(8,128)(2,1)} %get-tuple-element.27), channel_id=1, source_target_pairs={{0,32},{1,33},{16,48},{17,49},{32,0},{33,1},{48,16},{49,17},{2,34}... | collective-permute-start | bytes 786440 | tf_op jit(solution)/shard_map/ppermute | solution.py:344
  50.8 35.8 %collective-permute-start.11 = (bf16[32,32,128]{2,1,0:T(8,128)(2,1)}, bf16[32,32,128]{2,1,0:T(8,128)(2,1)}, u32[]{:S(2)}, u32[]{:S(2)}) collective-permute-start(bf16[32,32,128]{2,1,0:T(8,128)(2,1)} %get-tuple-element.28), channel_id=1, source_target_pairs={{0,33},{1,32},{16,49},{17,48},{32,1},{33,0},{48,17},{49,16},{2,35}... | collective-permute-start | bytes 786440 | tf_op jit(solution)/shard_map/ppermute | solution.py:344
  52.1 18.0 %copy-start.1 = (bf16[32,32,128]{2,1,0:T(8,128)(2,1)}, bf16[32,32,128]{2,1,0:T(8,128)(2,1)S(1)}, u32[]{:S(2)}) copy-start(bf16[32,32,128]{2,1,0:T(8,128)(2,1)S(1)} %collective-permute-done.7.refs_1_) | copy-start | bytes 786436
  52.1 34.4 %collective-permute-start.12 = (bf16[32,32,128]{2,1,0:T(8,128)(2,1)}, bf16[32,32,128]{2,1,0:T(8,128)(2,1)}, u32[]{:S(2)}, u32[]{:S(2)}) collective-permute-start(bf16[32,32,128]{2,1,0:T(8,128)(2,1)} %get-tuple-element.29), channel_id=1, source_target_pairs={{0,48},{1,49},{16,0},{17,1},{32,16},{33,17},{48,32},{49,33},{2,50}... | collective-permute-start | bytes 786440 | tf_op jit(solution)/shard_map/ppermute | solution.py:344
  53.8 32.8 %collective-permute-start.13 = (bf16[32,32,128]{2,1,0:T(8,128)(2,1)}, bf16[32,32,128]{2,1,0:T(8,128)(2,1)}, u32[]{:S(2)}, u32[]{:S(2)}) collective-permute-start(bf16[32,32,128]{2,1,0:T(8,128)(2,1)} %get-tuple-element.30), channel_id=1, source_target_pairs={{0,49},{1,48},{16,1},{17,0},{32,17},{33,16},{48,33},{49,32},{2,51}... | collective-permute-start | bytes 786440 | tf_op jit(solution)/shard_map/ppermute | solution.py:344
  56.3 24.0 %copy-start.19 = (s32[8]{0:T(128)}, s32[8]{0:T(128)S(1)}, u32[]{:S(2)}) copy-start(s32[8]{0:T(128)S(1)} %select_reduce_fusion.mine_ref) | copy-start | bytes 100
  56.9 11.8 %all-to-all-start.1 = ((s32[8,1,8]{2,1,0:T(1,128)}), s32[8,1,8]{2,1,0:T(1,128)S(1)}, u32[]{:S(2)}, u32[]{:S(2)}) async-start(s32[8,1,8]{2,1,0:T(1,128)} %broadcast_in_dim.43), calls=%async_computation.1 | async-start | bytes 8192 | tf_op jit(solution)/shard_map/all_to_all | solution.py:371
  70.1 10.2 %all-to-all-start.2 = ((s32[8,1,64]{2,1,0:T(1,128)}), s32[8,1,64]{2,1,0:T(1,128)S(1)}, u32[]{:S(2)}, u32[]{:S(2)}) async-start(s32[8,1,64]{2,1,0:T(1,128)} %broadcast_in_dim.45), calls=%async_computation.2 | async-start | bytes 8192 | tf_op jit(solution)/shard_map/all_to_all | solution.py:374
  75.5 11.0 %copy-start.13 = (s32[1,8]{1,0:T(1,128)S(1)}, s32[1,8]{1,0:T(1,128)}, u32[]{:S(2)}) copy-start(s32[1,8]{1,0:T(1,128)} %send_ref.3) | copy-start | bytes 100
  89.8 6.4 %copy-start.18 = (s32[8,11]{1,0:T(8,128)S(1)}, s32[8,11]{1,0:T(8,128)}, u32[]{:S(2)}) copy-start(s32[8,11]{1,0:T(8,128)} %get-tuple-element.20) | copy-start | bytes 1060
  89.8 17.7 %copy-start.8 = (s32[16,12]{1,0:T(8,128)S(1)}, s32[16,12]{1,0:T(8,128)}, u32[]{:S(2)}) copy-start(s32[16,12]{1,0:T(8,128)} %get-tuple-element.22.at_ref) | copy-start | bytes 2308
  92.4 18.5 %collective-permute-start.14 = (bf16[2,64,768]{2,1,0:T(8,128)(2,1)}, bf16[2,64,768]{2,1,0:T(8,128)(2,1)S(1)}, u32[]{:S(2)}, u32[]{:S(2)}) collective-permute-start(bf16[2,64,768]{2,1,0:T(8,128)(2,1)} %get-tuple-element.32), channel_id=1, source_target_pairs={{0,64},{64,128},{128,192},{192,0},{1,65},{65,129},{129,193},{193,1... | collective-permute-start | bytes 589832 | tf_op jit(solution)/shard_map/ppermute | solution.py:336
  93.0 17.9 %collective-permute-start.15 = (bf16[2,64,768]{2,1,0:T(8,128)(2,1)}, bf16[2,64,768]{2,1,0:T(8,128)(2,1)S(1)}, u32[]{:S(2)}, u32[]{:S(2)}) collective-permute-start(bf16[2,64,768]{2,1,0:T(8,128)(2,1)} %get-tuple-element.33), channel_id=1, source_target_pairs={{0,128},{64,192},{128,0},{192,64},{1,129},{65,193},{129,1},{193,65... | collective-permute-start | bytes 589832 | tf_op jit(solution)/shard_map/ppermute | solution.py:336
  95.0 15.9 %collective-permute-start.16 = (bf16[2,64,768]{2,1,0:T(8,128)(2,1)S(1)}, bf16[2,64,768]{2,1,0:T(8,128)(2,1)S(1)}, u32[]{:S(2)}, u32[]{:S(2)}) collective-permute-start(bf16[2,64,768]{2,1,0:T(8,128)(2,1)S(1)} %get-tuple-element.34), channel_id=1, source_target_pairs={{0,192},{64,0},{128,64},{192,128},{1,193},{65,1},{129,65},{193,129... | collective-permute-start | bytes 589832 | tf_op jit(solution)/shard_map/ppermute | solution.py:336
  107.4 3.5 %copy-start.12 = (s32[8,128]{1,0:T(8,128)S(1)}, s32[8,128]{1,0:T(8,128)}, u32[]{:S(2)}) copy-start(s32[8,128]{1,0:T(8,128)} %get-tuple-element.21.next_ref) | copy-start | bytes 12292
  107.4 3.5 %copy-start.14 = (s32[1,8]{1,0:T(1,128)S(1)}, s32[1,8]{1,0:T(1,128)}, u32[]{:S(2)}) copy-start(s32[1,8]{1,0:T(1,128)} %slots_ref.3) | copy-start | bytes 100
  (9 other events, 9.7 us)
where the time goes:
time: 115 us; the launch traced here: 114 us
  starting transfers between devices  45.5 us (40%)
  Pallas kernels  23.6 us (21%)
  waiting for transfers between devices  18.8 us (16%)
  local copies, waits for them, and re-layouts  12.3 us (11%)
  blocking collectives  9.54 us (8%)
  other arithmetic  3.59 us (3%)
    ppermute x10, starting transfers between devices, shift(): lax.ppermute(value, axis, [(i, (i + by) % size) for i in range(size)])  20.6 us
    all_to_all x1, blocking collectives, per_device(): lax.all_to_all(follower_labels, 'grp', split_axis=0, concat_axis=0, tiled...  9.54 us
    unnamed x42, local copies, waits for them, and re-layouts  8.05 us
    ppermute x7, starting transfers between devices, cross(): return lax.ppermute(value, ('x', 'core'), pairs)  7.77 us
    all_to_all x1, waiting for transfers between devices, per_device(): lax.all_to_all(jnp.broadcast_to(mine[None, :], (NZ, HALF)), 'z', split_ax...  6.03 us
    pallas_call x1, Pallas kernels, places(): pl.pallas_call(places_kernel, out_shape=[jax.ShapeDtypeStruct((ROWS, SLOT...  5.54 us
    all_to_all x1, waiting for transfers between devices, per_device(): lax.all_to_all(codes, 'grp', split_axis=0, concat_axis=0, tiled=True)  5.17 us
    all_to_all x1, starting transfers between devices, per_device(): lax.all_to_all(lists, ('x', 'core'), split_axis=0, concat_axis=0, tiled=T...  4.83 us
  transfers between devices with their start and end apart: 21, of which 4 were waited for; matrix products, arithmetic and copies ran while one was open for 6% of the time, Pallas kernels for 14%

commit v1 on v0

v1 whole, which is shorter than its diff:
```python
import jax
import jax.numpy as jnp
from jax import lax
from jax.experimental import pallas as pl
from jax.experimental.pallas import tpu as pltpu
from jax.sharding import Mesh, PartitionSpec as P

BLK = 64
K = 11
C = 4
ROWS = 16
HALF = 8
NG, NX, NZ, NC = 4, 4, 8, 2
N_DEV = NX * NZ * NC
LANES = 128
SLOTS = 12
WIDE = SLOTS * BLK
TABLE = N_DEV * C
CHUNKS = 1
CK = 32 // CHUNKS
AXES = ("grp", "x", "z", "core")
ORDER = (1, 2, 4, 5, 6, 3, 7, 0)

VMEM = pl.BlockSpec(memory_space=pltpu.VMEM)
SMEM = pl.BlockSpec(memory_space=pltpu.SMEM)
LIMIT = pltpu.CompilerParams(vmem_limit_bytes=12 * 1024 * 1024)


def low_lanes(shape):
    return lax.broadcasted_iota(jnp.int32, shape, 1) < BLK


def products_kernel(p_ref, a_ref, perm_ref, y_ref):
    def row(i, carry):
        y = lax.dot_general(
            p_ref[i], a_ref[i], (((0,), (0,)), ((), ())), preferred_element_type=jnp.float32
        )
        y = jnp.concatenate([y, jnp.zeros((BLK, BLK), jnp.float32)], axis=1)
        y = jnp.where(i < HALF, y, pltpu.roll(y, BLK, 1)).astype(jnp.bfloat16)
        for t in range(WIDE // LANES):
            span = slice(t * LANES, (t + 1) * LANES)
            y_ref[i, :, span] = jnp.dot(
                y[:, span], perm_ref[...], preferred_element_type=jnp.float32
            ).astype(jnp.bfloat16)
        return carry

    lax.fori_loop(0, ROWS, row, 0, unroll=4)


def products(blocks, stiffness, perm):
    return pl.pallas_call(
        products_kernel,
        out_shape=jax.ShapeDtypeStruct((ROWS, BLK, WIDE), jnp.bfloat16),
        compiler_params=LIMIT,
        cost_estimate=pl.CostEstimate(
            flops=2 * ROWS * BLK * BLK * WIDE * 3, bytes_accessed=3_200_000, transcendentals=0
        ),
        name="products",
    )(blocks, stiffness, perm)


def select_kernel(wanted_ref, place_ref, *refs):
    held, outs = refs[:NZ], refs[NZ:]
    x, z, c = place_ref[1], place_ref[2], place_ref[3]
    for i, b in enumerate(ORDER):
        target = ((x + b // NC) & (NX - 1)) * NC + (c ^ (b % NC))
        for s in range(NZ):
            home = ((z - s) & (NZ - 1)) * C
            for m in range(C):
                outs[i][home + m] = held[s][wanted_ref[target, home + m]]


def select(wanted, place, held):
    shape = jax.ShapeDtypeStruct((NZ * C, CK, LANES), jnp.bfloat16)
    return pl.pallas_call(
        select_kernel,
        out_shape=[shape] * (NX * NC),
        in_specs=[SMEM, SMEM] + [VMEM] * NZ,
        out_specs=[VMEM] * (NX * NC),
        compiler_params=LIMIT,
        name="select",
    )(wanted, place, *held)


def fill(table, own_ref, parts, sems):
    n = NX * NC
    copies = []
    for h in range(CHUNKS):
        for b in range(n):
            spot = table.at[pl.ds(b * NZ * C, NZ * C), pl.ds(h * CK, CK)]
            copies.append(pltpu.make_async_copy(parts[h * n + b], spot, sems.at[h * n + b]))
    for copy in copies:
        copy.start()
    table[TABLE:TABLE + ROWS] = own_ref[...]
    table[TABLE + ROWS] = jnp.zeros((32, LANES), jnp.bfloat16)
    for copy in copies:
        copy.wait()


def row_tiles(i, table, at_ref, y_ref, emit):
    low = low_lanes((32, LANES))
    zero = jnp.zeros((32, LANES), jnp.bfloat16)
    for t in range(SLOTS // 2):
        a = table[at_ref[i, 2 * t]]
        b = table[at_ref[i, 2 * t + 1]]
        rhs = jnp.concatenate([
            jnp.where(low, a, zero),
            jnp.where(low, pltpu.roll(a, BLK, 1), zero),
            jnp.where(low, zero, pltpu.roll(b, BLK, 1)),
            jnp.where(low, zero, b),
        ], axis=0)
        span = slice(t * LANES, (t + 1) * LANES)
        emit(span, jnp.dot(
            y_ref[i, :, span], rhs, preferred_element_type=jnp.float32
        ).astype(jnp.bfloat16))


def follower_kernel(at_ref, place_ref, send_ref, own_ref, y_ref, labels_ref, *refs):
    n = NX * NC * CHUNKS
    parts, outs, table, sems = refs[:n], refs[n:n + NG], refs[n + NG], refs[n + NG + 1]
    fill(table, own_ref, parts, sems)
    for s in range(NG):
        target = (place_ref[0] + s) & (NG - 1)
        for q in range(2):
            spot = target * 2 + q
            row = HALF + send_ref[0, spot]

            def emit(span, value, s=s, q=q):
                outs[s][q, :, span] = value

            row_tiles(row, table, at_ref, y_ref, emit)
            label = labels_ref[pl.ds(spot, 1), :]
            outs[s][q, 0:1, 0:K] = (label >> 4).astype(jnp.float32).astype(jnp.bfloat16)
            outs[s][q, 16:17, 0:K] = (label & 15).astype(jnp.float32).astype(jnp.bfloat16)


def leader_kernel(at_ref, y_ref, table, out):
    def row(i, carry):
        def emit(span, value):
            out[i, :, span] = value

        row_tiles(i, table, at_ref, y_ref, emit)
        return carry

    lax.fori_loop(0, HALF, row, 0)


ROW_COST = pl.CostEstimate(flops=2 * 8 * 6 * BLK * LANES * LANES, bytes_accessed=5_000_000, transcendentals=0)
ANY = pl.BlockSpec(memory_space=pltpu.HBM)


def followers(at, place, send, own, y, labels, parts):
    shape = jax.ShapeDtypeStruct((2, BLK, WIDE), jnp.bfloat16)
    table = jax.ShapeDtypeStruct((TABLE + ROWS + 1, 32, LANES), jnp.bfloat16)
    return pl.pallas_call(
        follower_kernel,
        out_shape=[shape] * NG + [table],
        in_specs=[SMEM] * 3 + [VMEM] * 3 + [ANY] * len(parts),
        out_specs=[VMEM] * (NG + 1),
        scratch_shapes=[pltpu.SemaphoreType.DMA((len(parts),))],
        compiler_params=LIMIT,
        cost_estimate=ROW_COST,
        name="followers",
    )(at, place, send, own, y, labels, *parts)


def leaders(at, y, table):
    return pl.pallas_call(
        leader_kernel,
        out_shape=jax.ShapeDtypeStruct((HALF, BLK, WIDE), jnp.bfloat16),
        in_specs=[SMEM] + [VMEM] * 2,
        out_specs=VMEM,
        compiler_params=LIMIT,
        cost_estimate=ROW_COST,
        name="leaders",
    )(at, y, table)


def label_kernel(place_ref, columns_ref, fetch_ref, codes_ref, mine_ref, send_ref, lead_ref, follow_ref):
    g, x, z, c = (place_ref[i] for i in range(4))
    device = x * (NZ * NC) + z * NC + c

    def slot(i, k):
        column = columns_ref[i, k]
        ghost = jnp.maximum(column - ROWS, 0)
        peer = ghost >> 2
        local = column < ROWS
        row = jnp.where(local, jnp.maximum(column, 0), fetch_ref[peer, ghost & 3])
        late = jnp.maximum(row - HALF, 0)
        group = ((peer >> 4) * NC + (peer & 1)) * HALF
        code = jnp.where(local, mine_ref[late], codes_ref[(peer >> 1) & (NZ - 1), group + late])
        code = jnp.where(row < HALF, g * HALF + row, code)
        label = ((code >> 3) * N_DEV + jnp.where(local, device, peer)) * HALF + (code & 7)
        return jnp.where(column >= 0, label, -1)

    def row(i, carry):
        follower = send_ref[0, i] + HALF
        for k in range(K):
            lead_ref[i, k] = slot(i, k)
            follow_ref[i, k] = slot(follower, k)
        return carry

    lax.fori_loop(0, HALF, row, 0)


def label_rows(place, columns, fetch, codes, mine, send):
    labels = jax.ShapeDtypeStruct((HALF, K), jnp.int32)
    return pl.pallas_call(
        label_kernel,
        out_shape=[labels, labels],
        in_specs=[SMEM] * 6,
        out_specs=[SMEM] * 2,
        name="labels",
    )(place, columns, fetch, codes, mine, send)


def merge_kernel(place_ref, slots_ref, lead_ref, own_labels_ref, *refs):
    parts, out, labels_ref = refs[:NG], refs[NG], refs[NG + 1]
    tiles, stage, sems, digits, work, steps_ref, next_ref, next_sem = refs[NG + 2:]
    per = SLOTS // 2

    lane = lax.broadcasted_iota(jnp.int32, (HALF, LANES), 1)
    for s in range(NG):
        for q in range(2):
            high = parts[s][q, 0:1, 0:LANES].astype(jnp.float32)
            rest = parts[s][q, 16:17, 0:LANES].astype(jnp.float32)
            digits[2 * s + q:2 * s + q + 1, :] = (high * 16.0 + rest).astype(jnp.int32)
    spots = []
    for n in range(HALF):
        spot = slots_ref[0, n]
        spots.append(((place_ref[0] - (spot >> 1)) & (NG - 1)) * 2 + (spot & 1))
        work[n:n + 1, :] = digits[pl.ds(spots[n], 1), :]
    labels = jnp.where(lane < 2 * K, pltpu.roll(work[...], K, 1), -1)
    work[...] = labels
    work[:, 0:K] = own_labels_ref[...]
    labels = work[...]
    labels_ref[...] = work[:, 0:2 * K]
    twice = jnp.where(lane < 2 * K, labels, pltpu.roll(labels, 2 * K, 1))
    steps = jnp.full((HALF, LANES), 2 * K, jnp.int32)
    for d in range(2 * K - 1, 0, -1):
        steps = jnp.where(pltpu.roll(twice, LANES - d, 1) == labels, d, steps)
    steps = jnp.where((lane < 2 * K) & (labels >= 0), steps, 2 * K)
    usual = jnp.where((lane == 0) | (lane == K), K, 2 * K)
    odd = jnp.max(jnp.where(steps != usual, 1, 0), axis=1, keepdims=True)
    steps_ref[...] = jnp.where(lane == 2 * K, odd, steps)
    fetch = pltpu.make_async_copy(steps_ref, next_ref, next_sem)
    fetch.start()

    for t in range(per):
        span = slice(t * LANES, (t + 1) * LANES)
        for n in range(HALF):
            tiles[n * per + t] = lead_ref[n, :, span]
        for s in range(NG):
            for q in range(2):
                tiles[(HALF + 2 * s + q) * per + t] = parts[s][q, :, span]
    low = low_lanes((BLK, LANES))

    for n in range(HALF):
        f, l = (HALF + spots[n]) * per, n * per
        first = tiles[l].astype(jnp.float32)
        second = jnp.where(low, 0.0, tiles[f].astype(jnp.float32))
        tiles[f] = second.astype(jnp.bfloat16)
        stage[n, :, 0:LANES] = (first + pltpu.roll(second, BLK, 1)).astype(jnp.bfloat16)
        middle = tiles[l + per - 1].astype(jnp.float32) + second
        middle = middle + jnp.where(low, 0.0, pltpu.roll(first, BLK, 1))
        stage[n, :, 5 * LANES:6 * LANES] = middle.astype(jnp.bfloat16)
        for t in range(1, per - 1):
            stage[n, :, t * LANES:(t + 1) * LANES] = tiles[l + t]
        for t in range(1, per):
            stage[n, :, (5 + t) * LANES:(6 + t) * LANES] = tiles[f + t]

    def save(n):
        return pltpu.make_async_copy(stage.at[n], out.at[n], sems.at[n])

    fetch.wait()
    for n in range(HALF):
        f, l = (HALF + spots[n]) * per, n * per

        @pl.when(next_ref[n, 2 * K] != 0)
        def _(n=n, f=f, l=l):
            plain = (next_ref[n, 0] == K) & (next_ref[n, K] == K)
            for s in range(2 * K):
                step = next_ref[n, s]
                skip = plain if s in (0, K) else step == 2 * K

                @pl.when(jnp.logical_not(skip))
                def _(s=s, step=step):
                    home = s if s < K else s - K + 1

                    def block(t):
                        spot = jnp.where(t < K, t, t - K + 1)
                        value = tiles[jnp.where(t < K, l, f) + (spot >> 1)].astype(jnp.float32)
                        same = jnp.broadcast_to((spot & 1) == (home & 1), value.shape)
                        return jnp.where(same, value, pltpu.roll(value, BLK, 1))

                    def follow(t, step):
                        after = t + step
                        return jnp.where(after >= 2 * K, after - 2 * K, after)

                    def more(carry):
                        return carry[0] != s

                    def add(carry):
                        t, total = carry
                        return follow(t, next_ref[n, t]), total + block(t)

                    _, total = lax.while_loop(more, add, (follow(s, step), block(jnp.int32(s))))
                    span = slice((s // 2) * LANES, (s // 2 + 1) * LANES)
                    keep = low if s % 2 == 0 else jnp.logical_not(low)
                    stage[n, :, span] = jnp.where(
                        keep, total, stage[n, :, span].astype(jnp.float32)
                    ).astype(jnp.bfloat16)

        save(n).start()
    for n in range(HALF):
        save(n).wait()


def merge(place, slots, lead, own_labels, parts):
    return pl.pallas_call(
        merge_kernel,
        out_shape=[
            jax.ShapeDtypeStruct((HALF, BLK, 2 * K * BLK), jnp.bfloat16),
            jax.ShapeDtypeStruct((HALF, 2 * K), jnp.int32),
        ],
        in_specs=[SMEM] * 2 + [VMEM] * (2 + NG),
        out_specs=[pl.BlockSpec(memory_space=pl.ANY), VMEM],
        scratch_shapes=[
            pltpu.VMEM((2 * HALF * SLOTS // 2, BLK, LANES), jnp.bfloat16),
            pltpu.VMEM((HALF, BLK, 2 * K * BLK), jnp.bfloat16),
            pltpu.SemaphoreType.DMA((HALF,)),
            pltpu.VMEM((HALF, LANES), jnp.int32),
            pltpu.VMEM((HALF, LANES), jnp.int32),
            pltpu.VMEM((HALF, LANES), jnp.int32),
            pltpu.SMEM((HALF, LANES), jnp.int32),
            pltpu.SemaphoreType.DMA,
        ],
        compiler_params=LIMIT,
        name="merge",
    )(place, slots, lead, own_labels, *parts)


def shift(value, axis, size, by):
    if by == 0:
        return value
    return lax.ppermute(value, axis, [(i, (i + by) % size) for i in range(size)])


def cross(value, b):
    if b == 0:
        return value
    by, flip = b // NC, b % NC
    pairs = [
        (x * NC + c, ((x + by) % NX) * NC + (c ^ flip)) for x in range(NX) for c in range(NC)
    ]
    return lax.ppermute(value, ("x", "core"), pairs)


def per_device(stiffness, prolongator, columns, fetch_rows, send_order, partner_slot):
    g, x, z, c = (lax.axis_index(name) for name in AXES)
    device = x * (NZ * NC) + z * NC + c
    place = jnp.stack([g, x, z, c]).astype(jnp.int32)
    own = prolongator.reshape(ROWS, 32, LANES)

    held = []
    for h in range(CHUNKS):
        piece = own[:, h * CK:(h + 1) * CK]
        got = {0: piece}
        for s in (4, 2, 6, 1, 7):
            got[s] = shift(piece, "z", NZ, s)
        got[5] = shift(got[4], "z", NZ, 1)
        got[3] = shift(got[4], "z", NZ, NZ - 1)
        held.append([got[s] for s in range(NZ)])

    sending, slots = send_order[0], partner_slot[0]
    eight = jnp.arange(HALF, dtype=jnp.int32)
    codes = jnp.sum(jnp.where(slots[:, None] == eight[None, :], (g * HALF + eight)[:, None], 0), axis=0)
    returned = lax.all_to_all(codes, "grp", split_axis=0, concat_axis=0, tiled=True)
    mine = jnp.sum(jnp.where(sending[:, None] == eight[None, :], returned[:, None], 0), axis=0)

    lists = fetch_rows.reshape(NX, NZ, NC, C).transpose(0, 2, 1, 3).reshape(NX * NC, NZ * C)
    note = jnp.concatenate([lists, jnp.broadcast_to(mine[None, :], (NX * NC, HALF))], axis=1)
    wanted = lax.all_to_all(note, ("x", "core"), split_axis=0, concat_axis=0, tiled=True)
    plane = wanted[:, NZ * C:].reshape(1, NX * NC * HALF)
    every = lax.all_to_all(
        jnp.broadcast_to(plane, (NZ, NX * NC * HALF)), "z", split_axis=0, concat_axis=0, tiled=True
    )
    lead_labels, follower_labels = label_rows(place, columns, fetch_rows, every, mine, send_order)

    ghost = columns - ROWS
    peer = ghost >> 2
    way = ((x - (peer >> 4)) & (NX - 1)) * NC + (c ^ (peer & 1))
    at = way * (NZ * C) + ((peer >> 1) & (NZ - 1)) * C + (ghost & 3)
    at = jnp.where(columns < ROWS, TABLE + columns, at)
    at = jnp.where(columns >= 0, at, TABLE + ROWS).astype(jnp.int32)
    none = jnp.full((HALF, 1), TABLE + ROWS, jnp.int32)
    at = jnp.concatenate([
        jnp.concatenate([at[:HALF], none], axis=1),
        jnp.concatenate([none, at[HALF:]], axis=1),
    ])

    lane = jnp.arange(LANES, dtype=jnp.int32)
    inner = lane & (BLK - 1)
    source = (lane & BLK) + jnp.where(inner < 32, 2 * inner, 2 * (inner - 32) + 1)
    perm = (lane[:, None] == source[None, :]).astype(jnp.bfloat16)
    y = products(prolongator.reshape(ROWS, BLK, BLK), stiffness, perm)

    parts = []
    for h in range(CHUNKS):
        chosen = select(wanted, place, held[h])
        moved = {b: cross(chosen[i], b) for i, b in enumerate(ORDER)}
        parts += [moved[b] for b in range(NX * NC)]

    *sent, table = followers(at, place, send_order, own, y, follower_labels, parts)
    arrived = [sent[0]] + [shift(sent[s], "grp", NG, s) for s in range(1, NG)]
    lead = leaders(at, y, table)
    return tuple(merge(place, partner_slot, lead, lead_labels, arrived))


def solution(mesh):
    grid = Mesh(mesh.devices.reshape(NG, NX, NZ, NC), AXES)
    return jax.shard_map(
        per_device,
        mesh=grid,
        in_specs=(
            P(AXES, None, None),
            P(AXES, None),
            P(AXES, None),
            P(AXES, None),
            P(AXES, None),
            P(AXES, None),
        ),
        out_specs=(P(AXES, None, None), P(AXES, None)),
        check_vma=False,
    )
```

time: 115 us -> 96.9 us (0.84)
  blocking collectives: 9.54 us -> 0 us
  starting transfers between devices: 45.5 us -> 40.3 us
  Pallas kernels: 23.6 us -> 20.6 us
    all_to_all x1 -> x0, blocking collectives: 9.54 us -> none  [per_device(): lax.all_to_all(follower_labels, 'grp', split_axis=0, concat_axis=0, tiled...]
    all_to_all x3 -> x2, waiting for transfers between devices: 9.68 us -> 5.59 us  [the longest x1 3.65 us: per_device(): lax.all_to_all(note, ('x', 'core'), split_axis=0, concat_axis=0, tiled=True)]
    all_to_all x3 -> x2, starting transfers between devices: 12.7 us -> 8.91 us  [the longest x1 4.83 us: per_device(): lax.all_to_all(note, ('x', 'core'), split_axis=0, concat_axis=0, tiled=True)]
    ppermute x7, waiting for transfers between devices: 0.02 us -> 2.34 us  [cross(): return lax.ppermute(value, ('x', 'core'), pairs)]
    ppermute x10, waiting for transfers between devices: 3.96 us -> 6.24 us  [shift(): lax.ppermute(value, axis, [(i, (i + by) % size) for i in range(size)])]
    pallas_call x4 -> x3, Pallas kernels: 13.1 us -> 10.8 us  [the longest x1 4.58 us: label_rows(): pl.pallas_call(label_kernel, out_shape=[labels, labels], in_specs=[SMEM]...]
    all_to_all x1, waiting for transfers between devices: 5.17 us -> 3.61 us  [per_device(): lax.all_to_all(codes, 'grp', split_axis=0, concat_axis=0, tiled=True)]
    unnamed x42 -> x36, local copies, waits for them, and re-layouts: 8.05 us -> 9.35 us
  transfers between devices with their start and end apart: 21 -> 20, of which waited for: 4 -> 6; matrix products, arithmetic and copies ran while one was open for 6% -> 7% of each run, Pallas kernels for 14% -> 13%
where the time goes in v1:
time: 96.9 us; the launch traced here: 95.7 us
  starting transfers between devices  40.3 us (42%)
  Pallas kernels  20.6 us (21%)
  waiting for transfers between devices  17.8 us (18%)
  local copies, waits for them, and re-layouts  11.8 us (12%)
  other arithmetic  4.23 us (4%)
  between operations  1 us (1%)
    ppermute x10, starting transfers between devices, shift(): lax.ppermute(value, axis, [(i, (i + by) % size) for i in range(size)])  19.3 us
    unnamed x36, local copies, waits for them, and re-layouts  9.35 us
    ppermute x7, starting transfers between devices, cross(): return lax.ppermute(value, ('x', 'core'), pairs)  7.63 us
    ppermute x10, waiting for transfers between devices, shift(): lax.ppermute(value, axis, [(i, (i + by) % size) for i in range(size)])  6.24 us
    all_to_all x1, starting transfers between devices, per_device(): lax.all_to_all(note, ('x', 'core'), split_axis=0, concat_axis=0, tiled=True)  4.83 us
    pallas_call x1, Pallas kernels, products(): pl.pallas_call(products_kernel, out_shape=jax.ShapeDtypeStruct((ROWS, BLK...  4.83 us
    pallas_call x1, Pallas kernels, label_rows(): pl.pallas_call(label_kernel, out_shape=[labels, labels], in_specs=[SMEM]...  4.58 us
    all_to_all x1, starting transfers between devices, per_device(): lax.all_to_all(codes, 'grp', split_axis=0, concat_axis=0, tiled=True)  4.46 us
  transfers between devices with their start and end apart: 20, of which 6 were waited for; matrix products, arithmetic and copies ran while one was open for 7% of the time, Pallas kernels for 13%

profile of v1, /device:TPU:2, one launch (start us, length us, event | category | flops | bytes accessed | tf_op | source)
XLA Modules:
  0.0 95.7 jit_solution(12095970289094076257)
XLA Ops:
  0.6 1.0 %copy.23 = bf16[2,8,32,128]{3,2,1,0:T(8,128)(2,1)S(1)} copy(bf16[2,8,32,128]{3,1,2,0:T(8,128)(2,1)} %bitcast.31) | data formatting | bytes 262144
  1.7 5.9 %collective-permute-start.6 = (bf16[16,32,128]{2,1,0:T(8,128)(2,1)S(1)}, bf16[16,32,128]{2,1,0:T(8,128)(2,1)S(1)}, u32[]{:S(2)}, u32[]{:S(2)}) collective-permute-start(bf16[16,32,128]{2,1,0:T(8,128)(2,1)S(1)} %bitcast.20), channel_id=1, source_target_pairs={{0,14},{2,0},{4,2},{6,4},{8,6},{10,8},{12,10},{14,12},{1,15},{3,1}... | collective-permute-start | bytes 393224 | tf_op jit(solution)/shard_map/ppermute | solution.py:346
  7.6 1.5 %collective-permute-start.5 = (bf16[16,32,128]{2,1,0:T(8,128)(2,1)S(1)}, bf16[16,32,128]{2,1,0:T(8,128)(2,1)S(1)}, u32[]{:S(2)}, u32[]{:S(2)}) collective-permute-start(bf16[16,32,128]{2,1,0:T(8,128)(2,1)S(1)} %bitcast.21), channel_id=1, source_target_pairs={{0,12},{2,14},{4,0},{6,2},{8,4},{10,6},{12,8},{14,10},{1,13},{3,15... | collective-permute-start | bytes 393224 | tf_op jit(solution)/shard_map/ppermute | solution.py:346
  9.2 2.8 %collective-permute-start.1 = (bf16[16,32,128]{2,1,0:T(8,128)(2,1)S(1)}, bf16[16,32,128]{2,1,0:T(8,128)(2,1)S(1)}, u32[]{:S(2)}, u32[]{:S(2)}) collective-permute-start(bf16[16,32,128]{2,1,0:T(8,128)(2,1)S(1)} %bitcast.23), channel_id=1, source_target_pairs={{0,4},{2,6},{4,8},{6,10},{8,12},{10,14},{12,0},{14,2},{1,5},{3,7},... | collective-permute-start | bytes 393224 | tf_op jit(solution)/shard_map/ppermute | solution.py:346
  12.0 1.9 %collective-permute-start = (bf16[16,32,128]{2,1,0:T(8,128)(2,1)S(1)}, bf16[16,32,128]{2,1,0:T(8,128)(2,1)S(1)}, u32[]{:S(2)}, u32[]{:S(2)}) collective-permute-start(bf16[16,32,128]{2,1,0:T(8,128)(2,1)S(1)} %bitcast.24), channel_id=1, source_target_pairs={{0,2},{2,4},{4,6},{6,8},{8,10},{10,12},{12,14},{14,0},{1,3},{3,5},... | collective-permute-start | bytes 393224 | tf_op jit(solution)/shard_map/ppermute | solution.py:346
  15.3 4.5 %all-to-all-start = ((s32[4,2,1]{1,2,0:T(1,128)}), s32[4,2,1]{1,2,0:T(1,128)S(1)}, u32[]{:S(2)}, u32[]{:S(2)}) async-start(s32[4,2,1]{1,2,0:T(1,128)} %bitcast.8), calls=%async_computation | async-start | bytes 4096 | tf_op jit(solution)/shard_map/all_to_all | solution.py:378
  20.5 0.8 copy.22.fetch_ref
  21.4 3.6 %all-to-all-done = s32[4,2,1]{1,2,0:T(1,128)S(1)} async-done(((s32[4,2,1]{1,2,0:T(1,128)}), s32[4,2,1]{1,2,0:T(1,128)S(1)}, u32[]{:S(2)}, u32[]{:S(2)}) %all-to-all-start) | async-done | bytes 64 | tf_op jit(solution)/shard_map/all_to_all | solution.py:378
  27.6 2.2 %collective-permute-start.4 = (bf16[16,32,128]{2,1,0:T(8,128)(2,1)S(1)}, bf16[16,32,128]{2,1,0:T(8,128)(2,1)S(1)}, u32[]{:S(2)}, u32[]{:S(2)}) collective-permute-start(bf16[16,32,128]{2,1,0:T(8,128)(2,1)S(1)} %collective-permute-done.2.refs_4_), channel_id=1, source_target_pairs={{0,2},{2,4},{4,6},{6,8},{8,10},{10,12},{12,14},{14,0},{1,3},{3,5},... | collective-permute-start | bytes 393224 | tf_op jit(solution)/shard_map/ppermute | solution.py:346
  29.8 1.0 %collective-permute-start.3 = (bf16[16,32,128]{2,1,0:T(8,128)(2,1)S(1)}, bf16[16,32,128]{2,1,0:T(8,128)(2,1)S(1)}, u32[]{:S(2)}, u32[]{:S(2)}) collective-permute-start(bf16[16,32,128]{2,1,0:T(8,128)(2,1)S(1)} %collective-permute-done.2.refs_4_), channel_id=1, source_target_pairs={{0,14},{2,0},{4,2},{6,4},{8,6},{10,8},{12,10},{14,12},{1,15},{3,1}... | collective-permute-start | bytes 393224 | tf_op jit(solution)/shard_map/ppermute | solution.py:346
  31.4 4.8 %all-to-all-start.1 = ((s32[8,1,40]{2,1,0:T(1,128)}), s32[8,1,40]{2,1,0:T(1,128)S(1)}, u32[]{:S(2)}, u32[]{:S(2)}) async-start(s32[8,1,40]{2,1,0:T(1,128)} %bitcast.10), calls=%async_computation.1 | async-start | bytes 8192 | tf_op jit(solution)/shard_map/all_to_all | solution.py:383
  36.3 3.7 %all-to-all-done.1 = s32[8,1,40]{2,1,0:T(1,128)S(1)} async-done(((s32[8,1,40]{2,1,0:T(1,128)}), s32[8,1,40]{2,1,0:T(1,128)S(1)}, u32[]{:S(2)}, u32[]{:S(2)}) %all-to-all-start.1) | async-done | bytes 1312 | tf_op jit(solution)/shard_map/all_to_all | solution.py:383
  40.0 2.2 %select.7 = (bf16[32,32,128]{2,1,0:T(8,128)(2,1)S(1)}, bf16[32,32,128]{2,1,0:T(8,128)(2,1)S(1)}, bf16[32,32,128]{2,1,0:T(8,128)(2,1)}, bf16[32,32,128]{2,1,0:T(8...) custom-call(s32[8,40]{1,0:T(8,128)S(1)} %bitcast.27, ...), custom_call_target="tpu_custom_call" | custom-call | tf_op jit(solution)/shard_map/select/pallas_call | solution.py:75
  43.6 1.3 %collective-permute-start.9 = (bf16[32,32,128]{2,1,0:T(8,128)(2,1)}, bf16[32,32,128]{2,1,0:T(8,128)(2,1)}, u32[]{:S(2)}, u32[]{:S(2)}) collective-permute-start(bf16[32,32,128]{2,1,0:T(8,128)(2,1)} %get-tuple-element.21), channel_id=1, source_target_pairs={{0,17},{1,16},{16,33},{17,32},{32,49},{33,48},{48,1},{49,0},{2,19}... | collective-permute-start | bytes 786440 | tf_op jit(solution)/shard_map/ppermute | solution.py:356
  44.9 2.1 %collective-permute-start.10 = (bf16[32,32,128]{2,1,0:T(8,128)(2,1)}, bf16[32,32,128]{2,1,0:T(8,128)(2,1)}, u32[]{:S(2)}, u32[]{:S(2)}) collective-permute-start(bf16[32,32,128]{2,1,0:T(8,128)(2,1)} %get-tuple-element.22), channel_id=1, source_target_pairs={{0,32},{1,33},{16,48},{17,49},{32,0},{33,1},{48,16},{49,17},{2,34}... | collective-permute-start | bytes 786440 | tf_op jit(solution)/shard_map/ppermute | solution.py:356
  47.0 1.1 %collective-permute-start.11 = (bf16[32,32,128]{2,1,0:T(8,128)(2,1)}, bf16[32,32,128]{2,1,0:T(8,128)(2,1)}, u32[]{:S(2)}, u32[]{:S(2)}) collective-permute-start(bf16[32,32,128]{2,1,0:T(8,128)(2,1)} %get-tuple-element.23), channel_id=1, source_target_pairs={{0,33},{1,32},{16,49},{17,48},{32,1},{33,0},{48,17},{49,16},{2,35}... | collective-permute-start | bytes 786440 | tf_op jit(solution)/shard_map/ppermute | solution.py:356
  48.7 1.0 %collective-permute-start.12 = (bf16[32,32,128]{2,1,0:T(8,128)(2,1)}, bf16[32,32,128]{2,1,0:T(8,128)(2,1)}, u32[]{:S(2)}, u32[]{:S(2)}) collective-permute-start(bf16[32,32,128]{2,1,0:T(8,128)(2,1)} %get-tuple-element.24), channel_id=1, source_target_pairs={{0,48},{1,49},{16,0},{17,1},{32,16},{33,17},{48,32},{49,33},{2,50}... | collective-permute-start | bytes 786440 | tf_op jit(solution)/shard_map/ppermute | solution.py:356
  49.7 2.3 %collective-permute-done.8.refs_2_ = bf16[32,32,128]{2,1,0:T(8,128)(2,1)S(1)} collective-permute-done((bf16[32,32,128]{2,1,0:T(8,128)(2,1)S(1)}, bf16[32,32,128]{2,1,0:T(8,128)(2,1)S(1)}, u32[]{:S(2)}, u32[]{:S(2)}) %collective-permute-start.8) | collective-permute-done | bytes 262176 | tf_op jit(solution)/shard_map/ppermute | solution.py:356
  52.8 1.6 %collective-permute-start.13 = (bf16[32,32,128]{2,1,0:T(8,128)(2,1)}, bf16[32,32,128]{2,1,0:T(8,128)(2,1)}, u32[]{:S(2)}, u32[]{:S(2)}) collective-permute-start(bf16[32,32,128]{2,1,0:T(8,128)(2,1)} %get-tuple-element.25), channel_id=1, source_target_pairs={{0,49},{1,48},{16,1},{17,0},{32,17},{33,16},{48,33},{49,32},{2,51}... | collective-permute-start | bytes 786440 | tf_op jit(solution)/shard_map/ppermute | solution.py:356
  56.0 4.1 %all-to-all-start.2 = ((s32[8,1,64]{2,1,0:T(1,128)}), s32[8,1,64]{2,1,0:T(1,128)}, u32[]{:S(2)}, u32[]{:S(2)}) async-start(s32[8,1,64]{2,1,0:T(1,128)} %broadcast_in_dim.50), calls=%async_computation.2 | async-start | bytes 8192 | tf_op jit(solution)/shard_map/all_to_all | solution.py:385
  60.9 4.8 %products.1.y_ref = bf16[16,64,768]{2,1,0:T(8,128)(2,1)S(1)} custom-call(bf16[16,64,64]{2,1,0:T(8,128)(2,1)S(1)} %reshape.51.p_ref, bf16[16,64,704]{2,1,0:T(8,128)(2,1)S(1)} %copy-done, bf16[128,128]{1,0:T(8,128)(2,1)S(1)} %copy-done.7), custom_call_target="tpu_custom_call" | custom-call | flops 301989888 | bytes 3200000 | tf_op jit(solution)/shard_map/products/pallas_call | solution.py:51
  65.7 1.9 %all-to-all-done.2 = s32[8,1,64]{2,1,0:T(1,128)} async-done(((s32[8,1,64]{2,1,0:T(1,128)}), s32[8,1,64]{2,1,0:T(1,128)}, u32[]{:S(2)}, u32[]{:S(2)}) %all-to-all-start.2) | async-done | bytes 2080 | tf_op jit(solution)/shard_map/all_to_all | solution.py:385
  67.7 4.6 %labels.1 = (s32[8,11]{1,0:T(8,128)}, s32[8,11]{1,0:T(8,128)}) custom-call(s32[4]{0:T(128)} %copy-done.8, s32[16,11]{1,0:T(8,128)} %columns_ref.1, s32[64,4]{1,0:T(8,128)} %copy-done.15, s32[8,64]{1,0:T(8,128)} %bitcast.12.codes_ref, s32[8]{0:T(128)} %copy-done.16, s32[1,8]{1,0:T(1,128)} %send_ref.3), custom_call_target="tpu_custom_call" | custom-call | tf_op jit(solution)/shard_map/labels/pallas_call | solution.py:208
  72.3 0.9 copy-done.2
  73.3 0.9 copy-done.4
  74.2 0.9 copy-done.6
  76.5 2.7 %followers.1 = (bf16[2,64,768]{2,1,0:T(8,128)(2,1)S(1)}, bf16[2,64,768]{2,1,0:T(8,128)(2,1)S(1)}, bf16[2,64,768]{2,1,0:T(8,128)(2,1)S(1)}, bf16[2,64,768]{2,1,0:T(8,128)(2,1)S(1)}, bf16[273,32,128]{2,1,0:T(8,128)(2,1)S(1)}) custom-call(s32[16,12]{1,0:T(8,128)S(1)} %select_add_fusion.at_ref, s32[4]{0:T(128)S(1)} %copy-done.9, s32[1,8]{1,0:T(1,128)S(1)} %copy-done.12, ...), custom_call_target="tpu_custom_call" | custom-call | flops 100663296 | bytes 5000000 | tf_op jit(solution)/shard_map/followers/pallas_call | solution.py:155
  79.8 2.1 %collective-permute-start.15 = (bf16[2,64,768]{2,1,0:T(8,128)(2,1)S(1)}, bf16[2,64,768]{2,1,0:T(8,128)(2,1)S(1)}, u32[]{:S(2)}, u32[]{:S(2)}) collective-permute-start(bf16[2,64,768]{2,1,0:T(8,128)(2,1)S(1)} %get-tuple-element.30), channel_id=1, source_target_pairs={{0,128},{64,192},{128,0},{192,64},{1,129},{65,193},{129,1},{193,65... | collective-permute-start | bytes 589832 | tf_op jit(solution)/shard_map/ppermute | solution.py:346
  81.9 1.2 %collective-permute-start.16 = (bf16[2,64,768]{2,1,0:T(8,128)(2,1)S(1)}, bf16[2,64,768]{2,1,0:T(8,128)(2,1)S(1)}, u32[]{:S(2)}, u32[]{:S(2)}) collective-permute-start(bf16[2,64,768]{2,1,0:T(8,128)(2,1)S(1)} %get-tuple-element.31), channel_id=1, source_target_pairs={{0,192},{64,0},{128,64},{192,128},{1,193},{65,1},{129,65},{193,129... | collective-permute-start | bytes 589832 | tf_op jit(solution)/shard_map/ppermute | solution.py:346
  83.0 2.7 %leaders.1.lead_ref = bf16[8,64,768]{2,1,0:T(8,128)(2,1)S(1)} custom-call(s32[16,12]{1,0:T(8,128)S(1)} %select_add_fusion.at_ref, bf16[16,64,768]{2,1,0:T(8,128)(2,1)S(1)} %products.1.y_ref, bf16[273,32,128]{2,1,0:T(8,128)(2,1)S(1)} %get-tuple-element.26.table), custom_call_target="tpu_custom_call" | custom-call | flops 100663296 | bytes 5000000 | tf_op jit(solution)/shard_map/leaders/pallas_call | solution.py:168
  85.7 5.6 %collective-permute-done.14.refs_1_ = bf16[2,64,768]{2,1,0:T(8,128)(2,1)S(1)} collective-permute-done((bf16[2,64,768]{2,1,0:T(8,128)(2,1)S(1)}, bf16[2,64,768]{2,1,0:T(8,128)(2,1)S(1)}, u32[]{:S(2)}, u32[]{:S(2)}) %collective-permute-start.14) | collective-permute-done | bytes 196640 | tf_op jit(solution)/shard_map/ppermute | solution.py:346
  91.9 3.6 %merge.1 = (bf16[8,64,1408]{2,1,0:T(8,128)(2,1)}, s32[8,22]{1,0:T(8,128)}) custom-call(s32[4]{0:T(128)S(1)} %copy-done.9, s32[1,8]{1,0:T(1,128)S(1)} %copy-done.13, bf16[8,64,768]{2,1,0:T(8,128)(2,1)S(1)} %leaders.1.lead_ref, s32[8,11]{1,0:T(8,128)S(1)} %copy-done.10, bf16[2,64,768]{2,1,0:T(8,128)(2,1)S(1)} %get-tuple-element.28.refs_0_, ...), custom_call_target="tpu_custom_call" | custom-call | tf_op jit(solution)/shard_map/merge/pallas_call | solution.py:320
  (71 shorter events, 13.3 us)
Async XLA Ops:
  0.6 53.8 %copy-start.14 = (bf16[16,4096]{1,0:T(8,128)(2,1)S(1)}, bf16[16,4096]{1,0:T(8,128)(2,1)}, u32[]{:S(2)}) copy-start(bf16[16,4096]{1,0:T(8,128)(2,1)} %param.7) | copy-start | bytes 393220
  0.6 59.5 %copy-start = (bf16[16,64,704]{2,1,0:T(8,128)(2,1)S(1)}, bf16[16,64,704]{2,1,0:T(8,128)(2,1)}, u32[]{:S(2)}) copy-start(bf16[16,64,704]{2,1,0:T(8,128)(2,1)} %a_ref.1) | copy-start | bytes 4325380
  1.7 28.1 %collective-permute-start.6 = (bf16[16,32,128]{2,1,0:T(8,128)(2,1)S(1)}, bf16[16,32,128]{2,1,0:T(8,128)(2,1)S(1)}, u32[]{:S(2)}, u32[]{:S(2)}) collective-permute-start(bf16[16,32,128]{2,1,0:T(8,128)(2,1)S(1)} %bitcast.20), channel_id=1, source_target_pairs={{0,14},{2,0},{4,2},{6,4},{8,6},{10,8},{12,10},{14,12},{1,15},{3,1}... | collective-permute-start | bytes 393224 | tf_op jit(solution)/shard_map/ppermute | solution.py:346
  7.6 32.3 %collective-permute-start.5 = (bf16[16,32,128]{2,1,0:T(8,128)(2,1)S(1)}, bf16[16,32,128]{2,1,0:T(8,128)(2,1)S(1)}, u32[]{:S(2)}, u32[]{:S(2)}) collective-permute-start(bf16[16,32,128]{2,1,0:T(8,128)(2,1)S(1)} %bitcast.21), channel_id=1, source_target_pairs={{0,12},{2,14},{4,0},{6,2},{8,4},{10,6},{12,8},{14,10},{1,13},{3,15... | collective-permute-start | bytes 393224 | tf_op jit(solution)/shard_map/ppermute | solution.py:346
  9.1 18.5 %collective-permute-start.2 = (bf16[16,32,128]{2,1,0:T(8,128)(2,1)S(1)}, bf16[16,32,128]{2,1,0:T(8,128)(2,1)S(1)}, u32[]{:S(2)}, u32[]{:S(2)}) collective-permute-start(bf16[16,32,128]{2,1,0:T(8,128)(2,1)S(1)} %bitcast.22), channel_id=1, source_target_pairs={{0,8},{2,10},{4,12},{6,14},{8,0},{10,2},{12,4},{14,6},{1,9},{3,11}... | collective-permute-start | bytes 393224 | tf_op jit(solution)/shard_map/ppermute | solution.py:346
  9.2 30.8 %collective-permute-start.1 = (bf16[16,32,128]{2,1,0:T(8,128)(2,1)S(1)}, bf16[16,32,128]{2,1,0:T(8,128)(2,1)S(1)}, u32[]{:S(2)}, u32[]{:S(2)}) collective-permute-start(bf16[16,32,128]{2,1,0:T(8,128)(2,1)S(1)} %bitcast.23), channel_id=1, source_target_pairs={{0,4},{2,6},{4,8},{6,10},{8,12},{10,14},{12,0},{14,2},{1,5},{3,7},... | collective-permute-start | bytes 393224 | tf_op jit(solution)/shard_map/ppermute | solution.py:346
  12.0 28.0 %collective-permute-start = (bf16[16,32,128]{2,1,0:T(8,128)(2,1)S(1)}, bf16[16,32,128]{2,1,0:T(8,128)(2,1)S(1)}, u32[]{:S(2)}, u32[]{:S(2)}) collective-permute-start(bf16[16,32,128]{2,1,0:T(8,128)(2,1)S(1)} %bitcast.24), channel_id=1, source_target_pairs={{0,2},{2,4},{4,6},{6,8},{8,10},{10,12},{12,14},{14,0},{1,3},{3,5},... | collective-permute-start | bytes 393224 | tf_op jit(solution)/shard_map/ppermute | solution.py:346
  15.3 9.6 %all-to-all-start = ((s32[4,2,1]{1,2,0:T(1,128)}), s32[4,2,1]{1,2,0:T(1,128)S(1)}, u32[]{:S(2)}, u32[]{:S(2)}) async-start(s32[4,2,1]{1,2,0:T(1,128)} %bitcast.8), calls=%async_computation | async-start | bytes 4096 | tf_op jit(solution)/shard_map/all_to_all | solution.py:378
  21.3 5.8 %copy-start.15 = (s32[64,4]{1,0:T(8,128)}, s32[64,4]{1,0:T(8,128)S(1)}, u32[]{:S(2)}) copy-start(s32[64,4]{1,0:T(8,128)S(1)} %copy.22.fetch_ref) | copy-start | bytes 3076
  27.6 12.4 %collective-permute-start.4 = (bf16[16,32,128]{2,1,0:T(8,128)(2,1)S(1)}, bf16[16,32,128]{2,1,0:T(8,128)(2,1)S(1)}, u32[]{:S(2)}, u32[]{:S(2)}) collective-permute-start(bf16[16,32,128]{2,1,0:T(8,128)(2,1)S(1)} %collective-permute-done.2.refs_4_), channel_id=1, source_target_pairs={{0,2},{2,4},{4,6},{6,8},{8,10},{10,12},{12,14},{14,0},{1,3},{3,5},... | collective-permute-start | bytes 393224 | tf_op jit(solution)/shard_map/ppermute | solution.py:346
  29.8 10.2 %collective-permute-start.3 = (bf16[16,32,128]{2,1,0:T(8,128)(2,1)S(1)}, bf16[16,32,128]{2,1,0:T(8,128)(2,1)S(1)}, u32[]{:S(2)}, u32[]{:S(2)}) collective-permute-start(bf16[16,32,128]{2,1,0:T(8,128)(2,1)S(1)} %collective-permute-done.2.refs_4_), channel_id=1, source_target_pairs={{0,14},{2,0},{4,2},{6,4},{8,6},{10,8},{12,10},{14,12},{1,15},{3,1}... | collective-permute-start | bytes 393224 | tf_op jit(solution)/shard_map/ppermute | solution.py:346
  31.4 8.6 %all-to-all-start.1 = ((s32[8,1,40]{2,1,0:T(1,128)}), s32[8,1,40]{2,1,0:T(1,128)S(1)}, u32[]{:S(2)}, u32[]{:S(2)}) async-start(s32[8,1,40]{2,1,0:T(1,128)} %bitcast.10), calls=%async_computation.1 | async-start | bytes 8192 | tf_op jit(solution)/shard_map/all_to_all | solution.py:383
  36.3 29.4 %copy-start.8 = (s32[4]{0:T(128)}, s32[4]{0:T(128)S(1)}, u32[]{:S(2)}) copy-start(s32[4]{0:T(128)S(1)} %pad_add_fusion.1.place_ref) | copy-start | bytes 52
  42.2 0.7 copy-start.1
  43.0 5.1 %collective-permute-start.7 = (bf16[32,32,128]{2,1,0:T(8,128)(2,1)S(1)}, bf16[32,32,128]{2,1,0:T(8,128)(2,1)S(1)}, u32[]{:S(2)}, u32[]{:S(2)}) collective-permute-start(bf16[32,32,128]{2,1,0:T(8,128)(2,1)S(1)} %get-tuple-element.19), channel_id=1, source_target_pairs={{0,1},{1,0},{16,17},{17,16},{32,33},{33,32},{48,49},{49,48},{2,3},... | collective-permute-start | bytes 786440 | tf_op jit(solution)/shard_map/ppermute | solution.py:356
  43.0 9.1 %collective-permute-start.8 = (bf16[32,32,128]{2,1,0:T(8,128)(2,1)S(1)}, bf16[32,32,128]{2,1,0:T(8,128)(2,1)S(1)}, u32[]{:S(2)}, u32[]{:S(2)}) collective-permute-start(bf16[32,32,128]{2,1,0:T(8,128)(2,1)S(1)} %get-tuple-element.20), channel_id=1, source_target_pairs={{0,16},{1,17},{16,32},{17,33},{32,48},{33,49},{48,0},{49,1},{2,18}... | collective-permute-start | bytes 786440 | tf_op jit(solution)/shard_map/ppermute | solution.py:356
  43.6 28.7 %collective-permute-start.9 = (bf16[32,32,128]{2,1,0:T(8,128)(2,1)}, bf16[32,32,128]{2,1,0:T(8,128)(2,1)}, u32[]{:S(2)}, u32[]{:S(2)}) collective-permute-start(bf16[32,32,128]{2,1,0:T(8,128)(2,1)} %get-tuple-element.21), channel_id=1, source_target_pairs={{0,17},{1,16},{16,33},{17,32},{32,49},{33,48},{48,1},{49,0},{2,19}... | collective-permute-start | bytes 786440 | tf_op jit(solution)/shard_map/ppermute | solution.py:356
  44.9 27.4 %collective-permute-start.10 = (bf16[32,32,128]{2,1,0:T(8,128)(2,1)}, bf16[32,32,128]{2,1,0:T(8,128)(2,1)}, u32[]{:S(2)}, u32[]{:S(2)}) collective-permute-start(bf16[32,32,128]{2,1,0:T(8,128)(2,1)} %get-tuple-element.22), channel_id=1, source_target_pairs={{0,32},{1,33},{16,48},{17,49},{32,0},{33,1},{48,16},{49,17},{2,34}... | collective-permute-start | bytes 786440 | tf_op jit(solution)/shard_map/ppermute | solution.py:356
  47.0 25.3 %collective-permute-start.11 = (bf16[32,32,128]{2,1,0:T(8,128)(2,1)}, bf16[32,32,128]{2,1,0:T(8,128)(2,1)}, u32[]{:S(2)}, u32[]{:S(2)}) collective-permute-start(bf16[32,32,128]{2,1,0:T(8,128)(2,1)} %get-tuple-element.23), channel_id=1, source_target_pairs={{0,33},{1,32},{16,49},{17,48},{32,1},{33,0},{48,17},{49,16},{2,35}... | collective-permute-start | bytes 786440 | tf_op jit(solution)/shard_map/ppermute | solution.py:356
  48.7 23.5 %collective-permute-start.12 = (bf16[32,32,128]{2,1,0:T(8,128)(2,1)}, bf16[32,32,128]{2,1,0:T(8,128)(2,1)}, u32[]{:S(2)}, u32[]{:S(2)}) collective-permute-start(bf16[32,32,128]{2,1,0:T(8,128)(2,1)} %get-tuple-element.24), channel_id=1, source_target_pairs={{0,48},{1,49},{16,0},{17,1},{32,16},{33,17},{48,32},{49,33},{2,50}... | collective-permute-start | bytes 786440 | tf_op jit(solution)/shard_map/ppermute | solution.py:356
  52.8 19.5 %collective-permute-start.13 = (bf16[32,32,128]{2,1,0:T(8,128)(2,1)}, bf16[32,32,128]{2,1,0:T(8,128)(2,1)}, u32[]{:S(2)}, u32[]{:S(2)}) collective-permute-start(bf16[32,32,128]{2,1,0:T(8,128)(2,1)} %get-tuple-element.25), channel_id=1, source_target_pairs={{0,49},{1,48},{16,1},{17,0},{32,17},{33,16},{48,33},{49,32},{2,51}... | collective-permute-start | bytes 786440 | tf_op jit(solution)/shard_map/ppermute | solution.py:356
  56.0 11.6 %all-to-all-start.2 = ((s32[8,1,64]{2,1,0:T(1,128)}), s32[8,1,64]{2,1,0:T(1,128)}, u32[]{:S(2)}, u32[]{:S(2)}) async-start(s32[8,1,64]{2,1,0:T(1,128)} %broadcast_in_dim.50), calls=%async_computation.2 | async-start | bytes 8192 | tf_op jit(solution)/shard_map/all_to_all | solution.py:385
  60.1 0.8 copy-start.7
  60.9 11.4 %copy-start.12 = (s32[1,8]{1,0:T(1,128)S(1)}, s32[1,8]{1,0:T(1,128)}, u32[]{:S(2)}) copy-start(s32[1,8]{1,0:T(1,128)} %send_ref.3) | copy-start | bytes 100
  72.3 1.0 copy-start.2
  73.3 0.9 copy-start.4
  74.2 0.9 copy-start.6
  79.1 12.2 %collective-permute-start.14 = (bf16[2,64,768]{2,1,0:T(8,128)(2,1)S(1)}, bf16[2,64,768]{2,1,0:T(8,128)(2,1)S(1)}, u32[]{:S(2)}, u32[]{:S(2)}) collective-permute-start(bf16[2,64,768]{2,1,0:T(8,128)(2,1)S(1)} %get-tuple-element.29), channel_id=1, source_target_pairs={{0,64},{64,128},{128,192},{192,0},{1,65},{65,129},{129,193},{193,1... | collective-permute-start | bytes 589832 | tf_op jit(solution)/shard_map/ppermute | solution.py:346
  79.8 11.5 %collective-permute-start.15 = (bf16[2,64,768]{2,1,0:T(8,128)(2,1)S(1)}, bf16[2,64,768]{2,1,0:T(8,128)(2,1)S(1)}, u32[]{:S(2)}, u32[]{:S(2)}) collective-permute-start(bf16[2,64,768]{2,1,0:T(8,128)(2,1)S(1)} %get-tuple-element.30), channel_id=1, source_target_pairs={{0,128},{64,192},{128,0},{192,64},{1,129},{65,193},{129,1},{193,65... | collective-permute-start | bytes 589832 | tf_op jit(solution)/shard_map/ppermute | solution.py:346
  81.9 10.1 %collective-permute-start.16 = (bf16[2,64,768]{2,1,0:T(8,128)(2,1)S(1)}, bf16[2,64,768]{2,1,0:T(8,128)(2,1)S(1)}, u32[]{:S(2)}, u32[]{:S(2)}) collective-permute-start(bf16[2,64,768]{2,1,0:T(8,128)(2,1)S(1)} %get-tuple-element.31), channel_id=1, source_target_pairs={{0,192},{64,0},{128,64},{192,128},{1,193},{65,1},{129,65},{193,129... | collective-permute-start | bytes 589832 | tf_op jit(solution)/shard_map/ppermute | solution.py:346
  83.0 8.9 %copy-start.10 = (s32[8,11]{1,0:T(8,128)S(1)}, s32[8,11]{1,0:T(8,128)}, u32[]{:S(2)}) copy-start(s32[8,11]{1,0:T(8,128)} %get-tuple-element.27.own_labels_ref) | copy-start | bytes 1060
  83.0 8.9 %copy-start.13 = (s32[1,8]{1,0:T(1,128)S(1)}, s32[1,8]{1,0:T(1,128)}, u32[]{:S(2)}) copy-start(s32[1,8]{1,0:T(1,128)} %slots_ref.1) | copy-start | bytes 100
  (5 other events, 3.3 us)

commit v2 on v1

--- a/solution.py
+++ b/solution.py
@@ -23,6 +23,7 @@
 
 VMEM = pl.BlockSpec(memory_space=pltpu.VMEM)
 SMEM = pl.BlockSpec(memory_space=pltpu.SMEM)
+HBM = pl.BlockSpec(memory_space=pltpu.HBM)
 LIMIT = pltpu.CompilerParams(vmem_limit_bytes=12 * 1024 * 1024)
 
 
@@ -59,27 +60,36 @@
     )(blocks, stiffness, perm)
 
 
-def select_kernel(wanted_ref, place_ref, *refs):
-    held, outs = refs[:NZ], refs[NZ:]
-    x, z, c = place_ref[1], place_ref[2], place_ref[3]
+def select_kernel(wanted_ref, *refs):
+    n = NX * NC
+    held, outs, stage, sems = refs[:NZ], refs[NZ:NZ + n], refs[NZ + n], refs[NZ + n + 1]
+    x, z, c = (lax.axis_index(name) for name in AXES[1:])
+    copies = []
     for i, b in enumerate(ORDER):
         target = ((x + b // NC) & (NX - 1)) * NC + (c ^ (b % NC))
         for s in range(NZ):
             home = ((z - s) & (NZ - 1)) * C
             for m in range(C):
-                outs[i][home + m] = held[s][wanted_ref[target, home + m]]
-
-
-def select(wanted, place, held):
-    shape = jax.ShapeDtypeStruct((NZ * C, CK, LANES), jnp.bfloat16)
+                stage[i, home + m] = held[s][wanted_ref[target, 0, home + m]]
+        copy = pltpu.make_async_copy(stage.at[i], outs[i], sems.at[i])
+        copy.start()
+        copies.append(copy)
+    for copy in copies:
+        copy.wait()
+
+
+def select(wanted, held):
+    n = NX * NC
+    shape = (NZ * C, CK, LANES)
     return pl.pallas_call(
         select_kernel,
-        out_shape=[shape] * (NX * NC),
-        in_specs=[SMEM, SMEM] + [VMEM] * NZ,
-        out_specs=[VMEM] * (NX * NC),
+        out_shape=[jax.ShapeDtypeStruct(shape, jnp.bfloat16)] * n,
+        in_specs=[SMEM] + [VMEM] * NZ,
+        out_specs=[HBM] * n,
+        scratch_shapes=[pltpu.VMEM((n,) + shape, jnp.bfloat16), pltpu.SemaphoreType.DMA((n,))],
         compiler_params=LIMIT,
         name="select",
-    )(wanted, place, *held)
+    )(wanted, *held)
 
 
 def fill(table, own_ref, parts, sems):
@@ -115,12 +125,12 @@
         ).astype(jnp.bfloat16))
 
 
-def follower_kernel(at_ref, place_ref, send_ref, own_ref, y_ref, labels_ref, *refs):
+def follower_kernel(at_ref, send_ref, own_ref, y_ref, labels_ref, *refs):
     n = NX * NC * CHUNKS
     parts, outs, table, sems = refs[:n], refs[n:n + NG], refs[n + NG], refs[n + NG + 1]
     fill(table, own_ref, parts, sems)
     for s in range(NG):
-        target = (place_ref[0] + s) & (NG - 1)
+        target = (lax.axis_index(AXES[0]) + s) & (NG - 1)
         for q in range(2):
             spot = target * 2 + q
             row = HALF + send_ref[0, spot]
@@ -146,22 +156,21 @@
 
 
 ROW_COST = pl.CostEstimate(flops=2 * 8 * 6 * BLK * LANES * LANES, bytes_accessed=5_000_000, transcendentals=0)
-ANY = pl.BlockSpec(memory_space=pltpu.HBM)
-
-
-def followers(at, place, send, own, y, labels, parts):
+
+
+def followers(at, send, own, y, labels, parts):
     shape = jax.ShapeDtypeStruct((2, BLK, WIDE), jnp.bfloat16)
     table = jax.ShapeDtypeStruct((TABLE + ROWS + 1, 32, LANES), jnp.bfloat16)
     return pl.pallas_call(
         follower_kernel,
         out_shape=[shape] * NG + [table],
-        in_specs=[SMEM] * 3 + [VMEM] * 3 + [ANY] * len(parts),
+        in_specs=[SMEM] * 2 + [VMEM] * 3 + [HBM] * len(parts),
         out_specs=[VMEM] * (NG + 1),
         scratch_shapes=[pltpu.SemaphoreType.DMA((len(parts),))],
         compiler_params=LIMIT,
         cost_estimate=ROW_COST,
         name="followers",
-    )(at, place, send, own, y, labels, *parts)
+    )(at, send, own, y, labels, *parts)
 
 
 def leaders(at, y, table):
@@ -176,21 +185,69 @@
     )(at, y, table)
 
 
-def label_kernel(place_ref, columns_ref, fetch_ref, codes_ref, mine_ref, send_ref, lead_ref, follow_ref):
-    g, x, z, c = (place_ref[i] for i in range(4))
+NOTE = NZ * C + 2 * HALF
+
+
+def code_kernel(slots_ref, send_ref, codes_ref, order_ref):
+    g = lax.axis_index(AXES[0])
+    shape = (NG, 1, 2)
+    spot = lax.broadcasted_iota(jnp.int32, shape, 0) * 2 + lax.broadcasted_iota(jnp.int32, shape, 2)
+    lane = lax.broadcasted_iota(jnp.int32, (1, HALF), 1)
+    codes, order = jnp.zeros(shape, jnp.int32), jnp.zeros((1, HALF), jnp.int32)
+    for i in range(HALF):
+        codes = jnp.where(spot == slots_ref[0, i], g * HALF + i, codes)
+        order = jnp.where(lane == send_ref[0, i], i, order)
+    codes_ref[...] = codes
+    order_ref[...] = order
+
+
+def code_rows(slots, send):
+    return pl.pallas_call(
+        code_kernel,
+        out_shape=[
+            jax.ShapeDtypeStruct((NG, 1, 2), jnp.int32), jax.ShapeDtypeStruct((1, HALF), jnp.int32)
+        ],
+        in_specs=[SMEM] * 2,
+        out_specs=[VMEM] * 2,
+        name="codes",
+    )(slots, send)
+
+
+def note_kernel(lists_ref, order_ref, returned_ref, out):
+    first = NZ * C
+    for d in range(NX * NC):
+        out[d, :, 0:first] = lists_ref[d:d + 1, :]
+        out[d, :, first:first + HALF] = order_ref[...]
+        for t in range(NG):
+            out[d, :, first + HALF + 2 * t:first + HALF + 2 * t + 2] = returned_ref[t]
+
+
+def note_rows(lists, order, returned):
+    return pl.pallas_call(
+        note_kernel,
+        out_shape=jax.ShapeDtypeStruct((NX * NC, 1, NOTE), jnp.int32),
+        in_specs=[VMEM] * 3,
+        out_specs=VMEM,
+        name="note",
+    )(lists, order, returned)
+
+
+def label_kernel(columns_ref, fetch_ref, codes_ref, send_ref, lead_ref, follow_ref):
+    g, x, z, c = (lax.axis_index(name) for name in AXES)
     device = x * (NZ * NC) + z * NC + c
 
     def slot(i, k):
         column = columns_ref[i, k]
         ghost = jnp.maximum(column - ROWS, 0)
-        peer = ghost >> 2
         local = column < ROWS
-        row = jnp.where(local, jnp.maximum(column, 0), fetch_ref[peer, ghost & 3])
-        late = jnp.maximum(row - HALF, 0)
-        group = ((peer >> 4) * NC + (peer & 1)) * HALF
-        code = jnp.where(local, mine_ref[late], codes_ref[(peer >> 1) & (NZ - 1), group + late])
-        code = jnp.where(row < HALF, g * HALF + row, code)
-        label = ((code >> 3) * N_DEV + jnp.where(local, device, peer)) * HALF + (code & 7)
+        asked = ghost >> 2
+        peer = jnp.where(local, device, asked)
+        row = jnp.where(local, jnp.maximum(column, 0), fetch_ref[asked, ghost & 3])
+        group = ((peer >> 4) * NC + (peer & 1)) * 2 * HALF
+        line = (peer >> 1) & (NZ - 1)
+        spot = codes_ref[line, 0, group + jnp.maximum(row - HALF, 0)]
+        code = jnp.where(row < HALF, g * HALF + row, codes_ref[line, 0, group + HALF + spot])
+        label = ((code >> 3) * N_DEV + peer) * HALF + (code & 7)
         return jnp.where(column >= 0, label, -1)
 
     def row(i, carry):
@@ -203,18 +260,18 @@
     lax.fori_loop(0, HALF, row, 0)
 
 
-def label_rows(place, columns, fetch, codes, mine, send):
+def label_rows(columns, fetch, codes, send):
     labels = jax.ShapeDtypeStruct((HALF, K), jnp.int32)
     return pl.pallas_call(
         label_kernel,
         out_shape=[labels, labels],
-        in_specs=[SMEM] * 6,
+        in_specs=[SMEM] * 4,
         out_specs=[SMEM] * 2,
         name="labels",
-    )(place, columns, fetch, codes, mine, send)
-
-
-def merge_kernel(place_ref, slots_ref, lead_ref, own_labels_ref, *refs):
+    )(columns, fetch, codes, send)
+
+
+def merge_kernel(slots_ref, lead_ref, own_labels_ref, *refs):
     parts, out, labels_ref = refs[:NG], refs[NG], refs[NG + 1]
     tiles, stage, sems, digits, work, steps_ref, next_ref, next_sem = refs[NG + 2:]
     per = SLOTS // 2
@@ -228,7 +285,7 @@
     spots = []
     for n in range(HALF):
         spot = slots_ref[0, n]
-        spots.append(((place_ref[0] - (spot >> 1)) & (NG - 1)) * 2 + (spot & 1))
+        spots.append(((lax.axis_index(AXES[0]) - (spot >> 1)) & (NG - 1)) * 2 + (spot & 1))
         work[n:n + 1, :] = digits[pl.ds(spots[n], 1), :]
     labels = jnp.where(lane < 2 * K, pltpu.roll(work[...], K, 1), -1)
     work[...] = labels
@@ -316,14 +373,14 @@
         save(n).wait()
 
 
-def merge(place, slots, lead, own_labels, parts):
+def merge(slots, lead, own_labels, parts):
     return pl.pallas_call(
         merge_kernel,
         out_shape=[
             jax.ShapeDtypeStruct((HALF, BLK, 2 * K * BLK), jnp.bfloat16),
             jax.ShapeDtypeStruct((HALF, 2 * K), jnp.int32),
         ],
-        in_specs=[SMEM] * 2 + [VMEM] * (2 + NG),
+        in_specs=[SMEM] + [VMEM] * (2 + NG),
         out_specs=[pl.BlockSpec(memory_space=pl.ANY), VMEM],
         scratch_shapes=[
             pltpu.VMEM((2 * HALF * SLOTS // 2, BLK, LANES), jnp.bfloat16),
@@ -337,7 +394,7 @@
         ],
         compiler_params=LIMIT,
         name="merge",
-    )(place, slots, lead, own_labels, *parts)
+    )(slots, lead, own_labels, *parts)
 
 
 def shift(value, axis, size, by):
@@ -359,7 +416,6 @@
 def per_device(stiffness, prolongator, columns, fetch_rows, send_order, partner_slot):
     g, x, z, c = (lax.axis_index(name) for name in AXES)
     device = x * (NZ * NC) + z * NC + c
-    place = jnp.stack([g, x, z, c]).astype(jnp.int32)
     own = prolongator.reshape(ROWS, 32, LANES)
 
     held = []
@@ -372,20 +428,24 @@
         got[3] = shift(got[4], "z", NZ, NZ - 1)
         held.append([got[s] for s in range(NZ)])
 
-    sending, slots = send_order[0], partner_slot[0]
-    eight = jnp.arange(HALF, dtype=jnp.int32)
-    codes = jnp.sum(jnp.where(slots[:, None] == eight[None, :], (g * HALF + eight)[:, None], 0), axis=0)
+    codes, order = code_rows(partner_slot, send_order)
     returned = lax.all_to_all(codes, "grp", split_axis=0, concat_axis=0, tiled=True)
-    mine = jnp.sum(jnp.where(sending[:, None] == eight[None, :], returned[:, None], 0), axis=0)
+
+    lane = jnp.arange(LANES, dtype=jnp.int32)
+    inner = lane & (BLK - 1)
+    source = (lane & BLK) + jnp.where(inner < 32, 2 * inner, 2 * (inner - 32) + 1)
+    perm = (lane[:, None] == source[None, :]).astype(jnp.bfloat16)
+    y = products(prolongator.reshape(ROWS, BLK, BLK), stiffness, perm)
+    returned, y = lax.optimization_barrier((returned, y))
 
     lists = fetch_rows.reshape(NX, NZ, NC, C).transpose(0, 2, 1, 3).reshape(NX * NC, NZ * C)
-    note = jnp.concatenate([lists, jnp.broadcast_to(mine[None, :], (NX * NC, HALF))], axis=1)
+    note = note_rows(lists, order, returned)
     wanted = lax.all_to_all(note, ("x", "core"), split_axis=0, concat_axis=0, tiled=True)
-    plane = wanted[:, NZ * C:].reshape(1, NX * NC * HALF)
+    plane = wanted[:, :, NZ * C:].reshape(1, 1, NX * NC * 2 * HALF)
     every = lax.all_to_all(
-        jnp.broadcast_to(plane, (NZ, NX * NC * HALF)), "z", split_axis=0, concat_axis=0, tiled=True
+        jnp.broadcast_to(plane, (NZ, 1, NX * NC * 2 * HALF)), "z", split_axis=0, concat_axis=0, tiled=True
     )
-    lead_labels, follower_labels = label_rows(place, columns, fetch_rows, every, mine, send_order)
+    lead_labels, follower_labels = label_rows(columns, fetch_rows, every, send_order)
 
     ghost = columns - ROWS
     peer = ghost >> 2
@@ -399,22 +459,16 @@
         jnp.concatenate([none, at[HALF:]], axis=1),
     ])
 
-    lane = jnp.arange(LANES, dtype=jnp.int32)
-    inner = lane & (BLK - 1)
-    source = (lane & BLK) + jnp.where(inner < 32, 2 * inner, 2 * (inner - 32) + 1)
-    perm = (lane[:, None] == source[None, :]).astype(jnp.bfloat16)
-    y = products(prolongator.reshape(ROWS, BLK, BLK), stiffness, perm)
-
     parts = []
     for h in range(CHUNKS):
-        chosen = select(wanted, place, held[h])
+        chosen = select(wanted, held[h])
         moved = {b: cross(chosen[i], b) for i, b in enumerate(ORDER)}
-        parts += [moved[b] for b in range(NX * NC)]
-
-    *sent, table = followers(at, place, send_order, own, y, follower_labels, parts)
+        parts += [pltpu.with_memory_space_constraint(moved[b], pltpu.HBM) for b in range(NX * NC)]
+
+    *sent, table = followers(at, send_order, own, y, follower_labels, parts)
     arrived = [sent[0]] + [shift(sent[s], "grp", NG, s) for s in range(1, NG)]
     lead = leaders(at, y, table)
-    return tuple(merge(place, partner_slot, lead, lead_labels, arrived))
+    return tuple(merge(partner_slot, lead, lead_labels, arrived))
 
 
 def solution(mesh):

time: 96.9 us -> 97.8 us (level)
  blocking collectives: 0 us -> 8.56 us
  other arithmetic: 4.23 us -> 0.11 us
  Pallas kernels: 20.6 us -> 23.2 us
  starting transfers between devices: 40.3 us -> 38 us
  waiting for transfers between devices: 17.8 us -> 15.6 us
  local copies, waits for them, and re-layouts: 11.8 us -> 10.1 us
    all_to_all x0 -> x1, blocking collectives: none -> 8.56 us  [per_device(): lax.all_to_all(note, ('x', 'core'), split_axis=0, concat_axis=0, tiled=True)]
    all_to_all x2 -> x1, starting transfers between devices: 8.91 us -> 3.95 us  [per_device(): lax.all_to_all(jnp.broadcast_to(plane, (NZ, 1, NX * NC * 2 * HALF)), 'z',...]
    all_to_all x1, waiting for transfers between devices: 3.61 us -> 0.01 us  [per_device(): lax.all_to_all(codes, 'grp', split_axis=0, concat_axis=0, tiled=True)]
    ppermute x10, starting transfers between devices: 19.3 us -> 21.8 us  [shift(): lax.ppermute(value, axis, [(i, (i + by) % size) for i in range(size)])]
    pallas_call x1 -> x3, Pallas kernels: 2.23 us -> 4.27 us  [the longest x1 1.6 us: select(): pl.pallas_call(select_kernel, out_shape=[jax.ShapeDtypeStruct(shape, jnp....]
    all_to_all x2 -> x1, waiting for transfers between devices: 5.59 us -> 7.54 us  [per_device(): lax.all_to_all(jnp.broadcast_to(plane, (NZ, 1, NX * NC * 2 * HALF)), 'z',...]
    unnamed x36 -> x32, local copies, waits for them, and re-layouts: 9.35 us -> 7.49 us
    ppermute x10, waiting for transfers between devices: 6.24 us -> 4.59 us  [shift(): lax.ppermute(value, axis, [(i, (i + by) % size) for i in range(size)])]
  transfers between devices with their start and end apart: 20 -> 19, of which waited for: 6 -> 4; matrix products, arithmetic and copies ran while one was open for 7% -> 4% of each run, Pallas kernels for 13% -> 16%
where the time goes in v2:
time: 97.8 us; the launch traced here: 96.4 us
  starting transfers between devices  38 us (39%)
  Pallas kernels  23.2 us (24%)
  waiting for transfers between devices  15.6 us (16%)
  local copies, waits for them, and re-layouts  10.1 us (10%)
  blocking collectives  8.56 us (9%)
  between operations  0.98 us (1%)
    ppermute x10, starting transfers between devices, shift(): lax.ppermute(value, axis, [(i, (i + by) % size) for i in range(size)])  21.8 us
    all_to_all x1, blocking collectives, per_device(): lax.all_to_all(note, ('x', 'core'), split_axis=0, concat_axis=0, tiled=True)  8.56 us
    ppermute x7, starting transfers between devices, cross(): return lax.ppermute(value, ('x', 'core'), pairs)  7.77 us
    all_to_all x1, waiting for transfers between devices, per_device(): lax.all_to_all(jnp.broadcast_to(plane, (NZ, 1, NX * NC * 2 * HALF)), 'z',...  7.54 us
    unnamed x32, local copies, waits for them, and re-layouts  7.49 us
    pallas_call x1, Pallas kernels, label_rows(): pl.pallas_call(label_kernel, out_shape=[labels, labels], in_specs=[SMEM]...  4.9 us
    pallas_call x1, Pallas kernels, products(): pl.pallas_call(products_kernel, out_shape=jax.ShapeDtypeStruct((ROWS, BLK...  4.84 us
    ppermute x10, waiting for transfers between devices, shift(): lax.ppermute(value, axis, [(i, (i + by) % size) for i in range(size)])  4.59 us
  transfers between devices with their start and end apart: 19, of which 4 were waited for; matrix products, arithmetic and copies ran while one was open for 4% of the time, Pallas kernels for 16%

profile of v2, /device:TPU:2, one launch (start us, length us, event | category | flops | bytes accessed | tf_op | source)
XLA Modules:
  0.0 96.4 jit_solution(8058916321383205074)
XLA Ops:
  0.6 0.9 copy.13
  1.6 7.3 %collective-permute-start.2 = (bf16[16,32,128]{2,1,0:T(8,128)(2,1)S(1)}, bf16[16,32,128]{2,1,0:T(8,128)(2,1)S(1)}, u32[]{:S(2)}, u32[]{:S(2)}) collective-permute-start(bf16[16,32,128]{2,1,0:T(8,128)(2,1)S(1)} %bitcast.7), channel_id=1, source_target_pairs={{0,8},{2,10},{4,12},{6,14},{8,0},{10,2},{12,4},{14,6},{1,9},{3,11}... | collective-permute-start | bytes 393224 | tf_op jit(solution)/shard_map/ppermute | solution.py:403
  9.0 2.8 %collective-permute-start.1 = (bf16[16,32,128]{2,1,0:T(8,128)(2,1)S(1)}, bf16[16,32,128]{2,1,0:T(8,128)(2,1)S(1)}, u32[]{:S(2)}, u32[]{:S(2)}) collective-permute-start(bf16[16,32,128]{2,1,0:T(8,128)(2,1)S(1)} %bitcast.10), channel_id=1, source_target_pairs={{0,4},{2,6},{4,8},{6,10},{8,12},{10,14},{12,0},{14,2},{1,5},{3,7},... | collective-permute-start | bytes 393224 | tf_op jit(solution)/shard_map/ppermute | solution.py:403
  11.9 1.9 %collective-permute-start = (bf16[16,32,128]{2,1,0:T(8,128)(2,1)S(1)}, bf16[16,32,128]{2,1,0:T(8,128)(2,1)S(1)}, u32[]{:S(2)}, u32[]{:S(2)}) collective-permute-start(bf16[16,32,128]{2,1,0:T(8,128)(2,1)S(1)} %bitcast.11), channel_id=1, source_target_pairs={{0,2},{2,4},{4,6},{6,8},{8,10},{10,12},{12,14},{14,0},{1,3},{3,5},... | collective-permute-start | bytes 393224 | tf_op jit(solution)/shard_map/ppermute | solution.py:403
  13.8 1.3 %codes.1 = (s32[4,1,2]{2,1,0:T(1,128)}, s32[1,8]{1,0:T(1,128)}) custom-call(s32[1,8]{1,0:T(1,128)} %slots_ref.3, s32[1,8]{1,0:T(1,128)} %send_ref.5), custom_call_target="tpu_custom_call" | custom-call | tf_op jit(solution)/shard_map/codes/pallas_call | solution.py:205
  15.1 4.5 %all-to-all-start = ((s32[4,1,2]{2,1,0:T(1,128)}), s32[4,1,2]{2,1,0:T(1,128)S(1)}, u32[]{:S(2)}, u32[]{:S(2)}) async-start(s32[4,1,2]{2,1,0:T(1,128)} %get-tuple-element.21), calls=%async_computation | async-start | bytes 4096 | tf_op jit(solution)/shard_map/all_to_all | solution.py:432
  19.5 2.3 %collective-permute-start.4 = (bf16[16,32,128]{2,1,0:T(8,128)(2,1)S(1)}, bf16[16,32,128]{2,1,0:T(8,128)(2,1)S(1)}, u32[]{:S(2)}, u32[]{:S(2)}) collective-permute-start(bf16[16,32,128]{2,1,0:T(8,128)(2,1)S(1)} %collective-permute-done.2.refs_4_), channel_id=1, source_target_pairs={{0,2},{2,4},{4,6},{6,8},{8,10},{10,12},{12,14},{14,0},{1,3},{3,5},... | collective-permute-start | bytes 393224 | tf_op jit(solution)/shard_map/ppermute | solution.py:403
  21.8 1.0 %collective-permute-start.3 = (bf16[16,32,128]{2,1,0:T(8,128)(2,1)S(1)}, bf16[16,32,128]{2,1,0:T(8,128)(2,1)S(1)}, u32[]{:S(2)}, u32[]{:S(2)}) collective-permute-start(bf16[16,32,128]{2,1,0:T(8,128)(2,1)S(1)} %collective-permute-done.2.refs_4_), channel_id=1, source_target_pairs={{0,14},{2,0},{4,2},{6,4},{8,6},{10,8},{12,10},{14,12},{1,15},{3,1}... | collective-permute-start | bytes 393224 | tf_op jit(solution)/shard_map/ppermute | solution.py:403
  22.9 1.2 %reshape.33.p_ref = bf16[16,64,64]{2,1,0:T(8,128)(2,1)S(1)} reshape(bf16[16,4096]{1,0:T(8,128)(2,1)} %param.7) | data formatting | bytes 262144 | tf_op jit(solution)/shard_map/reshape | solution.py:438
  24.1 0.8 copy.12.fetch_ref
  25.5 1.4 %copy-done = bf16[16,64,704]{2,1,0:T(8,128)(2,1)S(1)} copy-done((bf16[16,64,704]{2,1,0:T(8,128)(2,1)S(1)}, bf16[16,64,704]{2,1,0:T(8,128)(2,1)}, u32[]{:S(2)}) %copy-start) | copy-done | bytes 1441816
  26.9 4.8 %products.1.y_ref = bf16[16,64,768]{2,1,0:T(8,128)(2,1)S(1)} custom-call(bf16[16,64,64]{2,1,0:T(8,128)(2,1)S(1)} %reshape.33.p_ref, bf16[16,64,704]{2,1,0:T(8,128)(2,1)S(1)} %copy-done, bf16[128,128]{1,0:T(8,128)(2,1)S(1)} %fusion.perm_ref), custom_call_target="tpu_custom_call" | custom-call | flops 301989888 | bytes 3200000 | tf_op jit(solution)/shard_map/products/pallas_call | solution.py:52
  32.4 1.4 %note.1 = s32[8,1,48]{2,1,0:T(1,128)} custom-call(s32[8,32]{1,0:T(8,128)} %reshape.36.lists_ref, s32[1,8]{1,0:T(1,128)} %get-tuple-element.23.order_ref, s32[4,1,2]{2,1,0:T(1,128)} %copy-done.14), custom_call_target="tpu_custom_call" | custom-call | tf_op jit(solution)/shard_map/note/pallas_call | solution.py:226
  33.8 8.6 %all_to_all.15.wanted_ref = s32[8,1,48]{2,1,0:T(1,128)S(1)} all-to-all(s32[8,1,48]{2,1,0:T(1,128)} %note.1), channel_id=1, replica_groups=mesh['grp'=4,'x'=4,'z'=8,'core'=2] {'x','core'}, dimensions={0} | all-to-all | bytes 3072 | tf_op jit(solution)/shard_map/all_to_all | solution.py:443
  42.4 1.6 %select.7 = (bf16[32,32,128]{2,1,0:T(8,128)(2,1)}, bf16[32,32,128]{2,1,0:T(8,128)(2,1)}, bf16[32,32,128]{2,1,0:T(8,128)(2,1)S(1)}, bf16[32,32,128]{2,1,0:T(8,128...) custom-call(s32[8,1,48]{2,1,0:T(1,128)S(1)} %all_to_all.15.wanted_re, ...), custom_call_target="tpu_custom_call" | custom-call | tf_op jit(solution)/shard_map/select/pallas_call | solution.py:84
  45.4 0.7 copy-done.7
  46.7 1.4 %collective-permute-start.9 = (bf16[32,32,128]{2,1,0:T(8,128)(2,1)}, bf16[32,32,128]{2,1,0:T(8,128)(2,1)S(1)}, u32[]{:S(2)}, u32[]{:S(2)}) collective-permute-start(bf16[32,32,128]{2,1,0:T(8,128)(2,1)} %copy-done.7), channel_id=1, source_target_pairs={{0,17},{1,16},{16,33},{17,32},{32,49},{33,48},{48,1},{49,0},{2,19}... | collective-permute-start | bytes 786440 | tf_op jit(solution)/shard_map/ppermute | solution.py:413
  48.0 2.1 %collective-permute-start.10 = (bf16[32,32,128]{2,1,0:T(8,128)(2,1)}, bf16[32,32,128]{2,1,0:T(8,128)(2,1)}, u32[]{:S(2)}, u32[]{:S(2)}) collective-permute-start(bf16[32,32,128]{2,1,0:T(8,128)(2,1)} %copy-done.6), channel_id=1, source_target_pairs={{0,32},{1,33},{16,48},{17,49},{32,0},{33,1},{48,16},{49,17},{2,34}... | collective-permute-start | bytes 786440 | tf_op jit(solution)/shard_map/ppermute | solution.py:413
  50.1 1.1 %collective-permute-start.11 = (bf16[32,32,128]{2,1,0:T(8,128)(2,1)S(1)}, bf16[32,32,128]{2,1,0:T(8,128)(2,1)}, u32[]{:S(2)}, u32[]{:S(2)}) collective-permute-start(bf16[32,32,128]{2,1,0:T(8,128)(2,1)S(1)} %get-tuple-element.31), channel_id=1, source_target_pairs={{0,33},{1,32},{16,49},{17,48},{32,1},{33,0},{48,17},{49,16},{2,35}... | collective-permute-start | bytes 786440 | tf_op jit(solution)/shard_map/ppermute | solution.py:413
  51.2 1.1 %collective-permute-start.12 = (bf16[32,32,128]{2,1,0:T(8,128)(2,1)S(1)}, bf16[32,32,128]{2,1,0:T(8,128)(2,1)}, u32[]{:S(2)}, u32[]{:S(2)}) collective-permute-start(bf16[32,32,128]{2,1,0:T(8,128)(2,1)S(1)} %get-tuple-element.32), channel_id=1, source_target_pairs={{0,48},{1,49},{16,0},{17,1},{32,16},{33,17},{48,32},{49,33},{2,50}... | collective-permute-start | bytes 786440 | tf_op jit(solution)/shard_map/ppermute | solution.py:413
  52.3 3.1 %collective-permute-done.8.refs_2_ = bf16[32,32,128]{2,1,0:T(8,128)(2,1)S(1)} collective-permute-done((bf16[32,32,128]{2,1,0:T(8,128)(2,1)}, bf16[32,32,128]{2,1,0:T(8,128)(2,1)S(1)}, u32[]{:S(2)}, u32[]{:S(2)}) %collective-permute-start.8) | collective-permute-done | bytes 262176 | tf_op jit(solution)/shard_map/ppermute | solution.py:413
  55.4 1.6 %collective-permute-start.13 = (bf16[32,32,128]{2,1,0:T(8,128)(2,1)S(1)}, bf16[32,32,128]{2,1,0:T(8,128)(2,1)}, u32[]{:S(2)}, u32[]{:S(2)}) collective-permute-start(bf16[32,32,128]{2,1,0:T(8,128)(2,1)S(1)} %get-tuple-element.33), channel_id=1, source_target_pairs={{0,49},{1,48},{16,1},{17,0},{32,17},{33,16},{48,33},{49,32},{2,51}... | collective-permute-start | bytes 786440 | tf_op jit(solution)/shard_map/ppermute | solution.py:413
  57.8 3.9 %all-to-all-start.2 = ((s32[8,1,128]{2,1,0:T(1,128)}), s32[8,1,128]{2,1,0:T(1,128)S(1)}, u32[]{:S(2)}, u32[]{:S(2)}) async-start(s32[8,1,128]{2,1,0:T(1,128)} %broadcast_in_dim.15), calls=%async_computation.2 | async-start | bytes 8192 | tf_op jit(solution)/shard_map/all_to_all | solution.py:445
  61.8 7.5 %all-to-all-done.2.codes_ref = s32[8,1,128]{2,1,0:T(1,128)S(1)} async-done(((s32[8,1,128]{2,1,0:T(1,128)}), s32[8,1,128]{2,1,0:T(1,128)S(1)}, u32[]{:S(2)}, u32[]{:S(2)}) %all-to-all-start.2) | async-done | bytes 4128 | tf_op jit(solution)/shard_map/all_to_all | solution.py:445
  70.0 4.9 %labels.1 = (s32[8,11]{1,0:T(8,128)}, s32[8,11]{1,0:T(8,128)}) custom-call(s32[16,11]{1,0:T(8,128)} %columns_ref.1, s32[64,4]{1,0:T(8,128)} %copy-done.8, s32[8,1,128]{2,1,0:T(1,128)} %copy-done.13, s32[1,8]{1,0:T(1,128)} %send_ref.5), custom_call_target="tpu_custom_call" | custom-call | tf_op jit(solution)/shard_map/labels/pallas_call | solution.py:265
  76.3 2.9 %followers.1 = (bf16[2,64,768]{2,1,0:T(8,128)(2,1)S(1)}, bf16[2,64,768]{2,1,0:T(8,128)(2,1)S(1)}, bf16[2,64,768]{2,1,0:T(8,128)(2,1)S(1)}, bf16[2,64,768]{2,1,0:T(8,128)(2,1)S(1)}, bf16[273,32,128]{2,1,0:T(8,128)(2,1)S(1)}) custom-call(s32[16,12]{1,0:T(8,128)S(1)} %select_add_fusion.at_ref, s32[1,8]{1,0:T(1,128)S(1)} %copy-done.4, ...), custom_call_target="tpu_custom_call" | custom-call | flops 100663296 | bytes 5000000 | tf_op jit(solution)/shard_map/followers/pallas_call | solution.py:164
  79.1 2.1 %collective-permute-start.14 = (bf16[2,64,768]{2,1,0:T(8,128)(2,1)S(1)}, bf16[2,64,768]{2,1,0:T(8,128)(2,1)S(1)}, u32[]{:S(2)}, u32[]{:S(2)}) collective-permute-start(bf16[2,64,768]{2,1,0:T(8,128)(2,1)S(1)} %get-tuple-element.37), channel_id=1, source_target_pairs={{0,64},{64,128},{128,192},{192,0},{1,65},{65,129},{129,193},{193,1... | collective-permute-start | bytes 589832 | tf_op jit(solution)/shard_map/ppermute | solution.py:403
  81.2 2.7 %collective-permute-start.15 = (bf16[2,64,768]{2,1,0:T(8,128)(2,1)S(1)}, bf16[2,64,768]{2,1,0:T(8,128)(2,1)S(1)}, u32[]{:S(2)}, u32[]{:S(2)}) collective-permute-start(bf16[2,64,768]{2,1,0:T(8,128)(2,1)S(1)} %get-tuple-element.38), channel_id=1, source_target_pairs={{0,128},{64,192},{128,0},{192,64},{1,129},{65,193},{129,1},{193,65... | collective-permute-start | bytes 589832 | tf_op jit(solution)/shard_map/ppermute | solution.py:403
  83.9 1.5 %collective-permute-start.16 = (bf16[2,64,768]{2,1,0:T(8,128)(2,1)S(1)}, bf16[2,64,768]{2,1,0:T(8,128)(2,1)S(1)}, u32[]{:S(2)}, u32[]{:S(2)}) collective-permute-start(bf16[2,64,768]{2,1,0:T(8,128)(2,1)S(1)} %get-tuple-element.39), channel_id=1, source_target_pairs={{0,192},{64,0},{128,64},{192,128},{1,193},{65,1},{129,65},{193,129... | collective-permute-start | bytes 589832 | tf_op jit(solution)/shard_map/ppermute | solution.py:403
  85.4 2.7 %leaders.1.lead_ref = bf16[8,64,768]{2,1,0:T(8,128)(2,1)S(1)} custom-call(s32[16,12]{1,0:T(8,128)S(1)} %select_add_fusion.at_ref, bf16[16,64,768]{2,1,0:T(8,128)(2,1)S(1)} %products.1.y_ref, bf16[273,32,128]{2,1,0:T(8,128)(2,1)S(1)} %get-tuple-element.34.table), custom_call_target="tpu_custom_call" | custom-call | flops 100663296 | bytes 5000000 | tf_op jit(solution)/shard_map/leaders/pallas_call | solution.py:177
  88.1 4.6 %collective-permute-done.15.refs_2_ = bf16[2,64,768]{2,1,0:T(8,128)(2,1)S(1)} collective-permute-done((bf16[2,64,768]{2,1,0:T(8,128)(2,1)S(1)}, bf16[2,64,768]{2,1,0:T(8,128)(2,1)S(1)}, u32[]{:S(2)}, u32[]{:S(2)}) %collective-permute-start.15) | collective-permute-done | bytes 196640 | tf_op jit(solution)/shard_map/ppermute | solution.py:403
  92.7 3.6 %merge.1 = (bf16[8,64,1408]{2,1,0:T(8,128)(2,1)}, s32[8,22]{1,0:T(8,128)}) custom-call(s32[1,8]{1,0:T(1,128)S(1)} %copy-done.5, bf16[8,64,768]{2,1,0:T(8,128)(2,1)S(1)} %leaders.1.lead_ref, s32[8,11]{1,0:T(8,128)S(1)} %copy-done.2, bf16[2,64,768]{2,1,0:T(8,128)(2,1)S(1)} %get-tuple-element.36.refs_0_, ...), custom_call_target="tpu_custom_call" | custom-call | tf_op jit(solution)/shard_map/merge/pallas_call | solution.py:377
  (58 shorter events, 6.3 us)
Async XLA Ops:
  1.6 18.0 %collective-permute-start.2 = (bf16[16,32,128]{2,1,0:T(8,128)(2,1)S(1)}, bf16[16,32,128]{2,1,0:T(8,128)(2,1)S(1)}, u32[]{:S(2)}, u32[]{:S(2)}) collective-permute-start(bf16[16,32,128]{2,1,0:T(8,128)(2,1)S(1)} %bitcast.7), channel_id=1, source_target_pairs={{0,8},{2,10},{4,12},{6,14},{8,0},{10,2},{12,4},{14,6},{1,9},{3,11}... | collective-permute-start | bytes 393224 | tf_op jit(solution)/shard_map/ppermute | solution.py:403
  8.8 13.0 %collective-permute-start.6 = (bf16[16,32,128]{2,1,0:T(8,128)(2,1)S(1)}, bf16[16,32,128]{2,1,0:T(8,128)(2,1)S(1)}, u32[]{:S(2)}, u32[]{:S(2)}) collective-permute-start(bf16[16,32,128]{2,1,0:T(8,128)(2,1)S(1)} %bitcast.8), channel_id=1, source_target_pairs={{0,14},{2,0},{4,2},{6,4},{8,6},{10,8},{12,10},{14,12},{1,15},{3,1}... | collective-permute-start | bytes 393224 | tf_op jit(solution)/shard_map/ppermute | solution.py:403
  8.9 33.4 %collective-permute-start.5 = (bf16[16,32,128]{2,1,0:T(8,128)(2,1)S(1)}, bf16[16,32,128]{2,1,0:T(8,128)(2,1)S(1)}, u32[]{:S(2)}, u32[]{:S(2)}) collective-permute-start(bf16[16,32,128]{2,1,0:T(8,128)(2,1)S(1)} %bitcast.9), channel_id=1, source_target_pairs={{0,12},{2,14},{4,0},{6,2},{8,4},{10,6},{12,8},{14,10},{1,13},{3,15... | collective-permute-start | bytes 393224 | tf_op jit(solution)/shard_map/ppermute | solution.py:403
  9.0 33.3 %collective-permute-start.1 = (bf16[16,32,128]{2,1,0:T(8,128)(2,1)S(1)}, bf16[16,32,128]{2,1,0:T(8,128)(2,1)S(1)}, u32[]{:S(2)}, u32[]{:S(2)}) collective-permute-start(bf16[16,32,128]{2,1,0:T(8,128)(2,1)S(1)} %bitcast.10), channel_id=1, source_target_pairs={{0,4},{2,6},{4,8},{6,10},{8,12},{10,14},{12,0},{14,2},{1,5},{3,7},... | collective-permute-start | bytes 393224 | tf_op jit(solution)/shard_map/ppermute | solution.py:403
  11.9 30.5 %collective-permute-start = (bf16[16,32,128]{2,1,0:T(8,128)(2,1)S(1)}, bf16[16,32,128]{2,1,0:T(8,128)(2,1)S(1)}, u32[]{:S(2)}, u32[]{:S(2)}) collective-permute-start(bf16[16,32,128]{2,1,0:T(8,128)(2,1)S(1)} %bitcast.11), channel_id=1, source_target_pairs={{0,2},{2,4},{4,6},{6,8},{8,10},{10,12},{12,14},{14,0},{1,3},{3,5},... | collective-permute-start | bytes 393224 | tf_op jit(solution)/shard_map/ppermute | solution.py:403
  15.1 16.7 %all-to-all-start = ((s32[4,1,2]{2,1,0:T(1,128)}), s32[4,1,2]{2,1,0:T(1,128)S(1)}, u32[]{:S(2)}, u32[]{:S(2)}) async-start(s32[4,1,2]{2,1,0:T(1,128)} %get-tuple-element.21), calls=%async_computation | async-start | bytes 4096 | tf_op jit(solution)/shard_map/all_to_all | solution.py:432
  19.5 22.8 %collective-permute-start.4 = (bf16[16,32,128]{2,1,0:T(8,128)(2,1)S(1)}, bf16[16,32,128]{2,1,0:T(8,128)(2,1)S(1)}, u32[]{:S(2)}, u32[]{:S(2)}) collective-permute-start(bf16[16,32,128]{2,1,0:T(8,128)(2,1)S(1)} %collective-permute-done.2.refs_4_), channel_id=1, source_target_pairs={{0,2},{2,4},{4,6},{6,8},{8,10},{10,12},{12,14},{14,0},{1,3},{3,5},... | collective-permute-start | bytes 393224 | tf_op jit(solution)/shard_map/ppermute | solution.py:403
  21.8 20.5 %collective-permute-start.3 = (bf16[16,32,128]{2,1,0:T(8,128)(2,1)S(1)}, bf16[16,32,128]{2,1,0:T(8,128)(2,1)S(1)}, u32[]{:S(2)}, u32[]{:S(2)}) collective-permute-start(bf16[16,32,128]{2,1,0:T(8,128)(2,1)S(1)} %collective-permute-done.2.refs_4_), channel_id=1, source_target_pairs={{0,14},{2,0},{4,2},{6,4},{8,6},{10,8},{12,10},{14,12},{1,15},{3,1}... | collective-permute-start | bytes 393224 | tf_op jit(solution)/shard_map/ppermute | solution.py:403
  24.8 6.9 %copy-start.8 = (s32[64,4]{1,0:T(8,128)}, s32[64,4]{1,0:T(8,128)S(1)}, u32[]{:S(2)}) copy-start(s32[64,4]{1,0:T(8,128)S(1)} %copy.12.fetch_ref) | copy-start | bytes 3076
  25.5 1.4 %copy-start = (bf16[16,64,704]{2,1,0:T(8,128)(2,1)S(1)}, bf16[16,64,704]{2,1,0:T(8,128)(2,1)}, u32[]{:S(2)}) copy-start(bf16[16,64,704]{2,1,0:T(8,128)(2,1)} %a_ref.1) | copy-start | bytes 4325380
  26.9 19.7 %copy-start.12 = (s32[16,11]{1,0:T(8,128)S(1)}, s32[16,11]{1,0:T(8,128)}, u32[]{:S(2)}) copy-start(s32[16,11]{1,0:T(8,128)} %columns_ref.1) | copy-start | bytes 2116
  26.9 48.7 %copy-start.4 = (s32[1,8]{1,0:T(1,128)S(1)}, s32[1,8]{1,0:T(1,128)}, u32[]{:S(2)}) copy-start(s32[1,8]{1,0:T(1,128)} %send_ref.5) | copy-start | bytes 100
  44.0 0.7 copy-start.1
  44.7 0.7 copy-start.6
  45.4 0.7 copy-start.7
  46.1 5.1 %collective-permute-start.7 = (bf16[32,32,128]{2,1,0:T(8,128)(2,1)}, bf16[32,32,128]{2,1,0:T(8,128)(2,1)S(1)}, u32[]{:S(2)}, u32[]{:S(2)}) collective-permute-start(bf16[32,32,128]{2,1,0:T(8,128)(2,1)} %get-tuple-element.27), channel_id=1, source_target_pairs={{0,1},{1,0},{16,17},{17,16},{32,33},{33,32},{48,49},{49,48},{2,3},... | collective-permute-start | bytes 786440 | tf_op jit(solution)/shard_map/ppermute | solution.py:413
  46.1 9.3 %collective-permute-start.8 = (bf16[32,32,128]{2,1,0:T(8,128)(2,1)}, bf16[32,32,128]{2,1,0:T(8,128)(2,1)S(1)}, u32[]{:S(2)}, u32[]{:S(2)}) collective-permute-start(bf16[32,32,128]{2,1,0:T(8,128)(2,1)} %get-tuple-element.28), channel_id=1, source_target_pairs={{0,16},{1,17},{16,32},{17,33},{32,48},{33,49},{48,0},{49,1},{2,18}... | collective-permute-start | bytes 786440 | tf_op jit(solution)/shard_map/ppermute | solution.py:413
  46.7 28.2 %collective-permute-start.9 = (bf16[32,32,128]{2,1,0:T(8,128)(2,1)}, bf16[32,32,128]{2,1,0:T(8,128)(2,1)S(1)}, u32[]{:S(2)}, u32[]{:S(2)}) collective-permute-start(bf16[32,32,128]{2,1,0:T(8,128)(2,1)} %copy-done.7), channel_id=1, source_target_pairs={{0,17},{1,16},{16,33},{17,32},{32,49},{33,48},{48,1},{49,0},{2,19}... | collective-permute-start | bytes 786440 | tf_op jit(solution)/shard_map/ppermute | solution.py:413
  48.0 26.9 %collective-permute-start.10 = (bf16[32,32,128]{2,1,0:T(8,128)(2,1)}, bf16[32,32,128]{2,1,0:T(8,128)(2,1)}, u32[]{:S(2)}, u32[]{:S(2)}) collective-permute-start(bf16[32,32,128]{2,1,0:T(8,128)(2,1)} %copy-done.6), channel_id=1, source_target_pairs={{0,32},{1,33},{16,48},{17,49},{32,0},{33,1},{48,16},{49,17},{2,34}... | collective-permute-start | bytes 786440 | tf_op jit(solution)/shard_map/ppermute | solution.py:413
  50.1 24.8 %collective-permute-start.11 = (bf16[32,32,128]{2,1,0:T(8,128)(2,1)S(1)}, bf16[32,32,128]{2,1,0:T(8,128)(2,1)}, u32[]{:S(2)}, u32[]{:S(2)}) collective-permute-start(bf16[32,32,128]{2,1,0:T(8,128)(2,1)S(1)} %get-tuple-element.31), channel_id=1, source_target_pairs={{0,33},{1,32},{16,49},{17,48},{32,1},{33,0},{48,17},{49,16},{2,35}... | collective-permute-start | bytes 786440 | tf_op jit(solution)/shard_map/ppermute | solution.py:413
  51.2 24.0 %copy-start.9 = (bf16[32,32,128]{2,1,0:T(8,128)(2,1)}, bf16[32,32,128]{2,1,0:T(8,128)(2,1)S(1)}, u32[]{:S(2)}) copy-start(bf16[32,32,128]{2,1,0:T(8,128)(2,1)S(1)} %collective-permute-done.7.refs_1_) | copy-start | bytes 786436
  51.2 23.7 %collective-permute-start.12 = (bf16[32,32,128]{2,1,0:T(8,128)(2,1)S(1)}, bf16[32,32,128]{2,1,0:T(8,128)(2,1)}, u32[]{:S(2)}, u32[]{:S(2)}) collective-permute-start(bf16[32,32,128]{2,1,0:T(8,128)(2,1)S(1)} %get-tuple-element.32), channel_id=1, source_target_pairs={{0,48},{1,49},{16,0},{17,1},{32,16},{33,17},{48,32},{49,33},{2,50}... | collective-permute-start | bytes 786440 | tf_op jit(solution)/shard_map/ppermute | solution.py:413
  55.4 19.8 %copy-start.10 = (bf16[32,32,128]{2,1,0:T(8,128)(2,1)}, bf16[32,32,128]{2,1,0:T(8,128)(2,1)S(1)}, u32[]{:S(2)}) copy-start(bf16[32,32,128]{2,1,0:T(8,128)(2,1)S(1)} %collective-permute-done.8.refs_2_) | copy-start | bytes 786436
  55.4 19.8 %collective-permute-start.13 = (bf16[32,32,128]{2,1,0:T(8,128)(2,1)S(1)}, bf16[32,32,128]{2,1,0:T(8,128)(2,1)}, u32[]{:S(2)}, u32[]{:S(2)}) collective-permute-start(bf16[32,32,128]{2,1,0:T(8,128)(2,1)S(1)} %get-tuple-element.33), channel_id=1, source_target_pairs={{0,49},{1,48},{16,1},{17,0},{32,17},{33,16},{48,33},{49,32},{2,51}... | collective-permute-start | bytes 786440 | tf_op jit(solution)/shard_map/ppermute | solution.py:413
  57.8 11.6 %all-to-all-start.2 = ((s32[8,1,128]{2,1,0:T(1,128)}), s32[8,1,128]{2,1,0:T(1,128)S(1)}, u32[]{:S(2)}, u32[]{:S(2)}) async-start(s32[8,1,128]{2,1,0:T(1,128)} %broadcast_in_dim.15), calls=%async_computation.2 | async-start | bytes 8192 | tf_op jit(solution)/shard_map/all_to_all | solution.py:445
  74.9 0.7 copy-start.11
  75.6 0.7 copy-start.3
  79.1 8.9 %collective-permute-start.14 = (bf16[2,64,768]{2,1,0:T(8,128)(2,1)S(1)}, bf16[2,64,768]{2,1,0:T(8,128)(2,1)S(1)}, u32[]{:S(2)}, u32[]{:S(2)}) collective-permute-start(bf16[2,64,768]{2,1,0:T(8,128)(2,1)S(1)} %get-tuple-element.37), channel_id=1, source_target_pairs={{0,64},{64,128},{128,192},{192,0},{1,65},{65,129},{129,193},{193,1... | collective-permute-start | bytes 589832 | tf_op jit(solution)/shard_map/ppermute | solution.py:403
  81.2 11.4 %collective-permute-start.15 = (bf16[2,64,768]{2,1,0:T(8,128)(2,1)S(1)}, bf16[2,64,768]{2,1,0:T(8,128)(2,1)S(1)}, u32[]{:S(2)}, u32[]{:S(2)}) collective-permute-start(bf16[2,64,768]{2,1,0:T(8,128)(2,1)S(1)} %get-tuple-element.38), channel_id=1, source_target_pairs={{0,128},{64,192},{128,0},{192,64},{1,129},{65,193},{129,1},{193,65... | collective-permute-start | bytes 589832 | tf_op jit(solution)/shard_map/ppermute | solution.py:403
  83.9 8.7 %collective-permute-start.16 = (bf16[2,64,768]{2,1,0:T(8,128)(2,1)S(1)}, bf16[2,64,768]{2,1,0:T(8,128)(2,1)S(1)}, u32[]{:S(2)}, u32[]{:S(2)}) collective-permute-start(bf16[2,64,768]{2,1,0:T(8,128)(2,1)S(1)} %get-tuple-element.39), channel_id=1, source_target_pairs={{0,192},{64,0},{128,64},{192,128},{1,193},{65,1},{129,65},{193,129... | collective-permute-start | bytes 589832 | tf_op jit(solution)/shard_map/ppermute | solution.py:403
  85.4 7.3 %copy-start.2 = (s32[8,11]{1,0:T(8,128)S(1)}, s32[8,11]{1,0:T(8,128)}, u32[]{:S(2)}) copy-start(s32[8,11]{1,0:T(8,128)} %get-tuple-element.35.own_labels_ref) | copy-start | bytes 1060
  85.4 7.3 %copy-start.5 = (s32[1,8]{1,0:T(1,128)S(1)}, s32[1,8]{1,0:T(1,128)}, u32[]{:S(2)}) copy-start(s32[1,8]{1,0:T(1,128)} %slots_ref.3) | copy-start | bytes 100
  (2 other events, 1.2 us)

commit v3 on v2

--- a/solution.py
+++ b/solution.py
@@ -273,7 +273,7 @@
 
 def merge_kernel(slots_ref, lead_ref, own_labels_ref, *refs):
     parts, out, labels_ref = refs[:NG], refs[NG], refs[NG + 1]
-    tiles, stage, sems, digits, work, steps_ref, next_ref, next_sem = refs[NG + 2:]
+    follow, tiles, stage, sems, digits, work, steps_ref, next_ref, next_sem = refs[NG + 2:]
     per = SLOTS // 2
 
     lane = lax.broadcasted_iota(jnp.int32, (HALF, LANES), 1)
@@ -303,38 +303,37 @@
     fetch = pltpu.make_async_copy(steps_ref, next_ref, next_sem)
     fetch.start()
 
-    for t in range(per):
-        span = slice(t * LANES, (t + 1) * LANES)
-        for n in range(HALF):
-            tiles[n * per + t] = lead_ref[n, :, span]
-        for s in range(NG):
-            for q in range(2):
-                tiles[(HALF + 2 * s + q) * per + t] = parts[s][q, :, span]
+    for s in range(NG):
+        follow[2 * s:2 * s + 2] = parts[s][...]
     low = low_lanes((BLK, LANES))
 
+    def save(n):
+        return pltpu.make_async_copy(stage.at[n], out.at[n], sems.at[n])
+
+    fetch.wait()
     for n in range(HALF):
-        f, l = (HALF + spots[n]) * per, n * per
-        first = tiles[l].astype(jnp.float32)
-        second = jnp.where(low, 0.0, tiles[f].astype(jnp.float32))
-        tiles[f] = second.astype(jnp.bfloat16)
+        f = spots[n]
+
+        def lead(t):
+            return lead_ref[n, :, t * LANES:(t + 1) * LANES]
+
+        def part(t):
+            return follow[f, :, t * LANES:(t + 1) * LANES]
+
+        first = lead(0).astype(jnp.float32)
+        second = jnp.where(low, 0.0, part(0).astype(jnp.float32))
         stage[n, :, 0:LANES] = (first + pltpu.roll(second, BLK, 1)).astype(jnp.bfloat16)
-        middle = tiles[l + per - 1].astype(jnp.float32) + second
+        middle = lead(per - 1).astype(jnp.float32) + second
         middle = middle + jnp.where(low, 0.0, pltpu.roll(first, BLK, 1))
         stage[n, :, 5 * LANES:6 * LANES] = middle.astype(jnp.bfloat16)
-        for t in range(1, per - 1):
-            stage[n, :, t * LANES:(t + 1) * LANES] = tiles[l + t]
-        for t in range(1, per):
-            stage[n, :, (5 + t) * LANES:(6 + t) * LANES] = tiles[f + t]
-
-    def save(n):
-        return pltpu.make_async_copy(stage.at[n], out.at[n], sems.at[n])
-
-    fetch.wait()
-    for n in range(HALF):
-        f, l = (HALF + spots[n]) * per, n * per
+        stage[n, :, LANES:5 * LANES] = lead_ref[n, :, LANES:5 * LANES]
+        stage[n, :, 6 * LANES:] = follow[f, :, LANES:]
 
         @pl.when(next_ref[n, 2 * K] != 0)
-        def _(n=n, f=f, l=l):
+        def _(n=n, lead=lead, part=part):
+            for t in range(per):
+                tiles[t] = lead(t).astype(jnp.float32)
+                tiles[per + t] = part(t).astype(jnp.float32)
             plain = (next_ref[n, 0] == K) & (next_ref[n, K] == K)
             for s in range(2 * K):
                 step = next_ref[n, s]
@@ -342,26 +341,26 @@
 
                 @pl.when(jnp.logical_not(skip))
                 def _(s=s, step=step):
-                    home = s if s < K else s - K + 1
+                    home = s if s < K else s + 2
 
                     def block(t):
-                        spot = jnp.where(t < K, t, t - K + 1)
-                        value = tiles[jnp.where(t < K, l, f) + (spot >> 1)].astype(jnp.float32)
+                        spot = jnp.where(t < K, t, t + 2)
+                        value = tiles[spot >> 1]
                         same = jnp.broadcast_to((spot & 1) == (home & 1), value.shape)
                         return jnp.where(same, value, pltpu.roll(value, BLK, 1))
 
-                    def follow(t, step):
-                        after = t + step
-                        return jnp.where(after >= 2 * K, after - 2 * K, after)
+                    def after(t, step):
+                        t = t + step
+                        return jnp.where(t >= 2 * K, t - 2 * K, t)
 
                     def more(carry):
                         return carry[0] != s
 
                     def add(carry):
                         t, total = carry
-                        return follow(t, next_ref[n, t]), total + block(t)
-
-                    _, total = lax.while_loop(more, add, (follow(s, step), block(jnp.int32(s))))
+                        return after(t, next_ref[n, t]), total + block(t)
+
+                    _, total = lax.while_loop(more, add, (after(s, step), block(jnp.int32(s))))
                     span = slice((s // 2) * LANES, (s // 2 + 1) * LANES)
                     keep = low if s % 2 == 0 else jnp.logical_not(low)
                     stage[n, :, span] = jnp.where(
@@ -383,7 +382,8 @@
         in_specs=[SMEM] + [VMEM] * (2 + NG),
         out_specs=[pl.BlockSpec(memory_space=pl.ANY), VMEM],
         scratch_shapes=[
-            pltpu.VMEM((2 * HALF * SLOTS // 2, BLK, LANES), jnp.bfloat16),
+            pltpu.VMEM((2 * NG, BLK, WIDE), jnp.bfloat16),
+            pltpu.VMEM((SLOTS, BLK, LANES), jnp.float32),
             pltpu.VMEM((HALF, BLK, 2 * K * BLK), jnp.bfloat16),
             pltpu.SemaphoreType.DMA((HALF,)),
             pltpu.VMEM((HALF, LANES), jnp.int32),
@@ -436,11 +436,11 @@
     source = (lane & BLK) + jnp.where(inner < 32, 2 * inner, 2 * (inner - 32) + 1)
     perm = (lane[:, None] == source[None, :]).astype(jnp.bfloat16)
     y = products(prolongator.reshape(ROWS, BLK, BLK), stiffness, perm)
-    returned, y = lax.optimization_barrier((returned, y))
 
     lists = fetch_rows.reshape(NX, NZ, NC, C).transpose(0, 2, 1, 3).reshape(NX * NC, NZ * C)
     note = note_rows(lists, order, returned)
     wanted = lax.all_to_all(note, ("x", "core"), split_axis=0, concat_axis=0, tiled=True)
+    wanted, y = lax.optimization_barrier((wanted, y))
     plane = wanted[:, :, NZ * C:].reshape(1, 1, NX * NC * 2 * HALF)
     every = lax.all_to_all(
         jnp.broadcast_to(plane, (NZ, 1, NX * NC * 2 * HALF)), "z", split_axis=0, concat_axis=0, tiled=True

time: 97.8 us -> 94.8 us (0.969)
  blocking collectives: 8.56 us -> 0 us
  starting transfers between devices: 38 us -> 41.7 us
  waiting for transfers between devices: 15.6 us -> 17.7 us
    all_to_all x1 -> x0, blocking collectives: 8.56 us -> none  [per_device(): lax.all_to_all(note, ('x', 'core'), split_axis=0, concat_axis=0, tiled=True)]
    all_to_all x0 -> x1, starting transfers between devices: none -> 4.83 us  [per_device(): lax.all_to_all(note, ('x', 'core'), split_axis=0, concat_axis=0, tiled=True)]
    ppermute x7, waiting for transfers between devices: 3.42 us -> 5.22 us  [cross(): return lax.ppermute(value, ('x', 'core'), pairs)]
    ppermute x7, starting transfers between devices: 7.77 us -> 6.71 us  [cross(): return lax.ppermute(value, ('x', 'core'), pairs)]
  transfers between devices with their start and end apart: 19 -> 20, of which waited for: 4 -> 4; matrix products, arithmetic and copies ran while one was open for 4% -> 4% of each run, Pallas kernels for 16% -> 16%
where the time goes in v3:
time: 94.8 us; the launch traced here: 93.7 us
  starting transfers between devices  41.7 us (44%)
  Pallas kernels  23.5 us (25%)
  waiting for transfers between devices  17.7 us (19%)
  local copies, waits for them, and re-layouts  9.72 us (10%)
  between operations  1.01 us (1%)
    ppermute x10, starting transfers between devices, shift(): lax.ppermute(value, axis, [(i, (i + by) % size) for i in range(size)])  21.8 us
    all_to_all x1, waiting for transfers between devices, per_device(): lax.all_to_all(jnp.broadcast_to(plane, (NZ, 1, NX * NC * 2 * HALF)), 'z',...  7.53 us
    unnamed x32, local copies, waits for them, and re-layouts  7.1 us
    ppermute x7, starting transfers between devices, cross(): return lax.ppermute(value, ('x', 'core'), pairs)  6.71 us
    ppermute x7, waiting for transfers between devices, cross(): return lax.ppermute(value, ('x', 'core'), pairs)  5.22 us
    ppermute x10, waiting for transfers between devices, shift(): lax.ppermute(value, axis, [(i, (i + by) % size) for i in range(size)])  4.96 us
    pallas_call x1, Pallas kernels, label_rows(): pl.pallas_call(label_kernel, out_shape=[labels, labels], in_specs=[SMEM]...  4.9 us
    all_to_all x1, starting transfers between devices, per_device(): lax.all_to_all(note, ('x', 'core'), split_axis=0, concat_axis=0, tiled=True)  4.83 us
  transfers between devices with their start and end apart: 20, of which 4 were waited for; matrix products, arithmetic and copies ran while one was open for 4% of the time, Pallas kernels for 16%

profile of v3, /device:TPU:2, one launch (start us, length us, event | category | flops | bytes accessed | tf_op | source)
XLA Modules:
  0.0 93.7 jit_solution(16691375335207615009)
XLA Ops:
  0.6 0.9 copy.13
  1.6 7.3 %collective-permute-start.2 = (bf16[16,32,128]{2,1,0:T(8,128)(2,1)S(1)}, bf16[16,32,128]{2,1,0:T(8,128)(2,1)S(1)}, u32[]{:S(2)}, u32[]{:S(2)}) collective-permute-start(bf16[16,32,128]{2,1,0:T(8,128)(2,1)S(1)} %bitcast.7), channel_id=1, source_target_pairs={{0,8},{2,10},{4,12},{6,14},{8,0},{10,2},{12,4},{14,6},{1,9},{3,11}... | collective-permute-start | bytes 393224 | tf_op jit(solution)/shard_map/ppermute | solution.py:403
  9.0 2.8 %collective-permute-start.1 = (bf16[16,32,128]{2,1,0:T(8,128)(2,1)S(1)}, bf16[16,32,128]{2,1,0:T(8,128)(2,1)S(1)}, u32[]{:S(2)}, u32[]{:S(2)}) collective-permute-start(bf16[16,32,128]{2,1,0:T(8,128)(2,1)S(1)} %bitcast.10), channel_id=1, source_target_pairs={{0,4},{2,6},{4,8},{6,10},{8,12},{10,14},{12,0},{14,2},{1,5},{3,7},... | collective-permute-start | bytes 393224 | tf_op jit(solution)/shard_map/ppermute | solution.py:403
  11.9 1.9 %collective-permute-start = (bf16[16,32,128]{2,1,0:T(8,128)(2,1)S(1)}, bf16[16,32,128]{2,1,0:T(8,128)(2,1)S(1)}, u32[]{:S(2)}, u32[]{:S(2)}) collective-permute-start(bf16[16,32,128]{2,1,0:T(8,128)(2,1)S(1)} %bitcast.11), channel_id=1, source_target_pairs={{0,2},{2,4},{4,6},{6,8},{8,10},{10,12},{12,14},{14,0},{1,3},{3,5},... | collective-permute-start | bytes 393224 | tf_op jit(solution)/shard_map/ppermute | solution.py:403
  13.8 1.3 %codes.1 = (s32[4,1,2]{2,1,0:T(1,128)}, s32[1,8]{1,0:T(1,128)}) custom-call(s32[1,8]{1,0:T(1,128)} %slots_ref.3, s32[1,8]{1,0:T(1,128)} %send_ref.5), custom_call_target="tpu_custom_call" | custom-call | tf_op jit(solution)/shard_map/codes/pallas_call | solution.py:205
  15.1 4.5 %all-to-all-start = ((s32[4,1,2]{2,1,0:T(1,128)}), s32[4,1,2]{2,1,0:T(1,128)S(1)}, u32[]{:S(2)}, u32[]{:S(2)}) async-start(s32[4,1,2]{2,1,0:T(1,128)} %get-tuple-element.22), calls=%async_computation | async-start | bytes 4096 | tf_op jit(solution)/shard_map/all_to_all | solution.py:432
  19.5 2.3 %collective-permute-start.4 = (bf16[16,32,128]{2,1,0:T(8,128)(2,1)S(1)}, bf16[16,32,128]{2,1,0:T(8,128)(2,1)S(1)}, u32[]{:S(2)}, u32[]{:S(2)}) collective-permute-start(bf16[16,32,128]{2,1,0:T(8,128)(2,1)S(1)} %collective-permute-done.2.refs_4_), channel_id=1, source_target_pairs={{0,2},{2,4},{4,6},{6,8},{8,10},{10,12},{12,14},{14,0},{1,3},{3,5},... | collective-permute-start | bytes 393224 | tf_op jit(solution)/shard_map/ppermute | solution.py:403
  21.8 1.0 %collective-permute-start.3 = (bf16[16,32,128]{2,1,0:T(8,128)(2,1)S(1)}, bf16[16,32,128]{2,1,0:T(8,128)(2,1)S(1)}, u32[]{:S(2)}, u32[]{:S(2)}) collective-permute-start(bf16[16,32,128]{2,1,0:T(8,128)(2,1)S(1)} %collective-permute-done.2.refs_4_), channel_id=1, source_target_pairs={{0,14},{2,0},{4,2},{6,4},{8,6},{10,8},{12,10},{14,12},{1,15},{3,1}... | collective-permute-start | bytes 393224 | tf_op jit(solution)/shard_map/ppermute | solution.py:403
  22.9 1.2 %reshape.35.p_ref = bf16[16,64,64]{2,1,0:T(8,128)(2,1)S(1)} reshape(bf16[16,4096]{1,0:T(8,128)(2,1)} %param.7) | data formatting | bytes 262144 | tf_op jit(solution)/shard_map/reshape | solution.py:438
  24.1 0.8 copy.10.fetch_ref
  26.1 1.4 %note.1 = s32[8,1,48]{2,1,0:T(1,128)} custom-call(s32[8,32]{1,0:T(8,128)} %reshape.34.lists_ref, s32[1,8]{1,0:T(1,128)} %get-tuple-element.21.order_ref, s32[4,1,2]{2,1,0:T(1,128)} %copy-done.14), custom_call_target="tpu_custom_call" | custom-call | tf_op jit(solution)/shard_map/note/pallas_call | solution.py:226
  27.5 4.8 %all-to-all-start.1 = ((s32[8,1,48]{2,1,0:T(1,128)}), s32[8,1,48]{2,1,0:T(1,128)S(1)}, u32[]{:S(2)}, u32[]{:S(2)}) async-start(s32[8,1,48]{2,1,0:T(1,128)} %note.1), calls=%async_computation.1 | async-start | bytes 8192 | tf_op jit(solution)/shard_map/all_to_all | solution.py:442
  32.3 1.4 %copy-done = bf16[16,64,704]{2,1,0:T(8,128)(2,1)S(1)} copy-done((bf16[16,64,704]{2,1,0:T(8,128)(2,1)S(1)}, bf16[16,64,704]{2,1,0:T(8,128)(2,1)}, u32[]{:S(2)}) %copy-start) | copy-done | bytes 1441816
  33.7 4.8 %products.1.y_ref = bf16[16,64,768]{2,1,0:T(8,128)(2,1)S(1)} custom-call(bf16[16,64,64]{2,1,0:T(8,128)(2,1)S(1)} %reshape.35.p_ref, bf16[16,64,704]{2,1,0:T(8,128)(2,1)S(1)} %copy-done, bf16[128,128]{1,0:T(8,128)(2,1)S(1)} %fusion.perm_ref), custom_call_target="tpu_custom_call" | custom-call | flops 301989888 | bytes 3200000 | tf_op jit(solution)/shard_map/products/pallas_call | solution.py:52
  38.6 1.6 %select.7 = (bf16[32,32,128]{2,1,0:T(8,128)(2,1)}, bf16[32,32,128]{2,1,0:T(8,128)(2,1)}, bf16[32,32,128]{2,1,0:T(8,128)(2,1)S(1)}, bf16[32,32,128]{2,1,0:T(8,128...) custom-call(s32[8,1,48]{2,1,0:T(1,128)S(1)} %all-to-all-done.1.wante, ...), custom_call_target="tpu_custom_call" | custom-call | tf_op jit(solution)/shard_map/select/pallas_call | solution.py:84
  42.5 1.5 %collective-permute-start.8 = (bf16[32,32,128]{2,1,0:T(8,128)(2,1)}, bf16[32,32,128]{2,1,0:T(8,128)(2,1)S(1)}, u32[]{:S(2)}, u32[]{:S(2)}) collective-permute-start(bf16[32,32,128]{2,1,0:T(8,128)(2,1)} %get-tuple-element.28), channel_id=1, source_target_pairs={{0,16},{1,17},{16,32},{17,33},{32,48},{33,49},{48,0},{49,1},{2,18}... | collective-permute-start | bytes 786440 | tf_op jit(solution)/shard_map/ppermute | solution.py:413
  44.0 0.9 collective-permute-start.9
  44.9 1.5 %collective-permute-start.10 = (bf16[32,32,128]{2,1,0:T(8,128)(2,1)}, bf16[32,32,128]{2,1,0:T(8,128)(2,1)}, u32[]{:S(2)}, u32[]{:S(2)}) collective-permute-start(bf16[32,32,128]{2,1,0:T(8,128)(2,1)} %copy-done.6), channel_id=1, source_target_pairs={{0,32},{1,33},{16,48},{17,49},{32,0},{33,1},{48,16},{49,17},{2,34}... | collective-permute-start | bytes 786440 | tf_op jit(solution)/shard_map/ppermute | solution.py:413
  46.4 1.8 %collective-permute-start.11 = (bf16[32,32,128]{2,1,0:T(8,128)(2,1)S(1)}, bf16[32,32,128]{2,1,0:T(8,128)(2,1)}, u32[]{:S(2)}, u32[]{:S(2)}) collective-permute-start(bf16[32,32,128]{2,1,0:T(8,128)(2,1)S(1)} %get-tuple-element.31), channel_id=1, source_target_pairs={{0,33},{1,32},{16,49},{17,48},{32,1},{33,0},{48,17},{49,16},{2,35}... | collective-permute-start | bytes 786440 | tf_op jit(solution)/shard_map/ppermute | solution.py:413
  48.2 0.9 collective-permute-start.12
  49.1 2.8 %collective-permute-done.8.refs_2_ = bf16[32,32,128]{2,1,0:T(8,128)(2,1)S(1)} collective-permute-done((bf16[32,32,128]{2,1,0:T(8,128)(2,1)}, bf16[32,32,128]{2,1,0:T(8,128)(2,1)S(1)}, u32[]{:S(2)}, u32[]{:S(2)}) %collective-permute-start.8) | collective-permute-done | bytes 262176 | tf_op jit(solution)/shard_map/ppermute | solution.py:413
  52.7 4.0 %all-to-all-start.2 = ((s32[8,1,128]{2,1,0:T(1,128)}), s32[8,1,128]{2,1,0:T(1,128)S(1)}, u32[]{:S(2)}, u32[]{:S(2)}) async-start(s32[8,1,128]{2,1,0:T(1,128)} %broadcast_in_dim.15), calls=%async_computation.2 | async-start | bytes 8192 | tf_op jit(solution)/shard_map/all_to_all | solution.py:445
  56.7 7.5 %all-to-all-done.2.codes_ref = s32[8,1,128]{2,1,0:T(1,128)S(1)} async-done(((s32[8,1,128]{2,1,0:T(1,128)}), s32[8,1,128]{2,1,0:T(1,128)S(1)}, u32[]{:S(2)}, u32[]{:S(2)}) %all-to-all-start.2) | async-done | bytes 4128 | tf_op jit(solution)/shard_map/all_to_all | solution.py:445
  64.8 4.9 %labels.1 = (s32[8,11]{1,0:T(8,128)}, s32[8,11]{1,0:T(8,128)}) custom-call(s32[16,11]{1,0:T(8,128)} %columns_ref.1, s32[64,4]{1,0:T(8,128)} %copy-done.8, s32[8,1,128]{2,1,0:T(1,128)} %copy-done.13, s32[1,8]{1,0:T(1,128)} %send_ref.5), custom_call_target="tpu_custom_call" | custom-call | tf_op jit(solution)/shard_map/labels/pallas_call | solution.py:265
  69.8 2.4 %collective-permute-done.13.refs_7_ = bf16[32,32,128]{2,1,0:T(8,128)(2,1)} collective-permute-done((bf16[32,32,128]{2,1,0:T(8,128)(2,1)S(1)}, bf16[32,32,128]{2,1,0:T(8,128)(2,1)}, u32[]{:S(2)}, u32[]{:S(2)}) %collective-permute-start.13) | collective-permute-done | bytes 262176 | tf_op jit(solution)/shard_map/ppermute | solution.py:413
  72.9 2.9 %followers.1 = (bf16[2,64,768]{2,1,0:T(8,128)(2,1)S(1)}, bf16[2,64,768]{2,1,0:T(8,128)(2,1)S(1)}, bf16[2,64,768]{2,1,0:T(8,128)(2,1)S(1)}, bf16[2,64,768]{2,1,0:T(8,128)(2,1)S(1)}, bf16[273,32,128]{2,1,0:T(8,128)(2,1)S(1)}) custom-call(s32[16,12]{1,0:T(8,128)S(1)} %select_add_fusion.at_ref, s32[1,8]{1,0:T(1,128)S(1)} %copy-done.4, ...), custom_call_target="tpu_custom_call" | custom-call | flops 100663296 | bytes 5000000 | tf_op jit(solution)/shard_map/followers/pallas_call | solution.py:164
  75.8 2.1 %collective-permute-start.14 = (bf16[2,64,768]{2,1,0:T(8,128)(2,1)S(1)}, bf16[2,64,768]{2,1,0:T(8,128)(2,1)S(1)}, u32[]{:S(2)}, u32[]{:S(2)}) collective-permute-start(bf16[2,64,768]{2,1,0:T(8,128)(2,1)S(1)} %get-tuple-element.37), channel_id=1, source_target_pairs={{0,64},{64,128},{128,192},{192,0},{1,65},{65,129},{129,193},{193,1... | collective-permute-start | bytes 589832 | tf_op jit(solution)/shard_map/ppermute | solution.py:403
  77.9 2.7 %collective-permute-start.15 = (bf16[2,64,768]{2,1,0:T(8,128)(2,1)S(1)}, bf16[2,64,768]{2,1,0:T(8,128)(2,1)S(1)}, u32[]{:S(2)}, u32[]{:S(2)}) collective-permute-start(bf16[2,64,768]{2,1,0:T(8,128)(2,1)S(1)} %get-tuple-element.38), channel_id=1, source_target_pairs={{0,128},{64,192},{128,0},{192,64},{1,129},{65,193},{129,1},{193,65... | collective-permute-start | bytes 589832 | tf_op jit(solution)/shard_map/ppermute | solution.py:403
  80.5 1.5 %collective-permute-start.16 = (bf16[2,64,768]{2,1,0:T(8,128)(2,1)S(1)}, bf16[2,64,768]{2,1,0:T(8,128)(2,1)S(1)}, u32[]{:S(2)}, u32[]{:S(2)}) collective-permute-start(bf16[2,64,768]{2,1,0:T(8,128)(2,1)S(1)} %get-tuple-element.39), channel_id=1, source_target_pairs={{0,192},{64,0},{128,64},{192,128},{1,193},{65,1},{129,65},{193,129... | collective-permute-start | bytes 589832 | tf_op jit(solution)/shard_map/ppermute | solution.py:403
  82.0 2.7 %leaders.1.lead_ref = bf16[8,64,768]{2,1,0:T(8,128)(2,1)S(1)} custom-call(s32[16,12]{1,0:T(8,128)S(1)} %select_add_fusion.at_ref, bf16[16,64,768]{2,1,0:T(8,128)(2,1)S(1)} %products.1.y_ref, bf16[273,32,128]{2,1,0:T(8,128)(2,1)S(1)} %get-tuple-element.34.table), custom_call_target="tpu_custom_call" | custom-call | flops 100663296 | bytes 5000000 | tf_op jit(solution)/shard_map/leaders/pallas_call | solution.py:177
  84.7 4.9 %collective-permute-done.15.refs_2_ = bf16[2,64,768]{2,1,0:T(8,128)(2,1)S(1)} collective-permute-done((bf16[2,64,768]{2,1,0:T(8,128)(2,1)S(1)}, bf16[2,64,768]{2,1,0:T(8,128)(2,1)S(1)}, u32[]{:S(2)}, u32[]{:S(2)}) %collective-permute-start.15) | collective-permute-done | bytes 196640 | tf_op jit(solution)/shard_map/ppermute | solution.py:403
  89.7 3.9 %merge.1 = (bf16[8,64,1408]{2,1,0:T(8,128)(2,1)}, s32[8,22]{1,0:T(8,128)}) custom-call(s32[1,8]{1,0:T(1,128)S(1)} %copy-done.5, bf16[8,64,768]{2,1,0:T(8,128)(2,1)S(1)} %leaders.1.lead_ref, s32[8,11]{1,0:T(8,128)S(1)} %copy-done.2, bf16[2,64,768]{2,1,0:T(8,128)(2,1)S(1)} %get-tuple-element.36.refs_0_, ...), custom_call_target="tpu_custom_call" | custom-call | tf_op jit(solution)/shard_map/merge/pallas_call | solution.py:376
  (59 shorter events, 5.9 us)
Async XLA Ops:
  1.6 18.0 %collective-permute-start.2 = (bf16[16,32,128]{2,1,0:T(8,128)(2,1)S(1)}, bf16[16,32,128]{2,1,0:T(8,128)(2,1)S(1)}, u32[]{:S(2)}, u32[]{:S(2)}) collective-permute-start(bf16[16,32,128]{2,1,0:T(8,128)(2,1)S(1)} %bitcast.7), channel_id=1, source_target_pairs={{0,8},{2,10},{4,12},{6,14},{8,0},{10,2},{12,4},{14,6},{1,9},{3,11}... | collective-permute-start | bytes 393224 | tf_op jit(solution)/shard_map/ppermute | solution.py:403
  8.8 13.0 %collective-permute-start.6 = (bf16[16,32,128]{2,1,0:T(8,128)(2,1)S(1)}, bf16[16,32,128]{2,1,0:T(8,128)(2,1)S(1)}, u32[]{:S(2)}, u32[]{:S(2)}) collective-permute-start(bf16[16,32,128]{2,1,0:T(8,128)(2,1)S(1)} %bitcast.8), channel_id=1, source_target_pairs={{0,14},{2,0},{4,2},{6,4},{8,6},{10,8},{12,10},{14,12},{1,15},{3,1}... | collective-permute-start | bytes 393224 | tf_op jit(solution)/shard_map/ppermute | solution.py:403
  8.9 29.6 %collective-permute-start.5 = (bf16[16,32,128]{2,1,0:T(8,128)(2,1)S(1)}, bf16[16,32,128]{2,1,0:T(8,128)(2,1)S(1)}, u32[]{:S(2)}, u32[]{:S(2)}) collective-permute-start(bf16[16,32,128]{2,1,0:T(8,128)(2,1)S(1)} %bitcast.9), channel_id=1, source_target_pairs={{0,12},{2,14},{4,0},{6,2},{8,4},{10,6},{12,8},{14,10},{1,13},{3,15... | collective-permute-start | bytes 393224 | tf_op jit(solution)/shard_map/ppermute | solution.py:403
  9.0 29.6 %collective-permute-start.1 = (bf16[16,32,128]{2,1,0:T(8,128)(2,1)S(1)}, bf16[16,32,128]{2,1,0:T(8,128)(2,1)S(1)}, u32[]{:S(2)}, u32[]{:S(2)}) collective-permute-start(bf16[16,32,128]{2,1,0:T(8,128)(2,1)S(1)} %bitcast.10), channel_id=1, source_target_pairs={{0,4},{2,6},{4,8},{6,10},{8,12},{10,14},{12,0},{14,2},{1,5},{3,7},... | collective-permute-start | bytes 393224 | tf_op jit(solution)/shard_map/ppermute | solution.py:403
  11.9 26.7 %collective-permute-start = (bf16[16,32,128]{2,1,0:T(8,128)(2,1)S(1)}, bf16[16,32,128]{2,1,0:T(8,128)(2,1)S(1)}, u32[]{:S(2)}, u32[]{:S(2)}) collective-permute-start(bf16[16,32,128]{2,1,0:T(8,128)(2,1)S(1)} %bitcast.11), channel_id=1, source_target_pairs={{0,2},{2,4},{4,6},{6,8},{8,10},{10,12},{12,14},{14,0},{1,3},{3,5},... | collective-permute-start | bytes 393224 | tf_op jit(solution)/shard_map/ppermute | solution.py:403
  15.1 10.5 %all-to-all-start = ((s32[4,1,2]{2,1,0:T(1,128)}), s32[4,1,2]{2,1,0:T(1,128)S(1)}, u32[]{:S(2)}, u32[]{:S(2)}) async-start(s32[4,1,2]{2,1,0:T(1,128)} %get-tuple-element.22), calls=%async_computation | async-start | bytes 4096 | tf_op jit(solution)/shard_map/all_to_all | solution.py:432
  19.5 19.1 %collective-permute-start.4 = (bf16[16,32,128]{2,1,0:T(8,128)(2,1)S(1)}, bf16[16,32,128]{2,1,0:T(8,128)(2,1)S(1)}, u32[]{:S(2)}, u32[]{:S(2)}) collective-permute-start(bf16[16,32,128]{2,1,0:T(8,128)(2,1)S(1)} %collective-permute-done.2.refs_4_), channel_id=1, source_target_pairs={{0,2},{2,4},{4,6},{6,8},{8,10},{10,12},{12,14},{14,0},{1,3},{3,5},... | collective-permute-start | bytes 393224 | tf_op jit(solution)/shard_map/ppermute | solution.py:403
  21.8 16.8 %collective-permute-start.3 = (bf16[16,32,128]{2,1,0:T(8,128)(2,1)S(1)}, bf16[16,32,128]{2,1,0:T(8,128)(2,1)S(1)}, u32[]{:S(2)}, u32[]{:S(2)}) collective-permute-start(bf16[16,32,128]{2,1,0:T(8,128)(2,1)S(1)} %collective-permute-done.2.refs_4_), channel_id=1, source_target_pairs={{0,14},{2,0},{4,2},{6,4},{8,6},{10,8},{12,10},{14,12},{1,15},{3,1}... | collective-permute-start | bytes 393224 | tf_op jit(solution)/shard_map/ppermute | solution.py:403
  24.8 13.7 %copy-start.8 = (s32[64,4]{1,0:T(8,128)}, s32[64,4]{1,0:T(8,128)S(1)}, u32[]{:S(2)}) copy-start(s32[64,4]{1,0:T(8,128)S(1)} %copy.10.fetch_ref) | copy-start | bytes 3076
  27.5 11.1 %all-to-all-start.1 = ((s32[8,1,48]{2,1,0:T(1,128)}), s32[8,1,48]{2,1,0:T(1,128)S(1)}, u32[]{:S(2)}, u32[]{:S(2)}) async-start(s32[8,1,48]{2,1,0:T(1,128)} %note.1), calls=%async_computation.1 | async-start | bytes 8192 | tf_op jit(solution)/shard_map/all_to_all | solution.py:442
  32.3 1.4 %copy-start = (bf16[16,64,704]{2,1,0:T(8,128)(2,1)S(1)}, bf16[16,64,704]{2,1,0:T(8,128)(2,1)}, u32[]{:S(2)}) copy-start(bf16[16,64,704]{2,1,0:T(8,128)(2,1)} %a_ref.1) | copy-start | bytes 4325380
  33.7 10.3 %copy-start.12 = (s32[16,11]{1,0:T(8,128)S(1)}, s32[16,11]{1,0:T(8,128)}, u32[]{:S(2)}) copy-start(s32[16,11]{1,0:T(8,128)} %columns_ref.1) | copy-start | bytes 2116
  33.7 38.5 %copy-start.4 = (s32[1,8]{1,0:T(1,128)S(1)}, s32[1,8]{1,0:T(1,128)}, u32[]{:S(2)}) copy-start(s32[1,8]{1,0:T(1,128)} %send_ref.5) | copy-start | bytes 100
  40.2 0.7 copy-start.1
  41.0 0.7 copy-start.6
  41.7 0.7 copy-start.7
  42.4 5.9 %collective-permute-start.7 = (bf16[32,32,128]{2,1,0:T(8,128)(2,1)}, bf16[32,32,128]{2,1,0:T(8,128)(2,1)S(1)}, u32[]{:S(2)}, u32[]{:S(2)}) collective-permute-start(bf16[32,32,128]{2,1,0:T(8,128)(2,1)} %get-tuple-element.27), channel_id=1, source_target_pairs={{0,1},{1,0},{16,17},{17,16},{32,33},{33,32},{48,49},{49,48},{2,3},... | collective-permute-start | bytes 786440 | tf_op jit(solution)/shard_map/ppermute | solution.py:413
  42.5 9.3 %collective-permute-start.8 = (bf16[32,32,128]{2,1,0:T(8,128)(2,1)}, bf16[32,32,128]{2,1,0:T(8,128)(2,1)S(1)}, u32[]{:S(2)}, u32[]{:S(2)}) collective-permute-start(bf16[32,32,128]{2,1,0:T(8,128)(2,1)} %get-tuple-element.28), channel_id=1, source_target_pairs={{0,16},{1,17},{16,32},{17,33},{32,48},{33,49},{48,0},{49,1},{2,18}... | collective-permute-start | bytes 786440 | tf_op jit(solution)/shard_map/ppermute | solution.py:413
  44.0 25.7 %collective-permute-start.9 = (bf16[32,32,128]{2,1,0:T(8,128)(2,1)}, bf16[32,32,128]{2,1,0:T(8,128)(2,1)S(1)}, u32[]{:S(2)}, u32[]{:S(2)}) collective-permute-start(bf16[32,32,128]{2,1,0:T(8,128)(2,1)} %copy-done.7), channel_id=1, source_target_pairs={{0,17},{1,16},{16,33},{17,32},{32,49},{33,48},{48,1},{49,0},{2,19}... | collective-permute-start | bytes 786440 | tf_op jit(solution)/shard_map/ppermute | solution.py:413
  44.9 24.8 %collective-permute-start.10 = (bf16[32,32,128]{2,1,0:T(8,128)(2,1)}, bf16[32,32,128]{2,1,0:T(8,128)(2,1)}, u32[]{:S(2)}, u32[]{:S(2)}) collective-permute-start(bf16[32,32,128]{2,1,0:T(8,128)(2,1)} %copy-done.6), channel_id=1, source_target_pairs={{0,32},{1,33},{16,48},{17,49},{32,0},{33,1},{48,16},{49,17},{2,34}... | collective-permute-start | bytes 786440 | tf_op jit(solution)/shard_map/ppermute | solution.py:413
  46.4 23.4 %collective-permute-start.11 = (bf16[32,32,128]{2,1,0:T(8,128)(2,1)S(1)}, bf16[32,32,128]{2,1,0:T(8,128)(2,1)}, u32[]{:S(2)}, u32[]{:S(2)}) collective-permute-start(bf16[32,32,128]{2,1,0:T(8,128)(2,1)S(1)} %get-tuple-element.31), channel_id=1, source_target_pairs={{0,33},{1,32},{16,49},{17,48},{32,1},{33,0},{48,17},{49,16},{2,35}... | collective-permute-start | bytes 786440 | tf_op jit(solution)/shard_map/ppermute | solution.py:413
  48.2 24.0 %copy-start.9 = (bf16[32,32,128]{2,1,0:T(8,128)(2,1)}, bf16[32,32,128]{2,1,0:T(8,128)(2,1)S(1)}, u32[]{:S(2)}) copy-start(bf16[32,32,128]{2,1,0:T(8,128)(2,1)S(1)} %collective-permute-done.7.refs_1_) | copy-start | bytes 786436
  48.2 21.5 %collective-permute-start.12 = (bf16[32,32,128]{2,1,0:T(8,128)(2,1)S(1)}, bf16[32,32,128]{2,1,0:T(8,128)(2,1)}, u32[]{:S(2)}, u32[]{:S(2)}) collective-permute-start(bf16[32,32,128]{2,1,0:T(8,128)(2,1)S(1)} %get-tuple-element.32), channel_id=1, source_target_pairs={{0,48},{1,49},{16,0},{17,1},{32,16},{33,17},{48,32},{49,33},{2,50}... | collective-permute-start | bytes 786440 | tf_op jit(solution)/shard_map/ppermute | solution.py:413
  51.9 20.3 %copy-start.10 = (bf16[32,32,128]{2,1,0:T(8,128)(2,1)}, bf16[32,32,128]{2,1,0:T(8,128)(2,1)S(1)}, u32[]{:S(2)}) copy-start(bf16[32,32,128]{2,1,0:T(8,128)(2,1)S(1)} %collective-permute-done.8.refs_2_) | copy-start | bytes 786436
  51.9 20.3 %collective-permute-start.13 = (bf16[32,32,128]{2,1,0:T(8,128)(2,1)S(1)}, bf16[32,32,128]{2,1,0:T(8,128)(2,1)}, u32[]{:S(2)}, u32[]{:S(2)}) collective-permute-start(bf16[32,32,128]{2,1,0:T(8,128)(2,1)S(1)} %get-tuple-element.33), channel_id=1, source_target_pairs={{0,49},{1,48},{16,1},{17,0},{32,17},{33,16},{48,33},{49,32},{2,51}... | collective-permute-start | bytes 786440 | tf_op jit(solution)/shard_map/ppermute | solution.py:413
  52.7 11.6 %all-to-all-start.2 = ((s32[8,1,128]{2,1,0:T(1,128)}), s32[8,1,128]{2,1,0:T(1,128)S(1)}, u32[]{:S(2)}, u32[]{:S(2)}) async-start(s32[8,1,128]{2,1,0:T(1,128)} %broadcast_in_dim.15), calls=%async_computation.2 | async-start | bytes 8192 | tf_op jit(solution)/shard_map/all_to_all | solution.py:445
  69.7 2.5 %copy-start.11 = (bf16[32,32,128]{2,1,0:T(8,128)(2,1)}, bf16[32,32,128]{2,1,0:T(8,128)(2,1)S(1)}, u32[]{:S(2)}) copy-start(bf16[32,32,128]{2,1,0:T(8,128)(2,1)S(1)} %collective-permute-done.9.refs_3_) | copy-start | bytes 786436
  75.8 8.9 %collective-permute-start.14 = (bf16[2,64,768]{2,1,0:T(8,128)(2,1)S(1)}, bf16[2,64,768]{2,1,0:T(8,128)(2,1)S(1)}, u32[]{:S(2)}, u32[]{:S(2)}) collective-permute-start(bf16[2,64,768]{2,1,0:T(8,128)(2,1)S(1)} %get-tuple-element.37), channel_id=1, source_target_pairs={{0,64},{64,128},{128,192},{192,0},{1,65},{65,129},{129,193},{193,1... | collective-permute-start | bytes 589832 | tf_op jit(solution)/shard_map/ppermute | solution.py:403
  77.9 11.8 %collective-permute-start.15 = (bf16[2,64,768]{2,1,0:T(8,128)(2,1)S(1)}, bf16[2,64,768]{2,1,0:T(8,128)(2,1)S(1)}, u32[]{:S(2)}, u32[]{:S(2)}) collective-permute-start(bf16[2,64,768]{2,1,0:T(8,128)(2,1)S(1)} %get-tuple-element.38), channel_id=1, source_target_pairs={{0,128},{64,192},{128,0},{192,64},{1,129},{65,193},{129,1},{193,65... | collective-permute-start | bytes 589832 | tf_op jit(solution)/shard_map/ppermute | solution.py:403
  80.5 9.1 %collective-permute-start.16 = (bf16[2,64,768]{2,1,0:T(8,128)(2,1)S(1)}, bf16[2,64,768]{2,1,0:T(8,128)(2,1)S(1)}, u32[]{:S(2)}, u32[]{:S(2)}) collective-permute-start(bf16[2,64,768]{2,1,0:T(8,128)(2,1)S(1)} %get-tuple-element.39), channel_id=1, source_target_pairs={{0,192},{64,0},{128,64},{192,128},{1,193},{65,1},{129,65},{193,129... | collective-permute-start | bytes 589832 | tf_op jit(solution)/shard_map/ppermute | solution.py:403
  82.0 7.6 %copy-start.2 = (s32[8,11]{1,0:T(8,128)S(1)}, s32[8,11]{1,0:T(8,128)}, u32[]{:S(2)}) copy-start(s32[8,11]{1,0:T(8,128)} %get-tuple-element.35.own_labels_ref) | copy-start | bytes 1060
  82.0 7.6 %copy-start.5 = (s32[1,8]{1,0:T(1,128)S(1)}, s32[1,8]{1,0:T(1,128)}, u32[]{:S(2)}) copy-start(s32[1,8]{1,0:T(1,128)} %slots_ref.3) | copy-start | bytes 100
  (3 other events, 1.9 us)

commit v4 on v3

--- a/solution.py
+++ b/solution.py
@@ -31,33 +31,47 @@
     return lax.broadcasted_iota(jnp.int32, shape, 1) < BLK
 
 
-def products_kernel(p_ref, a_ref, perm_ref, y_ref):
-    def row(i, carry):
-        y = lax.dot_general(
-            p_ref[i], a_ref[i], (((0,), (0,)), ((), ())), preferred_element_type=jnp.float32
-        )
-        y = jnp.concatenate([y, jnp.zeros((BLK, BLK), jnp.float32)], axis=1)
-        y = jnp.where(i < HALF, y, pltpu.roll(y, BLK, 1)).astype(jnp.bfloat16)
-        for t in range(WIDE // LANES):
-            span = slice(t * LANES, (t + 1) * LANES)
-            y_ref[i, :, span] = jnp.dot(
-                y[:, span], perm_ref[...], preferred_element_type=jnp.float32
-            ).astype(jnp.bfloat16)
-        return carry
-
-    lax.fori_loop(0, ROWS, row, 0, unroll=4)
+STEP = 4
+
+
+def products_kernel(p_ref, perm_ref, a_hbm, y_ref, a_ref, sems):
+    def load(h):
+        rows = pl.ds(h * STEP, STEP)
+        return pltpu.make_async_copy(a_hbm.at[rows], a_ref.at[rows], sems.at[h])
+
+    for h in range(ROWS // STEP):
+        load(h).start()
+    for h in range(ROWS // STEP):
+        load(h).wait()
+        for i in range(h * STEP, (h + 1) * STEP):
+            y = lax.dot_general(
+                p_ref[i], a_ref[i], (((0,), (0,)), ((), ())), preferred_element_type=jnp.float32
+            )
+            pad = jnp.zeros((BLK, BLK), jnp.float32)
+            y = jnp.concatenate([y, pad] if i < HALF else [pad, y], axis=1).astype(jnp.bfloat16)
+            for t in range(WIDE // LANES):
+                span = slice(t * LANES, (t + 1) * LANES)
+                y_ref[i, :, span] = jnp.dot(
+                    y[:, span], perm_ref[...], preferred_element_type=jnp.float32
+                ).astype(jnp.bfloat16)
 
 
 def products(blocks, stiffness, perm):
     return pl.pallas_call(
         products_kernel,
         out_shape=jax.ShapeDtypeStruct((ROWS, BLK, WIDE), jnp.bfloat16),
+        in_specs=[VMEM, VMEM, HBM],
+        out_specs=VMEM,
+        scratch_shapes=[
+            pltpu.VMEM((ROWS, BLK, K * BLK), jnp.bfloat16),
+            pltpu.SemaphoreType.DMA((ROWS // STEP,)),
+        ],
         compiler_params=LIMIT,
         cost_estimate=pl.CostEstimate(
             flops=2 * ROWS * BLK * BLK * WIDE * 3, bytes_accessed=3_200_000, transcendentals=0
         ),
         name="products",
-    )(blocks, stiffness, perm)
+    )(blocks, perm, stiffness)
 
 
 def select_kernel(wanted_ref, *refs):
@@ -125,31 +139,42 @@
         ).astype(jnp.bfloat16))
 
 
-def follower_kernel(at_ref, send_ref, own_ref, y_ref, labels_ref, *refs):
+def label_row(i, address_ref, offset_ref, codes_ref):
+    lane = lax.broadcasted_iota(jnp.int32, (1, LANES), 1)
+    labels = jnp.full((1, LANES), -1, jnp.int32)
+    for k in range(K):
+        address = address_ref[i, k]
+        spot = jnp.maximum(address, 0)
+        code = jnp.where(address < 0, 0, codes_ref[spot >> 6, 0, spot & 63])
+        labels = jnp.where(lane == k, offset_ref[i, k] + code, labels)
+    return labels
+
+
+def follower_kernel(at_ref, send_ref, address_ref, offset_ref, codes_ref, own_ref, y_ref, *refs):
     n = NX * NC * CHUNKS
     parts, outs, table, sems = refs[:n], refs[n:n + NG], refs[n + NG], refs[n + NG + 1]
     fill(table, own_ref, parts, sems)
     for s in range(NG):
         target = (lax.axis_index(AXES[0]) + s) & (NG - 1)
         for q in range(2):
-            spot = target * 2 + q
-            row = HALF + send_ref[0, spot]
+            row = HALF + send_ref[0, target * 2 + q]
 
             def emit(span, value, s=s, q=q):
                 outs[s][q, :, span] = value
 
             row_tiles(row, table, at_ref, y_ref, emit)
-            label = labels_ref[pl.ds(spot, 1), :]
-            outs[s][q, 0:1, 0:K] = (label >> 4).astype(jnp.float32).astype(jnp.bfloat16)
-            outs[s][q, 16:17, 0:K] = (label & 15).astype(jnp.float32).astype(jnp.bfloat16)
-
-
-def leader_kernel(at_ref, y_ref, table, out):
+            labels = label_row(row, address_ref, offset_ref, codes_ref)[:, 0:BLK]
+            outs[s][q, 0:1, 0:BLK] = (labels >> 4).astype(jnp.float32).astype(jnp.bfloat16)
+            outs[s][q, 16:17, 0:BLK] = (labels & 15).astype(jnp.float32).astype(jnp.bfloat16)
+
+
+def leader_kernel(at_ref, address_ref, offset_ref, codes_ref, y_ref, table, out, labels_ref):
     def row(i, carry):
         def emit(span, value):
             out[i, :, span] = value
 
         row_tiles(i, table, at_ref, y_ref, emit)
+        labels_ref[pl.ds(i, 1), :] = label_row(i, address_ref, offset_ref, codes_ref)
         return carry
 
     lax.fori_loop(0, HALF, row, 0)
@@ -158,117 +183,127 @@
 ROW_COST = pl.CostEstimate(flops=2 * 8 * 6 * BLK * LANES * LANES, bytes_accessed=5_000_000, transcendentals=0)
 
 
-def followers(at, send, own, y, labels, parts):
+def followers(at, send, address, offset, codes, own, y, parts):
     shape = jax.ShapeDtypeStruct((2, BLK, WIDE), jnp.bfloat16)
     table = jax.ShapeDtypeStruct((TABLE + ROWS + 1, 32, LANES), jnp.bfloat16)
     return pl.pallas_call(
         follower_kernel,
         out_shape=[shape] * NG + [table],
-        in_specs=[SMEM] * 2 + [VMEM] * 3 + [HBM] * len(parts),
+        in_specs=[SMEM] * 5 + [VMEM] * 2 + [HBM] * len(parts),
         out_specs=[VMEM] * (NG + 1),
         scratch_shapes=[pltpu.SemaphoreType.DMA((len(parts),))],
         compiler_params=LIMIT,
         cost_estimate=ROW_COST,
         name="followers",
-    )(at, send, own, y, labels, *parts)
-
-
-def leaders(at, y, table):
+    )(at, send, address, offset, codes, own, y, *parts)
+
+
+def leaders(at, address, offset, codes, y, table):
     return pl.pallas_call(
         leader_kernel,
-        out_shape=jax.ShapeDtypeStruct((HALF, BLK, WIDE), jnp.bfloat16),
-        in_specs=[SMEM] + [VMEM] * 2,
-        out_specs=VMEM,
+        out_shape=[
+            jax.ShapeDtypeStruct((HALF, BLK, WIDE), jnp.bfloat16),
+            jax.ShapeDtypeStruct((HALF, LANES), jnp.int32),
+        ],
+        in_specs=[SMEM] * 4 + [VMEM] * 2,
+        out_specs=[VMEM] * 2,
         compiler_params=LIMIT,
         cost_estimate=ROW_COST,
         name="leaders",
-    )(at, y, table)
-
-
-NOTE = NZ * C + 2 * HALF
-
-
-def code_kernel(slots_ref, send_ref, codes_ref, order_ref):
+    )(at, address, offset, codes, y, table)
+
+
+def code_kernel(slots_ref, codes_ref):
     g = lax.axis_index(AXES[0])
     shape = (NG, 1, 2)
     spot = lax.broadcasted_iota(jnp.int32, shape, 0) * 2 + lax.broadcasted_iota(jnp.int32, shape, 2)
-    lane = lax.broadcasted_iota(jnp.int32, (1, HALF), 1)
-    codes, order = jnp.zeros(shape, jnp.int32), jnp.zeros((1, HALF), jnp.int32)
+    codes = jnp.zeros(shape, jnp.int32)
     for i in range(HALF):
-        codes = jnp.where(spot == slots_ref[0, i], g * HALF + i, codes)
-        order = jnp.where(lane == send_ref[0, i], i, order)
+        codes = jnp.where(spot == slots_ref[0, i], g * (N_DEV * HALF) + i, codes)
     codes_ref[...] = codes
-    order_ref[...] = order
-
-
-def code_rows(slots, send):
+
+
+def code_rows(slots):
     return pl.pallas_call(
         code_kernel,
-        out_shape=[
-            jax.ShapeDtypeStruct((NG, 1, 2), jnp.int32), jax.ShapeDtypeStruct((1, HALF), jnp.int32)
-        ],
+        out_shape=jax.ShapeDtypeStruct((NG, 1, 2), jnp.int32),
+        in_specs=[SMEM],
+        out_specs=VMEM,
+        name="codes",
+    )(slots)
+
+
+def spread_kernel(send_ref, returned_ref, out):
+    lane = lax.broadcasted_iota(jnp.int32, (NX * NC, 1, HALF), 2)
+    mine = jnp.zeros((NX * NC, 1, HALF), jnp.int32)
+    for t in range(NG):
+        for q in range(2):
+            mine = jnp.where(lane == send_ref[0, 2 * t + q], returned_ref[t, 0, q], mine)
+    out[...] = mine
+
+
+def spread(send, returned):
+    return pl.pallas_call(
+        spread_kernel,
+        out_shape=jax.ShapeDtypeStruct((NX * NC, 1, HALF), jnp.int32),
         in_specs=[SMEM] * 2,
-        out_specs=[VMEM] * 2,
-        name="codes",
-    )(slots, send)
-
-
-def note_kernel(lists_ref, order_ref, returned_ref, out):
-    first = NZ * C
+        out_specs=VMEM,
+        name="spread",
+    )(send, returned)
+
+
+def plane_kernel(plane_ref, out, row_ref):
     for d in range(NX * NC):
-        out[d, :, 0:first] = lists_ref[d:d + 1, :]
-        out[d, :, first:first + HALF] = order_ref[...]
-        for t in range(NG):
-            out[d, :, first + HALF + 2 * t:first + HALF + 2 * t + 2] = returned_ref[t]
-
-
-def note_rows(lists, order, returned):
-    return pl.pallas_call(
-        note_kernel,
-        out_shape=jax.ShapeDtypeStruct((NX * NC, 1, NOTE), jnp.int32),
-        in_specs=[VMEM] * 3,
+        row_ref[:, d * HALF:(d + 1) * HALF] = plane_ref[d]
+    for z in range(NZ):
+        out[z] = row_ref[...]
+
+
+def plane_rows(plane):
+    return pl.pallas_call(
+        plane_kernel,
+        out_shape=jax.ShapeDtypeStruct((NZ, 1, NX * NC * HALF), jnp.int32),
+        in_specs=[VMEM],
         out_specs=VMEM,
-        name="note",
-    )(lists, order, returned)
-
-
-def label_kernel(columns_ref, fetch_ref, codes_ref, send_ref, lead_ref, follow_ref):
+        scratch_shapes=[pltpu.VMEM((1, NX * NC * HALF), jnp.int32)],
+        name="plane",
+    )(plane)
+
+
+def address_kernel(columns_ref, fetch_ref, address_ref, offset_ref):
     g, x, z, c = (lax.axis_index(name) for name in AXES)
     device = x * (NZ * NC) + z * NC + c
 
-    def slot(i, k):
-        column = columns_ref[i, k]
-        ghost = jnp.maximum(column - ROWS, 0)
-        local = column < ROWS
-        asked = ghost >> 2
-        peer = jnp.where(local, device, asked)
-        row = jnp.where(local, jnp.maximum(column, 0), fetch_ref[asked, ghost & 3])
-        group = ((peer >> 4) * NC + (peer & 1)) * 2 * HALF
-        line = (peer >> 1) & (NZ - 1)
-        spot = codes_ref[line, 0, group + jnp.maximum(row - HALF, 0)]
-        code = jnp.where(row < HALF, g * HALF + row, codes_ref[line, 0, group + HALF + spot])
-        label = ((code >> 3) * N_DEV + peer) * HALF + (code & 7)
-        return jnp.where(column >= 0, label, -1)
-
     def row(i, carry):
-        follower = send_ref[0, i] + HALF
         for k in range(K):
-            lead_ref[i, k] = slot(i, k)
-            follow_ref[i, k] = slot(follower, k)
+            column = columns_ref[i, k]
+            ghost = jnp.maximum(column - ROWS, 0)
+            local = column < ROWS
+            asked = ghost >> 2
+            peer = jnp.where(local, device, asked)
+            row = jnp.where(local, jnp.maximum(column, 0), fetch_ref[asked, ghost & 3])
+            group = ((peer >> 4) * NC + (peer & 1)) * HALF
+            spot = ((peer >> 1) & (NZ - 1)) * (NX * NC * HALF) + group + row - HALF
+            late = row >= HALF
+            present = column >= 0
+            offset = peer * HALF + jnp.where(late, 0, g * (N_DEV * HALF) + row)
+            address_ref[i, k] = jnp.where(late & present, spot, -1)
+            offset_ref[i, k] = jnp.where(present, offset, -1)
         return carry
 
-    lax.fori_loop(0, HALF, row, 0)
-
-
-def label_rows(columns, fetch, codes, send):
-    labels = jax.ShapeDtypeStruct((HALF, K), jnp.int32)
-    return pl.pallas_call(
-        label_kernel,
-        out_shape=[labels, labels],
-        in_specs=[SMEM] * 4,
+    lax.fori_loop(0, ROWS, row, 0)
+
+
+def addresses(columns, fetch):
+    shape = jax.ShapeDtypeStruct((ROWS, K), jnp.int32)
+    return pl.pallas_call(
+        address_kernel,
+        out_shape=[shape, shape],
+        in_specs=[SMEM] * 2,
         out_specs=[SMEM] * 2,
-        name="labels",
-    )(columns, fetch, codes, send)
+        cost_estimate=pl.CostEstimate(flops=1_000_000, bytes_accessed=2_000_000, transcendentals=0),
+        name="addresses",
+    )(columns, fetch)
 
 
 def merge_kernel(slots_ref, lead_ref, own_labels_ref, *refs):
@@ -289,7 +324,7 @@
         work[n:n + 1, :] = digits[pl.ds(spots[n], 1), :]
     labels = jnp.where(lane < 2 * K, pltpu.roll(work[...], K, 1), -1)
     work[...] = labels
-    work[:, 0:K] = own_labels_ref[...]
+    work[:, 0:K] = own_labels_ref[:, 0:K]
     labels = work[...]
     labels_ref[...] = work[:, 0:2 * K]
     twice = jnp.where(lane < 2 * K, labels, pltpu.roll(labels, 2 * K, 1))
@@ -428,8 +463,8 @@
         got[3] = shift(got[4], "z", NZ, NZ - 1)
         held.append([got[s] for s in range(NZ)])
 
-    codes, order = code_rows(partner_slot, send_order)
-    returned = lax.all_to_all(codes, "grp", split_axis=0, concat_axis=0, tiled=True)
+    lists = fetch_rows.reshape(NX, NZ, NC, C).transpose(0, 2, 1, 3).reshape(NX * NC, 1, NZ * C)
+    wanted = lax.all_to_all(lists, ("x", "core"), split_axis=0, concat_axis=0, tiled=True)
 
     lane = jnp.arange(LANES, dtype=jnp.int32)
     inner = lane & (BLK - 1)
@@ -437,15 +472,12 @@
     perm = (lane[:, None] == source[None, :]).astype(jnp.bfloat16)
     y = products(prolongator.reshape(ROWS, BLK, BLK), stiffness, perm)
 
-    lists = fetch_rows.reshape(NX, NZ, NC, C).transpose(0, 2, 1, 3).reshape(NX * NC, NZ * C)
-    note = note_rows(lists, order, returned)
-    wanted = lax.all_to_all(note, ("x", "core"), split_axis=0, concat_axis=0, tiled=True)
-    wanted, y = lax.optimization_barrier((wanted, y))
-    plane = wanted[:, :, NZ * C:].reshape(1, 1, NX * NC * 2 * HALF)
-    every = lax.all_to_all(
-        jnp.broadcast_to(plane, (NZ, 1, NX * NC * 2 * HALF)), "z", split_axis=0, concat_axis=0, tiled=True
+    returned = lax.all_to_all(code_rows(partner_slot), "grp", split_axis=0, concat_axis=0, tiled=True)
+    plane = lax.all_to_all(
+        spread(send_order, returned), ("x", "core"), split_axis=0, concat_axis=0, tiled=True
     )
-    lead_labels, follower_labels = label_rows(columns, fetch_rows, every, send_order)
+    codes = lax.all_to_all(plane_rows(plane), "z", split_axis=0, concat_axis=0, tiled=True)
+    address, offset = addresses(columns, fetch_rows)
 
     ghost = columns - ROWS
     peer = ghost >> 2
@@ -465,9 +497,9 @@
         moved = {b: cross(chosen[i], b) for i, b in enumerate(ORDER)}
         parts += [pltpu.with_memory_space_constraint(moved[b], pltpu.HBM) for b in range(NX * NC)]
 
-    *sent, table = followers(at, send_order, own, y, follower_labels, parts)
+    *sent, table = followers(at, send_order, address, offset, codes, own, y, parts)
     arrived = [sent[0]] + [shift(sent[s], "grp", NG, s) for s in range(1, NG)]
-    lead = leaders(at, y, table)
+    lead, lead_labels = leaders(at, address, offset, codes, y, table)
     return tuple(merge(partner_slot, lead, lead_labels, arrived))
 
 

time: 94.8 us -> 102 us (1.076)
  starting transfers between devices: 41.7 us -> 46.9 us
  local copies, waits for them, and re-layouts: 9.72 us -> 7.47 us
  Pallas kernels: 23.5 us -> 25.7 us
  waiting for transfers between devices: 17.7 us -> 19 us
  other arithmetic: 0.11 us -> 1.41 us
    all_to_all x3 -> x4, waiting for transfers between devices: 7.53 us -> 12.7 us  [the longest x1 12.7 us: per_device(): lax.all_to_all(spread(send_order, returned), ('x', 'core'), split_axis=0,...]
    all_to_all x3 -> x4, starting transfers between devices: 13.2 us -> 18.2 us  [the longest x1 4.94 us: per_device(): lax.all_to_all(spread(send_order, returned), ('x', 'core'), split_axis=0,...]
    ppermute x7, waiting for transfers between devices: 5.22 us -> 2.02 us  [cross(): return lax.ppermute(value, ('x', 'core'), pairs)]
    pallas_call x4 -> x5, Pallas kernels: 10.3 us -> 11.3 us  [the longest x1 4.26 us: addresses(): pl.pallas_call(address_kernel, out_shape=[shape, shape], in_specs=[SMEM]...]
    unnamed x32 -> x28, local copies, waits for them, and re-layouts: 7.1 us -> 6.55 us
  transfers between devices with their start and end apart: 20 -> 21, of which waited for: 4 -> 3; matrix products, arithmetic and copies ran while one was open for 4% -> 3% of each run, Pallas kernels for 16% -> 18%
where the time goes in v4:
time: 102 us; the launch traced here: 101 us
  starting transfers between devices  46.9 us (46%)
  Pallas kernels  25.7 us (25%)
  waiting for transfers between devices  19 us (19%)
  local copies, waits for them, and re-layouts  7.47 us (7%)
  other arithmetic  1.41 us (1%)
    ppermute x10, starting transfers between devices, shift(): lax.ppermute(value, axis, [(i, (i + by) % size) for i in range(size)])  21.7 us
    all_to_all x1, waiting for transfers between devices, per_device(): lax.all_to_all(spread(send_order, returned), ('x', 'core'), split_axis=0,...  12.7 us
    ppermute x7, starting transfers between devices, cross(): return lax.ppermute(value, ('x', 'core'), pairs)  7.03 us
    unnamed x28, local copies, waits for them, and re-layouts  6.55 us
    all_to_all x1, starting transfers between devices, per_device(): lax.all_to_all(spread(send_order, returned), ('x', 'core'), split_axis=0,...  4.94 us
    all_to_all x1, starting transfers between devices, per_device(): lax.all_to_all(lists, ('x', 'core'), split_axis=0, concat_axis=0, tiled=T...  4.83 us
    pallas_call x1, Pallas kernels, products(): pl.pallas_call(products_kernel, out_shape=jax.ShapeDtypeStruct((ROWS, BLK...  4.78 us
    all_to_all x1, starting transfers between devices, per_device(): lax.all_to_all(code_rows(partner_slot), 'grp', split_axis=0, concat_axis=...  4.46 us
  transfers between devices with their start and end apart: 21, of which 3 were waited for; matrix products, arithmetic and copies ran while one was open for 3% of the time, Pallas kernels for 18%

profile of v4, /device:TPU:2, one launch (start us, length us, event | category | flops | bytes accessed | tf_op | source)
XLA Modules:
  0.0 101.5 jit_solution(5183700767537718374)
XLA Ops:
  0.6 1.0 %copy.14 = bf16[2,8,32,128]{3,2,1,0:T(8,128)(2,1)S(1)} copy(bf16[2,8,32,128]{3,1,2,0:T(8,128)(2,1)} %bitcast.15) | data formatting | bytes 262144
  1.7 7.3 %collective-permute-start.2 = (bf16[16,32,128]{2,1,0:T(8,128)(2,1)S(1)}, bf16[16,32,128]{2,1,0:T(8,128)(2,1)S(1)}, u32[]{:S(2)}, u32[]{:S(2)}) collective-permute-start(bf16[16,32,128]{2,1,0:T(8,128)(2,1)S(1)} %bitcast.8), channel_id=1, source_target_pairs={{0,8},{2,10},{4,12},{6,14},{8,0},{10,2},{12,4},{14,6},{1,9},{3,11}... | collective-permute-start | bytes 393224 | tf_op jit(solution)/shard_map/ppermute | solution.py:438
  9.2 2.8 %collective-permute-start.1 = (bf16[16,32,128]{2,1,0:T(8,128)(2,1)S(1)}, bf16[16,32,128]{2,1,0:T(8,128)(2,1)S(1)}, u32[]{:S(2)}, u32[]{:S(2)}) collective-permute-start(bf16[16,32,128]{2,1,0:T(8,128)(2,1)S(1)} %bitcast.11), channel_id=1, source_target_pairs={{0,4},{2,6},{4,8},{6,10},{8,12},{10,14},{12,0},{14,2},{1,5},{3,7},... | collective-permute-start | bytes 393224 | tf_op jit(solution)/shard_map/ppermute | solution.py:438
  12.0 1.9 %collective-permute-start = (bf16[16,32,128]{2,1,0:T(8,128)(2,1)S(1)}, bf16[16,32,128]{2,1,0:T(8,128)(2,1)S(1)}, u32[]{:S(2)}, u32[]{:S(2)}) collective-permute-start(bf16[16,32,128]{2,1,0:T(8,128)(2,1)S(1)} %bitcast.12), channel_id=1, source_target_pairs={{0,2},{2,4},{4,6},{6,8},{8,10},{10,12},{12,14},{14,0},{1,3},{3,5},... | collective-permute-start | bytes 393224 | tf_op jit(solution)/shard_map/ppermute | solution.py:438
  13.9 0.8 copy.10.fetch_ref
  15.4 4.8 %all-to-all-start.3 = ((s32[8,1,32]{2,1,0:T(1,128)}), s32[8,1,32]{2,1,0:T(1,128)S(1)}, u32[]{:S(2)}, u32[]{:S(2)}) async-start(s32[8,1,32]{2,1,0:T(1,128)} %bitcast.2), calls=%async_computation.3 | async-start | bytes 8192 | tf_op jit(solution)/shard_map/all_to_all | solution.py:467
  20.2 2.2 %collective-permute-start.4 = (bf16[16,32,128]{2,1,0:T(8,128)(2,1)S(1)}, bf16[16,32,128]{2,1,0:T(8,128)(2,1)S(1)}, u32[]{:S(2)}, u32[]{:S(2)}) collective-permute-start(bf16[16,32,128]{2,1,0:T(8,128)(2,1)S(1)} %collective-permute-done.2.refs_4_), channel_id=1, source_target_pairs={{0,2},{2,4},{4,6},{6,8},{8,10},{10,12},{12,14},{14,0},{1,3},{3,5},... | collective-permute-start | bytes 393224 | tf_op jit(solution)/shard_map/ppermute | solution.py:438
  22.4 1.0 collective-permute-start.3
  24.2 1.3 %codes.1 = s32[4,1,2]{2,1,0:T(1,128)} custom-call(s32[1,8]{1,0:T(1,128)} %slots_ref.3), custom_call_target="tpu_custom_call" | custom-call | tf_op jit(solution)/shard_map/codes/pallas_call | solution.py:227
  25.4 4.5 %all-to-all-start = ((s32[4,1,2]{2,1,0:T(1,128)}), s32[4,1,2]{2,1,0:T(1,128)S(1)}, u32[]{:S(2)}, u32[]{:S(2)}) async-start(s32[4,1,2]{2,1,0:T(1,128)} %codes.1), calls=%async_computation | async-start | bytes 4096 | tf_op jit(solution)/shard_map/all_to_all | solution.py:475
  29.9 2.1 %select.7 = (bf16[32,32,128]{2,1,0:T(8,128)(2,1)S(1)}, bf16[32,32,128]{2,1,0:T(8,128)(2,1)S(1)}, bf16[32,32,128]{2,1,0:T(8,128)(2,1)}, bf16[32,32,128]{2,1,0:T(8...) custom-call(s32[8,1,32]{2,1,0:T(1,128)S(1)} %all-to-all-done.3.wante, ...), custom_call_target="tpu_custom_call" | custom-call | tf_op jit(solution)/shard_map/select/pallas_call | solution.py:98
  32.7 1.5 %collective-permute-start.8 = (bf16[32,32,128]{2,1,0:T(8,128)(2,1)S(1)}, bf16[32,32,128]{2,1,0:T(8,128)(2,1)S(1)}, u32[]{:S(2)}, u32[]{:S(2)}) collective-permute-start(bf16[32,32,128]{2,1,0:T(8,128)(2,1)S(1)} %get-tuple-element.23), channel_id=1, source_target_pairs={{0,16},{1,17},{16,32},{17,33},{32,48},{33,49},{48,0},{49,1},{2,18}... | collective-permute-start | bytes 786440 | tf_op jit(solution)/shard_map/ppermute | solution.py:448
  34.8 1.0 collective-permute-start.9
  35.8 1.5 %collective-permute-start.10 = (bf16[32,32,128]{2,1,0:T(8,128)(2,1)}, bf16[32,32,128]{2,1,0:T(8,128)(2,1)}, u32[]{:S(2)}, u32[]{:S(2)}) collective-permute-start(bf16[32,32,128]{2,1,0:T(8,128)(2,1)} %get-tuple-element.25), channel_id=1, source_target_pairs={{0,32},{1,33},{16,48},{17,49},{32,0},{33,1},{48,16},{49,17},{2,34}... | collective-permute-start | bytes 786440 | tf_op jit(solution)/shard_map/ppermute | solution.py:448
  37.3 1.7 %collective-permute-start.11 = (bf16[32,32,128]{2,1,0:T(8,128)(2,1)}, bf16[32,32,128]{2,1,0:T(8,128)(2,1)}, u32[]{:S(2)}, u32[]{:S(2)}) collective-permute-start(bf16[32,32,128]{2,1,0:T(8,128)(2,1)} %get-tuple-element.26), channel_id=1, source_target_pairs={{0,33},{1,32},{16,49},{17,48},{32,1},{33,0},{48,17},{49,16},{2,35}... | collective-permute-start | bytes 786440 | tf_op jit(solution)/shard_map/ppermute | solution.py:448
  39.0 0.9 collective-permute-start.12
  39.8 2.0 %collective-permute-done.8.refs_2_ = bf16[32,32,128]{2,1,0:T(8,128)(2,1)S(1)} collective-permute-done((bf16[32,32,128]{2,1,0:T(8,128)(2,1)S(1)}, bf16[32,32,128]{2,1,0:T(8,128)(2,1)S(1)}, u32[]{:S(2)}, u32[]{:S(2)}) %collective-permute-start.8) | collective-permute-done | bytes 262176 | tf_op jit(solution)/shard_map/ppermute | solution.py:448
  43.7 1.3 %spread.1 = s32[8,1,8]{2,1,0:T(1,128)} custom-call(s32[1,8]{1,0:T(1,128)} %send_ref.3, s32[4,1,2]{2,1,0:T(1,128)} %copy-done.12), custom_call_target="tpu_custom_call" | custom-call | tf_op jit(solution)/shard_map/spread/pallas_call | solution.py:246
  45.0 4.9 %all-to-all-start.1 = ((s32[8,1,8]{2,1,0:T(1,128)}), s32[8,1,8]{2,1,0:T(1,128)S(1)}, u32[]{:S(2)}, u32[]{:S(2)}) async-start(s32[8,1,8]{2,1,0:T(1,128)} %spread.1), calls=%async_computation.1 | async-start | bytes 8192 | tf_op jit(solution)/shard_map/all_to_all | solution.py:476
  50.3 12.7 %all-to-all-done.1.plane_ref = s32[8,1,8]{2,1,0:T(1,128)S(1)} async-done(((s32[8,1,8]{2,1,0:T(1,128)}), s32[8,1,8]{2,1,0:T(1,128)S(1)}, u32[]{:S(2)}, u32[]{:S(2)}) %all-to-all-start.1) | async-done | bytes 288 | tf_op jit(solution)/shard_map/all_to_all | solution.py:476
  63.5 1.4 %plane.1 = s32[8,1,64]{2,1,0:T(1,128)} custom-call(s32[8,1,8]{2,1,0:T(1,128)} %copy-done.11), custom_call_target="tpu_custom_call" | custom-call | tf_op jit(solution)/shard_map/plane/pallas_call | solution.py:263
  64.9 3.9 %all-to-all-start.2 = ((s32[8,1,64]{2,1,0:T(1,128)}), s32[8,1,64]{2,1,0:T(1,128)S(1)}, u32[]{:S(2)}, u32[]{:S(2)}) async-start(s32[8,1,64]{2,1,0:T(1,128)} %plane.1), calls=%async_computation.2 | async-start | bytes 8192 | tf_op jit(solution)/shard_map/all_to_all | solution.py:479
  68.9 0.7 copy-done.2
  69.6 4.8 %products.1.y_ref = bf16[16,64,768]{2,1,0:T(8,128)(2,1)S(1)} custom-call(bf16[16,64,64]{2,1,0:T(8,128)(2,1)S(1)} %reshape.29.p_ref, bf16[128,128]{1,0:T(8,128)(2,1)S(1)} %copy-done.2, bf16[16,64,704]{2,1,0:T(8,128)(2,1)S(1)} %copy-done), custom_call_target="tpu_custom_call" | custom-call | flops 301989888 | bytes 3200000 | tf_op jit(solution)/shard_map/products/pallas_call | solution.py:60
  74.4 4.3 %addresses.1 = (s32[16,11]{1,0:T(8,128)}, s32[16,11]{1,0:T(8,128)}) custom-call(s32[16,11]{1,0:T(8,128)} %columns_ref.1, s32[64,4]{1,0:T(8,128)} %copy-done.8), custom_call_target="tpu_custom_call" | custom-call | flops 1000000 | bytes 2000000 | tf_op jit(solution)/shard_map/addresses/pallas_call | solution.py:299
  80.1 3.3 %followers.1 = (bf16[2,64,768]{2,1,0:T(8,128)(2,1)S(1)}, bf16[2,64,768]{2,1,0:T(8,128)(2,1)S(1)}, bf16[2,64,768]{2,1,0:T(8,128)(2,1)S(1)}, bf16[2,64,768]{2,1,0:T(8,128)(2,1)S(1)}, bf16[273,32,128]{2,1,0:T(8,128)(2,1)S(1)}) custom-call(s32[16,12]{1,0:T(8,128)S(1)} %select_add_fusion.at_ref, s32[1,8]{1,0:T(1,128)S(1)} %copy-done.6, s32[16,11]{1,0:T(8,128)S(1)} %copy-done.3, ...), custom_call_target="tpu_custom_call" | custom-call | flops 100663296 | bytes 5000000 | tf_op jit(solution)/shard_map/followers/pallas_call | solution.py:189
  83.5 2.1 %collective-permute-start.14 = (bf16[2,64,768]{2,1,0:T(8,128)(2,1)S(1)}, bf16[2,64,768]{2,1,0:T(8,128)(2,1)S(1)}, u32[]{:S(2)}, u32[]{:S(2)}) collective-permute-start(bf16[2,64,768]{2,1,0:T(8,128)(2,1)S(1)} %get-tuple-element.33), channel_id=1, source_target_pairs={{0,64},{64,128},{128,192},{192,0},{1,65},{65,129},{129,193},{193,1... | collective-permute-start | bytes 589832 | tf_op jit(solution)/shard_map/ppermute | solution.py:438
  85.6 2.7 %collective-permute-start.15 = (bf16[2,64,768]{2,1,0:T(8,128)(2,1)S(1)}, bf16[2,64,768]{2,1,0:T(8,128)(2,1)S(1)}, u32[]{:S(2)}, u32[]{:S(2)}) collective-permute-start(bf16[2,64,768]{2,1,0:T(8,128)(2,1)S(1)} %get-tuple-element.34), channel_id=1, source_target_pairs={{0,128},{64,192},{128,0},{192,64},{1,129},{65,193},{129,1},{193,65... | collective-permute-start | bytes 589832 | tf_op jit(solution)/shard_map/ppermute | solution.py:438
  88.2 1.5 %collective-permute-start.16 = (bf16[2,64,768]{2,1,0:T(8,128)(2,1)S(1)}, bf16[2,64,768]{2,1,0:T(8,128)(2,1)S(1)}, u32[]{:S(2)}, u32[]{:S(2)}) collective-permute-start(bf16[2,64,768]{2,1,0:T(8,128)(2,1)S(1)} %get-tuple-element.35), channel_id=1, source_target_pairs={{0,192},{64,0},{128,64},{192,128},{1,193},{65,1},{129,65},{193,129... | collective-permute-start | bytes 589832 | tf_op jit(solution)/shard_map/ppermute | solution.py:438
  89.7 3.1 %leaders.1 = (bf16[8,64,768]{2,1,0:T(8,128)(2,1)S(1)}, s32[8,128]{1,0:T(8,128)S(1)}) custom-call(s32[16,12]{1,0:T(8,128)S(1)} %select_add_fusion.at_ref, s32[16,11]{1,0:T(8,128)S(1)} %copy-done.3, s32[16,11]{1,0:T(8,128)S(1)} %copy-done.4, s32[8,1,64]{2,1,0:T(1,128)S(1)} %all-to-all-done.2.codes_ref, bf16[16,64,768]{2,1,0:T(8,128)(2,1)S(1)} %products.1.y_ref, ...), custom_call_target="tpu_custom_call" | custom-call | flops 100663296 | bytes 5000000 | tf_op jit(solution)/shard_map/leaders/pallas_call | solution.py:202
  92.8 4.3 %collective-permute-done.15.refs_2_ = bf16[2,64,768]{2,1,0:T(8,128)(2,1)S(1)} collective-permute-done((bf16[2,64,768]{2,1,0:T(8,128)(2,1)S(1)}, bf16[2,64,768]{2,1,0:T(8,128)(2,1)S(1)}, u32[]{:S(2)}, u32[]{:S(2)}) %collective-permute-start.15) | collective-permute-done | bytes 196640 | tf_op jit(solution)/shard_map/ppermute | solution.py:438
  97.1 4.3 %merge.1 = (bf16[8,64,1408]{2,1,0:T(8,128)(2,1)}, s32[8,22]{1,0:T(8,128)}) custom-call(s32[1,8]{1,0:T(1,128)S(1)} %copy-done.5, bf16[8,64,768]{2,1,0:T(8,128)(2,1)S(1)} %get-tuple-element.30.lead_ref, s32[8,128]{1,0:T(8,128)S(1)} %get-tuple-element.31.own_labels_ref, bf16[2,64,768]{2,1,0:T(8,128)(2,1)S(1)} %get-tuple-element.32.refs_0_, ...), custom_call_target="tpu_custom_call" | custom-call | tf_op jit(solution)/shard_map/merge/pallas_call | solution.py:411
  (55 shorter events, 7.1 us)
Async XLA Ops:
  0.6 49.4 %copy-start.7 = (bf16[16,4096]{1,0:T(8,128)(2,1)S(1)}, bf16[16,4096]{1,0:T(8,128)(2,1)}, u32[]{:S(2)}) copy-start(bf16[16,4096]{1,0:T(8,128)(2,1)} %param.7) | copy-start | bytes 393220
  0.6 68.2 %copy-start = (bf16[16,64,704]{2,1,0:T(8,128)(2,1)S(1)}, bf16[16,64,704]{2,1,0:T(8,128)(2,1)}, u32[]{:S(2)}) copy-start(bf16[16,64,704]{2,1,0:T(8,128)(2,1)} %a_hbm.1) | copy-start | bytes 4325380
  1.7 18.5 %collective-permute-start.2 = (bf16[16,32,128]{2,1,0:T(8,128)(2,1)S(1)}, bf16[16,32,128]{2,1,0:T(8,128)(2,1)S(1)}, u32[]{:S(2)}, u32[]{:S(2)}) collective-permute-start(bf16[16,32,128]{2,1,0:T(8,128)(2,1)S(1)} %bitcast.8), channel_id=1, source_target_pairs={{0,8},{2,10},{4,12},{6,14},{8,0},{10,2},{12,4},{14,6},{1,9},{3,11}... | collective-permute-start | bytes 393224 | tf_op jit(solution)/shard_map/ppermute | solution.py:438
  9.0 13.5 %collective-permute-start.6 = (bf16[16,32,128]{2,1,0:T(8,128)(2,1)S(1)}, bf16[16,32,128]{2,1,0:T(8,128)(2,1)S(1)}, u32[]{:S(2)}, u32[]{:S(2)}) collective-permute-start(bf16[16,32,128]{2,1,0:T(8,128)(2,1)S(1)} %bitcast.9), channel_id=1, source_target_pairs={{0,14},{2,0},{4,2},{6,4},{8,6},{10,8},{12,10},{14,12},{1,15},{3,1}... | collective-permute-start | bytes 393224 | tf_op jit(solution)/shard_map/ppermute | solution.py:438
  9.1 20.8 %collective-permute-start.5 = (bf16[16,32,128]{2,1,0:T(8,128)(2,1)S(1)}, bf16[16,32,128]{2,1,0:T(8,128)(2,1)S(1)}, u32[]{:S(2)}, u32[]{:S(2)}) collective-permute-start(bf16[16,32,128]{2,1,0:T(8,128)(2,1)S(1)} %bitcast.10), channel_id=1, source_target_pairs={{0,12},{2,14},{4,0},{6,2},{8,4},{10,6},{12,8},{14,10},{1,13},{3,15... | collective-permute-start | bytes 393224 | tf_op jit(solution)/shard_map/ppermute | solution.py:438
  9.2 20.7 %collective-permute-start.1 = (bf16[16,32,128]{2,1,0:T(8,128)(2,1)S(1)}, bf16[16,32,128]{2,1,0:T(8,128)(2,1)S(1)}, u32[]{:S(2)}, u32[]{:S(2)}) collective-permute-start(bf16[16,32,128]{2,1,0:T(8,128)(2,1)S(1)} %bitcast.11), channel_id=1, source_target_pairs={{0,4},{2,6},{4,8},{6,10},{8,12},{10,14},{12,0},{14,2},{1,5},{3,7},... | collective-permute-start | bytes 393224 | tf_op jit(solution)/shard_map/ppermute | solution.py:438
  12.0 17.9 %collective-permute-start = (bf16[16,32,128]{2,1,0:T(8,128)(2,1)S(1)}, bf16[16,32,128]{2,1,0:T(8,128)(2,1)S(1)}, u32[]{:S(2)}, u32[]{:S(2)}) collective-permute-start(bf16[16,32,128]{2,1,0:T(8,128)(2,1)S(1)} %bitcast.12), channel_id=1, source_target_pairs={{0,2},{2,4},{4,6},{6,8},{8,10},{10,12},{12,14},{14,0},{1,3},{3,5},... | collective-permute-start | bytes 393224 | tf_op jit(solution)/shard_map/ppermute | solution.py:438
  14.7 50.2 %copy-start.8 = (s32[64,4]{1,0:T(8,128)}, s32[64,4]{1,0:T(8,128)S(1)}, u32[]{:S(2)}) copy-start(s32[64,4]{1,0:T(8,128)S(1)} %copy.10.fetch_ref) | copy-start | bytes 3076
  15.4 10.1 %all-to-all-start.3 = ((s32[8,1,32]{2,1,0:T(1,128)}), s32[8,1,32]{2,1,0:T(1,128)S(1)}, u32[]{:S(2)}, u32[]{:S(2)}) async-start(s32[8,1,32]{2,1,0:T(1,128)} %bitcast.2), calls=%async_computation.3 | async-start | bytes 8192 | tf_op jit(solution)/shard_map/all_to_all | solution.py:467
  20.2 9.7 %collective-permute-start.4 = (bf16[16,32,128]{2,1,0:T(8,128)(2,1)S(1)}, bf16[16,32,128]{2,1,0:T(8,128)(2,1)S(1)}, u32[]{:S(2)}, u32[]{:S(2)}) collective-permute-start(bf16[16,32,128]{2,1,0:T(8,128)(2,1)S(1)} %collective-permute-done.2.refs_4_), channel_id=1, source_target_pairs={{0,2},{2,4},{4,6},{6,8},{8,10},{10,12},{12,14},{14,0},{1,3},{3,5},... | collective-permute-start | bytes 393224 | tf_op jit(solution)/shard_map/ppermute | solution.py:438
  22.4 7.5 %collective-permute-start.3 = (bf16[16,32,128]{2,1,0:T(8,128)(2,1)S(1)}, bf16[16,32,128]{2,1,0:T(8,128)(2,1)S(1)}, u32[]{:S(2)}, u32[]{:S(2)}) collective-permute-start(bf16[16,32,128]{2,1,0:T(8,128)(2,1)S(1)} %collective-permute-done.2.refs_4_), channel_id=1, source_target_pairs={{0,14},{2,0},{4,2},{6,4},{8,6},{10,8},{12,10},{14,12},{1,15},{3,1}... | collective-permute-start | bytes 393224 | tf_op jit(solution)/shard_map/ppermute | solution.py:438
  25.4 17.7 %all-to-all-start = ((s32[4,1,2]{2,1,0:T(1,128)}), s32[4,1,2]{2,1,0:T(1,128)S(1)}, u32[]{:S(2)}, u32[]{:S(2)}) async-start(s32[4,1,2]{2,1,0:T(1,128)} %codes.1), calls=%async_computation | async-start | bytes 4096 | tf_op jit(solution)/shard_map/all_to_all | solution.py:475
  32.0 0.7 copy-start.1
  32.7 6.2 %collective-permute-start.7 = (bf16[32,32,128]{2,1,0:T(8,128)(2,1)S(1)}, bf16[32,32,128]{2,1,0:T(8,128)(2,1)S(1)}, u32[]{:S(2)}, u32[]{:S(2)}) collective-permute-start(bf16[32,32,128]{2,1,0:T(8,128)(2,1)S(1)} %get-tuple-element.22), channel_id=1, source_target_pairs={{0,1},{1,0},{16,17},{17,16},{32,33},{33,32},{48,49},{49,48},{2,3},... | collective-permute-start | bytes 786440 | tf_op jit(solution)/shard_map/ppermute | solution.py:448
  32.7 9.1 %collective-permute-start.8 = (bf16[32,32,128]{2,1,0:T(8,128)(2,1)S(1)}, bf16[32,32,128]{2,1,0:T(8,128)(2,1)S(1)}, u32[]{:S(2)}, u32[]{:S(2)}) collective-permute-start(bf16[32,32,128]{2,1,0:T(8,128)(2,1)S(1)} %get-tuple-element.23), channel_id=1, source_target_pairs={{0,16},{1,17},{16,32},{17,33},{32,48},{33,49},{48,0},{49,1},{2,18}... | collective-permute-start | bytes 786440 | tf_op jit(solution)/shard_map/ppermute | solution.py:448
  34.8 43.9 %collective-permute-start.9 = (bf16[32,32,128]{2,1,0:T(8,128)(2,1)}, bf16[32,32,128]{2,1,0:T(8,128)(2,1)}, u32[]{:S(2)}, u32[]{:S(2)}) collective-permute-start(bf16[32,32,128]{2,1,0:T(8,128)(2,1)} %get-tuple-element.24), channel_id=1, source_target_pairs={{0,17},{1,16},{16,33},{17,32},{32,49},{33,48},{48,1},{49,0},{2,19}... | collective-permute-start | bytes 786440 | tf_op jit(solution)/shard_map/ppermute | solution.py:448
  35.8 42.9 %collective-permute-start.10 = (bf16[32,32,128]{2,1,0:T(8,128)(2,1)}, bf16[32,32,128]{2,1,0:T(8,128)(2,1)}, u32[]{:S(2)}, u32[]{:S(2)}) collective-permute-start(bf16[32,32,128]{2,1,0:T(8,128)(2,1)} %get-tuple-element.25), channel_id=1, source_target_pairs={{0,32},{1,33},{16,48},{17,49},{32,0},{33,1},{48,16},{49,17},{2,34}... | collective-permute-start | bytes 786440 | tf_op jit(solution)/shard_map/ppermute | solution.py:448
  37.3 41.4 %collective-permute-start.11 = (bf16[32,32,128]{2,1,0:T(8,128)(2,1)}, bf16[32,32,128]{2,1,0:T(8,128)(2,1)}, u32[]{:S(2)}, u32[]{:S(2)}) collective-permute-start(bf16[32,32,128]{2,1,0:T(8,128)(2,1)} %get-tuple-element.26), channel_id=1, source_target_pairs={{0,33},{1,32},{16,49},{17,48},{32,1},{33,0},{48,17},{49,16},{2,35}... | collective-permute-start | bytes 786440 | tf_op jit(solution)/shard_map/ppermute | solution.py:448
  39.0 2.9 %copy-start.9 = (bf16[32,32,128]{2,1,0:T(8,128)(2,1)}, bf16[32,32,128]{2,1,0:T(8,128)(2,1)S(1)}, u32[]{:S(2)}) copy-start(bf16[32,32,128]{2,1,0:T(8,128)(2,1)S(1)} %collective-permute-done.7.refs_1_) | copy-start | bytes 786436
  39.0 39.8 %collective-permute-start.12 = (bf16[32,32,128]{2,1,0:T(8,128)(2,1)}, bf16[32,32,128]{2,1,0:T(8,128)(2,1)}, u32[]{:S(2)}, u32[]{:S(2)}) collective-permute-start(bf16[32,32,128]{2,1,0:T(8,128)(2,1)} %get-tuple-element.27), channel_id=1, source_target_pairs={{0,48},{1,49},{16,0},{17,1},{32,16},{33,17},{48,32},{49,33},{2,50}... | collective-permute-start | bytes 786440 | tf_op jit(solution)/shard_map/ppermute | solution.py:448
  41.8 0.7 copy-start.10
  42.5 36.2 %collective-permute-start.13 = (bf16[32,32,128]{2,1,0:T(8,128)(2,1)}, bf16[32,32,128]{2,1,0:T(8,128)(2,1)}, u32[]{:S(2)}, u32[]{:S(2)}) collective-permute-start(bf16[32,32,128]{2,1,0:T(8,128)(2,1)} %get-tuple-element.28), channel_id=1, source_target_pairs={{0,49},{1,48},{16,1},{17,0},{32,17},{33,16},{48,33},{49,32},{2,51}... | collective-permute-start | bytes 786440 | tf_op jit(solution)/shard_map/ppermute | solution.py:448
  45.0 18.0 %all-to-all-start.1 = ((s32[8,1,8]{2,1,0:T(1,128)}), s32[8,1,8]{2,1,0:T(1,128)S(1)}, u32[]{:S(2)}, u32[]{:S(2)}) async-start(s32[8,1,8]{2,1,0:T(1,128)} %spread.1), calls=%async_computation.1 | async-start | bytes 8192 | tf_op jit(solution)/shard_map/all_to_all | solution.py:476
  64.9 13.8 %all-to-all-start.2 = ((s32[8,1,64]{2,1,0:T(1,128)}), s32[8,1,64]{2,1,0:T(1,128)S(1)}, u32[]{:S(2)}, u32[]{:S(2)}) async-start(s32[8,1,64]{2,1,0:T(1,128)} %plane.1), calls=%async_computation.2 | async-start | bytes 8192 | tf_op jit(solution)/shard_map/all_to_all | solution.py:479
  68.8 0.8 copy-start.2
  69.6 9.1 %copy-start.6 = (s32[1,8]{1,0:T(1,128)S(1)}, s32[1,8]{1,0:T(1,128)}, u32[]{:S(2)}) copy-start(s32[1,8]{1,0:T(1,128)} %send_ref.3) | copy-start | bytes 100
  78.7 0.7 copy-start.3
  79.4 0.7 copy-start.4
  83.5 9.3 %collective-permute-start.14 = (bf16[2,64,768]{2,1,0:T(8,128)(2,1)S(1)}, bf16[2,64,768]{2,1,0:T(8,128)(2,1)S(1)}, u32[]{:S(2)}, u32[]{:S(2)}) collective-permute-start(bf16[2,64,768]{2,1,0:T(8,128)(2,1)S(1)} %get-tuple-element.33), channel_id=1, source_target_pairs={{0,64},{64,128},{128,192},{192,0},{1,65},{65,129},{129,193},{193,1... | collective-permute-start | bytes 589832 | tf_op jit(solution)/shard_map/ppermute | solution.py:438
  85.6 11.5 %collective-permute-start.15 = (bf16[2,64,768]{2,1,0:T(8,128)(2,1)S(1)}, bf16[2,64,768]{2,1,0:T(8,128)(2,1)S(1)}, u32[]{:S(2)}, u32[]{:S(2)}) collective-permute-start(bf16[2,64,768]{2,1,0:T(8,128)(2,1)S(1)} %get-tuple-element.34), channel_id=1, source_target_pairs={{0,128},{64,192},{128,0},{192,64},{1,129},{65,193},{129,1},{193,65... | collective-permute-start | bytes 589832 | tf_op jit(solution)/shard_map/ppermute | solution.py:438
  88.2 8.8 %collective-permute-start.16 = (bf16[2,64,768]{2,1,0:T(8,128)(2,1)S(1)}, bf16[2,64,768]{2,1,0:T(8,128)(2,1)S(1)}, u32[]{:S(2)}, u32[]{:S(2)}) collective-permute-start(bf16[2,64,768]{2,1,0:T(8,128)(2,1)S(1)} %get-tuple-element.35), channel_id=1, source_target_pairs={{0,192},{64,0},{128,64},{192,128},{1,193},{65,1},{129,65},{193,129... | collective-permute-start | bytes 589832 | tf_op jit(solution)/shard_map/ppermute | solution.py:438
  89.7 7.4 %copy-start.5 = (s32[1,8]{1,0:T(1,128)S(1)}, s32[1,8]{1,0:T(1,128)}, u32[]{:S(2)}) copy-start(s32[1,8]{1,0:T(1,128)} %slots_ref.3) | copy-start | bytes 100
  (2 other events, 1.2 us)

commit v5 on v4

--- a/solution.py
+++ b/solution.py
@@ -16,6 +16,7 @@
 SLOTS = 12
 WIDE = SLOTS * BLK
 TABLE = N_DEV * C
+SPOTS, LABELS = 512, 4096
 CHUNKS = 1
 CK = 32 // CHUNKS
 AXES = ("grp", "x", "z", "core")
@@ -34,36 +35,44 @@
 STEP = 4
 
 
-def products_kernel(p_ref, perm_ref, a_hbm, y_ref, a_ref, sems):
+def products_kernel(p_ref, a_hbm, y_ref, a_ref, work, sems):
     def load(h):
         rows = pl.ds(h * STEP, STEP)
         return pltpu.make_async_copy(a_hbm.at[rows], a_ref.at[rows], sems.at[h])
 
     for h in range(ROWS // STEP):
         load(h).start()
+    row = lax.broadcasted_iota(jnp.int32, (LANES, LANES), 0)
+    lane = lax.broadcasted_iota(jnp.int32, (LANES, LANES), 1)
+    inner = lane & (BLK - 1)
+    source = (lane & BLK) + jnp.where(inner < 32, 2 * inner, 2 * (inner - 32) + 1)
+    perm = jnp.where(row == source, 1.0, 0.0).astype(jnp.bfloat16)
+    pad = jnp.zeros((BLK, BLK), jnp.float32)
     for h in range(ROWS // STEP):
         load(h).wait()
-        for i in range(h * STEP, (h + 1) * STEP):
+        for i in range(STEP):
             y = lax.dot_general(
-                p_ref[i], a_ref[i], (((0,), (0,)), ((), ())), preferred_element_type=jnp.float32
+                p_ref[h * STEP + i], a_ref[h * STEP + i], (((0,), (0,)), ((), ())),
+                preferred_element_type=jnp.float32,
             )
-            pad = jnp.zeros((BLK, BLK), jnp.float32)
-            y = jnp.concatenate([y, pad] if i < HALF else [pad, y], axis=1).astype(jnp.bfloat16)
-            for t in range(WIDE // LANES):
-                span = slice(t * LANES, (t + 1) * LANES)
-                y_ref[i, :, span] = jnp.dot(
-                    y[:, span], perm_ref[...], preferred_element_type=jnp.float32
-                ).astype(jnp.bfloat16)
-
-
-def products(blocks, stiffness, perm):
+            y = jnp.concatenate([y, pad] if h * STEP + i < HALF else [pad, y], axis=1)
+            work[h, i * BLK:(i + 1) * BLK] = y.astype(jnp.bfloat16)
+        for t in range(WIDE // LANES):
+            span = slice(t * LANES, (t + 1) * LANES)
+            y_ref[h * STEP:(h + 1) * STEP, :, span] = jnp.dot(
+                work[h, :, span], perm, preferred_element_type=jnp.float32
+            ).astype(jnp.bfloat16).reshape(STEP, BLK, LANES)
+
+
+def products(blocks, stiffness):
     return pl.pallas_call(
         products_kernel,
         out_shape=jax.ShapeDtypeStruct((ROWS, BLK, WIDE), jnp.bfloat16),
-        in_specs=[VMEM, VMEM, HBM],
+        in_specs=[VMEM, HBM],
         out_specs=VMEM,
         scratch_shapes=[
             pltpu.VMEM((ROWS, BLK, K * BLK), jnp.bfloat16),
+            pltpu.VMEM((ROWS // STEP, STEP * BLK, WIDE), jnp.bfloat16),
             pltpu.SemaphoreType.DMA((ROWS // STEP,)),
         ],
         compiler_params=LIMIT,
@@ -71,7 +80,7 @@
             flops=2 * ROWS * BLK * BLK * WIDE * 3, bytes_accessed=3_200_000, transcendentals=0
         ),
         name="products",
-    )(blocks, perm, stiffness)
+    )(blocks, stiffness)
 
 
 def select_kernel(wanted_ref, *refs):
@@ -121,12 +130,14 @@
         copy.wait()
 
 
-def row_tiles(i, table, at_ref, y_ref, emit):
+def row_tiles(i, late, table, slot_ref, y_ref, emit):
     low = low_lanes((32, LANES))
     zero = jnp.zeros((32, LANES), jnp.bfloat16)
     for t in range(SLOTS // 2):
-        a = table[at_ref[i, 2 * t]]
-        b = table[at_ref[i, 2 * t + 1]]
+        a, b = (
+            table[slot_ref[i, k] & (SPOTS - 1) if 0 <= k < K else TABLE + ROWS]
+            for k in (2 * t - late, 2 * t + 1 - late)
+        )
         rhs = jnp.concatenate([
             jnp.where(low, a, zero),
             jnp.where(low, pltpu.roll(a, BLK, 1), zero),
@@ -139,18 +150,20 @@
         ).astype(jnp.bfloat16))
 
 
-def label_row(i, address_ref, offset_ref, codes_ref):
+def label_row(i, slot_ref, codes_ref):
     lane = lax.broadcasted_iota(jnp.int32, (1, LANES), 1)
     labels = jnp.full((1, LANES), -1, jnp.int32)
     for k in range(K):
-        address = address_ref[i, k]
+        word = slot_ref[i, k]
+        address = (word >> 21) - 1
         spot = jnp.maximum(address, 0)
         code = jnp.where(address < 0, 0, codes_ref[spot >> 6, 0, spot & 63])
-        labels = jnp.where(lane == k, offset_ref[i, k] + code, labels)
+        offset = ((word >> 9) & (LABELS - 1)) - 1
+        labels = jnp.where(lane == k, offset + code, labels)
     return labels
 
 
-def follower_kernel(at_ref, send_ref, address_ref, offset_ref, codes_ref, own_ref, y_ref, *refs):
+def follower_kernel(slot_ref, send_ref, codes_ref, own_ref, y_ref, *refs):
     n = NX * NC * CHUNKS
     parts, outs, table, sems = refs[:n], refs[n:n + NG], refs[n + NG], refs[n + NG + 1]
     fill(table, own_ref, parts, sems)
@@ -162,19 +175,19 @@
             def emit(span, value, s=s, q=q):
                 outs[s][q, :, span] = value
 
-            row_tiles(row, table, at_ref, y_ref, emit)
-            labels = label_row(row, address_ref, offset_ref, codes_ref)[:, 0:BLK]
+            row_tiles(row, 1, table, slot_ref, y_ref, emit)
+            labels = label_row(row, slot_ref, codes_ref)[:, 0:BLK]
             outs[s][q, 0:1, 0:BLK] = (labels >> 4).astype(jnp.float32).astype(jnp.bfloat16)
             outs[s][q, 16:17, 0:BLK] = (labels & 15).astype(jnp.float32).astype(jnp.bfloat16)
 
 
-def leader_kernel(at_ref, address_ref, offset_ref, codes_ref, y_ref, table, out, labels_ref):
+def leader_kernel(slot_ref, codes_ref, y_ref, table, out, labels_ref):
     def row(i, carry):
         def emit(span, value):
             out[i, :, span] = value
 
-        row_tiles(i, table, at_ref, y_ref, emit)
-        labels_ref[pl.ds(i, 1), :] = label_row(i, address_ref, offset_ref, codes_ref)
+        row_tiles(i, 0, table, slot_ref, y_ref, emit)
+        labels_ref[pl.ds(i, 1), :] = label_row(i, slot_ref, codes_ref)
         return carry
 
     lax.fori_loop(0, HALF, row, 0)
@@ -183,34 +196,34 @@
 ROW_COST = pl.CostEstimate(flops=2 * 8 * 6 * BLK * LANES * LANES, bytes_accessed=5_000_000, transcendentals=0)
 
 
-def followers(at, send, address, offset, codes, own, y, parts):
+def followers(slots, send, codes, own, y, parts):
     shape = jax.ShapeDtypeStruct((2, BLK, WIDE), jnp.bfloat16)
     table = jax.ShapeDtypeStruct((TABLE + ROWS + 1, 32, LANES), jnp.bfloat16)
     return pl.pallas_call(
         follower_kernel,
         out_shape=[shape] * NG + [table],
-        in_specs=[SMEM] * 5 + [VMEM] * 2 + [HBM] * len(parts),
+        in_specs=[SMEM] * 3 + [VMEM] * 2 + [HBM] * len(parts),
         out_specs=[VMEM] * (NG + 1),
         scratch_shapes=[pltpu.SemaphoreType.DMA((len(parts),))],
         compiler_params=LIMIT,
         cost_estimate=ROW_COST,
         name="followers",
-    )(at, send, address, offset, codes, own, y, *parts)
-
-
-def leaders(at, address, offset, codes, y, table):
+    )(slots, send, codes, own, y, *parts)
+
+
+def leaders(slots, codes, y, table):
     return pl.pallas_call(
         leader_kernel,
         out_shape=[
             jax.ShapeDtypeStruct((HALF, BLK, WIDE), jnp.bfloat16),
             jax.ShapeDtypeStruct((HALF, LANES), jnp.int32),
         ],
-        in_specs=[SMEM] * 4 + [VMEM] * 2,
+        in_specs=[SMEM] * 2 + [VMEM] * 2,
         out_specs=[VMEM] * 2,
         compiler_params=LIMIT,
         cost_estimate=ROW_COST,
         name="leaders",
-    )(at, address, offset, codes, y, table)
+    )(slots, codes, y, table)
 
 
 def code_kernel(slots_ref, codes_ref):
@@ -233,33 +246,37 @@
     )(slots)
 
 
-def spread_kernel(send_ref, returned_ref, out):
+NOTE = NZ * C + HALF
+
+
+def note_kernel(send_ref, lists_ref, returned_ref, out):
     lane = lax.broadcasted_iota(jnp.int32, (NX * NC, 1, HALF), 2)
     mine = jnp.zeros((NX * NC, 1, HALF), jnp.int32)
     for t in range(NG):
         for q in range(2):
-            mine = jnp.where(lane == send_ref[0, 2 * t + q], returned_ref[t, 0, q], mine)
-    out[...] = mine
-
-
-def spread(send, returned):
-    return pl.pallas_call(
-        spread_kernel,
-        out_shape=jax.ShapeDtypeStruct((NX * NC, 1, HALF), jnp.int32),
-        in_specs=[SMEM] * 2,
+            mine = jnp.where(lane == send_ref[0, 2 * t + q], returned_ref[t:t + 1, :, q:q + 1], mine)
+    out[:, :, 0:NZ * C] = lists_ref[...]
+    out[:, :, NZ * C:] = mine
+
+
+def note_rows(send, lists, returned):
+    return pl.pallas_call(
+        note_kernel,
+        out_shape=jax.ShapeDtypeStruct((NX * NC, 1, NOTE), jnp.int32),
+        in_specs=[SMEM, VMEM, VMEM],
         out_specs=VMEM,
-        name="spread",
-    )(send, returned)
-
-
-def plane_kernel(plane_ref, out, row_ref):
+        name="note",
+    )(send, lists, returned)
+
+
+def plane_kernel(note_ref, out, row_ref):
     for d in range(NX * NC):
-        row_ref[:, d * HALF:(d + 1) * HALF] = plane_ref[d]
+        row_ref[:, d * HALF:(d + 1) * HALF] = note_ref[d][:, NZ * C:]
     for z in range(NZ):
         out[z] = row_ref[...]
 
 
-def plane_rows(plane):
+def plane_rows(note):
     return pl.pallas_call(
         plane_kernel,
         out_shape=jax.ShapeDtypeStruct((NZ, 1, NX * NC * HALF), jnp.int32),
@@ -267,10 +284,10 @@
         out_specs=VMEM,
         scratch_shapes=[pltpu.VMEM((1, NX * NC * HALF), jnp.int32)],
         name="plane",
-    )(plane)
-
-
-def address_kernel(columns_ref, fetch_ref, address_ref, offset_ref):
+    )(note)
+
+
+def slot_kernel(columns_ref, fetch_ref, slot_ref):
     g, x, z, c = (lax.axis_index(name) for name in AXES)
     device = x * (NZ * NC) + z * NC + c
 
@@ -282,27 +299,27 @@
             asked = ghost >> 2
             peer = jnp.where(local, device, asked)
             row = jnp.where(local, jnp.maximum(column, 0), fetch_ref[asked, ghost & 3])
-            group = ((peer >> 4) * NC + (peer & 1)) * HALF
-            spot = ((peer >> 1) & (NZ - 1)) * (NX * NC * HALF) + group + row - HALF
+            px, pz, pc = peer >> 4, (peer >> 1) & (NZ - 1), peer & 1
+            way = ((x - px) & (NX - 1)) * NC + (c ^ pc)
+            at = jnp.where(local, TABLE + row, way * (NZ * C) + pz * C + (ghost & 3))
             late = row >= HALF
-            present = column >= 0
-            offset = peer * HALF + jnp.where(late, 0, g * (N_DEV * HALF) + row)
-            address_ref[i, k] = jnp.where(late & present, spot, -1)
-            offset_ref[i, k] = jnp.where(present, offset, -1)
+            spot = jnp.where(late, pz * (NX * NC * HALF) + (px * NC + pc) * HALF + row - HALF + 1, 0)
+            offset = peer * HALF + 1 + jnp.where(late, 0, g * (N_DEV * HALF) + row)
+            word = spot * (LABELS * SPOTS) + offset * SPOTS + at
+            slot_ref[i, k] = jnp.where(column >= 0, word, TABLE + ROWS)
         return carry
 
     lax.fori_loop(0, ROWS, row, 0)
 
 
-def addresses(columns, fetch):
-    shape = jax.ShapeDtypeStruct((ROWS, K), jnp.int32)
-    return pl.pallas_call(
-        address_kernel,
-        out_shape=[shape, shape],
+def slot_words(columns, fetch):
+    return pl.pallas_call(
+        slot_kernel,
+        out_shape=jax.ShapeDtypeStruct((ROWS, K), jnp.int32),
         in_specs=[SMEM] * 2,
-        out_specs=[SMEM] * 2,
+        out_specs=SMEM,
         cost_estimate=pl.CostEstimate(flops=1_000_000, bytes_accessed=2_000_000, transcendentals=0),
-        name="addresses",
+        name="slots",
     )(columns, fetch)
 
 
@@ -463,33 +480,13 @@
         got[3] = shift(got[4], "z", NZ, NZ - 1)
         held.append([got[s] for s in range(NZ)])
 
+    returned = lax.all_to_all(code_rows(partner_slot), "grp", split_axis=0, concat_axis=0, tiled=True)
     lists = fetch_rows.reshape(NX, NZ, NC, C).transpose(0, 2, 1, 3).reshape(NX * NC, 1, NZ * C)
-    wanted = lax.all_to_all(lists, ("x", "core"), split_axis=0, concat_axis=0, tiled=True)
-
-    lane = jnp.arange(LANES, dtype=jnp.int32)
-    inner = lane & (BLK - 1)
-    source = (lane & BLK) + jnp.where(inner < 32, 2 * inner, 2 * (inner - 32) + 1)
-    perm = (lane[:, None] == source[None, :]).astype(jnp.bfloat16)
-    y = products(prolongator.reshape(ROWS, BLK, BLK), stiffness, perm)
-
-    returned = lax.all_to_all(code_rows(partner_slot), "grp", split_axis=0, concat_axis=0, tiled=True)
-    plane = lax.all_to_all(
-        spread(send_order, returned), ("x", "core"), split_axis=0, concat_axis=0, tiled=True
-    )
-    codes = lax.all_to_all(plane_rows(plane), "z", split_axis=0, concat_axis=0, tiled=True)
-    address, offset = addresses(columns, fetch_rows)
-
-    ghost = columns - ROWS
-    peer = ghost >> 2
-    way = ((x - (peer >> 4)) & (NX - 1)) * NC + (c ^ (peer & 1))
-    at = way * (NZ * C) + ((peer >> 1) & (NZ - 1)) * C + (ghost & 3)
-    at = jnp.where(columns < ROWS, TABLE + columns, at)
-    at = jnp.where(columns >= 0, at, TABLE + ROWS).astype(jnp.int32)
-    none = jnp.full((HALF, 1), TABLE + ROWS, jnp.int32)
-    at = jnp.concatenate([
-        jnp.concatenate([at[:HALF], none], axis=1),
-        jnp.concatenate([none, at[HALF:]], axis=1),
-    ])
+    note = note_rows(send_order, lists, returned)
+    wanted = lax.all_to_all(note, ("x", "core"), split_axis=0, concat_axis=0, tiled=True)
+    wanted, words = lax.optimization_barrier((wanted, slot_words(columns, fetch_rows)))
+    codes = lax.all_to_all(plane_rows(wanted), "z", split_axis=0, concat_axis=0, tiled=True)
+    y = products(prolongator.reshape(ROWS, BLK, BLK), stiffness)
 
     parts = []
     for h in range(CHUNKS):
@@ -497,9 +494,9 @@
         moved = {b: cross(chosen[i], b) for i, b in enumerate(ORDER)}
         parts += [pltpu.with_memory_space_constraint(moved[b], pltpu.HBM) for b in range(NX * NC)]
 
-    *sent, table = followers(at, send_order, address, offset, codes, own, y, parts)
+    *sent, table = followers(words, send_order, codes, own, y, parts)
     arrived = [sent[0]] + [shift(sent[s], "grp", NG, s) for s in range(1, NG)]
-    lead, lead_labels = leaders(at, address, offset, codes, y, table)
+    lead, lead_labels = leaders(words, codes, y, table)
     return tuple(merge(partner_slot, lead, lead_labels, arrived))
 
 

time: 102 us -> 99.1 us (0.972)
  waiting for transfers between devices: 19 us -> 27.2 us
  starting transfers between devices: 46.9 us -> 41.1 us
  local copies, waits for them, and re-layouts: 7.47 us -> 4.72 us
  Pallas kernels: 25.7 us -> 23.9 us
  other arithmetic: 1.41 us -> 0 us
    all_to_all x3 -> x2, waiting for transfers between devices: 12.7 us -> 4.65 us  [the longest x1 4.65 us: per_device(): lax.all_to_all(plane_rows(wanted), 'z', split_axis=0, concat_axis=0, tile...]
    ppermute x7, waiting for transfers between devices: 2.02 us -> 8.59 us  [cross(): return lax.ppermute(value, ('x', 'core'), pairs)]
    ppermute x10, waiting for transfers between devices: 4.3 us -> 10.3 us  [shift(): lax.ppermute(value, axis, [(i, (i + by) % size) for i in range(size)])]
    all_to_all x3 -> x2, starting transfers between devices: 13.7 us -> 9 us  [the longest x1 4.83 us: per_device(): lax.all_to_all(note, ('x', 'core'), split_axis=0, concat_axis=0, tiled=True)]
    all_to_all x1, waiting for transfers between devices: 0.01 us -> 3.65 us  [per_device(): lax.all_to_all(code_rows(partner_slot), 'grp', split_axis=0, concat_axis=...]
    unnamed x28 -> x24, local copies, waits for them, and re-layouts: 6.55 us -> 3.81 us
    pallas_call x1, Pallas kernels: 4.78 us -> 3 us  [products(): pl.pallas_call(products_kernel, out_shape=jax.ShapeDtypeStruct((ROWS, BLK...]
    ppermute x10, starting transfers between devices: 21.7 us -> 20.6 us  [shift(): lax.ppermute(value, axis, [(i, (i + by) % size) for i in range(size)])]
  transfers between devices with their start and end apart: 21 -> 20, of which waited for: 3 -> 8; matrix products, arithmetic and copies ran while one was open for 3% -> 2% of each run, Pallas kernels for 18% -> 15%
where the time goes in v5:
time: 99.1 us; the launch traced here: 97.8 us
  starting transfers between devices  41.1 us (41%)
  waiting for transfers between devices  27.2 us (27%)
  Pallas kernels  23.9 us (24%)
  local copies, waits for them, and re-layouts  4.72 us (5%)
    ppermute x10, starting transfers between devices, shift(): lax.ppermute(value, axis, [(i, (i + by) % size) for i in range(size)])  20.6 us
    ppermute x10, waiting for transfers between devices, shift(): lax.ppermute(value, axis, [(i, (i + by) % size) for i in range(size)])  10.3 us
    ppermute x7, waiting for transfers between devices, cross(): return lax.ppermute(value, ('x', 'core'), pairs)  8.59 us
    ppermute x7, starting transfers between devices, cross(): return lax.ppermute(value, ('x', 'core'), pairs)  6.96 us
    all_to_all x1, starting transfers between devices, per_device(): lax.all_to_all(note, ('x', 'core'), split_axis=0, concat_axis=0, tiled=True)  4.83 us
    pallas_call x1, Pallas kernels, slot_words(): pl.pallas_call(slot_kernel, out_shape=jax.ShapeDtypeStruct((ROWS, K), jnp...  4.8 us
    all_to_all x1, waiting for transfers between devices, per_device(): lax.all_to_all(plane_rows(wanted), 'z', split_axis=0, concat_axis=0, tile...  4.65 us
    all_to_all x1, starting transfers between devices, per_device(): lax.all_to_all(code_rows(partner_slot), 'grp', split_axis=0, concat_axis=...  4.46 us
  transfers between devices with their start and end apart: 20, of which 8 were waited for; matrix products, arithmetic and copies ran while one was open for 2% of the time, Pallas kernels for 15%

profile of v5, /device:TPU:2, one launch (start us, length us, event | category | flops | bytes accessed | tf_op | source)
XLA Modules:
  0.0 97.8 jit_solution(9974434413110954563)
XLA Ops:
  0.6 1.0 %copy.14 = bf16[2,8,32,128]{3,2,1,0:T(8,128)(2,1)S(1)} copy(bf16[2,8,32,128]{3,1,2,0:T(8,128)(2,1)} %bitcast.15) | data formatting | bytes 262144
  1.7 7.3 %collective-permute-start.2 = (bf16[16,32,128]{2,1,0:T(8,128)(2,1)S(1)}, bf16[16,32,128]{2,1,0:T(8,128)(2,1)S(1)}, u32[]{:S(2)}, u32[]{:S(2)}) collective-permute-start(bf16[16,32,128]{2,1,0:T(8,128)(2,1)S(1)} %bitcast.8), channel_id=1, source_target_pairs={{0,8},{2,10},{4,12},{6,14},{8,0},{10,2},{12,4},{14,6},{1,9},{3,11}... | collective-permute-start | bytes 393224 | tf_op jit(solution)/shard_map/ppermute | solution.py:455
  9.2 2.8 %collective-permute-start.1 = (bf16[16,32,128]{2,1,0:T(8,128)(2,1)S(1)}, bf16[16,32,128]{2,1,0:T(8,128)(2,1)S(1)}, u32[]{:S(2)}, u32[]{:S(2)}) collective-permute-start(bf16[16,32,128]{2,1,0:T(8,128)(2,1)S(1)} %bitcast.11), channel_id=1, source_target_pairs={{0,4},{2,6},{4,8},{6,10},{8,12},{10,14},{12,0},{14,2},{1,5},{3,7},... | collective-permute-start | bytes 393224 | tf_op jit(solution)/shard_map/ppermute | solution.py:455
  12.0 1.9 %collective-permute-start = (bf16[16,32,128]{2,1,0:T(8,128)(2,1)S(1)}, bf16[16,32,128]{2,1,0:T(8,128)(2,1)S(1)}, u32[]{:S(2)}, u32[]{:S(2)}) collective-permute-start(bf16[16,32,128]{2,1,0:T(8,128)(2,1)S(1)} %bitcast.12), channel_id=1, source_target_pairs={{0,2},{2,4},{4,6},{6,8},{8,10},{10,12},{12,14},{14,0},{1,3},{3,5},... | collective-permute-start | bytes 393224 | tf_op jit(solution)/shard_map/ppermute | solution.py:455
  13.9 2.8 %collective-permute-start.4 = (bf16[16,32,128]{2,1,0:T(8,128)(2,1)S(1)}, bf16[16,32,128]{2,1,0:T(8,128)(2,1)S(1)}, u32[]{:S(2)}, u32[]{:S(2)}) collective-permute-start(bf16[16,32,128]{2,1,0:T(8,128)(2,1)S(1)} %collective-permute-done.2.refs_4_), channel_id=1, source_target_pairs={{0,2},{2,4},{4,6},{6,8},{8,10},{10,12},{12,14},{14,0},{1,3},{3,5},... | collective-permute-start | bytes 393224 | tf_op jit(solution)/shard_map/ppermute | solution.py:455
  16.7 3.9 %collective-permute-done.6.refs_7_ = bf16[16,32,128]{2,1,0:T(8,128)(2,1)S(1)} collective-permute-done((bf16[16,32,128]{2,1,0:T(8,128)(2,1)S(1)}, bf16[16,32,128]{2,1,0:T(8,128)(2,1)S(1)}, u32[]{:S(2)}, u32[]{:S(2)}) %collective-permute-start.6) | collective-permute-done | bytes 131104 | tf_op jit(solution)/shard_map/ppermute | solution.py:455
  20.7 1.7 %collective-permute-start.3 = (bf16[16,32,128]{2,1,0:T(8,128)(2,1)S(1)}, bf16[16,32,128]{2,1,0:T(8,128)(2,1)S(1)}, u32[]{:S(2)}, u32[]{:S(2)}) collective-permute-start(bf16[16,32,128]{2,1,0:T(8,128)(2,1)S(1)} %collective-permute-done.2.refs_4_), channel_id=1, source_target_pairs={{0,14},{2,0},{4,2},{6,4},{8,6},{10,8},{12,10},{14,12},{1,15},{3,1}... | collective-permute-start | bytes 393224 | tf_op jit(solution)/shard_map/ppermute | solution.py:455
  22.4 1.3 %codes.1 = s32[4,1,2]{2,1,0:T(1,128)} custom-call(s32[1,8]{1,0:T(1,128)} %slots_ref.3), custom_call_target="tpu_custom_call" | custom-call | tf_op jit(solution)/shard_map/codes/pallas_call | solution.py:240
  23.7 4.5 %all-to-all-start = ((s32[4,1,2]{2,1,0:T(1,128)}), s32[4,1,2]{2,1,0:T(1,128)S(1)}, u32[]{:S(2)}, u32[]{:S(2)}) async-start(s32[4,1,2]{2,1,0:T(1,128)} %codes.1), calls=%async_computation | async-start | bytes 4096 | tf_op jit(solution)/shard_map/all_to_all | solution.py:483
  29.6 3.7 %all-to-all-done.returned_ref = s32[4,1,2]{2,1,0:T(1,128)S(1)} async-done(((s32[4,1,2]{2,1,0:T(1,128)}), s32[4,1,2]{2,1,0:T(1,128)S(1)}, u32[]{:S(2)}, u32[]{:S(2)}) %all-to-all-start) | async-done | bytes 64 | tf_op jit(solution)/shard_map/all_to_all | solution.py:483
  33.8 1.4 %note.1 = s32[8,1,40]{2,1,0:T(1,128)} custom-call(s32[1,8]{1,0:T(1,128)} %send_ref.3, s32[8,1,32]{2,1,0:T(1,128)} %bitcast.17, s32[4,1,2]{2,1,0:T(1,128)} %copy-done.10), custom_call_target="tpu_custom_call" | custom-call | tf_op jit(solution)/shard_map/note/pallas_call | solution.py:263
  35.3 4.8 %all-to-all-start.1 = ((s32[8,1,40]{2,1,0:T(1,128)}), s32[8,1,40]{2,1,0:T(1,128)S(1)}, u32[]{:S(2)}, u32[]{:S(2)}) async-start(s32[8,1,40]{2,1,0:T(1,128)} %note.1), calls=%async_computation.1 | async-start | bytes 8192 | tf_op jit(solution)/shard_map/all_to_all | solution.py:486
  40.1 4.8 %slots.1.slot_ref = s32[16,11]{1,0:T(8,128)} custom-call(s32[16,11]{1,0:T(8,128)} %columns_ref.1, s32[64,4]{1,0:T(8,128)} %copy-done.7), custom_call_target="tpu_custom_call" | custom-call | flops 1000000 | bytes 2000000 | tf_op jit(solution)/shard_map/slots/pallas_call | solution.py:316
  45.0 2.1 %select.1 = (bf16[32,32,128]{2,1,0:T(8,128)(2,1)S(1)}, bf16[32,32,128]{2,1,0:T(8,128)(2,1)S(1)}, bf16[32,32,128]{2,1,0:T(8,128)(2,1)}, bf16[32,32,128]{2,1,0:T(8...) custom-call(s32[8,1,40]{2,1,0:T(1,128)S(1)} %all-to-all-done.1.note_, ...), custom_call_target="tpu_custom_call" | custom-call | tf_op jit(solution)/shard_map/select/pallas_call | solution.py:107
  47.9 1.5 %collective-permute-start.8 = (bf16[32,32,128]{2,1,0:T(8,128)(2,1)S(1)}, bf16[32,32,128]{2,1,0:T(8,128)(2,1)S(1)}, u32[]{:S(2)}, u32[]{:S(2)}) collective-permute-start(bf16[32,32,128]{2,1,0:T(8,128)(2,1)S(1)} %get-tuple-element.23), channel_id=1, source_target_pairs={{0,16},{1,17},{16,32},{17,33},{32,48},{33,49},{48,0},{49,1},{2,18}... | collective-permute-start | bytes 786440 | tf_op jit(solution)/shard_map/ppermute | solution.py:465
  49.4 0.8 collective-permute-start.9
  50.2 1.5 %collective-permute-start.10 = (bf16[32,32,128]{2,1,0:T(8,128)(2,1)}, bf16[32,32,128]{2,1,0:T(8,128)(2,1)}, u32[]{:S(2)}, u32[]{:S(2)}) collective-permute-start(bf16[32,32,128]{2,1,0:T(8,128)(2,1)} %get-tuple-element.25), channel_id=1, source_target_pairs={{0,32},{1,33},{16,48},{17,49},{32,0},{33,1},{48,16},{49,17},{2,34}... | collective-permute-start | bytes 786440 | tf_op jit(solution)/shard_map/ppermute | solution.py:465
  51.7 1.8 %collective-permute-start.11 = (bf16[32,32,128]{2,1,0:T(8,128)(2,1)}, bf16[32,32,128]{2,1,0:T(8,128)(2,1)}, u32[]{:S(2)}, u32[]{:S(2)}) collective-permute-start(bf16[32,32,128]{2,1,0:T(8,128)(2,1)} %get-tuple-element.26), channel_id=1, source_target_pairs={{0,33},{1,32},{16,49},{17,48},{32,1},{33,0},{48,17},{49,16},{2,35}... | collective-permute-start | bytes 786440 | tf_op jit(solution)/shard_map/ppermute | solution.py:465
  53.5 0.9 collective-permute-start.12
  54.4 2.7 %collective-permute-done.8.refs_2_ = bf16[32,32,128]{2,1,0:T(8,128)(2,1)S(1)} collective-permute-done((bf16[32,32,128]{2,1,0:T(8,128)(2,1)S(1)}, bf16[32,32,128]{2,1,0:T(8,128)(2,1)S(1)}, u32[]{:S(2)}, u32[]{:S(2)}) %collective-permute-start.8) | collective-permute-done | bytes 262176 | tf_op jit(solution)/shard_map/ppermute | solution.py:465
  58.3 1.4 %plane.1 = s32[8,1,64]{2,1,0:T(1,128)} custom-call(s32[8,1,40]{2,1,0:T(1,128)} %copy-done.3), custom_call_target="tpu_custom_call" | custom-call | tf_op jit(solution)/shard_map/plane/pallas_call | solution.py:280
  59.7 4.2 %all-to-all-start.2 = ((s32[8,1,64]{2,1,0:T(1,128)}), s32[8,1,64]{2,1,0:T(1,128)S(1)}, u32[]{:S(2)}, u32[]{:S(2)}) async-start(s32[8,1,64]{2,1,0:T(1,128)} %plane.1), calls=%async_computation.2 | async-start | bytes 8192 | tf_op jit(solution)/shard_map/all_to_all | solution.py:488
  63.9 3.0 %products.1.y_ref = bf16[16,64,768]{2,1,0:T(8,128)(2,1)S(1)} custom-call(bf16[16,64,64]{2,1,0:T(8,128)(2,1)S(1)} %reshape.18.p_ref, bf16[16,64,704]{2,1,0:T(8,128)(2,1)S(1)} %copy-done), custom_call_target="tpu_custom_call" | custom-call | flops 301989888 | bytes 3200000 | tf_op jit(solution)/shard_map/products/pallas_call | solution.py:68
  66.9 4.6 %all-to-all-done.2.codes_ref = s32[8,1,64]{2,1,0:T(1,128)S(1)} async-done(((s32[8,1,64]{2,1,0:T(1,128)}), s32[8,1,64]{2,1,0:T(1,128)S(1)}, u32[]{:S(2)}, u32[]{:S(2)}) %all-to-all-start.2) | async-done | bytes 2080 | tf_op jit(solution)/shard_map/all_to_all | solution.py:488
  72.0 5.5 %collective-permute-done.13.refs_7_ = bf16[32,32,128]{2,1,0:T(8,128)(2,1)} collective-permute-done((bf16[32,32,128]{2,1,0:T(8,128)(2,1)}, bf16[32,32,128]{2,1,0:T(8,128)(2,1)}, u32[]{:S(2)}, u32[]{:S(2)}) %collective-permute-start.13) | collective-permute-done | bytes 262176 | tf_op jit(solution)/shard_map/ppermute | solution.py:465
  77.5 3.2 %followers.1 = (bf16[2,64,768]{2,1,0:T(8,128)(2,1)S(1)}, bf16[2,64,768]{2,1,0:T(8,128)(2,1)S(1)}, bf16[2,64,768]{2,1,0:T(8,128)(2,1)S(1)}, bf16[2,64,768]{2,1,0:T(8,128)(2,1)S(1)}, bf16[273,32,128]{2,1,0:T(8,128)(2,1)S(1)}) custom-call(s32[16,11]{1,0:T(8,128)S(1)} %copy-done.2, s32[1,8]{1,0:T(1,128)S(1)} %copy-done.5, ...), custom_call_target="tpu_custom_call" | custom-call | flops 100663296 | bytes 5000000 | tf_op jit(solution)/shard_map/followers/pallas_call | solution.py:202
  80.7 0.8 collective-permute-start.14
  81.5 1.9 %collective-permute-start.15 = (bf16[2,64,768]{2,1,0:T(8,128)(2,1)S(1)}, bf16[2,64,768]{2,1,0:T(8,128)(2,1)S(1)}, u32[]{:S(2)}, u32[]{:S(2)}) collective-permute-start(bf16[2,64,768]{2,1,0:T(8,128)(2,1)S(1)} %get-tuple-element.34), channel_id=1, source_target_pairs={{0,128},{64,192},{128,0},{192,64},{1,129},{65,193},{129,1},{193,65... | collective-permute-start | bytes 589832 | tf_op jit(solution)/shard_map/ppermute | solution.py:455
  83.4 1.2 %collective-permute-start.16 = (bf16[2,64,768]{2,1,0:T(8,128)(2,1)S(1)}, bf16[2,64,768]{2,1,0:T(8,128)(2,1)S(1)}, u32[]{:S(2)}, u32[]{:S(2)}) collective-permute-start(bf16[2,64,768]{2,1,0:T(8,128)(2,1)S(1)} %get-tuple-element.35), channel_id=1, source_target_pairs={{0,192},{64,0},{128,64},{192,128},{1,193},{65,1},{129,65},{193,129... | collective-permute-start | bytes 589832 | tf_op jit(solution)/shard_map/ppermute | solution.py:455
  84.6 2.8 %leaders.1 = (bf16[8,64,768]{2,1,0:T(8,128)(2,1)S(1)}, s32[8,128]{1,0:T(8,128)S(1)}) custom-call(s32[16,11]{1,0:T(8,128)S(1)} %copy-done.2, s32[8,1,64]{2,1,0:T(1,128)S(1)} %all-to-all-done.2.codes_ref, bf16[16,64,768]{2,1,0:T(8,128)(2,1)S(1)} %products.1.y_ref, bf16[273,32,128]{2,1,0:T(8,128)(2,1)S(1)} %get-tuple-element.29.table), custom_call_target="tpu_custom_call" | custom-call | flops 100663296 | bytes 5000000 | tf_op jit(solution)/shard_map/leaders/pallas_call | solution.py:215
  87.4 5.7 %collective-permute-done.14.refs_1_ = bf16[2,64,768]{2,1,0:T(8,128)(2,1)S(1)} collective-permute-done((bf16[2,64,768]{2,1,0:T(8,128)(2,1)S(1)}, bf16[2,64,768]{2,1,0:T(8,128)(2,1)S(1)}, u32[]{:S(2)}, u32[]{:S(2)}) %collective-permute-start.14) | collective-permute-done | bytes 196640 | tf_op jit(solution)/shard_map/ppermute | solution.py:455
  93.8 3.9 %merge.1 = (bf16[8,64,1408]{2,1,0:T(8,128)(2,1)}, s32[8,22]{1,0:T(8,128)}) custom-call(s32[1,8]{1,0:T(1,128)S(1)} %copy-done.4, bf16[8,64,768]{2,1,0:T(8,128)(2,1)S(1)} %get-tuple-element.30.lead_ref, s32[8,128]{1,0:T(8,128)S(1)} %get-tuple-element.31.own_labels_ref, bf16[2,64,768]{2,1,0:T(8,128)(2,1)S(1)} %get-tuple-element.32.refs_0_, ...), custom_call_target="tpu_custom_call" | custom-call | tf_op jit(solution)/shard_map/merge/pallas_call | solution.py:428
  (44 shorter events, 5.5 us)
Async XLA Ops:
  0.6 57.4 %copy-start.6 = (bf16[16,4096]{1,0:T(8,128)(2,1)S(1)}, bf16[16,4096]{1,0:T(8,128)(2,1)}, u32[]{:S(2)}) copy-start(bf16[16,4096]{1,0:T(8,128)(2,1)} %param.7) | copy-start | bytes 393220
  0.6 63.2 %copy-start = (bf16[16,64,704]{2,1,0:T(8,128)(2,1)S(1)}, bf16[16,64,704]{2,1,0:T(8,128)(2,1)}, u32[]{:S(2)}) copy-start(bf16[16,64,704]{2,1,0:T(8,128)(2,1)} %a_hbm.1) | copy-start | bytes 4325380
  1.7 12.2 %collective-permute-start.2 = (bf16[16,32,128]{2,1,0:T(8,128)(2,1)S(1)}, bf16[16,32,128]{2,1,0:T(8,128)(2,1)S(1)}, u32[]{:S(2)}, u32[]{:S(2)}) collective-permute-start(bf16[16,32,128]{2,1,0:T(8,128)(2,1)S(1)} %bitcast.8), channel_id=1, source_target_pairs={{0,8},{2,10},{4,12},{6,14},{8,0},{10,2},{12,4},{14,6},{1,9},{3,11}... | collective-permute-start | bytes 393224 | tf_op jit(solution)/shard_map/ppermute | solution.py:455
  9.0 11.7 %collective-permute-start.6 = (bf16[16,32,128]{2,1,0:T(8,128)(2,1)S(1)}, bf16[16,32,128]{2,1,0:T(8,128)(2,1)S(1)}, u32[]{:S(2)}, u32[]{:S(2)}) collective-permute-start(bf16[16,32,128]{2,1,0:T(8,128)(2,1)S(1)} %bitcast.9), channel_id=1, source_target_pairs={{0,14},{2,0},{4,2},{6,4},{8,6},{10,8},{12,10},{14,12},{1,15},{3,1}... | collective-permute-start | bytes 393224 | tf_op jit(solution)/shard_map/ppermute | solution.py:455
  9.1 35.8 %collective-permute-start.5 = (bf16[16,32,128]{2,1,0:T(8,128)(2,1)S(1)}, bf16[16,32,128]{2,1,0:T(8,128)(2,1)S(1)}, u32[]{:S(2)}, u32[]{:S(2)}) collective-permute-start(bf16[16,32,128]{2,1,0:T(8,128)(2,1)S(1)} %bitcast.10), channel_id=1, source_target_pairs={{0,12},{2,14},{4,0},{6,2},{8,4},{10,6},{12,8},{14,10},{1,13},{3,15... | collective-permute-start | bytes 393224 | tf_op jit(solution)/shard_map/ppermute | solution.py:455
  9.2 35.7 %collective-permute-start.1 = (bf16[16,32,128]{2,1,0:T(8,128)(2,1)S(1)}, bf16[16,32,128]{2,1,0:T(8,128)(2,1)S(1)}, u32[]{:S(2)}, u32[]{:S(2)}) collective-permute-start(bf16[16,32,128]{2,1,0:T(8,128)(2,1)S(1)} %bitcast.11), channel_id=1, source_target_pairs={{0,4},{2,6},{4,8},{6,10},{8,12},{10,14},{12,0},{14,2},{1,5},{3,7},... | collective-permute-start | bytes 393224 | tf_op jit(solution)/shard_map/ppermute | solution.py:455
  12.0 32.9 %collective-permute-start = (bf16[16,32,128]{2,1,0:T(8,128)(2,1)S(1)}, bf16[16,32,128]{2,1,0:T(8,128)(2,1)S(1)}, u32[]{:S(2)}, u32[]{:S(2)}) collective-permute-start(bf16[16,32,128]{2,1,0:T(8,128)(2,1)S(1)} %bitcast.12), channel_id=1, source_target_pairs={{0,2},{2,4},{4,6},{6,8},{8,10},{10,12},{12,14},{14,0},{1,3},{3,5},... | collective-permute-start | bytes 393224 | tf_op jit(solution)/shard_map/ppermute | solution.py:455
  13.9 31.0 %collective-permute-start.4 = (bf16[16,32,128]{2,1,0:T(8,128)(2,1)S(1)}, bf16[16,32,128]{2,1,0:T(8,128)(2,1)S(1)}, u32[]{:S(2)}, u32[]{:S(2)}) collective-permute-start(bf16[16,32,128]{2,1,0:T(8,128)(2,1)S(1)} %collective-permute-done.2.refs_4_), channel_id=1, source_target_pairs={{0,2},{2,4},{4,6},{6,8},{8,10},{10,12},{12,14},{14,0},{1,3},{3,5},... | collective-permute-start | bytes 393224 | tf_op jit(solution)/shard_map/ppermute | solution.py:455
  20.7 24.3 %collective-permute-start.3 = (bf16[16,32,128]{2,1,0:T(8,128)(2,1)S(1)}, bf16[16,32,128]{2,1,0:T(8,128)(2,1)S(1)}, u32[]{:S(2)}, u32[]{:S(2)}) collective-permute-start(bf16[16,32,128]{2,1,0:T(8,128)(2,1)S(1)} %collective-permute-done.2.refs_4_), channel_id=1, source_target_pairs={{0,14},{2,0},{4,2},{6,4},{8,6},{10,8},{12,10},{14,12},{1,15},{3,1}... | collective-permute-start | bytes 393224 | tf_op jit(solution)/shard_map/ppermute | solution.py:455
  23.7 9.6 %all-to-all-start = ((s32[4,1,2]{2,1,0:T(1,128)}), s32[4,1,2]{2,1,0:T(1,128)S(1)}, u32[]{:S(2)}, u32[]{:S(2)}) async-start(s32[4,1,2]{2,1,0:T(1,128)} %codes.1), calls=%async_computation | async-start | bytes 4096 | tf_op jit(solution)/shard_map/all_to_all | solution.py:483
  28.9 11.2 %copy-start.7 = (s32[64,4]{1,0:T(8,128)}, s32[64,4]{1,0:T(8,128)S(1)}, u32[]{:S(2)}) copy-start(s32[64,4]{1,0:T(8,128)S(1)} %copy.10.fetch_ref) | copy-start | bytes 3076
  33.2 0.6 copy-start.10
  35.3 9.6 %all-to-all-start.1 = ((s32[8,1,40]{2,1,0:T(1,128)}), s32[8,1,40]{2,1,0:T(1,128)S(1)}, u32[]{:S(2)}, u32[]{:S(2)}) async-start(s32[8,1,40]{2,1,0:T(1,128)} %note.1), calls=%async_computation.1 | async-start | bytes 8192 | tf_op jit(solution)/shard_map/all_to_all | solution.py:486
  44.9 13.4 %copy-start.3 = (s32[8,1,40]{2,1,0:T(1,128)}, s32[8,1,40]{2,1,0:T(1,128)S(1)}, u32[]{:S(2)}) copy-start(s32[8,1,40]{2,1,0:T(1,128)S(1)} %all-to-all-done.1.note_ref.wanted_ref) | copy-start | bytes 3844
  47.0 0.7 copy-start.1
  47.7 5.8 %collective-permute-start.7 = (bf16[32,32,128]{2,1,0:T(8,128)(2,1)S(1)}, bf16[32,32,128]{2,1,0:T(8,128)(2,1)S(1)}, u32[]{:S(2)}, u32[]{:S(2)}) collective-permute-start(bf16[32,32,128]{2,1,0:T(8,128)(2,1)S(1)} %get-tuple-element.22), channel_id=1, source_target_pairs={{0,1},{1,0},{16,17},{17,16},{32,33},{33,32},{48,49},{49,48},{2,3},... | collective-permute-start | bytes 786440 | tf_op jit(solution)/shard_map/ppermute | solution.py:465
  47.9 9.1 %collective-permute-start.8 = (bf16[32,32,128]{2,1,0:T(8,128)(2,1)S(1)}, bf16[32,32,128]{2,1,0:T(8,128)(2,1)S(1)}, u32[]{:S(2)}, u32[]{:S(2)}) collective-permute-start(bf16[32,32,128]{2,1,0:T(8,128)(2,1)S(1)} %get-tuple-element.23), channel_id=1, source_target_pairs={{0,16},{1,17},{16,32},{17,33},{32,48},{33,49},{48,0},{49,1},{2,18}... | collective-permute-start | bytes 786440 | tf_op jit(solution)/shard_map/ppermute | solution.py:465
  49.4 22.2 %collective-permute-start.9 = (bf16[32,32,128]{2,1,0:T(8,128)(2,1)}, bf16[32,32,128]{2,1,0:T(8,128)(2,1)}, u32[]{:S(2)}, u32[]{:S(2)}) collective-permute-start(bf16[32,32,128]{2,1,0:T(8,128)(2,1)} %get-tuple-element.24), channel_id=1, source_target_pairs={{0,17},{1,16},{16,33},{17,32},{32,49},{33,48},{48,1},{49,0},{2,19}... | collective-permute-start | bytes 786440 | tf_op jit(solution)/shard_map/ppermute | solution.py:465
  50.2 21.3 %collective-permute-start.10 = (bf16[32,32,128]{2,1,0:T(8,128)(2,1)}, bf16[32,32,128]{2,1,0:T(8,128)(2,1)}, u32[]{:S(2)}, u32[]{:S(2)}) collective-permute-start(bf16[32,32,128]{2,1,0:T(8,128)(2,1)} %get-tuple-element.25), channel_id=1, source_target_pairs={{0,32},{1,33},{16,48},{17,49},{32,0},{33,1},{48,16},{49,17},{2,34}... | collective-permute-start | bytes 786440 | tf_op jit(solution)/shard_map/ppermute | solution.py:465
  51.7 19.9 %collective-permute-start.11 = (bf16[32,32,128]{2,1,0:T(8,128)(2,1)}, bf16[32,32,128]{2,1,0:T(8,128)(2,1)}, u32[]{:S(2)}, u32[]{:S(2)}) collective-permute-start(bf16[32,32,128]{2,1,0:T(8,128)(2,1)} %get-tuple-element.26), channel_id=1, source_target_pairs={{0,33},{1,32},{16,49},{17,48},{32,1},{33,0},{48,17},{49,16},{2,35}... | collective-permute-start | bytes 786440 | tf_op jit(solution)/shard_map/ppermute | solution.py:465
  53.5 3.5 %copy-start.8 = (bf16[32,32,128]{2,1,0:T(8,128)(2,1)}, bf16[32,32,128]{2,1,0:T(8,128)(2,1)S(1)}, u32[]{:S(2)}) copy-start(bf16[32,32,128]{2,1,0:T(8,128)(2,1)S(1)} %collective-permute-done.7.refs_1_) | copy-start | bytes 786436
  53.5 18.5 %collective-permute-start.12 = (bf16[32,32,128]{2,1,0:T(8,128)(2,1)}, bf16[32,32,128]{2,1,0:T(8,128)(2,1)}, u32[]{:S(2)}, u32[]{:S(2)}) collective-permute-start(bf16[32,32,128]{2,1,0:T(8,128)(2,1)} %get-tuple-element.27), channel_id=1, source_target_pairs={{0,48},{1,49},{16,0},{17,1},{32,16},{33,17},{48,32},{49,33},{2,50}... | collective-permute-start | bytes 786440 | tf_op jit(solution)/shard_map/ppermute | solution.py:465
  57.0 0.7 copy-start.9
  57.7 19.8 %collective-permute-start.13 = (bf16[32,32,128]{2,1,0:T(8,128)(2,1)}, bf16[32,32,128]{2,1,0:T(8,128)(2,1)}, u32[]{:S(2)}, u32[]{:S(2)}) collective-permute-start(bf16[32,32,128]{2,1,0:T(8,128)(2,1)} %get-tuple-element.28), channel_id=1, source_target_pairs={{0,49},{1,48},{16,1},{17,0},{32,17},{33,16},{48,33},{49,32},{2,51}... | collective-permute-start | bytes 786440 | tf_op jit(solution)/shard_map/ppermute | solution.py:465
  59.7 11.9 %all-to-all-start.2 = ((s32[8,1,64]{2,1,0:T(1,128)}), s32[8,1,64]{2,1,0:T(1,128)S(1)}, u32[]{:S(2)}, u32[]{:S(2)}) async-start(s32[8,1,64]{2,1,0:T(1,128)} %plane.1), calls=%async_computation.2 | async-start | bytes 8192 | tf_op jit(solution)/shard_map/all_to_all | solution.py:488
  63.8 13.6 %copy-start.2 = (s32[16,11]{1,0:T(8,128)S(1)}, s32[16,11]{1,0:T(8,128)}, u32[]{:S(2)}) copy-start(s32[16,11]{1,0:T(8,128)} %slots.1.slot_ref) | copy-start | bytes 2116
  63.9 13.6 %copy-start.5 = (s32[1,8]{1,0:T(1,128)S(1)}, s32[1,8]{1,0:T(1,128)}, u32[]{:S(2)}) copy-start(s32[1,8]{1,0:T(1,128)} %send_ref.3) | copy-start | bytes 100
  80.7 12.4 %collective-permute-start.14 = (bf16[2,64,768]{2,1,0:T(8,128)(2,1)S(1)}, bf16[2,64,768]{2,1,0:T(8,128)(2,1)S(1)}, u32[]{:S(2)}, u32[]{:S(2)}) collective-permute-start(bf16[2,64,768]{2,1,0:T(8,128)(2,1)S(1)} %get-tuple-element.33), channel_id=1, source_target_pairs={{0,64},{64,128},{128,192},{192,0},{1,65},{65,129},{129,193},{193,1... | collective-permute-start | bytes 589832 | tf_op jit(solution)/shard_map/ppermute | solution.py:455
  81.5 11.6 %collective-permute-start.15 = (bf16[2,64,768]{2,1,0:T(8,128)(2,1)S(1)}, bf16[2,64,768]{2,1,0:T(8,128)(2,1)S(1)}, u32[]{:S(2)}, u32[]{:S(2)}) collective-permute-start(bf16[2,64,768]{2,1,0:T(8,128)(2,1)S(1)} %get-tuple-element.34), channel_id=1, source_target_pairs={{0,128},{64,192},{128,0},{192,64},{1,129},{65,193},{129,1},{193,65... | collective-permute-start | bytes 589832 | tf_op jit(solution)/shard_map/ppermute | solution.py:455
  83.4 10.3 %collective-permute-start.16 = (bf16[2,64,768]{2,1,0:T(8,128)(2,1)S(1)}, bf16[2,64,768]{2,1,0:T(8,128)(2,1)S(1)}, u32[]{:S(2)}, u32[]{:S(2)}) collective-permute-start(bf16[2,64,768]{2,1,0:T(8,128)(2,1)S(1)} %get-tuple-element.35), channel_id=1, source_target_pairs={{0,192},{64,0},{128,64},{192,128},{1,193},{65,1},{129,65},{193,129... | collective-permute-start | bytes 589832 | tf_op jit(solution)/shard_map/ppermute | solution.py:455
  84.6 9.2 %copy-start.4 = (s32[1,8]{1,0:T(1,128)S(1)}, s32[1,8]{1,0:T(1,128)}, u32[]{:S(2)}) copy-start(s32[1,8]{1,0:T(1,128)} %slots_ref.3) | copy-start | bytes 100

commit v6 on v5

--- a/solution.py
+++ b/solution.py
@@ -20,7 +20,7 @@
 CHUNKS = 1
 CK = 32 // CHUNKS
 AXES = ("grp", "x", "z", "core")
-ORDER = (1, 2, 4, 5, 6, 3, 7, 0)
+ORDER = (1, 2, 6, 4, 5, 3, 7, 0)
 
 VMEM = pl.BlockSpec(memory_space=pltpu.VMEM)
 SMEM = pl.BlockSpec(memory_space=pltpu.SMEM)
@@ -35,18 +35,14 @@
 STEP = 4
 
 
-def products_kernel(p_ref, a_hbm, y_ref, a_ref, work, sems):
+def products_kernel(p_ref, perm_ref, a_hbm, y_ref, a_ref, work, sems):
     def load(h):
         rows = pl.ds(h * STEP, STEP)
         return pltpu.make_async_copy(a_hbm.at[rows], a_ref.at[rows], sems.at[h])
 
     for h in range(ROWS // STEP):
         load(h).start()
-    row = lax.broadcasted_iota(jnp.int32, (LANES, LANES), 0)
-    lane = lax.broadcasted_iota(jnp.int32, (LANES, LANES), 1)
-    inner = lane & (BLK - 1)
-    source = (lane & BLK) + jnp.where(inner < 32, 2 * inner, 2 * (inner - 32) + 1)
-    perm = jnp.where(row == source, 1.0, 0.0).astype(jnp.bfloat16)
+    perm = perm_ref[...]
     pad = jnp.zeros((BLK, BLK), jnp.float32)
     for h in range(ROWS // STEP):
         load(h).wait()
@@ -64,11 +60,11 @@
             ).astype(jnp.bfloat16).reshape(STEP, BLK, LANES)
 
 
-def products(blocks, stiffness):
+def products(blocks, perm, stiffness):
     return pl.pallas_call(
         products_kernel,
         out_shape=jax.ShapeDtypeStruct((ROWS, BLK, WIDE), jnp.bfloat16),
-        in_specs=[VMEM, HBM],
+        in_specs=[VMEM, VMEM, HBM],
         out_specs=VMEM,
         scratch_shapes=[
             pltpu.VMEM((ROWS, BLK, K * BLK), jnp.bfloat16),
@@ -80,7 +76,7 @@
             flops=2 * ROWS * BLK * BLK * WIDE * 3, bytes_accessed=3_200_000, transcendentals=0
         ),
         name="products",
-    )(blocks, stiffness)
+    )(blocks, perm, stiffness)
 
 
 def select_kernel(wanted_ref, *refs):
@@ -484,9 +480,14 @@
     lists = fetch_rows.reshape(NX, NZ, NC, C).transpose(0, 2, 1, 3).reshape(NX * NC, 1, NZ * C)
     note = note_rows(send_order, lists, returned)
     wanted = lax.all_to_all(note, ("x", "core"), split_axis=0, concat_axis=0, tiled=True)
-    wanted, words = lax.optimization_barrier((wanted, slot_words(columns, fetch_rows)))
+    words = slot_words(columns, fetch_rows)
+    lane = jnp.arange(LANES, dtype=jnp.int32)
+    inner = lane & (BLK - 1)
+    source = (lane & BLK) + jnp.where(inner < 32, 2 * inner, 2 * (inner - 32) + 1)
+    perm = (lane[:, None] == source[None, :]).astype(jnp.bfloat16)
+    y = products(prolongator.reshape(ROWS, BLK, BLK), perm, stiffness)
+    wanted, y = lax.optimization_barrier((wanted, y))
     codes = lax.all_to_all(plane_rows(wanted), "z", split_axis=0, concat_axis=0, tiled=True)
-    y = products(prolongator.reshape(ROWS, BLK, BLK), stiffness)
 
     parts = []
     for h in range(CHUNKS):

time: 99.1 us -> 92.1 us (0.929)
  waiting for transfers between devices: 27.2 us -> 17.1 us
  local copies, waits for them, and re-layouts: 4.72 us -> 6.96 us
  starting transfers between devices: 41.1 us -> 42.4 us
    ppermute x10, waiting for transfers between devices: 10.3 us -> 4.83 us  [shift(): lax.ppermute(value, axis, [(i, (i + by) % size) for i in range(size)])]
    all_to_all x1, waiting for transfers between devices: 3.65 us -> 0.01 us  [per_device(): lax.all_to_all(code_rows(partner_slot), 'grp', split_axis=0, concat_axis=...]
    all_to_all x1, waiting for transfers between devices: 4.65 us -> 2.87 us  [per_device(): lax.all_to_all(plane_rows(wanted), 'z', split_axis=0, concat_axis=0, tile...]
    unnamed x24, local copies, waits for them, and re-layouts: 3.81 us -> 5.1 us
    ppermute x10, starting transfers between devices: 20.6 us -> 21.8 us  [shift(): lax.ppermute(value, axis, [(i, (i + by) % size) for i in range(size)])]
  transfers between devices with their start and end apart: 20 -> 20, of which waited for: 8 -> 5; matrix products, arithmetic and copies ran while one was open for 2% -> 3% of each run, Pallas kernels for 15% -> 16%
where the time goes in v6:
time: 92.1 us; the launch traced here: 90.8 us
  starting transfers between devices  42.4 us (46%)
  Pallas kernels  23.4 us (25%)
  waiting for transfers between devices  17.1 us (19%)
  local copies, waits for them, and re-layouts  6.96 us (8%)
  between operations  0.98 us (1%)
    ppermute x10, starting transfers between devices, shift(): lax.ppermute(value, axis, [(i, (i + by) % size) for i in range(size)])  21.8 us
    ppermute x7, waiting for transfers between devices, cross(): return lax.ppermute(value, ('x', 'core'), pairs)  9.39 us
    ppermute x7, starting transfers between devices, cross(): return lax.ppermute(value, ('x', 'core'), pairs)  7.36 us
    unnamed x24, local copies, waits for them, and re-layouts  5.1 us
    ppermute x10, waiting for transfers between devices, shift(): lax.ppermute(value, axis, [(i, (i + by) % size) for i in range(size)])  4.83 us
    all_to_all x1, starting transfers between devices, per_device(): lax.all_to_all(note, ('x', 'core'), split_axis=0, concat_axis=0, tiled=True)  4.83 us
    pallas_call x1, Pallas kernels, slot_words(): pl.pallas_call(slot_kernel, out_shape=jax.ShapeDtypeStruct((ROWS, K), jnp...  4.8 us
    all_to_all x1, starting transfers between devices, per_device(): lax.all_to_all(code_rows(partner_slot), 'grp', split_axis=0, concat_axis=...  4.46 us
  transfers between devices with their start and end apart: 20, of which 5 were waited for; matrix products, arithmetic and copies ran while one was open for 3% of the time, Pallas kernels for 16%

profile of v6, /device:TPU:2, one launch (start us, length us, event | category | flops | bytes accessed | tf_op | source)
XLA Modules:
  0.0 90.8 jit_solution(7506077498727070472)
XLA Ops:
  0.6 0.9 %copy.14 = bf16[2,8,32,128]{3,2,1,0:T(8,128)(2,1)S(1)} copy(bf16[2,8,32,128]{3,1,2,0:T(8,128)(2,1)} %bitcast.15) | data formatting | bytes 262144
  1.6 7.3 %collective-permute-start.2 = (bf16[16,32,128]{2,1,0:T(8,128)(2,1)S(1)}, bf16[16,32,128]{2,1,0:T(8,128)(2,1)S(1)}, u32[]{:S(2)}, u32[]{:S(2)}) collective-permute-start(bf16[16,32,128]{2,1,0:T(8,128)(2,1)S(1)} %bitcast.8), channel_id=1, source_target_pairs={{0,8},{2,10},{4,12},{6,14},{8,0},{10,2},{12,4},{14,6},{1,9},{3,11}... | collective-permute-start | bytes 393224 | tf_op jit(solution)/shard_map/ppermute | solution.py:451
  9.0 2.8 %collective-permute-start.1 = (bf16[16,32,128]{2,1,0:T(8,128)(2,1)S(1)}, bf16[16,32,128]{2,1,0:T(8,128)(2,1)S(1)}, u32[]{:S(2)}, u32[]{:S(2)}) collective-permute-start(bf16[16,32,128]{2,1,0:T(8,128)(2,1)S(1)} %bitcast.11), channel_id=1, source_target_pairs={{0,4},{2,6},{4,8},{6,10},{8,12},{10,14},{12,0},{14,2},{1,5},{3,7},... | collective-permute-start | bytes 393224 | tf_op jit(solution)/shard_map/ppermute | solution.py:451
  11.9 1.9 %collective-permute-start = (bf16[16,32,128]{2,1,0:T(8,128)(2,1)S(1)}, bf16[16,32,128]{2,1,0:T(8,128)(2,1)S(1)}, u32[]{:S(2)}, u32[]{:S(2)}) collective-permute-start(bf16[16,32,128]{2,1,0:T(8,128)(2,1)S(1)} %bitcast.12), channel_id=1, source_target_pairs={{0,2},{2,4},{4,6},{6,8},{8,10},{10,12},{12,14},{14,0},{1,3},{3,5},... | collective-permute-start | bytes 393224 | tf_op jit(solution)/shard_map/ppermute | solution.py:451
  13.8 1.3 %codes.1 = s32[4,1,2]{2,1,0:T(1,128)} custom-call(s32[1,8]{1,0:T(1,128)} %slots_ref.3), custom_call_target="tpu_custom_call" | custom-call | tf_op jit(solution)/shard_map/codes/pallas_call | solution.py:236
  15.0 4.5 %all-to-all-start = ((s32[4,1,2]{2,1,0:T(1,128)}), s32[4,1,2]{2,1,0:T(1,128)S(1)}, u32[]{:S(2)}, u32[]{:S(2)}) async-start(s32[4,1,2]{2,1,0:T(1,128)} %codes.1), calls=%async_computation | async-start | bytes 4096 | tf_op jit(solution)/shard_map/all_to_all | solution.py:479
  19.5 2.3 %collective-permute-start.4 = (bf16[16,32,128]{2,1,0:T(8,128)(2,1)S(1)}, bf16[16,32,128]{2,1,0:T(8,128)(2,1)S(1)}, u32[]{:S(2)}, u32[]{:S(2)}) collective-permute-start(bf16[16,32,128]{2,1,0:T(8,128)(2,1)S(1)} %collective-permute-done.2.refs_4_), channel_id=1, source_target_pairs={{0,2},{2,4},{4,6},{6,8},{8,10},{10,12},{12,14},{14,0},{1,3},{3,5},... | collective-permute-start | bytes 393224 | tf_op jit(solution)/shard_map/ppermute | solution.py:451
  21.8 1.0 %collective-permute-start.3 = (bf16[16,32,128]{2,1,0:T(8,128)(2,1)S(1)}, bf16[16,32,128]{2,1,0:T(8,128)(2,1)S(1)}, u32[]{:S(2)}, u32[]{:S(2)}) collective-permute-start(bf16[16,32,128]{2,1,0:T(8,128)(2,1)S(1)} %collective-permute-done.2.refs_4_), channel_id=1, source_target_pairs={{0,14},{2,0},{4,2},{6,4},{8,6},{10,8},{12,10},{14,12},{1,15},{3,1}... | collective-permute-start | bytes 393224 | tf_op jit(solution)/shard_map/ppermute | solution.py:451
  22.9 1.2 %reshape.31.p_ref = bf16[16,64,64]{2,1,0:T(8,128)(2,1)S(1)} reshape(bf16[16,4096]{1,0:T(8,128)(2,1)} %param.7) | data formatting | bytes 262144 | tf_op jit(solution)/shard_map/reshape | solution.py:488
  26.1 1.4 %note.1 = s32[8,1,40]{2,1,0:T(1,128)} custom-call(s32[1,8]{1,0:T(1,128)} %send_ref.3, s32[8,1,32]{2,1,0:T(1,128)} %bitcast.17, s32[4,1,2]{2,1,0:T(1,128)} %copy-done.10), custom_call_target="tpu_custom_call" | custom-call | tf_op jit(solution)/shard_map/note/pallas_call | solution.py:259
  27.5 4.8 %all-to-all-start.1 = ((s32[8,1,40]{2,1,0:T(1,128)}), s32[8,1,40]{2,1,0:T(1,128)S(1)}, u32[]{:S(2)}, u32[]{:S(2)}) async-start(s32[8,1,40]{2,1,0:T(1,128)} %note.1), calls=%async_computation.1 | async-start | bytes 8192 | tf_op jit(solution)/shard_map/all_to_all | solution.py:482
  32.4 1.4 %copy-done = bf16[16,64,704]{2,1,0:T(8,128)(2,1)S(1)} copy-done((bf16[16,64,704]{2,1,0:T(8,128)(2,1)S(1)}, bf16[16,64,704]{2,1,0:T(8,128)(2,1)}, u32[]{:S(2)}) %copy-start) | copy-done | bytes 1441816
  33.8 3.0 %products.1.y_ref = bf16[16,64,768]{2,1,0:T(8,128)(2,1)S(1)} custom-call(bf16[16,64,64]{2,1,0:T(8,128)(2,1)S(1)} %reshape.31.p_ref, bf16[128,128]{1,0:T(8,128)(2,1)S(1)} %fusion.perm_ref, bf16[16,64,704]{2,1,0:T(8,128)(2,1)S(1)} %copy-done), custom_call_target="tpu_custom_call" | custom-call | flops 301989888 | bytes 3200000 | tf_op jit(solution)/shard_map/products/pallas_call | solution.py:64
  36.8 2.0 %select.1 = (bf16[32,32,128]{2,1,0:T(8,128)(2,1)S(1)}, bf16[32,32,128]{2,1,0:T(8,128)(2,1)S(1)}, bf16[32,32,128]{2,1,0:T(8,128)(2,1)S(1)}, bf16[32,32,128]{2,1,0...) custom-call(s32[8,1,40]{2,1,0:T(1,128)S(1)} %all-to-all-done.1.note_, ...), custom_call_target="tpu_custom_call" | custom-call | tf_op jit(solution)/shard_map/select/pallas_call | solution.py:103
  39.7 1.5 %collective-permute-start.8 = (bf16[32,32,128]{2,1,0:T(8,128)(2,1)S(1)}, bf16[32,32,128]{2,1,0:T(8,128)(2,1)S(1)}, u32[]{:S(2)}, u32[]{:S(2)}) collective-permute-start(bf16[32,32,128]{2,1,0:T(8,128)(2,1)S(1)} %get-tuple-element.23), channel_id=1, source_target_pairs={{0,16},{1,17},{16,32},{17,33},{32,48},{33,49},{48,0},{49,1},{2,18}... | collective-permute-start | bytes 786440 | tf_op jit(solution)/shard_map/ppermute | solution.py:461
  41.1 0.9 collective-permute-start.9
  42.0 1.5 %collective-permute-start.10 = (bf16[32,32,128]{2,1,0:T(8,128)(2,1)}, bf16[32,32,128]{2,1,0:T(8,128)(2,1)}, u32[]{:S(2)}, u32[]{:S(2)}) collective-permute-start(bf16[32,32,128]{2,1,0:T(8,128)(2,1)} %get-tuple-element.25), channel_id=1, source_target_pairs={{0,32},{1,33},{16,48},{17,49},{32,0},{33,1},{48,16},{49,17},{2,34}... | collective-permute-start | bytes 786440 | tf_op jit(solution)/shard_map/ppermute | solution.py:461
  43.4 1.8 %collective-permute-start.11 = (bf16[32,32,128]{2,1,0:T(8,128)(2,1)S(1)}, bf16[32,32,128]{2,1,0:T(8,128)(2,1)}, u32[]{:S(2)}, u32[]{:S(2)}) collective-permute-start(bf16[32,32,128]{2,1,0:T(8,128)(2,1)S(1)} %get-tuple-element.26), channel_id=1, source_target_pairs={{0,33},{1,32},{16,49},{17,48},{32,1},{33,0},{48,17},{49,16},{2,35}... | collective-permute-start | bytes 786440 | tf_op jit(solution)/shard_map/ppermute | solution.py:461
  46.1 2.7 %collective-permute-done.8.refs_2_ = bf16[32,32,128]{2,1,0:T(8,128)(2,1)S(1)} collective-permute-done((bf16[32,32,128]{2,1,0:T(8,128)(2,1)S(1)}, bf16[32,32,128]{2,1,0:T(8,128)(2,1)S(1)}, u32[]{:S(2)}, u32[]{:S(2)}) %collective-permute-start.8) | collective-permute-done | bytes 262176 | tf_op jit(solution)/shard_map/ppermute | solution.py:461
  49.5 1.4 %plane.1 = s32[8,1,64]{2,1,0:T(1,128)} custom-call(s32[8,1,40]{2,1,0:T(1,128)} %copy-done.3), custom_call_target="tpu_custom_call" | custom-call | tf_op jit(solution)/shard_map/plane/pallas_call | solution.py:276
  50.9 3.9 %all-to-all-start.2 = ((s32[8,1,64]{2,1,0:T(1,128)}), s32[8,1,64]{2,1,0:T(1,128)S(1)}, u32[]{:S(2)}, u32[]{:S(2)}) async-start(s32[8,1,64]{2,1,0:T(1,128)} %plane.1), calls=%async_computation.2 | async-start | bytes 8192 | tf_op jit(solution)/shard_map/all_to_all | solution.py:490
  54.8 4.8 %slots.1.slot_ref = s32[16,11]{1,0:T(8,128)} custom-call(s32[16,11]{1,0:T(8,128)} %columns_ref.1, s32[64,4]{1,0:T(8,128)} %copy-done.6), custom_call_target="tpu_custom_call" | custom-call | flops 1000000 | bytes 2000000 | tf_op jit(solution)/shard_map/slots/pallas_call | solution.py:312
  59.7 2.9 %all-to-all-done.2.codes_ref = s32[8,1,64]{2,1,0:T(1,128)S(1)} async-done(((s32[8,1,64]{2,1,0:T(1,128)}), s32[8,1,64]{2,1,0:T(1,128)S(1)}, u32[]{:S(2)}, u32[]{:S(2)}) %all-to-all-start.2) | async-done | bytes 2080 | tf_op jit(solution)/shard_map/all_to_all | solution.py:490
  62.5 1.2 %collective-permute-done.12.refs_6_ = bf16[32,32,128]{2,1,0:T(8,128)(2,1)} collective-permute-done((bf16[32,32,128]{2,1,0:T(8,128)(2,1)S(1)}, bf16[32,32,128]{2,1,0:T(8,128)(2,1)}, u32[]{:S(2)}, u32[]{:S(2)}) %collective-permute-start.12) | collective-permute-done | bytes 262176 | tf_op jit(solution)/shard_map/ppermute | solution.py:461
  63.8 5.5 %collective-permute-done.13.refs_7_ = bf16[32,32,128]{2,1,0:T(8,128)(2,1)} collective-permute-done((bf16[32,32,128]{2,1,0:T(8,128)(2,1)S(1)}, bf16[32,32,128]{2,1,0:T(8,128)(2,1)}, u32[]{:S(2)}, u32[]{:S(2)}) %collective-permute-start.13) | collective-permute-done | bytes 262176 | tf_op jit(solution)/shard_map/ppermute | solution.py:461
  70.0 3.2 %followers.1 = (bf16[2,64,768]{2,1,0:T(8,128)(2,1)S(1)}, bf16[2,64,768]{2,1,0:T(8,128)(2,1)S(1)}, bf16[2,64,768]{2,1,0:T(8,128)(2,1)S(1)}, bf16[2,64,768]{2,1,0:T(8,128)(2,1)S(1)}, bf16[273,32,128]{2,1,0:T(8,128)(2,1)S(1)}) custom-call(s32[16,11]{1,0:T(8,128)S(1)} %copy-done.2, s32[1,8]{1,0:T(1,128)S(1)} %copy-done.5, ...), custom_call_target="tpu_custom_call" | custom-call | flops 100663296 | bytes 5000000 | tf_op jit(solution)/shard_map/followers/pallas_call | solution.py:198
  73.2 2.1 %collective-permute-start.14 = (bf16[2,64,768]{2,1,0:T(8,128)(2,1)S(1)}, bf16[2,64,768]{2,1,0:T(8,128)(2,1)S(1)}, u32[]{:S(2)}, u32[]{:S(2)}) collective-permute-start(bf16[2,64,768]{2,1,0:T(8,128)(2,1)S(1)} %get-tuple-element.33), channel_id=1, source_target_pairs={{0,64},{64,128},{128,192},{192,0},{1,65},{65,129},{129,193},{193,1... | collective-permute-start | bytes 589832 | tf_op jit(solution)/shard_map/ppermute | solution.py:451
  75.3 2.7 %collective-permute-start.15 = (bf16[2,64,768]{2,1,0:T(8,128)(2,1)S(1)}, bf16[2,64,768]{2,1,0:T(8,128)(2,1)S(1)}, u32[]{:S(2)}, u32[]{:S(2)}) collective-permute-start(bf16[2,64,768]{2,1,0:T(8,128)(2,1)S(1)} %get-tuple-element.34), channel_id=1, source_target_pairs={{0,128},{64,192},{128,0},{192,64},{1,129},{65,193},{129,1},{193,65... | collective-permute-start | bytes 589832 | tf_op jit(solution)/shard_map/ppermute | solution.py:451
  78.0 1.5 %collective-permute-start.16 = (bf16[2,64,768]{2,1,0:T(8,128)(2,1)S(1)}, bf16[2,64,768]{2,1,0:T(8,128)(2,1)S(1)}, u32[]{:S(2)}, u32[]{:S(2)}) collective-permute-start(bf16[2,64,768]{2,1,0:T(8,128)(2,1)S(1)} %get-tuple-element.35), channel_id=1, source_target_pairs={{0,192},{64,0},{128,64},{192,128},{1,193},{65,1},{129,65},{193,129... | collective-permute-start | bytes 589832 | tf_op jit(solution)/shard_map/ppermute | solution.py:451
  79.4 2.8 %leaders.1 = (bf16[8,64,768]{2,1,0:T(8,128)(2,1)S(1)}, s32[8,128]{1,0:T(8,128)S(1)}) custom-call(s32[16,11]{1,0:T(8,128)S(1)} %copy-done.2, s32[8,1,64]{2,1,0:T(1,128)S(1)} %all-to-all-done.2.codes_ref, bf16[16,64,768]{2,1,0:T(8,128)(2,1)S(1)} %products.1.y_ref, bf16[273,32,128]{2,1,0:T(8,128)(2,1)S(1)} %get-tuple-element.29.table), custom_call_target="tpu_custom_call" | custom-call | flops 100663296 | bytes 5000000 | tf_op jit(solution)/shard_map/leaders/pallas_call | solution.py:211
  82.3 4.8 %collective-permute-done.15.refs_2_ = bf16[2,64,768]{2,1,0:T(8,128)(2,1)S(1)} collective-permute-done((bf16[2,64,768]{2,1,0:T(8,128)(2,1)S(1)}, bf16[2,64,768]{2,1,0:T(8,128)(2,1)S(1)}, u32[]{:S(2)}, u32[]{:S(2)}) %collective-permute-start.15) | collective-permute-done | bytes 196640 | tf_op jit(solution)/shard_map/ppermute | solution.py:451
  87.1 3.5 %merge.1 = (bf16[8,64,1408]{2,1,0:T(8,128)(2,1)}, s32[8,22]{1,0:T(8,128)}) custom-call(s32[1,8]{1,0:T(1,128)S(1)} %copy-done.4, bf16[8,64,768]{2,1,0:T(8,128)(2,1)S(1)} %get-tuple-element.30.lead_ref, s32[8,128]{1,0:T(8,128)S(1)} %get-tuple-element.31.own_labels_ref, bf16[2,64,768]{2,1,0:T(8,128)(2,1)S(1)} %get-tuple-element.32.refs_0_, ...), custom_call_target="tpu_custom_call" | custom-call | tf_op jit(solution)/shard_map/merge/pallas_call | solution.py:424
  (46 shorter events, 5.5 us)
Async XLA Ops:
  1.6 18.0 %collective-permute-start.2 = (bf16[16,32,128]{2,1,0:T(8,128)(2,1)S(1)}, bf16[16,32,128]{2,1,0:T(8,128)(2,1)S(1)}, u32[]{:S(2)}, u32[]{:S(2)}) collective-permute-start(bf16[16,32,128]{2,1,0:T(8,128)(2,1)S(1)} %bitcast.8), channel_id=1, source_target_pairs={{0,8},{2,10},{4,12},{6,14},{8,0},{10,2},{12,4},{14,6},{1,9},{3,11}... | collective-permute-start | bytes 393224 | tf_op jit(solution)/shard_map/ppermute | solution.py:451
  8.8 13.0 %collective-permute-start.6 = (bf16[16,32,128]{2,1,0:T(8,128)(2,1)S(1)}, bf16[16,32,128]{2,1,0:T(8,128)(2,1)S(1)}, u32[]{:S(2)}, u32[]{:S(2)}) collective-permute-start(bf16[16,32,128]{2,1,0:T(8,128)(2,1)S(1)} %bitcast.9), channel_id=1, source_target_pairs={{0,14},{2,0},{4,2},{6,4},{8,6},{10,8},{12,10},{14,12},{1,15},{3,1}... | collective-permute-start | bytes 393224 | tf_op jit(solution)/shard_map/ppermute | solution.py:451
  8.9 27.8 %collective-permute-start.5 = (bf16[16,32,128]{2,1,0:T(8,128)(2,1)S(1)}, bf16[16,32,128]{2,1,0:T(8,128)(2,1)S(1)}, u32[]{:S(2)}, u32[]{:S(2)}) collective-permute-start(bf16[16,32,128]{2,1,0:T(8,128)(2,1)S(1)} %bitcast.10), channel_id=1, source_target_pairs={{0,12},{2,14},{4,0},{6,2},{8,4},{10,6},{12,8},{14,10},{1,13},{3,15... | collective-permute-start | bytes 393224 | tf_op jit(solution)/shard_map/ppermute | solution.py:451
  9.0 27.8 %collective-permute-start.1 = (bf16[16,32,128]{2,1,0:T(8,128)(2,1)S(1)}, bf16[16,32,128]{2,1,0:T(8,128)(2,1)S(1)}, u32[]{:S(2)}, u32[]{:S(2)}) collective-permute-start(bf16[16,32,128]{2,1,0:T(8,128)(2,1)S(1)} %bitcast.11), channel_id=1, source_target_pairs={{0,4},{2,6},{4,8},{6,10},{8,12},{10,14},{12,0},{14,2},{1,5},{3,7},... | collective-permute-start | bytes 393224 | tf_op jit(solution)/shard_map/ppermute | solution.py:451
  11.9 24.9 %collective-permute-start = (bf16[16,32,128]{2,1,0:T(8,128)(2,1)S(1)}, bf16[16,32,128]{2,1,0:T(8,128)(2,1)S(1)}, u32[]{:S(2)}, u32[]{:S(2)}) collective-permute-start(bf16[16,32,128]{2,1,0:T(8,128)(2,1)S(1)} %bitcast.12), channel_id=1, source_target_pairs={{0,2},{2,4},{4,6},{6,8},{8,10},{10,12},{12,14},{14,0},{1,3},{3,5},... | collective-permute-start | bytes 393224 | tf_op jit(solution)/shard_map/ppermute | solution.py:451
  15.0 10.5 %all-to-all-start = ((s32[4,1,2]{2,1,0:T(1,128)}), s32[4,1,2]{2,1,0:T(1,128)S(1)}, u32[]{:S(2)}, u32[]{:S(2)}) async-start(s32[4,1,2]{2,1,0:T(1,128)} %codes.1), calls=%async_computation | async-start | bytes 4096 | tf_op jit(solution)/shard_map/all_to_all | solution.py:479
  19.5 17.3 %collective-permute-start.4 = (bf16[16,32,128]{2,1,0:T(8,128)(2,1)S(1)}, bf16[16,32,128]{2,1,0:T(8,128)(2,1)S(1)}, u32[]{:S(2)}, u32[]{:S(2)}) collective-permute-start(bf16[16,32,128]{2,1,0:T(8,128)(2,1)S(1)} %collective-permute-done.2.refs_4_), channel_id=1, source_target_pairs={{0,2},{2,4},{4,6},{6,8},{8,10},{10,12},{12,14},{14,0},{1,3},{3,5},... | collective-permute-start | bytes 393224 | tf_op jit(solution)/shard_map/ppermute | solution.py:451
  21.8 15.0 %collective-permute-start.3 = (bf16[16,32,128]{2,1,0:T(8,128)(2,1)S(1)}, bf16[16,32,128]{2,1,0:T(8,128)(2,1)S(1)}, u32[]{:S(2)}, u32[]{:S(2)}) collective-permute-start(bf16[16,32,128]{2,1,0:T(8,128)(2,1)S(1)} %collective-permute-done.2.refs_4_), channel_id=1, source_target_pairs={{0,14},{2,0},{4,2},{6,4},{8,6},{10,8},{12,10},{14,12},{1,15},{3,1}... | collective-permute-start | bytes 393224 | tf_op jit(solution)/shard_map/ppermute | solution.py:451
  24.8 11.9 %copy-start.6 = (s32[64,4]{1,0:T(8,128)}, s32[64,4]{1,0:T(8,128)S(1)}, u32[]{:S(2)}) copy-start(s32[64,4]{1,0:T(8,128)S(1)} %copy.10.fetch_ref) | copy-start | bytes 3076
  25.5 0.6 copy-start.10
  27.5 9.2 %all-to-all-start.1 = ((s32[8,1,40]{2,1,0:T(1,128)}), s32[8,1,40]{2,1,0:T(1,128)S(1)}, u32[]{:S(2)}, u32[]{:S(2)}) async-start(s32[8,1,40]{2,1,0:T(1,128)} %note.1), calls=%async_computation.1 | async-start | bytes 8192 | tf_op jit(solution)/shard_map/all_to_all | solution.py:482
  32.4 1.4 %copy-start = (bf16[16,64,704]{2,1,0:T(8,128)(2,1)S(1)}, bf16[16,64,704]{2,1,0:T(8,128)(2,1)}, u32[]{:S(2)}) copy-start(bf16[16,64,704]{2,1,0:T(8,128)(2,1)} %a_hbm.1) | copy-start | bytes 4325380
  33.8 35.5 %copy-start.5 = (s32[1,8]{1,0:T(1,128)S(1)}, s32[1,8]{1,0:T(1,128)}, u32[]{:S(2)}) copy-start(s32[1,8]{1,0:T(1,128)} %send_ref.3) | copy-start | bytes 100
  36.8 12.8 %copy-start.3 = (s32[8,1,40]{2,1,0:T(1,128)}, s32[8,1,40]{2,1,0:T(1,128)S(1)}, u32[]{:S(2)}) copy-start(s32[8,1,40]{2,1,0:T(1,128)S(1)} %all-to-all-done.1.note_ref.wanted_ref) | copy-start | bytes 3844
  38.8 0.7 copy-start.1
  39.5 5.8 %collective-permute-start.7 = (bf16[32,32,128]{2,1,0:T(8,128)(2,1)S(1)}, bf16[32,32,128]{2,1,0:T(8,128)(2,1)S(1)}, u32[]{:S(2)}, u32[]{:S(2)}) collective-permute-start(bf16[32,32,128]{2,1,0:T(8,128)(2,1)S(1)} %get-tuple-element.22), channel_id=1, source_target_pairs={{0,1},{1,0},{16,17},{17,16},{32,33},{33,32},{48,49},{49,48},{2,3},... | collective-permute-start | bytes 786440 | tf_op jit(solution)/shard_map/ppermute | solution.py:461
  39.7 9.1 %collective-permute-start.8 = (bf16[32,32,128]{2,1,0:T(8,128)(2,1)S(1)}, bf16[32,32,128]{2,1,0:T(8,128)(2,1)S(1)}, u32[]{:S(2)}, u32[]{:S(2)}) collective-permute-start(bf16[32,32,128]{2,1,0:T(8,128)(2,1)S(1)} %get-tuple-element.23), channel_id=1, source_target_pairs={{0,16},{1,17},{16,32},{17,33},{32,48},{33,49},{48,0},{49,1},{2,18}... | collective-permute-start | bytes 786440 | tf_op jit(solution)/shard_map/ppermute | solution.py:461
  41.1 21.4 %collective-permute-start.9 = (bf16[32,32,128]{2,1,0:T(8,128)(2,1)}, bf16[32,32,128]{2,1,0:T(8,128)(2,1)S(1)}, u32[]{:S(2)}, u32[]{:S(2)}) collective-permute-start(bf16[32,32,128]{2,1,0:T(8,128)(2,1)} %get-tuple-element.24), channel_id=1, source_target_pairs={{0,17},{1,16},{16,33},{17,32},{32,49},{33,48},{48,1},{49,0},{2,19}... | collective-permute-start | bytes 786440 | tf_op jit(solution)/shard_map/ppermute | solution.py:461
  42.0 20.5 %collective-permute-start.10 = (bf16[32,32,128]{2,1,0:T(8,128)(2,1)}, bf16[32,32,128]{2,1,0:T(8,128)(2,1)}, u32[]{:S(2)}, u32[]{:S(2)}) collective-permute-start(bf16[32,32,128]{2,1,0:T(8,128)(2,1)} %get-tuple-element.25), channel_id=1, source_target_pairs={{0,32},{1,33},{16,48},{17,49},{32,0},{33,1},{48,16},{49,17},{2,34}... | collective-permute-start | bytes 786440 | tf_op jit(solution)/shard_map/ppermute | solution.py:461
  43.4 19.1 %collective-permute-start.11 = (bf16[32,32,128]{2,1,0:T(8,128)(2,1)S(1)}, bf16[32,32,128]{2,1,0:T(8,128)(2,1)}, u32[]{:S(2)}, u32[]{:S(2)}) collective-permute-start(bf16[32,32,128]{2,1,0:T(8,128)(2,1)S(1)} %get-tuple-element.26), channel_id=1, source_target_pairs={{0,33},{1,32},{16,49},{17,48},{32,1},{33,0},{48,17},{49,16},{2,35}... | collective-permute-start | bytes 786440 | tf_op jit(solution)/shard_map/ppermute | solution.py:461
  45.3 24.0 %copy-start.7 = (bf16[32,32,128]{2,1,0:T(8,128)(2,1)}, bf16[32,32,128]{2,1,0:T(8,128)(2,1)S(1)}, u32[]{:S(2)}) copy-start(bf16[32,32,128]{2,1,0:T(8,128)(2,1)S(1)} %collective-permute-done.7.refs_1_) | copy-start | bytes 786436
  45.3 18.5 %collective-permute-start.12 = (bf16[32,32,128]{2,1,0:T(8,128)(2,1)S(1)}, bf16[32,32,128]{2,1,0:T(8,128)(2,1)}, u32[]{:S(2)}, u32[]{:S(2)}) collective-permute-start(bf16[32,32,128]{2,1,0:T(8,128)(2,1)S(1)} %get-tuple-element.27), channel_id=1, source_target_pairs={{0,48},{1,49},{16,0},{17,1},{32,16},{33,17},{48,32},{49,33},{2,50}... | collective-permute-start | bytes 786440 | tf_op jit(solution)/shard_map/ppermute | solution.py:461
  48.8 20.5 %copy-start.8 = (bf16[32,32,128]{2,1,0:T(8,128)(2,1)}, bf16[32,32,128]{2,1,0:T(8,128)(2,1)S(1)}, u32[]{:S(2)}) copy-start(bf16[32,32,128]{2,1,0:T(8,128)(2,1)S(1)} %collective-permute-done.8.refs_2_) | copy-start | bytes 786436
  48.8 20.5 %collective-permute-start.13 = (bf16[32,32,128]{2,1,0:T(8,128)(2,1)S(1)}, bf16[32,32,128]{2,1,0:T(8,128)(2,1)}, u32[]{:S(2)}, u32[]{:S(2)}) collective-permute-start(bf16[32,32,128]{2,1,0:T(8,128)(2,1)S(1)} %get-tuple-element.28), channel_id=1, source_target_pairs={{0,49},{1,48},{16,1},{17,0},{32,17},{33,16},{48,33},{49,32},{2,51}... | collective-permute-start | bytes 786440 | tf_op jit(solution)/shard_map/ppermute | solution.py:461
  50.9 11.6 %all-to-all-start.2 = ((s32[8,1,64]{2,1,0:T(1,128)}), s32[8,1,64]{2,1,0:T(1,128)S(1)}, u32[]{:S(2)}, u32[]{:S(2)}) async-start(s32[8,1,64]{2,1,0:T(1,128)} %plane.1), calls=%async_computation.2 | async-start | bytes 8192 | tf_op jit(solution)/shard_map/all_to_all | solution.py:490
  62.5 6.7 %copy-start.9 = (bf16[32,32,128]{2,1,0:T(8,128)(2,1)}, bf16[32,32,128]{2,1,0:T(8,128)(2,1)S(1)}, u32[]{:S(2)}) copy-start(bf16[32,32,128]{2,1,0:T(8,128)(2,1)S(1)} %collective-permute-done.9.refs_3_) | copy-start | bytes 786436
  69.3 0.7 copy-start.2
  73.2 9.1 %collective-permute-start.14 = (bf16[2,64,768]{2,1,0:T(8,128)(2,1)S(1)}, bf16[2,64,768]{2,1,0:T(8,128)(2,1)S(1)}, u32[]{:S(2)}, u32[]{:S(2)}) collective-permute-start(bf16[2,64,768]{2,1,0:T(8,128)(2,1)S(1)} %get-tuple-element.33), channel_id=1, source_target_pairs={{0,64},{64,128},{128,192},{192,0},{1,65},{65,129},{129,193},{193,1... | collective-permute-start | bytes 589832 | tf_op jit(solution)/shard_map/ppermute | solution.py:451
  75.3 11.8 %collective-permute-start.15 = (bf16[2,64,768]{2,1,0:T(8,128)(2,1)S(1)}, bf16[2,64,768]{2,1,0:T(8,128)(2,1)S(1)}, u32[]{:S(2)}, u32[]{:S(2)}) collective-permute-start(bf16[2,64,768]{2,1,0:T(8,128)(2,1)S(1)} %get-tuple-element.34), channel_id=1, source_target_pairs={{0,128},{64,192},{128,0},{192,64},{1,129},{65,193},{129,1},{193,65... | collective-permute-start | bytes 589832 | tf_op jit(solution)/shard_map/ppermute | solution.py:451
  78.0 9.1 %collective-permute-start.16 = (bf16[2,64,768]{2,1,0:T(8,128)(2,1)S(1)}, bf16[2,64,768]{2,1,0:T(8,128)(2,1)S(1)}, u32[]{:S(2)}, u32[]{:S(2)}) collective-permute-start(bf16[2,64,768]{2,1,0:T(8,128)(2,1)S(1)} %get-tuple-element.35), channel_id=1, source_target_pairs={{0,192},{64,0},{128,64},{192,128},{1,193},{65,1},{129,65},{193,129... | collective-permute-start | bytes 589832 | tf_op jit(solution)/shard_map/ppermute | solution.py:451
  79.4 7.7 %copy-start.4 = (s32[1,8]{1,0:T(1,128)S(1)}, s32[1,8]{1,0:T(1,128)}, u32[]{:S(2)}) copy-start(s32[1,8]{1,0:T(1,128)} %slots_ref.3) | copy-start | bytes 100

commit v7 on v6

--- a/solution.py
+++ b/solution.py
@@ -1,3 +1,5 @@
+import functools
+
 import jax
 import jax.numpy as jnp
 from jax import lax
@@ -20,7 +22,7 @@
 CHUNKS = 1
 CK = 32 // CHUNKS
 AXES = ("grp", "x", "z", "core")
-ORDER = (1, 2, 6, 4, 5, 3, 7, 0)
+ORDER = ((2, 6, 4, 5, 1), (3, 7), (0,))
 
 VMEM = pl.BlockSpec(memory_space=pltpu.VMEM)
 SMEM = pl.BlockSpec(memory_space=pltpu.SMEM)
@@ -79,12 +81,12 @@
     )(blocks, perm, stiffness)
 
 
-def select_kernel(wanted_ref, *refs):
-    n = NX * NC
+def select_kernel(targets, wanted_ref, *refs):
+    n = len(targets)
     held, outs, stage, sems = refs[:NZ], refs[NZ:NZ + n], refs[NZ + n], refs[NZ + n + 1]
     x, z, c = (lax.axis_index(name) for name in AXES[1:])
     copies = []
-    for i, b in enumerate(ORDER):
+    for i, b in enumerate(targets):
         target = ((x + b // NC) & (NX - 1)) * NC + (c ^ (b % NC))
         for s in range(NZ):
             home = ((z - s) & (NZ - 1)) * C
@@ -97,11 +99,11 @@
         copy.wait()
 
 
-def select(wanted, held):
-    n = NX * NC
+def select(targets, wanted, held):
+    n = len(targets)
     shape = (NZ * C, CK, LANES)
     return pl.pallas_call(
-        select_kernel,
+        functools.partial(select_kernel, targets),
         out_shape=[jax.ShapeDtypeStruct(shape, jnp.bfloat16)] * n,
         in_specs=[SMEM] + [VMEM] * NZ,
         out_specs=[HBM] * n,
@@ -159,22 +161,28 @@
     return labels
 
 
-def follower_kernel(slot_ref, send_ref, codes_ref, own_ref, y_ref, *refs):
-    n = NX * NC * CHUNKS
-    parts, outs, table, sems = refs[:n], refs[n:n + NG], refs[n + NG], refs[n + NG + 1]
-    fill(table, own_ref, parts, sems)
-    for s in range(NG):
+def follower_kernel(shifts, slot_ref, send_ref, codes_ref, y_ref, *refs):
+    outs = refs[len(refs) - len(shifts):]
+    table = refs[0]
+    for i, s in enumerate(shifts):
         target = (lax.axis_index(AXES[0]) + s) & (NG - 1)
         for q in range(2):
             row = HALF + send_ref[0, target * 2 + q]
 
-            def emit(span, value, s=s, q=q):
-                outs[s][q, :, span] = value
+            def emit(span, value, i=i, q=q):
+                outs[i][q, :, span] = value
 
             row_tiles(row, 1, table, slot_ref, y_ref, emit)
             labels = label_row(row, slot_ref, codes_ref)[:, 0:BLK]
-            outs[s][q, 0:1, 0:BLK] = (labels >> 4).astype(jnp.float32).astype(jnp.bfloat16)
-            outs[s][q, 16:17, 0:BLK] = (labels & 15).astype(jnp.float32).astype(jnp.bfloat16)
+            outs[i][q, 0:1, 0:BLK] = (labels >> 4).astype(jnp.float32).astype(jnp.bfloat16)
+            outs[i][q, 16:17, 0:BLK] = (labels & 15).astype(jnp.float32).astype(jnp.bfloat16)
+
+
+def first_kernel(shifts, slot_ref, send_ref, codes_ref, y_ref, own_ref, *refs):
+    n = NX * NC * CHUNKS
+    parts, outs, table, sems = refs[:n], refs[n:n + len(shifts)], refs[-2], refs[-1]
+    fill(table, own_ref, parts, sems)
+    follower_kernel(shifts, slot_ref, send_ref, codes_ref, y_ref, table, *outs)
 
 
 def leader_kernel(slot_ref, codes_ref, y_ref, table, out, labels_ref):
@@ -192,19 +200,32 @@
 ROW_COST = pl.CostEstimate(flops=2 * 8 * 6 * BLK * LANES * LANES, bytes_accessed=5_000_000, transcendentals=0)
 
 
-def followers(slots, send, codes, own, y, parts):
+def first_followers(shifts, slots, send, codes, own, y, parts):
     shape = jax.ShapeDtypeStruct((2, BLK, WIDE), jnp.bfloat16)
     table = jax.ShapeDtypeStruct((TABLE + ROWS + 1, 32, LANES), jnp.bfloat16)
     return pl.pallas_call(
-        follower_kernel,
-        out_shape=[shape] * NG + [table],
+        functools.partial(first_kernel, shifts),
+        out_shape=[shape] * len(shifts) + [table],
         in_specs=[SMEM] * 3 + [VMEM] * 2 + [HBM] * len(parts),
-        out_specs=[VMEM] * (NG + 1),
+        out_specs=[VMEM] * (len(shifts) + 1),
         scratch_shapes=[pltpu.SemaphoreType.DMA((len(parts),))],
         compiler_params=LIMIT,
         cost_estimate=ROW_COST,
+        name="first",
+    )(slots, send, codes, y, own, *parts)
+
+
+def followers(shifts, slots, send, codes, y, table):
+    shape = jax.ShapeDtypeStruct((2, BLK, WIDE), jnp.bfloat16)
+    return pl.pallas_call(
+        functools.partial(follower_kernel, shifts),
+        out_shape=[shape] * len(shifts),
+        in_specs=[SMEM] * 3 + [VMEM] * 2,
+        out_specs=[VMEM] * len(shifts),
+        compiler_params=LIMIT,
+        cost_estimate=ROW_COST,
         name="followers",
-    )(slots, send, codes, own, y, *parts)
+    )(slots, send, codes, y, table)
 
 
 def leaders(slots, codes, y, table):
@@ -480,7 +501,7 @@
     lists = fetch_rows.reshape(NX, NZ, NC, C).transpose(0, 2, 1, 3).reshape(NX * NC, 1, NZ * C)
     note = note_rows(send_order, lists, returned)
     wanted = lax.all_to_all(note, ("x", "core"), split_axis=0, concat_axis=0, tiled=True)
-    words = slot_words(columns, fetch_rows)
+    words = pltpu.with_memory_space_constraint(slot_words(columns, fetch_rows), pltpu.HBM)
     lane = jnp.arange(LANES, dtype=jnp.int32)
     inner = lane & (BLK - 1)
     source = (lane & BLK) + jnp.where(inner < 32, 2 * inner, 2 * (inner - 32) + 1)
@@ -491,12 +512,17 @@
 
     parts = []
     for h in range(CHUNKS):
-        chosen = select(wanted, held[h])
-        moved = {b: cross(chosen[i], b) for i, b in enumerate(ORDER)}
+        chosen = []
+        for targets in ORDER:
+            chosen += select(targets, wanted, held[h])
+            wanted, chosen[-1] = lax.optimization_barrier((wanted, chosen[-1]))
+        moved = {b: cross(chosen[i], b) for i, b in enumerate(sum(ORDER, ()))}
         parts += [pltpu.with_memory_space_constraint(moved[b], pltpu.HBM) for b in range(NX * NC)]
 
-    *sent, table = followers(words, send_order, codes, own, y, parts)
-    arrived = [sent[0]] + [shift(sent[s], "grp", NG, s) for s in range(1, NG)]
+    sent = {}
+    sent[2], table = first_followers((2,), words, send_order, codes, own, y, parts)
+    sent[1], sent[3], sent[0] = followers((1, 3, 0), words, send_order, codes, y, table)
+    arrived = [shift(sent[s], "grp", NG, s) for s in range(NG)]
     lead, lead_labels = leaders(words, codes, y, table)
     return tuple(merge(partner_slot, lead, lead_labels, arrived))
 

time: 92.1 us -> 88.1 us (0.957)
  waiting for transfers between devices: 17.1 us -> 8.51 us
  Pallas kernels: 23.4 us -> 26.6 us
    ppermute x7, waiting for transfers between devices: 9.39 us -> 5.82 us  [cross(): return lax.ppermute(value, ('x', 'core'), pairs)]
    ppermute x10, waiting for transfers between devices: 4.83 us -> 1.96 us  [shift(): lax.ppermute(value, axis, [(i, (i + by) % size) for i in range(size)])]
    pallas_call x2 -> x5, Pallas kernels: 5.19 us -> 7.7 us  [the longest x3 3.44 us: select(): pl.pallas_call(functools.partial(select_kernel, targets), out_shape=[jax....]
    all_to_all x1, waiting for transfers between devices: 2.87 us -> 0.73 us  [per_device(): lax.all_to_all(plane_rows(wanted), 'z', split_axis=0, concat_axis=0, tile...]
    unnamed x24 -> x22, local copies, waits for them, and re-layouts: 5.1 us -> 5.8 us
  transfers between devices with their start and end apart: 20 -> 20, of which waited for: 5 -> 4; matrix products, arithmetic and copies ran while one was open for 3% -> 3% of each run, Pallas kernels for 16% -> 21%
where the time goes in v7:
time: 88.1 us; the launch traced here: 86.9 us
  starting transfers between devices  43.1 us (49%)
  Pallas kernels  26.6 us (30%)
  waiting for transfers between devices  8.51 us (10%)
  local copies, waits for them, and re-layouts  7.65 us (9%)
  between operations  1.01 us (1%)
    ppermute x10, starting transfers between devices, shift(): lax.ppermute(value, axis, [(i, (i + by) % size) for i in range(size)])  22.5 us
    ppermute x7, starting transfers between devices, cross(): return lax.ppermute(value, ('x', 'core'), pairs)  7.38 us
    ppermute x7, waiting for transfers between devices, cross(): return lax.ppermute(value, ('x', 'core'), pairs)  5.82 us
    unnamed x22, local copies, waits for them, and re-layouts  5.8 us
    all_to_all x1, starting transfers between devices, per_device(): lax.all_to_all(note, ('x', 'core'), split_axis=0, concat_axis=0, tiled=True)  4.83 us
    pallas_call x1, Pallas kernels, slot_words(): pl.pallas_call(slot_kernel, out_shape=jax.ShapeDtypeStruct((ROWS, K), jnp...  4.8 us
    all_to_all x1, starting transfers between devices, per_device(): lax.all_to_all(code_rows(partner_slot), 'grp', split_axis=0, concat_axis=...  4.46 us
    pallas_call x1, Pallas kernels, merge(): pl.pallas_call(merge_kernel, out_shape=[jax.ShapeDtypeStruct((HALF, BLK,...  4.22 us
  transfers between devices with their start and end apart: 20, of which 4 were waited for; matrix products, arithmetic and copies ran while one was open for 3% of the time, Pallas kernels for 21%

profile of v7, /device:TPU:2, one launch (start us, length us, event | category | flops | bytes accessed | tf_op | source)
XLA Modules:
  0.0 86.9 jit_solution(12271372201889381808)
XLA Ops:
  0.6 0.9 %copy.14 = bf16[2,8,32,128]{3,2,1,0:T(8,128)(2,1)S(1)} copy(bf16[2,8,32,128]{3,1,2,0:T(8,128)(2,1)} %bitcast.17) | data formatting | bytes 262144
  1.6 7.3 %collective-permute-start.2 = (bf16[16,32,128]{2,1,0:T(8,128)(2,1)S(1)}, bf16[16,32,128]{2,1,0:T(8,128)(2,1)S(1)}, u32[]{:S(2)}, u32[]{:S(2)}) collective-permute-start(bf16[16,32,128]{2,1,0:T(8,128)(2,1)S(1)} %bitcast.8), channel_id=1, source_target_pairs={{0,8},{2,10},{4,12},{6,14},{8,0},{10,2},{12,4},{14,6},{1,9},{3,11}... | collective-permute-start | bytes 393224 | tf_op jit(solution)/shard_map/ppermute | solution.py:472
  9.0 2.8 %collective-permute-start.1 = (bf16[16,32,128]{2,1,0:T(8,128)(2,1)S(1)}, bf16[16,32,128]{2,1,0:T(8,128)(2,1)S(1)}, u32[]{:S(2)}, u32[]{:S(2)}) collective-permute-start(bf16[16,32,128]{2,1,0:T(8,128)(2,1)S(1)} %bitcast.11), channel_id=1, source_target_pairs={{0,4},{2,6},{4,8},{6,10},{8,12},{10,14},{12,0},{14,2},{1,5},{3,7},... | collective-permute-start | bytes 393224 | tf_op jit(solution)/shard_map/ppermute | solution.py:472
  11.9 1.9 %collective-permute-start = (bf16[16,32,128]{2,1,0:T(8,128)(2,1)S(1)}, bf16[16,32,128]{2,1,0:T(8,128)(2,1)S(1)}, u32[]{:S(2)}, u32[]{:S(2)}) collective-permute-start(bf16[16,32,128]{2,1,0:T(8,128)(2,1)S(1)} %bitcast.12), channel_id=1, source_target_pairs={{0,2},{2,4},{4,6},{6,8},{8,10},{10,12},{12,14},{14,0},{1,3},{3,5},... | collective-permute-start | bytes 393224 | tf_op jit(solution)/shard_map/ppermute | solution.py:472
  13.8 1.3 %codes.1 = s32[4,1,2]{2,1,0:T(1,128)} custom-call(s32[1,8]{1,0:T(1,128)} %slots_ref.3), custom_call_target="tpu_custom_call" | custom-call | tf_op jit(solution)/shard_map/codes/pallas_call | solution.py:257
  15.0 4.5 %all-to-all-start = ((s32[4,1,2]{2,1,0:T(1,128)}), s32[4,1,2]{2,1,0:T(1,128)S(1)}, u32[]{:S(2)}, u32[]{:S(2)}) async-start(s32[4,1,2]{2,1,0:T(1,128)} %codes.1), calls=%async_computation | async-start | bytes 4096 | tf_op jit(solution)/shard_map/all_to_all | solution.py:500
  19.5 2.3 %collective-permute-start.4 = (bf16[16,32,128]{2,1,0:T(8,128)(2,1)S(1)}, bf16[16,32,128]{2,1,0:T(8,128)(2,1)S(1)}, u32[]{:S(2)}, u32[]{:S(2)}) collective-permute-start(bf16[16,32,128]{2,1,0:T(8,128)(2,1)S(1)} %collective-permute-done.2.refs_4_), channel_id=1, source_target_pairs={{0,2},{2,4},{4,6},{6,8},{8,10},{10,12},{12,14},{14,0},{1,3},{3,5},... | collective-permute-start | bytes 393224 | tf_op jit(solution)/shard_map/ppermute | solution.py:472
  21.8 1.0 %collective-permute-start.3 = (bf16[16,32,128]{2,1,0:T(8,128)(2,1)S(1)}, bf16[16,32,128]{2,1,0:T(8,128)(2,1)S(1)}, u32[]{:S(2)}, u32[]{:S(2)}) collective-permute-start(bf16[16,32,128]{2,1,0:T(8,128)(2,1)S(1)} %collective-permute-done.2.refs_4_), channel_id=1, source_target_pairs={{0,14},{2,0},{4,2},{6,4},{8,6},{10,8},{12,10},{14,12},{1,15},{3,1}... | collective-permute-start | bytes 393224 | tf_op jit(solution)/shard_map/ppermute | solution.py:472
  22.9 1.2 %reshape.31.p_ref = bf16[16,64,64]{2,1,0:T(8,128)(2,1)S(1)} reshape(bf16[16,4096]{1,0:T(8,128)(2,1)} %param.7) | data formatting | bytes 262144 | tf_op jit(solution)/shard_map/reshape | solution.py:509
  24.0 0.8 copy.10.fetch_ref
  26.1 1.4 %note.1 = s32[8,1,40]{2,1,0:T(1,128)} custom-call(s32[1,8]{1,0:T(1,128)} %send_ref.5, s32[8,1,32]{2,1,0:T(1,128)} %bitcast.19, s32[4,1,2]{2,1,0:T(1,128)} %copy-done.9), custom_call_target="tpu_custom_call" | custom-call | tf_op jit(solution)/shard_map/note/pallas_call | solution.py:280
  27.5 4.8 %all-to-all-start.1 = ((s32[8,1,40]{2,1,0:T(1,128)}), s32[8,1,40]{2,1,0:T(1,128)S(1)}, u32[]{:S(2)}, u32[]{:S(2)}) async-start(s32[8,1,40]{2,1,0:T(1,128)} %note.1), calls=%async_computation.1 | async-start | bytes 8192 | tf_op jit(solution)/shard_map/all_to_all | solution.py:503
  32.4 1.4 %copy-done = bf16[16,64,704]{2,1,0:T(8,128)(2,1)S(1)} copy-done((bf16[16,64,704]{2,1,0:T(8,128)(2,1)S(1)}, bf16[16,64,704]{2,1,0:T(8,128)(2,1)}, u32[]{:S(2)}) %copy-start) | copy-done | bytes 1441816
  33.8 2.9 %products.1.y_ref = bf16[16,64,768]{2,1,0:T(8,128)(2,1)S(1)} custom-call(bf16[16,64,64]{2,1,0:T(8,128)(2,1)S(1)} %reshape.31.p_ref, bf16[128,128]{1,0:T(8,128)(2,1)S(1)} %fusion.perm_ref, bf16[16,64,704]{2,1,0:T(8,128)(2,1)S(1)} %copy-done), custom_call_target="tpu_custom_call" | custom-call | flops 301989888 | bytes 3200000 | tf_op jit(solution)/shard_map/products/pallas_call | solution.py:66
  36.8 1.2 %select.3 = (bf16[32,32,128]{2,1,0:T(8,128)(2,1)S(1)}, bf16[32,32,128]{2,1,0:T(8,128)(2,1)S(1)}, bf16[32,32,128]{2,1,0:T(8,128)(2,1)S(1)}, bf16[32,32,128]{2,1,0:T(8,128)(2,1)S(1)}, bf16[32,32,128]{2,1,0:T(8,128)(2,1)S(1)}) custom-call(s32[8,1,40]{2,1,0:T(1,128)S(1)} %all-to-all-done.1.note_ref.wanted_ref, bf16[16,32,128]{2,1,0:T(8,128)(2,1)S(1)} %bitcast.13, ...), custom_call_target="tpu_custom_call" | custom-call | tf_op jit(solution)/shard_map/select/pallas_call | solution.py:105
  38.2 1.5 %collective-permute-start.8 = (bf16[32,32,128]{2,1,0:T(8,128)(2,1)S(1)}, bf16[32,32,128]{2,1,0:T(8,128)(2,1)S(1)}, u32[]{:S(2)}, u32[]{:S(2)}) collective-permute-start(bf16[32,32,128]{2,1,0:T(8,128)(2,1)S(1)} %get-tuple-element.31), channel_id=1, source_target_pairs={{0,16},{1,17},{16,32},{17,33},{32,48},{33,49},{48,0},{49,1},{2,18}... | collective-permute-start | bytes 786440 | tf_op jit(solution)/shard_map/ppermute | solution.py:482
  39.7 1.4 %collective-permute-start.10 = (bf16[32,32,128]{2,1,0:T(8,128)(2,1)S(1)}, bf16[32,32,128]{2,1,0:T(8,128)(2,1)}, u32[]{:S(2)}, u32[]{:S(2)}) collective-permute-start(bf16[32,32,128]{2,1,0:T(8,128)(2,1)S(1)} %get-tuple-element.33), channel_id=1, source_target_pairs={{0,32},{1,33},{16,48},{17,49},{32,0},{33,1},{48,16},{49,17},{2,34}... | collective-permute-start | bytes 786440 | tf_op jit(solution)/shard_map/ppermute | solution.py:482
  41.1 1.5 %collective-permute-start.11 = (bf16[32,32,128]{2,1,0:T(8,128)(2,1)S(1)}, bf16[32,32,128]{2,1,0:T(8,128)(2,1)}, u32[]{:S(2)}, u32[]{:S(2)}) collective-permute-start(bf16[32,32,128]{2,1,0:T(8,128)(2,1)S(1)} %get-tuple-element.34), channel_id=1, source_target_pairs={{0,33},{1,32},{16,49},{17,48},{32,1},{33,0},{48,17},{49,16},{2,35}... | collective-permute-start | bytes 786440 | tf_op jit(solution)/shard_map/ppermute | solution.py:482
  43.2 1.5 %select.4 = (bf16[32,32,128]{2,1,0:T(8,128)(2,1)}, bf16[32,32,128]{2,1,0:T(8,128)(2,1)}) custom-call(s32[8,1,40]{2,1,0:T(1,128)S(1)} %all-to-all-done.1.note_ref.wanted_ref, bf16[16,32,128]{2,1,0:T(8,128)(2,1)S(1)} %bitcast.14, bf16[16,32,128]{2,1,0:T(8,128)(2,1)S(1)} %collective-permute-done.refs_1_, ...), custom_call_target="tpu_custom_call" | custom-call | tf_op jit(solution)/shard_map/select/pallas_call | solution.py:105
  44.8 2.1 %collective-permute-start.13 = (bf16[32,32,128]{2,1,0:T(8,128)(2,1)}, bf16[32,32,128]{2,1,0:T(8,128)(2,1)}, u32[]{:S(2)}, u32[]{:S(2)}) collective-permute-start(bf16[32,32,128]{2,1,0:T(8,128)(2,1)} %get-tuple-element.36), channel_id=1, source_target_pairs={{0,49},{1,48},{16,1},{17,0},{32,17},{33,16},{48,33},{49,32},{2,51}... | collective-permute-start | bytes 786440 | tf_op jit(solution)/shard_map/ppermute | solution.py:482
  48.1 1.4 %plane.1 = s32[8,1,64]{2,1,0:T(1,128)} custom-call(s32[8,1,40]{2,1,0:T(1,128)} %copy-done.2), custom_call_target="tpu_custom_call" | custom-call | tf_op jit(solution)/shard_map/plane/pallas_call | solution.py:297
  49.5 4.0 %all-to-all-start.2 = ((s32[8,1,64]{2,1,0:T(1,128)}), s32[8,1,64]{2,1,0:T(1,128)S(1)}, u32[]{:S(2)}, u32[]{:S(2)}) async-start(s32[8,1,64]{2,1,0:T(1,128)} %plane.1), calls=%async_computation.2 | async-start | bytes 8192 | tf_op jit(solution)/shard_map/all_to_all | solution.py:511
  53.4 4.8 %slots.1.slot_ref = s32[16,11]{1,0:T(8,128)} custom-call(s32[16,11]{1,0:T(8,128)} %columns_ref.1, s32[64,4]{1,0:T(8,128)} %copy-done.6), custom_call_target="tpu_custom_call" | custom-call | flops 1000000 | bytes 2000000 | tf_op jit(solution)/shard_map/slots/pallas_call | solution.py:333
  58.9 0.7 select.5.refs_0_
  61.1 5.3 %collective-permute-done.13.refs_7_ = bf16[32,32,128]{2,1,0:T(8,128)(2,1)} collective-permute-done((bf16[32,32,128]{2,1,0:T(8,128)(2,1)}, bf16[32,32,128]{2,1,0:T(8,128)(2,1)}, u32[]{:S(2)}, u32[]{:S(2)}) %collective-permute-start.13) | collective-permute-done | bytes 262176 | tf_op jit(solution)/shard_map/ppermute | solution.py:482
  66.4 2.7 %first.1 = (bf16[2,64,768]{2,1,0:T(8,128)(2,1)S(1)}, bf16[273,32,128]{2,1,0:T(8,128)(2,1)S(1)}) custom-call(s32[16,11]{1,0:T(8,128)} %slots.1.slot_ref, s32[1,8]{1,0:T(1,128)S(1)} %copy-done.4, s32[8,1,64]{2,1,0:T(1,128)S(1)} %all-to-all-done.2.codes_ref, bf16[16,64,768]{2,1,0:T(8,128)(2,1)S(1)} %products.1.y_ref, bf16[16,32,128]{2,1,0:T(8,128)(2,1)S(1)} %bitcast.16, ...), custom_call_target="tpu_custom_call" | custom-call | flops 100663296 | bytes 5000000 | tf_op jit(solution)/shard_map/first/pallas_call | solution.py:206
  69.2 3.6 %collective-permute-start.15 = (bf16[2,64,768]{2,1,0:T(8,128)(2,1)S(1)}, bf16[2,64,768]{2,1,0:T(8,128)(2,1)S(1)}, u32[]{:S(2)}, u32[]{:S(2)}) collective-permute-start(bf16[2,64,768]{2,1,0:T(8,128)(2,1)S(1)} %get-tuple-element.42), channel_id=1, source_target_pairs={{0,128},{64,192},{128,0},{192,64},{1,129},{65,193},{129,1},{193,65... | collective-permute-start | bytes 589832 | tf_op jit(solution)/shard_map/ppermute | solution.py:472
  72.8 1.5 %followers.1 = (bf16[2,64,768]{2,1,0:T(8,128)(2,1)S(1)}, bf16[2,64,768]{2,1,0:T(8,128)(2,1)S(1)}, bf16[2,64,768]{2,1,0:T(8,128)(2,1)S(1)}) custom-call(s32[16,11]{1,0:T(8,128)} %slots.1.slot_ref, s32[1,8]{1,0:T(1,128)S(1)} %copy-done.4, s32[8,1,64]{2,1,0:T(1,128)S(1)} %all-to-all-done.2.codes_ref, bf16[16,64,768]{2,1,0:T(8,128)(2,1)S(1)} %products.1.y_ref, ...), custom_call_target="tpu_custom_call" | custom-call | flops 100663296 | bytes 5000000 | tf_op jit(solution)/shard_map/followers/pallas_call | solution.py:220
  75.0 2.7 %collective-permute-start.16 = (bf16[2,64,768]{2,1,0:T(8,128)(2,1)S(1)}, bf16[2,64,768]{2,1,0:T(8,128)(2,1)S(1)}, u32[]{:S(2)}, u32[]{:S(2)}) collective-permute-start(bf16[2,64,768]{2,1,0:T(8,128)(2,1)S(1)} %get-tuple-element.43), channel_id=1, source_target_pairs={{0,192},{64,0},{128,64},{192,128},{1,193},{65,1},{129,65},{193,129... | collective-permute-start | bytes 589832 | tf_op jit(solution)/shard_map/ppermute | solution.py:472
  77.7 2.9 %leaders.1 = (bf16[8,64,768]{2,1,0:T(8,128)(2,1)S(1)}, s32[8,128]{1,0:T(8,128)S(1)}) custom-call(s32[16,11]{1,0:T(8,128)} %slots.1.slot_ref, s32[8,1,64]{2,1,0:T(1,128)S(1)} %all-to-all-done.2.codes_ref, bf16[16,64,768]{2,1,0:T(8,128)(2,1)S(1)} %products.1.y_ref, bf16[273,32,128]{2,1,0:T(8,128)(2,1)S(1)} %get-tuple-element.37.table.refs_0_), custom_call_target="tpu_custom_call" | custom-call | flops 100663296 | bytes 5000000 | tf_op jit(solution)/shard_map/leaders/pallas_call | solution.py:232
  80.6 1.9 %collective-permute-done.14.refs_1_ = bf16[2,64,768]{2,1,0:T(8,128)(2,1)S(1)} collective-permute-done((bf16[2,64,768]{2,1,0:T(8,128)(2,1)S(1)}, bf16[2,64,768]{2,1,0:T(8,128)(2,1)S(1)}, u32[]{:S(2)}, u32[]{:S(2)}) %collective-permute-start.14) | collective-permute-done | bytes 196640 | tf_op jit(solution)/shard_map/ppermute | solution.py:472
  82.5 4.2 %merge.1 = (bf16[8,64,1408]{2,1,0:T(8,128)(2,1)}, s32[8,22]{1,0:T(8,128)}) custom-call(s32[1,8]{1,0:T(1,128)S(1)} %copy-done.5, bf16[8,64,768]{2,1,0:T(8,128)(2,1)S(1)} %get-tuple-element.38.lead_ref, s32[8,128]{1,0:T(8,128)S(1)} %get-tuple-element.39.own_labels_ref, bf16[2,64,768]{2,1,0:T(8,128)(2,1)S(1)} %get-tuple-element.40.refs_0_, ...), custom_call_target="tpu_custom_call" | custom-call | tf_op jit(solution)/shard_map/merge/pallas_call | solution.py:445
  (47 shorter events, 6.4 us)
Async XLA Ops:
  1.6 18.0 %collective-permute-start.2 = (bf16[16,32,128]{2,1,0:T(8,128)(2,1)S(1)}, bf16[16,32,128]{2,1,0:T(8,128)(2,1)S(1)}, u32[]{:S(2)}, u32[]{:S(2)}) collective-permute-start(bf16[16,32,128]{2,1,0:T(8,128)(2,1)S(1)} %bitcast.8), channel_id=1, source_target_pairs={{0,8},{2,10},{4,12},{6,14},{8,0},{10,2},{12,4},{14,6},{1,9},{3,11}... | collective-permute-start | bytes 393224 | tf_op jit(solution)/shard_map/ppermute | solution.py:472
  8.8 13.0 %collective-permute-start.6 = (bf16[16,32,128]{2,1,0:T(8,128)(2,1)S(1)}, bf16[16,32,128]{2,1,0:T(8,128)(2,1)S(1)}, u32[]{:S(2)}, u32[]{:S(2)}) collective-permute-start(bf16[16,32,128]{2,1,0:T(8,128)(2,1)S(1)} %bitcast.9), channel_id=1, source_target_pairs={{0,14},{2,0},{4,2},{6,4},{8,6},{10,8},{12,10},{14,12},{1,15},{3,1}... | collective-permute-start | bytes 393224 | tf_op jit(solution)/shard_map/ppermute | solution.py:472
  8.9 27.8 %collective-permute-start.5 = (bf16[16,32,128]{2,1,0:T(8,128)(2,1)S(1)}, bf16[16,32,128]{2,1,0:T(8,128)(2,1)S(1)}, u32[]{:S(2)}, u32[]{:S(2)}) collective-permute-start(bf16[16,32,128]{2,1,0:T(8,128)(2,1)S(1)} %bitcast.10), channel_id=1, source_target_pairs={{0,12},{2,14},{4,0},{6,2},{8,4},{10,6},{12,8},{14,10},{1,13},{3,15... | collective-permute-start | bytes 393224 | tf_op jit(solution)/shard_map/ppermute | solution.py:472
  9.0 27.7 %collective-permute-start.1 = (bf16[16,32,128]{2,1,0:T(8,128)(2,1)S(1)}, bf16[16,32,128]{2,1,0:T(8,128)(2,1)S(1)}, u32[]{:S(2)}, u32[]{:S(2)}) collective-permute-start(bf16[16,32,128]{2,1,0:T(8,128)(2,1)S(1)} %bitcast.11), channel_id=1, source_target_pairs={{0,4},{2,6},{4,8},{6,10},{8,12},{10,14},{12,0},{14,2},{1,5},{3,7},... | collective-permute-start | bytes 393224 | tf_op jit(solution)/shard_map/ppermute | solution.py:472
  11.9 24.9 %collective-permute-start = (bf16[16,32,128]{2,1,0:T(8,128)(2,1)S(1)}, bf16[16,32,128]{2,1,0:T(8,128)(2,1)S(1)}, u32[]{:S(2)}, u32[]{:S(2)}) collective-permute-start(bf16[16,32,128]{2,1,0:T(8,128)(2,1)S(1)} %bitcast.12), channel_id=1, source_target_pairs={{0,2},{2,4},{4,6},{6,8},{8,10},{10,12},{12,14},{14,0},{1,3},{3,5},... | collective-permute-start | bytes 393224 | tf_op jit(solution)/shard_map/ppermute | solution.py:472
  15.0 10.5 %all-to-all-start = ((s32[4,1,2]{2,1,0:T(1,128)}), s32[4,1,2]{2,1,0:T(1,128)S(1)}, u32[]{:S(2)}, u32[]{:S(2)}) async-start(s32[4,1,2]{2,1,0:T(1,128)} %codes.1), calls=%async_computation | async-start | bytes 4096 | tf_op jit(solution)/shard_map/all_to_all | solution.py:500
  19.5 17.3 %collective-permute-start.4 = (bf16[16,32,128]{2,1,0:T(8,128)(2,1)S(1)}, bf16[16,32,128]{2,1,0:T(8,128)(2,1)S(1)}, u32[]{:S(2)}, u32[]{:S(2)}) collective-permute-start(bf16[16,32,128]{2,1,0:T(8,128)(2,1)S(1)} %collective-permute-done.2.refs_4_), channel_id=1, source_target_pairs={{0,2},{2,4},{4,6},{6,8},{8,10},{10,12},{12,14},{14,0},{1,3},{3,5},... | collective-permute-start | bytes 393224 | tf_op jit(solution)/shard_map/ppermute | solution.py:472
  21.8 15.0 %collective-permute-start.3 = (bf16[16,32,128]{2,1,0:T(8,128)(2,1)S(1)}, bf16[16,32,128]{2,1,0:T(8,128)(2,1)S(1)}, u32[]{:S(2)}, u32[]{:S(2)}) collective-permute-start(bf16[16,32,128]{2,1,0:T(8,128)(2,1)S(1)} %collective-permute-done.2.refs_4_), channel_id=1, source_target_pairs={{0,14},{2,0},{4,2},{6,4},{8,6},{10,8},{12,10},{14,12},{1,15},{3,1}... | collective-permute-start | bytes 393224 | tf_op jit(solution)/shard_map/ppermute | solution.py:472
  24.8 11.9 %copy-start.6 = (s32[64,4]{1,0:T(8,128)}, s32[64,4]{1,0:T(8,128)S(1)}, u32[]{:S(2)}) copy-start(s32[64,4]{1,0:T(8,128)S(1)} %copy.10.fetch_ref) | copy-start | bytes 3076
  25.5 0.6 copy-start.9
  27.5 9.2 %all-to-all-start.1 = ((s32[8,1,40]{2,1,0:T(1,128)}), s32[8,1,40]{2,1,0:T(1,128)S(1)}, u32[]{:S(2)}, u32[]{:S(2)}) async-start(s32[8,1,40]{2,1,0:T(1,128)} %note.1), calls=%async_computation.1 | async-start | bytes 8192 | tf_op jit(solution)/shard_map/all_to_all | solution.py:503
  32.3 1.4 %copy-start = (bf16[16,64,704]{2,1,0:T(8,128)(2,1)S(1)}, bf16[16,64,704]{2,1,0:T(8,128)(2,1)}, u32[]{:S(2)}) copy-start(bf16[16,64,704]{2,1,0:T(8,128)(2,1)} %a_hbm.1) | copy-start | bytes 4325380
  36.7 29.7 %copy-start.4 = (s32[1,8]{1,0:T(1,128)S(1)}, s32[1,8]{1,0:T(1,128)}, u32[]{:S(2)}) copy-start(s32[1,8]{1,0:T(1,128)} %send_ref.5) | copy-start | bytes 100
  36.7 11.4 %copy-start.2 = (s32[8,1,40]{2,1,0:T(1,128)}, s32[8,1,40]{2,1,0:T(1,128)S(1)}, u32[]{:S(2)}) copy-start(s32[8,1,40]{2,1,0:T(1,128)S(1)} %all-to-all-done.1.note_ref.wanted_ref) | copy-start | bytes 3844
  38.0 6.7 %collective-permute-start.7 = (bf16[32,32,128]{2,1,0:T(8,128)(2,1)S(1)}, bf16[32,32,128]{2,1,0:T(8,128)(2,1)S(1)}, u32[]{:S(2)}, u32[]{:S(2)}) collective-permute-start(bf16[32,32,128]{2,1,0:T(8,128)(2,1)S(1)} %get-tuple-element.30), channel_id=1, source_target_pairs={{0,1},{1,0},{16,17},{17,16},{32,33},{33,32},{48,49},{49,48},{2,3},... | collective-permute-start | bytes 786440 | tf_op jit(solution)/shard_map/ppermute | solution.py:482
  38.2 9.1 %collective-permute-start.8 = (bf16[32,32,128]{2,1,0:T(8,128)(2,1)S(1)}, bf16[32,32,128]{2,1,0:T(8,128)(2,1)S(1)}, u32[]{:S(2)}, u32[]{:S(2)}) collective-permute-start(bf16[32,32,128]{2,1,0:T(8,128)(2,1)S(1)} %get-tuple-element.31), channel_id=1, source_target_pairs={{0,16},{1,17},{16,32},{17,33},{32,48},{33,49},{48,0},{49,1},{2,18}... | collective-permute-start | bytes 786440 | tf_op jit(solution)/shard_map/ppermute | solution.py:482
  39.7 21.4 %collective-permute-start.10 = (bf16[32,32,128]{2,1,0:T(8,128)(2,1)S(1)}, bf16[32,32,128]{2,1,0:T(8,128)(2,1)}, u32[]{:S(2)}, u32[]{:S(2)}) collective-permute-start(bf16[32,32,128]{2,1,0:T(8,128)(2,1)S(1)} %get-tuple-element.33), channel_id=1, source_target_pairs={{0,32},{1,33},{16,48},{17,49},{32,0},{33,1},{48,16},{49,17},{2,34}... | collective-permute-start | bytes 786440 | tf_op jit(solution)/shard_map/ppermute | solution.py:482
  41.1 20.0 %collective-permute-start.11 = (bf16[32,32,128]{2,1,0:T(8,128)(2,1)S(1)}, bf16[32,32,128]{2,1,0:T(8,128)(2,1)}, u32[]{:S(2)}, u32[]{:S(2)}) collective-permute-start(bf16[32,32,128]{2,1,0:T(8,128)(2,1)S(1)} %get-tuple-element.34), channel_id=1, source_target_pairs={{0,33},{1,32},{16,49},{17,48},{32,1},{33,0},{48,17},{49,16},{2,35}... | collective-permute-start | bytes 786440 | tf_op jit(solution)/shard_map/ppermute | solution.py:482
  42.6 18.5 %collective-permute-start.12 = (bf16[32,32,128]{2,1,0:T(8,128)(2,1)S(1)}, bf16[32,32,128]{2,1,0:T(8,128)(2,1)}, u32[]{:S(2)}, u32[]{:S(2)}) collective-permute-start(bf16[32,32,128]{2,1,0:T(8,128)(2,1)S(1)} %get-tuple-element.35), channel_id=1, source_target_pairs={{0,48},{1,49},{16,0},{17,1},{32,16},{33,17},{48,32},{49,33},{2,50}... | collective-permute-start | bytes 786440 | tf_op jit(solution)/shard_map/ppermute | solution.py:482
  44.7 2.6 %copy-start.7 = (bf16[32,32,128]{2,1,0:T(8,128)(2,1)}, bf16[32,32,128]{2,1,0:T(8,128)(2,1)S(1)}, u32[]{:S(2)}) copy-start(bf16[32,32,128]{2,1,0:T(8,128)(2,1)S(1)} %collective-permute-done.7.refs_1_) | copy-start | bytes 786436
  44.8 21.7 %collective-permute-start.13 = (bf16[32,32,128]{2,1,0:T(8,128)(2,1)}, bf16[32,32,128]{2,1,0:T(8,128)(2,1)}, u32[]{:S(2)}, u32[]{:S(2)}) collective-permute-start(bf16[32,32,128]{2,1,0:T(8,128)(2,1)} %get-tuple-element.36), channel_id=1, source_target_pairs={{0,49},{1,48},{16,1},{17,0},{32,17},{33,16},{48,33},{49,32},{2,51}... | collective-permute-start | bytes 786440 | tf_op jit(solution)/shard_map/ppermute | solution.py:482
  47.4 0.7 copy-start.8
  48.1 18.4 %collective-permute-start.9 = (bf16[32,32,128]{2,1,0:T(8,128)(2,1)}, bf16[32,32,128]{2,1,0:T(8,128)(2,1)}, u32[]{:S(2)}, u32[]{:S(2)}) collective-permute-start(bf16[32,32,128]{2,1,0:T(8,128)(2,1)} %get-tuple-element.32), channel_id=1, source_target_pairs={{0,17},{1,16},{16,33},{17,32},{32,49},{33,48},{48,1},{49,0},{2,19}... | collective-permute-start | bytes 786440 | tf_op jit(solution)/shard_map/ppermute | solution.py:482
  49.5 11.6 %all-to-all-start.2 = ((s32[8,1,64]{2,1,0:T(1,128)}), s32[8,1,64]{2,1,0:T(1,128)S(1)}, u32[]{:S(2)}, u32[]{:S(2)}) async-start(s32[8,1,64]{2,1,0:T(1,128)} %plane.1), calls=%async_computation.2 | async-start | bytes 8192 | tf_op jit(solution)/shard_map/all_to_all | solution.py:511
  58.2 0.7 copy-start.3
  59.7 0.7 copy-start.1
  69.2 11.4 %collective-permute-start.15 = (bf16[2,64,768]{2,1,0:T(8,128)(2,1)S(1)}, bf16[2,64,768]{2,1,0:T(8,128)(2,1)S(1)}, u32[]{:S(2)}, u32[]{:S(2)}) collective-permute-start(bf16[2,64,768]{2,1,0:T(8,128)(2,1)S(1)} %get-tuple-element.42), channel_id=1, source_target_pairs={{0,128},{64,192},{128,0},{192,64},{1,129},{65,193},{129,1},{193,65... | collective-permute-start | bytes 589832 | tf_op jit(solution)/shard_map/ppermute | solution.py:472
  74.4 8.2 %collective-permute-start.14 = (bf16[2,64,768]{2,1,0:T(8,128)(2,1)S(1)}, bf16[2,64,768]{2,1,0:T(8,128)(2,1)S(1)}, u32[]{:S(2)}, u32[]{:S(2)}) collective-permute-start(bf16[2,64,768]{2,1,0:T(8,128)(2,1)S(1)} %get-tuple-element.41), channel_id=1, source_target_pairs={{0,64},{64,128},{128,192},{192,0},{1,65},{65,129},{129,193},{193,1... | collective-permute-start | bytes 589832 | tf_op jit(solution)/shard_map/ppermute | solution.py:472
  75.0 7.5 %copy-start.5 = (s32[1,8]{1,0:T(1,128)S(1)}, s32[1,8]{1,0:T(1,128)}, u32[]{:S(2)}) copy-start(s32[1,8]{1,0:T(1,128)} %slots_ref.3) | copy-start | bytes 100
  75.0 7.5 %collective-permute-start.16 = (bf16[2,64,768]{2,1,0:T(8,128)(2,1)S(1)}, bf16[2,64,768]{2,1,0:T(8,128)(2,1)S(1)}, u32[]{:S(2)}, u32[]{:S(2)}) collective-permute-start(bf16[2,64,768]{2,1,0:T(8,128)(2,1)S(1)} %get-tuple-element.43), channel_id=1, source_target_pairs={{0,192},{64,0},{128,64},{192,128},{1,193},{65,1},{129,65},{193,129... | collective-permute-start | bytes 589832 | tf_op jit(solution)/shard_map/ppermute | solution.py:472

commit v8 on v7

--- a/solution.py
+++ b/solution.py
@@ -37,7 +37,7 @@
 STEP = 4
 
 
-def products_kernel(p_ref, perm_ref, a_hbm, y_ref, a_ref, work, sems):
+def products_kernel(own_ref, perm_ref, a_hbm, y_ref, a_ref, work, sems):
     def load(h):
         rows = pl.ds(h * STEP, STEP)
         return pltpu.make_async_copy(a_hbm.at[rows], a_ref.at[rows], sems.at[h])
@@ -49,8 +49,12 @@
     for h in range(ROWS // STEP):
         load(h).wait()
         for i in range(STEP):
+            block = own_ref[h * STEP + i]
+            block = jnp.concatenate([block, pltpu.roll(block, BLK, 1)], axis=0)
+            block = jnp.dot(perm[0:BLK, 0:BLK], block, preferred_element_type=jnp.float32)
+            block = block[:, 0:BLK].astype(jnp.bfloat16)
             y = lax.dot_general(
-                p_ref[h * STEP + i], a_ref[h * STEP + i], (((0,), (0,)), ((), ())),
+                block, a_ref[h * STEP + i], (((0,), (0,)), ((), ())),
                 preferred_element_type=jnp.float32,
             )
             y = jnp.concatenate([y, pad] if h * STEP + i < HALF else [pad, y], axis=1)
@@ -62,7 +66,7 @@
             ).astype(jnp.bfloat16).reshape(STEP, BLK, LANES)
 
 
-def products(blocks, perm, stiffness):
+def products(own, perm, stiffness):
     return pl.pallas_call(
         products_kernel,
         out_shape=jax.ShapeDtypeStruct((ROWS, BLK, WIDE), jnp.bfloat16),
@@ -78,7 +82,7 @@
             flops=2 * ROWS * BLK * BLK * WIDE * 3, bytes_accessed=3_200_000, transcendentals=0
         ),
         name="products",
-    )(blocks, perm, stiffness)
+    )(own, perm, stiffness)
 
 
 def select_kernel(targets, wanted_ref, *refs):
@@ -304,7 +308,7 @@
     )(note)
 
 
-def slot_kernel(columns_ref, fetch_ref, slot_ref):
+def slot_kernel(columns_ref, lists_ref, slot_ref):
     g, x, z, c = (lax.axis_index(name) for name in AXES)
     device = x * (NZ * NC) + z * NC + c
 
@@ -315,7 +319,8 @@
             local = column < ROWS
             asked = ghost >> 2
             peer = jnp.where(local, device, asked)
-            row = jnp.where(local, jnp.maximum(column, 0), fetch_ref[asked, ghost & 3])
+            wish = lists_ref[(asked >> 4) * NC + (asked & 1), 0, ((asked >> 1) & (NZ - 1)) * C + (ghost & 3)]
+            row = jnp.where(local, jnp.maximum(column, 0), wish)
             px, pz, pc = peer >> 4, (peer >> 1) & (NZ - 1), peer & 1
             way = ((x - px) & (NX - 1)) * NC + (c ^ pc)
             at = jnp.where(local, TABLE + row, way * (NZ * C) + pz * C + (ghost & 3))
@@ -329,7 +334,7 @@
     lax.fori_loop(0, ROWS, row, 0)
 
 
-def slot_words(columns, fetch):
+def slot_words(columns, lists):
     return pl.pallas_call(
         slot_kernel,
         out_shape=jax.ShapeDtypeStruct((ROWS, K), jnp.int32),
@@ -337,7 +342,7 @@
         out_specs=SMEM,
         cost_estimate=pl.CostEstimate(flops=1_000_000, bytes_accessed=2_000_000, transcendentals=0),
         name="slots",
-    )(columns, fetch)
+    )(columns, lists)
 
 
 def merge_kernel(slots_ref, lead_ref, own_labels_ref, *refs):
@@ -501,12 +506,12 @@
     lists = fetch_rows.reshape(NX, NZ, NC, C).transpose(0, 2, 1, 3).reshape(NX * NC, 1, NZ * C)
     note = note_rows(send_order, lists, returned)
     wanted = lax.all_to_all(note, ("x", "core"), split_axis=0, concat_axis=0, tiled=True)
-    words = pltpu.with_memory_space_constraint(slot_words(columns, fetch_rows), pltpu.HBM)
+    words = pltpu.with_memory_space_constraint(slot_words(columns, lists), pltpu.HBM)
     lane = jnp.arange(LANES, dtype=jnp.int32)
     inner = lane & (BLK - 1)
     source = (lane & BLK) + jnp.where(inner < 32, 2 * inner, 2 * (inner - 32) + 1)
     perm = (lane[:, None] == source[None, :]).astype(jnp.bfloat16)
-    y = products(prolongator.reshape(ROWS, BLK, BLK), perm, stiffness)
+    y = products(own, perm, stiffness)
     wanted, y = lax.optimization_barrier((wanted, y))
     codes = lax.all_to_all(plane_rows(wanted), "z", split_axis=0, concat_axis=0, tiled=True)
 

time: 88.1 us -> 89.5 us (1.016)
  Pallas kernels: 26.6 us -> 28.6 us
  local copies, waits for them, and re-layouts: 7.65 us -> 6.47 us
    pallas_call x1, Pallas kernels: 2.94 us -> 5.71 us  [products(): pl.pallas_call(products_kernel, out_shape=jax.ShapeDtypeStruct((ROWS, BLK...]
    reshape x1 -> x0, local copies, waits for them, and re-layouts: 1.18 us -> none  [per_device(): y = products(prolongator.reshape(ROWS, BLK, BLK), perm, stiffness)]
    unnamed x22 -> x20, local copies, waits for them, and re-layouts: 5.8 us -> 5.8 us
  transfers between devices with their start and end apart: 20 -> 20, of which waited for: 4 -> 5; matrix products, arithmetic and copies ran while one was open for 3% -> 2% of each run, Pallas kernels for 21% -> 24%
where the time goes in v8:
time: 89.5 us; the launch traced here: 87.8 us
  starting transfers between devices  42.9 us (48%)
  Pallas kernels  28.6 us (32%)
  waiting for transfers between devices  8.86 us (10%)
  local copies, waits for them, and re-layouts  6.47 us (7%)
  between operations  0.99 us (1%)
    ppermute x10, starting transfers between devices, shift(): lax.ppermute(value, axis, [(i, (i + by) % size) for i in range(size)])  22.1 us
    ppermute x7, starting transfers between devices, cross(): return lax.ppermute(value, ('x', 'core'), pairs)  7.12 us
    unnamed x20, local copies, waits for them, and re-layouts  5.8 us
    pallas_call x1, Pallas kernels, products(): pl.pallas_call(products_kernel, out_shape=jax.ShapeDtypeStruct((ROWS, BLK...  5.71 us
    ppermute x7, waiting for transfers between devices, cross(): return lax.ppermute(value, ('x', 'core'), pairs)  5.63 us
    all_to_all x1, starting transfers between devices, per_device(): lax.all_to_all(note, ('x', 'core'), split_axis=0, concat_axis=0, tiled=True)  4.83 us
    pallas_call x1, Pallas kernels, slot_words(): pl.pallas_call(slot_kernel, out_shape=jax.ShapeDtypeStruct((ROWS, K), jnp...  4.71 us
    all_to_all x1, starting transfers between devices, per_device(): lax.all_to_all(code_rows(partner_slot), 'grp', split_axis=0, concat_axis=...  4.46 us
  transfers between devices with their start and end apart: 20, of which 5 were waited for; matrix products, arithmetic and copies ran while one was open for 2% of the time, Pallas kernels for 24%

profile of v8, /device:TPU:2, one launch (start us, length us, event | category | flops | bytes accessed | tf_op | source)
XLA Modules:
  0.0 87.8 jit_solution(9460838719468608197)
XLA Ops:
  0.6 0.9 %copy.13 = bf16[2,8,32,128]{3,2,1,0:T(8,128)(2,1)S(1)} copy(bf16[2,8,32,128]{3,1,2,0:T(8,128)(2,1)} %bitcast.18) | data formatting | bytes 262144
  1.6 7.3 %collective-permute-start.2 = (bf16[16,32,128]{2,1,0:T(8,128)(2,1)S(1)}, bf16[16,32,128]{2,1,0:T(8,128)(2,1)S(1)}, u32[]{:S(2)}, u32[]{:S(2)}) collective-permute-start(bf16[16,32,128]{2,1,0:T(8,128)(2,1)S(1)} %bitcast.8), channel_id=1, source_target_pairs={{0,8},{2,10},{4,12},{6,14},{8,0},{10,2},{12,4},{14,6},{1,9},{3,11}... | collective-permute-start | bytes 393224 | tf_op jit(solution)/shard_map/ppermute | solution.py:477
  9.0 2.8 %collective-permute-start.1 = (bf16[16,32,128]{2,1,0:T(8,128)(2,1)S(1)}, bf16[16,32,128]{2,1,0:T(8,128)(2,1)S(1)}, u32[]{:S(2)}, u32[]{:S(2)}) collective-permute-start(bf16[16,32,128]{2,1,0:T(8,128)(2,1)S(1)} %bitcast.11), channel_id=1, source_target_pairs={{0,4},{2,6},{4,8},{6,10},{8,12},{10,14},{12,0},{14,2},{1,5},{3,7},... | collective-permute-start | bytes 393224 | tf_op jit(solution)/shard_map/ppermute | solution.py:477
  11.9 1.9 %collective-permute-start = (bf16[16,32,128]{2,1,0:T(8,128)(2,1)S(1)}, bf16[16,32,128]{2,1,0:T(8,128)(2,1)S(1)}, u32[]{:S(2)}, u32[]{:S(2)}) collective-permute-start(bf16[16,32,128]{2,1,0:T(8,128)(2,1)S(1)} %bitcast.12), channel_id=1, source_target_pairs={{0,2},{2,4},{4,6},{6,8},{8,10},{10,12},{12,14},{14,0},{1,3},{3,5},... | collective-permute-start | bytes 393224 | tf_op jit(solution)/shard_map/ppermute | solution.py:477
  13.8 1.3 %codes.1 = s32[4,1,2]{2,1,0:T(1,128)} custom-call(s32[1,8]{1,0:T(1,128)} %slots_ref.3), custom_call_target="tpu_custom_call" | custom-call | tf_op jit(solution)/shard_map/codes/pallas_call | solution.py:261
  15.0 4.5 %all-to-all-start = ((s32[4,1,2]{2,1,0:T(1,128)}), s32[4,1,2]{2,1,0:T(1,128)S(1)}, u32[]{:S(2)}, u32[]{:S(2)}) async-start(s32[4,1,2]{2,1,0:T(1,128)} %codes.1), calls=%async_computation | async-start | bytes 4096 | tf_op jit(solution)/shard_map/all_to_all | solution.py:505
  19.5 2.3 %collective-permute-start.4 = (bf16[16,32,128]{2,1,0:T(8,128)(2,1)S(1)}, bf16[16,32,128]{2,1,0:T(8,128)(2,1)S(1)}, u32[]{:S(2)}, u32[]{:S(2)}) collective-permute-start(bf16[16,32,128]{2,1,0:T(8,128)(2,1)S(1)} %collective-permute-done.2.refs_4_), channel_id=1, source_target_pairs={{0,2},{2,4},{4,6},{6,8},{8,10},{10,12},{12,14},{14,0},{1,3},{3,5},... | collective-permute-start | bytes 393224 | tf_op jit(solution)/shard_map/ppermute | solution.py:477
  21.8 1.0 %collective-permute-start.3 = (bf16[16,32,128]{2,1,0:T(8,128)(2,1)S(1)}, bf16[16,32,128]{2,1,0:T(8,128)(2,1)S(1)}, u32[]{:S(2)}, u32[]{:S(2)}) collective-permute-start(bf16[16,32,128]{2,1,0:T(8,128)(2,1)S(1)} %collective-permute-done.2.refs_4_), channel_id=1, source_target_pairs={{0,14},{2,0},{4,2},{6,4},{8,6},{10,8},{12,10},{14,12},{1,15},{3,1}... | collective-permute-start | bytes 393224 | tf_op jit(solution)/shard_map/ppermute | solution.py:477
  22.9 0.8 copy.9
  25.3 1.4 %note.1 = s32[8,1,40]{2,1,0:T(1,128)} custom-call(s32[1,8]{1,0:T(1,128)} %send_ref.5, s32[8,1,32]{2,1,0:T(1,128)} %bitcast.20, s32[4,1,2]{2,1,0:T(1,128)} %copy-done.8), custom_call_target="tpu_custom_call" | custom-call | tf_op jit(solution)/shard_map/note/pallas_call | solution.py:284
  26.7 4.8 %all-to-all-start.1 = ((s32[8,1,40]{2,1,0:T(1,128)}), s32[8,1,40]{2,1,0:T(1,128)S(1)}, u32[]{:S(2)}, u32[]{:S(2)}) async-start(s32[8,1,40]{2,1,0:T(1,128)} %note.1), calls=%async_computation.1 | async-start | bytes 8192 | tf_op jit(solution)/shard_map/all_to_all | solution.py:508
  31.6 1.4 %copy-done = bf16[16,64,704]{2,1,0:T(8,128)(2,1)S(1)} copy-done((bf16[16,64,704]{2,1,0:T(8,128)(2,1)S(1)}, bf16[16,64,704]{2,1,0:T(8,128)(2,1)}, u32[]{:S(2)}) %copy-start) | copy-done | bytes 1441816
  33.0 5.7 %products.1.y_ref = bf16[16,64,768]{2,1,0:T(8,128)(2,1)S(1)} custom-call(bf16[16,32,128]{2,1,0:T(8,128)(2,1)S(1)} %bitcast.13, bf16[128,128]{1,0:T(8,128)(2,1)S(1)} %fusion.perm_ref, bf16[16,64,704]{2,1,0:T(8,128)(2,1)S(1)} %copy-done), custom_call_target="tpu_custom_call" | custom-call | flops 301989888 | bytes 3200000 | tf_op jit(solution)/shard_map/products/pallas_call | solution.py:70
  38.8 1.2 %select.3 = (bf16[32,32,128]{2,1,0:T(8,128)(2,1)S(1)}, bf16[32,32,128]{2,1,0:T(8,128)(2,1)S(1)}, bf16[32,32,128]{2,1,0:T(8,128)(2,1)S(1)}, bf16[32,32,128]{2,1,0:T(8,128)(2,1)S(1)}, bf16[32,32,128]{2,1,0:T(8,128)(2,1)S(1)}) custom-call(s32[8,1,40]{2,1,0:T(1,128)S(1)} %all-to-all-done.1.note_ref.wanted_ref, bf16[16,32,128]{2,1,0:T(8,128)(2,1)S(1)} %bitcast.14, ...), custom_call_target="tpu_custom_call" | custom-call | tf_op jit(solution)/shard_map/select/pallas_call | solution.py:109
  40.2 1.5 %collective-permute-start.8 = (bf16[32,32,128]{2,1,0:T(8,128)(2,1)S(1)}, bf16[32,32,128]{2,1,0:T(8,128)(2,1)S(1)}, u32[]{:S(2)}, u32[]{:S(2)}) collective-permute-start(bf16[32,32,128]{2,1,0:T(8,128)(2,1)S(1)} %get-tuple-element.31), channel_id=1, source_target_pairs={{0,16},{1,17},{16,32},{17,33},{32,48},{33,49},{48,0},{49,1},{2,18}... | collective-permute-start | bytes 786440 | tf_op jit(solution)/shard_map/ppermute | solution.py:487
  41.7 0.9 %collective-permute-start.10 = (bf16[32,32,128]{2,1,0:T(8,128)(2,1)S(1)}, bf16[32,32,128]{2,1,0:T(8,128)(2,1)}, u32[]{:S(2)}, u32[]{:S(2)}) collective-permute-start(bf16[32,32,128]{2,1,0:T(8,128)(2,1)S(1)} %get-tuple-element.33), channel_id=1, source_target_pairs={{0,32},{1,33},{16,48},{17,49},{32,0},{33,1},{48,16},{49,17},{2,34}... | collective-permute-start | bytes 786440 | tf_op jit(solution)/shard_map/ppermute | solution.py:487
  42.6 2.0 %collective-permute-start.11 = (bf16[32,32,128]{2,1,0:T(8,128)(2,1)S(1)}, bf16[32,32,128]{2,1,0:T(8,128)(2,1)}, u32[]{:S(2)}, u32[]{:S(2)}) collective-permute-start(bf16[32,32,128]{2,1,0:T(8,128)(2,1)S(1)} %get-tuple-element.34), channel_id=1, source_target_pairs={{0,33},{1,32},{16,49},{17,48},{32,1},{33,0},{48,17},{49,16},{2,35}... | collective-permute-start | bytes 786440 | tf_op jit(solution)/shard_map/ppermute | solution.py:487
  45.2 1.5 %select.4 = (bf16[32,32,128]{2,1,0:T(8,128)(2,1)}, bf16[32,32,128]{2,1,0:T(8,128)(2,1)}) custom-call(s32[8,1,40]{2,1,0:T(1,128)S(1)} %all-to-all-done.1.note_ref.wanted_ref, bf16[16,32,128]{2,1,0:T(8,128)(2,1)S(1)} %bitcast.15, bf16[16,32,128]{2,1,0:T(8,128)(2,1)S(1)} %collective-permute-done.refs_1_, ...), custom_call_target="tpu_custom_call" | custom-call | tf_op jit(solution)/shard_map/select/pallas_call | solution.py:109
  46.7 1.9 %collective-permute-start.13 = (bf16[32,32,128]{2,1,0:T(8,128)(2,1)}, bf16[32,32,128]{2,1,0:T(8,128)(2,1)}, u32[]{:S(2)}, u32[]{:S(2)}) collective-permute-start(bf16[32,32,128]{2,1,0:T(8,128)(2,1)} %get-tuple-element.36), channel_id=1, source_target_pairs={{0,49},{1,48},{16,1},{17,0},{32,17},{33,16},{48,33},{49,32},{2,51}... | collective-permute-start | bytes 786440 | tf_op jit(solution)/shard_map/ppermute | solution.py:487
  48.6 0.8 collective-permute-done.8.refs_2_
  50.1 1.4 %plane.1 = s32[8,1,64]{2,1,0:T(1,128)} custom-call(s32[8,1,40]{2,1,0:T(1,128)} %copy-done.2), custom_call_target="tpu_custom_call" | custom-call | tf_op jit(solution)/shard_map/plane/pallas_call | solution.py:301
  51.5 4.4 %all-to-all-start.2 = ((s32[8,1,64]{2,1,0:T(1,128)}), s32[8,1,64]{2,1,0:T(1,128)S(1)}, u32[]{:S(2)}, u32[]{:S(2)}) async-start(s32[8,1,64]{2,1,0:T(1,128)} %plane.1), calls=%async_computation.2 | async-start | bytes 8192 | tf_op jit(solution)/shard_map/all_to_all | solution.py:516
  55.9 4.7 %slots.1.slot_ref = s32[16,11]{1,0:T(8,128)} custom-call(s32[16,11]{1,0:T(8,128)} %columns_ref.1, s32[8,1,32]{2,1,0:T(1,128)} %bitcast.21), custom_call_target="tpu_custom_call" | custom-call | flops 1000000 | bytes 2000000 | tf_op jit(solution)/shard_map/slots/pallas_call | solution.py:338
  62.7 0.8 all-to-all-done.2.codes_ref
  63.5 4.9 %collective-permute-done.13.refs_7_ = bf16[32,32,128]{2,1,0:T(8,128)(2,1)} collective-permute-done((bf16[32,32,128]{2,1,0:T(8,128)(2,1)}, bf16[32,32,128]{2,1,0:T(8,128)(2,1)}, u32[]{:S(2)}, u32[]{:S(2)}) %collective-permute-start.13) | collective-permute-done | bytes 262176 | tf_op jit(solution)/shard_map/ppermute | solution.py:487
  68.4 2.7 %first.1 = (bf16[2,64,768]{2,1,0:T(8,128)(2,1)S(1)}, bf16[273,32,128]{2,1,0:T(8,128)(2,1)S(1)}) custom-call(s32[16,11]{1,0:T(8,128)} %slots.1.slot_ref, s32[1,8]{1,0:T(1,128)S(1)} %copy-done.4, s32[8,1,64]{2,1,0:T(1,128)S(1)} %all-to-all-done.2.codes_ref, bf16[16,64,768]{2,1,0:T(8,128)(2,1)S(1)} %products.1.y_ref, bf16[16,32,128]{2,1,0:T(8,128)(2,1)S(1)} %bitcast.17, ...), custom_call_target="tpu_custom_call" | custom-call | flops 100663296 | bytes 5000000 | tf_op jit(solution)/shard_map/first/pallas_call | solution.py:210
  71.1 3.2 %collective-permute-start.15 = (bf16[2,64,768]{2,1,0:T(8,128)(2,1)S(1)}, bf16[2,64,768]{2,1,0:T(8,128)(2,1)S(1)}, u32[]{:S(2)}, u32[]{:S(2)}) collective-permute-start(bf16[2,64,768]{2,1,0:T(8,128)(2,1)S(1)} %get-tuple-element.42), channel_id=1, source_target_pairs={{0,128},{64,192},{128,0},{192,64},{1,129},{65,193},{129,1},{193,65... | collective-permute-start | bytes 589832 | tf_op jit(solution)/shard_map/ppermute | solution.py:477
  74.4 1.5 %followers.1 = (bf16[2,64,768]{2,1,0:T(8,128)(2,1)S(1)}, bf16[2,64,768]{2,1,0:T(8,128)(2,1)S(1)}, bf16[2,64,768]{2,1,0:T(8,128)(2,1)S(1)}) custom-call(s32[16,11]{1,0:T(8,128)} %slots.1.slot_ref, s32[1,8]{1,0:T(1,128)S(1)} %copy-done.4, s32[8,1,64]{2,1,0:T(1,128)S(1)} %all-to-all-done.2.codes_ref, bf16[16,64,768]{2,1,0:T(8,128)(2,1)S(1)} %products.1.y_ref, ...), custom_call_target="tpu_custom_call" | custom-call | flops 100663296 | bytes 5000000 | tf_op jit(solution)/shard_map/followers/pallas_call | solution.py:224
  76.5 2.7 %collective-permute-start.16 = (bf16[2,64,768]{2,1,0:T(8,128)(2,1)S(1)}, bf16[2,64,768]{2,1,0:T(8,128)(2,1)S(1)}, u32[]{:S(2)}, u32[]{:S(2)}) collective-permute-start(bf16[2,64,768]{2,1,0:T(8,128)(2,1)S(1)} %get-tuple-element.43), channel_id=1, source_target_pairs={{0,192},{64,0},{128,64},{192,128},{1,193},{65,1},{129,65},{193,129... | collective-permute-start | bytes 589832 | tf_op jit(solution)/shard_map/ppermute | solution.py:477
  79.2 2.9 %leaders.1 = (bf16[8,64,768]{2,1,0:T(8,128)(2,1)S(1)}, s32[8,128]{1,0:T(8,128)S(1)}) custom-call(s32[16,11]{1,0:T(8,128)} %slots.1.slot_ref, s32[8,1,64]{2,1,0:T(1,128)S(1)} %all-to-all-done.2.codes_ref, bf16[16,64,768]{2,1,0:T(8,128)(2,1)S(1)} %products.1.y_ref, bf16[273,32,128]{2,1,0:T(8,128)(2,1)S(1)} %get-tuple-element.37.table.refs_0_), custom_call_target="tpu_custom_call" | custom-call | flops 100663296 | bytes 5000000 | tf_op jit(solution)/shard_map/leaders/pallas_call | solution.py:236
  82.1 2.0 %collective-permute-done.14.refs_1_ = bf16[2,64,768]{2,1,0:T(8,128)(2,1)S(1)} collective-permute-done((bf16[2,64,768]{2,1,0:T(8,128)(2,1)S(1)}, bf16[2,64,768]{2,1,0:T(8,128)(2,1)S(1)}, u32[]{:S(2)}, u32[]{:S(2)}) %collective-permute-start.14) | collective-permute-done | bytes 196640 | tf_op jit(solution)/shard_map/ppermute | solution.py:477
  84.1 3.5 %merge.1 = (bf16[8,64,1408]{2,1,0:T(8,128)(2,1)}, s32[8,22]{1,0:T(8,128)}) custom-call(s32[1,8]{1,0:T(1,128)S(1)} %copy-done.5, bf16[8,64,768]{2,1,0:T(8,128)(2,1)S(1)} %get-tuple-element.38.lead_ref, s32[8,128]{1,0:T(8,128)S(1)} %get-tuple-element.39.own_labels_ref, bf16[2,64,768]{2,1,0:T(8,128)(2,1)S(1)} %get-tuple-element.40.refs_0_, ...), custom_call_target="tpu_custom_call" | custom-call | tf_op jit(solution)/shard_map/merge/pallas_call | solution.py:450
  (44 shorter events, 6.3 us)
Async XLA Ops:
  1.6 18.0 %collective-permute-start.2 = (bf16[16,32,128]{2,1,0:T(8,128)(2,1)S(1)}, bf16[16,32,128]{2,1,0:T(8,128)(2,1)S(1)}, u32[]{:S(2)}, u32[]{:S(2)}) collective-permute-start(bf16[16,32,128]{2,1,0:T(8,128)(2,1)S(1)} %bitcast.8), channel_id=1, source_target_pairs={{0,8},{2,10},{4,12},{6,14},{8,0},{10,2},{12,4},{14,6},{1,9},{3,11}... | collective-permute-start | bytes 393224 | tf_op jit(solution)/shard_map/ppermute | solution.py:477
  8.8 13.0 %collective-permute-start.6 = (bf16[16,32,128]{2,1,0:T(8,128)(2,1)S(1)}, bf16[16,32,128]{2,1,0:T(8,128)(2,1)S(1)}, u32[]{:S(2)}, u32[]{:S(2)}) collective-permute-start(bf16[16,32,128]{2,1,0:T(8,128)(2,1)S(1)} %bitcast.9), channel_id=1, source_target_pairs={{0,14},{2,0},{4,2},{6,4},{8,6},{10,8},{12,10},{14,12},{1,15},{3,1}... | collective-permute-start | bytes 393224 | tf_op jit(solution)/shard_map/ppermute | solution.py:477
  8.9 29.8 %collective-permute-start.5 = (bf16[16,32,128]{2,1,0:T(8,128)(2,1)S(1)}, bf16[16,32,128]{2,1,0:T(8,128)(2,1)S(1)}, u32[]{:S(2)}, u32[]{:S(2)}) collective-permute-start(bf16[16,32,128]{2,1,0:T(8,128)(2,1)S(1)} %bitcast.10), channel_id=1, source_target_pairs={{0,12},{2,14},{4,0},{6,2},{8,4},{10,6},{12,8},{14,10},{1,13},{3,15... | collective-permute-start | bytes 393224 | tf_op jit(solution)/shard_map/ppermute | solution.py:477
  9.0 29.7 %collective-permute-start.1 = (bf16[16,32,128]{2,1,0:T(8,128)(2,1)S(1)}, bf16[16,32,128]{2,1,0:T(8,128)(2,1)S(1)}, u32[]{:S(2)}, u32[]{:S(2)}) collective-permute-start(bf16[16,32,128]{2,1,0:T(8,128)(2,1)S(1)} %bitcast.11), channel_id=1, source_target_pairs={{0,4},{2,6},{4,8},{6,10},{8,12},{10,14},{12,0},{14,2},{1,5},{3,7},... | collective-permute-start | bytes 393224 | tf_op jit(solution)/shard_map/ppermute | solution.py:477
  11.9 26.9 %collective-permute-start = (bf16[16,32,128]{2,1,0:T(8,128)(2,1)S(1)}, bf16[16,32,128]{2,1,0:T(8,128)(2,1)S(1)}, u32[]{:S(2)}, u32[]{:S(2)}) collective-permute-start(bf16[16,32,128]{2,1,0:T(8,128)(2,1)S(1)} %bitcast.12), channel_id=1, source_target_pairs={{0,2},{2,4},{4,6},{6,8},{8,10},{10,12},{12,14},{14,0},{1,3},{3,5},... | collective-permute-start | bytes 393224 | tf_op jit(solution)/shard_map/ppermute | solution.py:477
  15.0 9.6 %all-to-all-start = ((s32[4,1,2]{2,1,0:T(1,128)}), s32[4,1,2]{2,1,0:T(1,128)S(1)}, u32[]{:S(2)}, u32[]{:S(2)}) async-start(s32[4,1,2]{2,1,0:T(1,128)} %codes.1), calls=%async_computation | async-start | bytes 4096 | tf_op jit(solution)/shard_map/all_to_all | solution.py:505
  19.5 19.2 %collective-permute-start.4 = (bf16[16,32,128]{2,1,0:T(8,128)(2,1)S(1)}, bf16[16,32,128]{2,1,0:T(8,128)(2,1)S(1)}, u32[]{:S(2)}, u32[]{:S(2)}) collective-permute-start(bf16[16,32,128]{2,1,0:T(8,128)(2,1)S(1)} %collective-permute-done.2.refs_4_), channel_id=1, source_target_pairs={{0,2},{2,4},{4,6},{6,8},{8,10},{10,12},{12,14},{14,0},{1,3},{3,5},... | collective-permute-start | bytes 393224 | tf_op jit(solution)/shard_map/ppermute | solution.py:477
  21.8 16.9 %collective-permute-start.3 = (bf16[16,32,128]{2,1,0:T(8,128)(2,1)S(1)}, bf16[16,32,128]{2,1,0:T(8,128)(2,1)S(1)}, u32[]{:S(2)}, u32[]{:S(2)}) collective-permute-start(bf16[16,32,128]{2,1,0:T(8,128)(2,1)S(1)} %collective-permute-done.2.refs_4_), channel_id=1, source_target_pairs={{0,14},{2,0},{4,2},{6,4},{8,6},{10,8},{12,10},{14,12},{1,15},{3,1}... | collective-permute-start | bytes 393224 | tf_op jit(solution)/shard_map/ppermute | solution.py:477
  24.7 0.6 copy-start.8
  26.7 12.0 %all-to-all-start.1 = ((s32[8,1,40]{2,1,0:T(1,128)}), s32[8,1,40]{2,1,0:T(1,128)S(1)}, u32[]{:S(2)}, u32[]{:S(2)}) async-start(s32[8,1,40]{2,1,0:T(1,128)} %note.1), calls=%async_computation.1 | async-start | bytes 8192 | tf_op jit(solution)/shard_map/all_to_all | solution.py:508
  31.5 1.4 %copy-start = (bf16[16,64,704]{2,1,0:T(8,128)(2,1)S(1)}, bf16[16,64,704]{2,1,0:T(8,128)(2,1)}, u32[]{:S(2)}) copy-start(bf16[16,64,704]{2,1,0:T(8,128)(2,1)} %a_hbm.1) | copy-start | bytes 4325380
  38.7 29.7 %copy-start.4 = (s32[1,8]{1,0:T(1,128)S(1)}, s32[1,8]{1,0:T(1,128)}, u32[]{:S(2)}) copy-start(s32[1,8]{1,0:T(1,128)} %send_ref.5) | copy-start | bytes 100
  38.7 11.4 %copy-start.2 = (s32[8,1,40]{2,1,0:T(1,128)}, s32[8,1,40]{2,1,0:T(1,128)S(1)}, u32[]{:S(2)}) copy-start(s32[8,1,40]{2,1,0:T(1,128)S(1)} %all-to-all-done.1.note_ref.wanted_ref) | copy-start | bytes 3844
  40.0 6.7 %collective-permute-start.7 = (bf16[32,32,128]{2,1,0:T(8,128)(2,1)S(1)}, bf16[32,32,128]{2,1,0:T(8,128)(2,1)S(1)}, u32[]{:S(2)}, u32[]{:S(2)}) collective-permute-start(bf16[32,32,128]{2,1,0:T(8,128)(2,1)S(1)} %get-tuple-element.30), channel_id=1, source_target_pairs={{0,1},{1,0},{16,17},{17,16},{32,33},{33,32},{48,49},{49,48},{2,3},... | collective-permute-start | bytes 786440 | tf_op jit(solution)/shard_map/ppermute | solution.py:487
  40.2 9.1 %collective-permute-start.8 = (bf16[32,32,128]{2,1,0:T(8,128)(2,1)S(1)}, bf16[32,32,128]{2,1,0:T(8,128)(2,1)S(1)}, u32[]{:S(2)}, u32[]{:S(2)}) collective-permute-start(bf16[32,32,128]{2,1,0:T(8,128)(2,1)S(1)} %get-tuple-element.31), channel_id=1, source_target_pairs={{0,16},{1,17},{16,32},{17,33},{32,48},{33,49},{48,0},{49,1},{2,18}... | collective-permute-start | bytes 786440 | tf_op jit(solution)/shard_map/ppermute | solution.py:487
  41.7 21.8 %collective-permute-start.10 = (bf16[32,32,128]{2,1,0:T(8,128)(2,1)S(1)}, bf16[32,32,128]{2,1,0:T(8,128)(2,1)}, u32[]{:S(2)}, u32[]{:S(2)}) collective-permute-start(bf16[32,32,128]{2,1,0:T(8,128)(2,1)S(1)} %get-tuple-element.33), channel_id=1, source_target_pairs={{0,32},{1,33},{16,48},{17,49},{32,0},{33,1},{48,16},{49,17},{2,34}... | collective-permute-start | bytes 786440 | tf_op jit(solution)/shard_map/ppermute | solution.py:487
  42.6 20.9 %collective-permute-start.11 = (bf16[32,32,128]{2,1,0:T(8,128)(2,1)S(1)}, bf16[32,32,128]{2,1,0:T(8,128)(2,1)}, u32[]{:S(2)}, u32[]{:S(2)}) collective-permute-start(bf16[32,32,128]{2,1,0:T(8,128)(2,1)S(1)} %get-tuple-element.34), channel_id=1, source_target_pairs={{0,33},{1,32},{16,49},{17,48},{32,1},{33,0},{48,17},{49,16},{2,35}... | collective-permute-start | bytes 786440 | tf_op jit(solution)/shard_map/ppermute | solution.py:487
  44.6 18.9 %collective-permute-start.12 = (bf16[32,32,128]{2,1,0:T(8,128)(2,1)S(1)}, bf16[32,32,128]{2,1,0:T(8,128)(2,1)}, u32[]{:S(2)}, u32[]{:S(2)}) collective-permute-start(bf16[32,32,128]{2,1,0:T(8,128)(2,1)S(1)} %get-tuple-element.35), channel_id=1, source_target_pairs={{0,48},{1,49},{16,0},{17,1},{32,16},{33,17},{48,32},{49,33},{2,50}... | collective-permute-start | bytes 786440 | tf_op jit(solution)/shard_map/ppermute | solution.py:487
  46.7 2.6 %copy-start.6 = (bf16[32,32,128]{2,1,0:T(8,128)(2,1)}, bf16[32,32,128]{2,1,0:T(8,128)(2,1)S(1)}, u32[]{:S(2)}) copy-start(bf16[32,32,128]{2,1,0:T(8,128)(2,1)S(1)} %collective-permute-done.7.refs_1_) | copy-start | bytes 786436
  46.7 21.7 %collective-permute-start.13 = (bf16[32,32,128]{2,1,0:T(8,128)(2,1)}, bf16[32,32,128]{2,1,0:T(8,128)(2,1)}, u32[]{:S(2)}, u32[]{:S(2)}) collective-permute-start(bf16[32,32,128]{2,1,0:T(8,128)(2,1)} %get-tuple-element.36), channel_id=1, source_target_pairs={{0,49},{1,48},{16,1},{17,0},{32,17},{33,16},{48,33},{49,32},{2,51}... | collective-permute-start | bytes 786440 | tf_op jit(solution)/shard_map/ppermute | solution.py:487
  49.3 0.7 copy-start.7
  50.0 18.4 %collective-permute-start.9 = (bf16[32,32,128]{2,1,0:T(8,128)(2,1)}, bf16[32,32,128]{2,1,0:T(8,128)(2,1)}, u32[]{:S(2)}, u32[]{:S(2)}) collective-permute-start(bf16[32,32,128]{2,1,0:T(8,128)(2,1)} %get-tuple-element.32), channel_id=1, source_target_pairs={{0,17},{1,16},{16,33},{17,32},{32,49},{33,48},{48,1},{49,0},{2,19}... | collective-permute-start | bytes 786440 | tf_op jit(solution)/shard_map/ppermute | solution.py:487
  51.5 12.1 %all-to-all-start.2 = ((s32[8,1,64]{2,1,0:T(1,128)}), s32[8,1,64]{2,1,0:T(1,128)S(1)}, u32[]{:S(2)}, u32[]{:S(2)}) async-start(s32[8,1,64]{2,1,0:T(1,128)} %plane.1), calls=%async_computation.2 | async-start | bytes 8192 | tf_op jit(solution)/shard_map/all_to_all | solution.py:516
  60.6 0.7 copy-start.3
  62.0 0.7 copy-start.1
  71.1 11.0 %collective-permute-start.15 = (bf16[2,64,768]{2,1,0:T(8,128)(2,1)S(1)}, bf16[2,64,768]{2,1,0:T(8,128)(2,1)S(1)}, u32[]{:S(2)}, u32[]{:S(2)}) collective-permute-start(bf16[2,64,768]{2,1,0:T(8,128)(2,1)S(1)} %get-tuple-element.42), channel_id=1, source_target_pairs={{0,128},{64,192},{128,0},{192,64},{1,129},{65,193},{129,1},{193,65... | collective-permute-start | bytes 589832 | tf_op jit(solution)/shard_map/ppermute | solution.py:477
  75.9 8.2 %collective-permute-start.14 = (bf16[2,64,768]{2,1,0:T(8,128)(2,1)S(1)}, bf16[2,64,768]{2,1,0:T(8,128)(2,1)S(1)}, u32[]{:S(2)}, u32[]{:S(2)}) collective-permute-start(bf16[2,64,768]{2,1,0:T(8,128)(2,1)S(1)} %get-tuple-element.41), channel_id=1, source_target_pairs={{0,64},{64,128},{128,192},{192,0},{1,65},{65,129},{129,193},{193,1... | collective-permute-start | bytes 589832 | tf_op jit(solution)/shard_map/ppermute | solution.py:477
  76.5 7.6 %copy-start.5 = (s32[1,8]{1,0:T(1,128)S(1)}, s32[1,8]{1,0:T(1,128)}, u32[]{:S(2)}) copy-start(s32[1,8]{1,0:T(1,128)} %slots_ref.3) | copy-start | bytes 100
  76.5 7.6 %collective-permute-start.16 = (bf16[2,64,768]{2,1,0:T(8,128)(2,1)S(1)}, bf16[2,64,768]{2,1,0:T(8,128)(2,1)S(1)}, u32[]{:S(2)}, u32[]{:S(2)}) collective-permute-start(bf16[2,64,768]{2,1,0:T(8,128)(2,1)S(1)} %get-tuple-element.43), channel_id=1, source_target_pairs={{0,192},{64,0},{128,64},{192,128},{1,193},{65,1},{129,65},{193,129... | collective-permute-start | bytes 589832 | tf_op jit(solution)/shard_map/ppermute | solution.py:477

commit v9 on v7

--- a/solution.py
+++ b/solution.py
@@ -520,8 +520,8 @@
         parts += [pltpu.with_memory_space_constraint(moved[b], pltpu.HBM) for b in range(NX * NC)]
 
     sent = {}
-    sent[2], table = first_followers((2,), words, send_order, codes, own, y, parts)
-    sent[1], sent[3], sent[0] = followers((1, 3, 0), words, send_order, codes, y, table)
+    sent[2], sent[1], table = first_followers((2, 1), words, send_order, codes, own, y, parts)
+    sent[3], sent[0] = followers((3, 0), words, send_order, codes, y, table)
     arrived = [shift(sent[s], "grp", NG, s) for s in range(NG)]
     lead, lead_labels = leaders(words, codes, y, table)
     return tuple(merge(partner_slot, lead, lead_labels, arrived))

time: 88.1 us -> 89.4 us (1.015)
  the two profiles are of different devices: /device:TPU:2 before, /device:TPU:11 now
where the time goes in v9:
time: 89.4 us; the launch traced here: 88 us
  starting transfers between devices  42.5 us (48%)
  Pallas kernels  26.2 us (29%)
  waiting for transfers between devices  10.5 us (12%)
  local copies, waits for them, and re-layouts  7.66 us (9%)
  between operations  1.02 us (1%)
    ppermute x10, starting transfers between devices, shift(): lax.ppermute(value, axis, [(i, (i + by) % size) for i in range(size)])  17.6 us
    ppermute x7, starting transfers between devices, cross(): return lax.ppermute(value, ('x', 'core'), pairs)  9.25 us
    all_to_all x1, starting transfers between devices, per_device(): lax.all_to_all(note, ('x', 'core'), split_axis=0, concat_axis=0, tiled=True)  7.66 us
    unnamed x22, local copies, waits for them, and re-layouts  5.8 us
    ppermute x10, waiting for transfers between devices, shift(): lax.ppermute(value, axis, [(i, (i + by) % size) for i in range(size)])  5.56 us
    ppermute x7, waiting for transfers between devices, cross(): return lax.ppermute(value, ('x', 'core'), pairs)  4.93 us
    pallas_call x1, Pallas kernels, slot_words(): pl.pallas_call(slot_kernel, out_shape=jax.ShapeDtypeStruct((ROWS, K), jnp...  4.8 us
    all_to_all x1, starting transfers between devices, per_device(): lax.all_to_all(code_rows(partner_slot), 'grp', split_axis=0, concat_axis=...  4.35 us
  transfers between devices with their start and end apart: 20, of which 3 were waited for; matrix products, arithmetic and copies ran while one was open for 3% of the time, Pallas kernels for 21%

profile of v9, /device:TPU:11, one launch (start us, length us, event | category | flops | bytes accessed | tf_op | source)
XLA Modules:
  0.0 88.0 jit_solution(902781334706127648)
XLA Ops:
  0.6 0.9 %copy.14 = bf16[2,8,32,128]{3,2,1,0:T(8,128)(2,1)S(1)} copy(bf16[2,8,32,128]{3,1,2,0:T(8,128)(2,1)} %bitcast.17) | data formatting | bytes 262144
  1.6 7.0 %collective-permute-start.2 = (bf16[16,32,128]{2,1,0:T(8,128)(2,1)S(1)}, bf16[16,32,128]{2,1,0:T(8,128)(2,1)S(1)}, u32[]{:S(2)}, u32[]{:S(2)}) collective-permute-start(bf16[16,32,128]{2,1,0:T(8,128)(2,1)S(1)} %bitcast.8), channel_id=1, source_target_pairs={{0,8},{2,10},{4,12},{6,14},{8,0},{10,2},{12,4},{14,6},{1,9},{3,11}... | collective-permute-start | bytes 393224 | tf_op jit(solution)/shard_map/ppermute | solution.py:472
  8.6 2.4 %collective-permute-start.1 = (bf16[16,32,128]{2,1,0:T(8,128)(2,1)S(1)}, bf16[16,32,128]{2,1,0:T(8,128)(2,1)S(1)}, u32[]{:S(2)}, u32[]{:S(2)}) collective-permute-start(bf16[16,32,128]{2,1,0:T(8,128)(2,1)S(1)} %bitcast.11), channel_id=1, source_target_pairs={{0,4},{2,6},{4,8},{6,10},{8,12},{10,14},{12,0},{14,2},{1,5},{3,7},... | collective-permute-start | bytes 393224 | tf_op jit(solution)/shard_map/ppermute | solution.py:472
  10.9 1.5 %collective-permute-start = (bf16[16,32,128]{2,1,0:T(8,128)(2,1)S(1)}, bf16[16,32,128]{2,1,0:T(8,128)(2,1)S(1)}, u32[]{:S(2)}, u32[]{:S(2)}) collective-permute-start(bf16[16,32,128]{2,1,0:T(8,128)(2,1)S(1)} %bitcast.12), channel_id=1, source_target_pairs={{0,2},{2,4},{4,6},{6,8},{8,10},{10,12},{12,14},{14,0},{1,3},{3,5},... | collective-permute-start | bytes 393224 | tf_op jit(solution)/shard_map/ppermute | solution.py:472
  12.4 1.3 %codes.1 = s32[4,1,2]{2,1,0:T(1,128)} custom-call(s32[1,8]{1,0:T(1,128)} %slots_ref.3), custom_call_target="tpu_custom_call" | custom-call | tf_op jit(solution)/shard_map/codes/pallas_call | solution.py:257
  13.6 4.3 %all-to-all-start = ((s32[4,1,2]{2,1,0:T(1,128)}), s32[4,1,2]{2,1,0:T(1,128)S(1)}, u32[]{:S(2)}, u32[]{:S(2)}) async-start(s32[4,1,2]{2,1,0:T(1,128)} %codes.1), calls=%async_computation | async-start | bytes 4096 | tf_op jit(solution)/shard_map/all_to_all | solution.py:500
  18.0 2.0 %collective-permute-start.4 = (bf16[16,32,128]{2,1,0:T(8,128)(2,1)S(1)}, bf16[16,32,128]{2,1,0:T(8,128)(2,1)S(1)}, u32[]{:S(2)}, u32[]{:S(2)}) collective-permute-start(bf16[16,32,128]{2,1,0:T(8,128)(2,1)S(1)} %collective-permute-done.2.refs_4_), channel_id=1, source_target_pairs={{0,2},{2,4},{4,6},{6,8},{8,10},{10,12},{12,14},{14,0},{1,3},{3,5},... | collective-permute-start | bytes 393224 | tf_op jit(solution)/shard_map/ppermute | solution.py:472
  20.8 1.2 %reshape.31.p_ref = bf16[16,64,64]{2,1,0:T(8,128)(2,1)S(1)} reshape(bf16[16,4096]{1,0:T(8,128)(2,1)} %param.7) | data formatting | bytes 262144 | tf_op jit(solution)/shard_map/reshape | solution.py:509
  22.0 0.8 copy.10.fetch_ref
  24.0 1.4 %note.1 = s32[8,1,40]{2,1,0:T(1,128)} custom-call(s32[1,8]{1,0:T(1,128)} %send_ref.5, s32[8,1,32]{2,1,0:T(1,128)} %bitcast.19, s32[4,1,2]{2,1,0:T(1,128)} %copy-done.9), custom_call_target="tpu_custom_call" | custom-call | tf_op jit(solution)/shard_map/note/pallas_call | solution.py:280
  25.4 7.7 %all-to-all-start.1 = ((s32[8,1,40]{2,1,0:T(1,128)}), s32[8,1,40]{2,1,0:T(1,128)S(1)}, u32[]{:S(2)}, u32[]{:S(2)}) async-start(s32[8,1,40]{2,1,0:T(1,128)} %note.1), calls=%async_computation.1 | async-start | bytes 8192 | tf_op jit(solution)/shard_map/all_to_all | solution.py:503
  33.1 1.4 %copy-done = bf16[16,64,704]{2,1,0:T(8,128)(2,1)S(1)} copy-done((bf16[16,64,704]{2,1,0:T(8,128)(2,1)S(1)}, bf16[16,64,704]{2,1,0:T(8,128)(2,1)}, u32[]{:S(2)}) %copy-start) | copy-done | bytes 1441816
  34.5 2.9 %products.1.y_ref = bf16[16,64,768]{2,1,0:T(8,128)(2,1)S(1)} custom-call(bf16[16,64,64]{2,1,0:T(8,128)(2,1)S(1)} %reshape.31.p_ref, bf16[128,128]{1,0:T(8,128)(2,1)S(1)} %fusion.perm_ref, bf16[16,64,704]{2,1,0:T(8,128)(2,1)S(1)} %copy-done), custom_call_target="tpu_custom_call" | custom-call | flops 301989888 | bytes 3200000 | tf_op jit(solution)/shard_map/products/pallas_call | solution.py:66
  37.6 1.2 %select.3 = (bf16[32,32,128]{2,1,0:T(8,128)(2,1)S(1)}, bf16[32,32,128]{2,1,0:T(8,128)(2,1)S(1)}, bf16[32,32,128]{2,1,0:T(8,128)(2,1)S(1)}, bf16[32,32,128]{2,1,0:T(8,128)(2,1)S(1)}, bf16[32,32,128]{2,1,0:T(8,128)(2,1)S(1)}) custom-call(s32[8,1,40]{2,1,0:T(1,128)S(1)} %all-to-all-done.1.note_ref.wanted_ref, bf16[16,32,128]{2,1,0:T(8,128)(2,1)S(1)} %bitcast.13, ...), custom_call_target="tpu_custom_call" | custom-call | tf_op jit(solution)/shard_map/select/pallas_call | solution.py:105
  39.2 1.2 %collective-permute-start.8 = (bf16[32,32,128]{2,1,0:T(8,128)(2,1)S(1)}, bf16[32,32,128]{2,1,0:T(8,128)(2,1)S(1)}, u32[]{:S(2)}, u32[]{:S(2)}) collective-permute-start(bf16[32,32,128]{2,1,0:T(8,128)(2,1)S(1)} %get-tuple-element.31), channel_id=1, source_target_pairs={{0,16},{1,17},{16,32},{17,33},{32,48},{33,49},{48,0},{49,1},{2,18}... | collective-permute-start | bytes 786440 | tf_op jit(solution)/shard_map/ppermute | solution.py:482
  40.4 1.2 %collective-permute-start.10 = (bf16[32,32,128]{2,1,0:T(8,128)(2,1)S(1)}, bf16[32,32,128]{2,1,0:T(8,128)(2,1)}, u32[]{:S(2)}, u32[]{:S(2)}) collective-permute-start(bf16[32,32,128]{2,1,0:T(8,128)(2,1)S(1)} %get-tuple-element.33), channel_id=1, source_target_pairs={{0,32},{1,33},{16,48},{17,49},{32,0},{33,1},{48,16},{49,17},{2,34}... | collective-permute-start | bytes 786440 | tf_op jit(solution)/shard_map/ppermute | solution.py:482
  41.6 2.4 %collective-permute-start.11 = (bf16[32,32,128]{2,1,0:T(8,128)(2,1)S(1)}, bf16[32,32,128]{2,1,0:T(8,128)(2,1)}, u32[]{:S(2)}, u32[]{:S(2)}) collective-permute-start(bf16[32,32,128]{2,1,0:T(8,128)(2,1)S(1)} %get-tuple-element.34), channel_id=1, source_target_pairs={{0,33},{1,32},{16,49},{17,48},{32,1},{33,0},{48,17},{49,16},{2,35}... | collective-permute-start | bytes 786440 | tf_op jit(solution)/shard_map/ppermute | solution.py:482
  44.3 1.5 %select.4 = (bf16[32,32,128]{2,1,0:T(8,128)(2,1)}, bf16[32,32,128]{2,1,0:T(8,128)(2,1)}) custom-call(s32[8,1,40]{2,1,0:T(1,128)S(1)} %all-to-all-done.1.note_ref.wanted_ref, bf16[16,32,128]{2,1,0:T(8,128)(2,1)S(1)} %bitcast.14, bf16[16,32,128]{2,1,0:T(8,128)(2,1)S(1)} %collective-permute-done.refs_1_, ...), custom_call_target="tpu_custom_call" | custom-call | tf_op jit(solution)/shard_map/select/pallas_call | solution.py:105
  45.8 1.8 %collective-permute-start.13 = (bf16[32,32,128]{2,1,0:T(8,128)(2,1)}, bf16[32,32,128]{2,1,0:T(8,128)(2,1)}, u32[]{:S(2)}, u32[]{:S(2)}) collective-permute-start(bf16[32,32,128]{2,1,0:T(8,128)(2,1)} %get-tuple-element.36), channel_id=1, source_target_pairs={{0,49},{1,48},{16,1},{17,0},{32,17},{33,16},{48,33},{49,32},{2,51}... | collective-permute-start | bytes 786440 | tf_op jit(solution)/shard_map/ppermute | solution.py:482
  48.4 1.9 %collective-permute-start.9 = (bf16[32,32,128]{2,1,0:T(8,128)(2,1)}, bf16[32,32,128]{2,1,0:T(8,128)(2,1)}, u32[]{:S(2)}, u32[]{:S(2)}) collective-permute-start(bf16[32,32,128]{2,1,0:T(8,128)(2,1)} %get-tuple-element.32), channel_id=1, source_target_pairs={{0,17},{1,16},{16,33},{17,32},{32,49},{33,48},{48,1},{49,0},{2,19}... | collective-permute-start | bytes 786440 | tf_op jit(solution)/shard_map/ppermute | solution.py:482
  50.3 1.4 %plane.1 = s32[8,1,64]{2,1,0:T(1,128)} custom-call(s32[8,1,40]{2,1,0:T(1,128)} %copy-done.2), custom_call_target="tpu_custom_call" | custom-call | tf_op jit(solution)/shard_map/plane/pallas_call | solution.py:297
  51.6 3.7 %all-to-all-start.2 = ((s32[8,1,64]{2,1,0:T(1,128)}), s32[8,1,64]{2,1,0:T(1,128)S(1)}, u32[]{:S(2)}, u32[]{:S(2)}) async-start(s32[8,1,64]{2,1,0:T(1,128)} %plane.1), calls=%async_computation.2 | async-start | bytes 8192 | tf_op jit(solution)/shard_map/all_to_all | solution.py:511
  55.3 4.8 %slots.1.slot_ref = s32[16,11]{1,0:T(8,128)} custom-call(s32[16,11]{1,0:T(8,128)} %columns_ref.1, s32[64,4]{1,0:T(8,128)} %copy-done.6), custom_call_target="tpu_custom_call" | custom-call | flops 1000000 | bytes 2000000 | tf_op jit(solution)/shard_map/slots/pallas_call | solution.py:333
  60.8 0.7 select.5.refs_0_
  62.3 4.9 %collective-permute-done.13.refs_7_ = bf16[32,32,128]{2,1,0:T(8,128)(2,1)} collective-permute-done((bf16[32,32,128]{2,1,0:T(8,128)(2,1)}, bf16[32,32,128]{2,1,0:T(8,128)(2,1)}, u32[]{:S(2)}, u32[]{:S(2)}) %collective-permute-start.13) | collective-permute-done | bytes 262176 | tf_op jit(solution)/shard_map/ppermute | solution.py:482
  67.2 2.9 %first.1 = (bf16[2,64,768]{2,1,0:T(8,128)(2,1)S(1)}, bf16[2,64,768]{2,1,0:T(8,128)(2,1)S(1)}, bf16[273,32,128]{2,1,0:T(8,128)(2,1)S(1)}) custom-call(s32[16,11]{1,0:T(8,128)} %slots.1.slot_ref, s32[1,8]{1,0:T(1,128)S(1)} %copy-done.4, s32[8,1,64]{2,1,0:T(1,128)S(1)} %all-to-all-done.2.codes_ref, bf16[16,64,768]{2,1,0:T(8,128)(2,1)S(1)} %products.1.y_ref, ...), custom_call_target="tpu_custom_call" | custom-call | flops 100663296 | bytes 5000000 | tf_op jit(solution)/shard_map/first/pallas_call | solution.py:206
  70.1 1.3 %collective-permute-start.14 = (bf16[2,64,768]{2,1,0:T(8,128)(2,1)S(1)}, bf16[2,64,768]{2,1,0:T(8,128)(2,1)S(1)}, u32[]{:S(2)}, u32[]{:S(2)}) collective-permute-start(bf16[2,64,768]{2,1,0:T(8,128)(2,1)S(1)} %get-tuple-element.41), channel_id=1, source_target_pairs={{0,64},{64,128},{128,192},{192,0},{1,65},{65,129},{129,193},{193,1... | collective-permute-start | bytes 589832 | tf_op jit(solution)/shard_map/ppermute | solution.py:472
  72.1 1.3 %followers.1 = (bf16[2,64,768]{2,1,0:T(8,128)(2,1)S(1)}, bf16[2,64,768]{2,1,0:T(8,128)(2,1)S(1)}) custom-call(s32[16,11]{1,0:T(8,128)} %slots.1.slot_ref, s32[1,8]{1,0:T(1,128)S(1)} %copy-done.4, s32[8,1,64]{2,1,0:T(1,128)S(1)} %all-to-all-done.2.codes_ref, bf16[16,64,768]{2,1,0:T(8,128)(2,1)S(1)} %products.1.y_ref, ...), custom_call_target="tpu_custom_call" | custom-call | flops 100663296 | bytes 5000000 | tf_op jit(solution)/shard_map/followers/pallas_call | solution.py:220
  73.4 2.0 %collective-permute-start.16 = (bf16[2,64,768]{2,1,0:T(8,128)(2,1)S(1)}, bf16[2,64,768]{2,1,0:T(8,128)(2,1)S(1)}, u32[]{:S(2)}, u32[]{:S(2)}) collective-permute-start(bf16[2,64,768]{2,1,0:T(8,128)(2,1)S(1)} %get-tuple-element.43), channel_id=1, source_target_pairs={{0,192},{64,0},{128,64},{192,128},{1,193},{65,1},{129,65},{193,129... | collective-permute-start | bytes 589832 | tf_op jit(solution)/shard_map/ppermute | solution.py:472
  75.5 2.9 %leaders.1 = (bf16[8,64,768]{2,1,0:T(8,128)(2,1)S(1)}, s32[8,128]{1,0:T(8,128)S(1)}) custom-call(s32[16,11]{1,0:T(8,128)} %slots.1.slot_ref, s32[8,1,64]{2,1,0:T(1,128)S(1)} %all-to-all-done.2.codes_ref, bf16[16,64,768]{2,1,0:T(8,128)(2,1)S(1)} %products.1.y_ref, bf16[273,32,128]{2,1,0:T(8,128)(2,1)S(1)} %get-tuple-element.37.table.refs_0_), custom_call_target="tpu_custom_call" | custom-call | flops 100663296 | bytes 5000000 | tf_op jit(solution)/shard_map/leaders/pallas_call | solution.py:232
  78.7 5.2 %collective-permute-done.16.refs_3_ = bf16[2,64,768]{2,1,0:T(8,128)(2,1)S(1)} collective-permute-done((bf16[2,64,768]{2,1,0:T(8,128)(2,1)S(1)}, bf16[2,64,768]{2,1,0:T(8,128)(2,1)S(1)}, u32[]{:S(2)}, u32[]{:S(2)}) %collective-permute-start.16) | collective-permute-done | bytes 196640 | tf_op jit(solution)/shard_map/ppermute | solution.py:472
  83.9 3.9 %merge.1 = (bf16[8,64,1408]{2,1,0:T(8,128)(2,1)}, s32[8,22]{1,0:T(8,128)}) custom-call(s32[1,8]{1,0:T(1,128)S(1)} %copy-done.5, bf16[8,64,768]{2,1,0:T(8,128)(2,1)S(1)} %get-tuple-element.38.lead_ref, s32[8,128]{1,0:T(8,128)S(1)} %get-tuple-element.39.own_labels_ref, bf16[2,64,768]{2,1,0:T(8,128)(2,1)S(1)} %get-tuple-element.40.refs_0_, ...), custom_call_target="tpu_custom_call" | custom-call | tf_op jit(solution)/shard_map/merge/pallas_call | solution.py:445
  (47 shorter events, 5.9 us)
Async XLA Ops:
  1.6 16.4 %collective-permute-start.2 = (bf16[16,32,128]{2,1,0:T(8,128)(2,1)S(1)}, bf16[16,32,128]{2,1,0:T(8,128)(2,1)S(1)}, u32[]{:S(2)}, u32[]{:S(2)}) collective-permute-start(bf16[16,32,128]{2,1,0:T(8,128)(2,1)S(1)} %bitcast.8), channel_id=1, source_target_pairs={{0,8},{2,10},{4,12},{6,14},{8,0},{10,2},{12,4},{14,6},{1,9},{3,11}... | collective-permute-start | bytes 393224 | tf_op jit(solution)/shard_map/ppermute | solution.py:472
  8.6 11.5 %collective-permute-start.6 = (bf16[16,32,128]{2,1,0:T(8,128)(2,1)S(1)}, bf16[16,32,128]{2,1,0:T(8,128)(2,1)S(1)}, u32[]{:S(2)}, u32[]{:S(2)}) collective-permute-start(bf16[16,32,128]{2,1,0:T(8,128)(2,1)S(1)} %bitcast.9), channel_id=1, source_target_pairs={{0,14},{2,0},{4,2},{6,4},{8,6},{10,8},{12,10},{14,12},{1,15},{3,1}... | collective-permute-start | bytes 393224 | tf_op jit(solution)/shard_map/ppermute | solution.py:472
  8.6 29.0 %collective-permute-start.5 = (bf16[16,32,128]{2,1,0:T(8,128)(2,1)S(1)}, bf16[16,32,128]{2,1,0:T(8,128)(2,1)S(1)}, u32[]{:S(2)}, u32[]{:S(2)}) collective-permute-start(bf16[16,32,128]{2,1,0:T(8,128)(2,1)S(1)} %bitcast.10), channel_id=1, source_target_pairs={{0,12},{2,14},{4,0},{6,2},{8,4},{10,6},{12,8},{14,10},{1,13},{3,15... | collective-permute-start | bytes 393224 | tf_op jit(solution)/shard_map/ppermute | solution.py:472
  8.6 29.0 %collective-permute-start.1 = (bf16[16,32,128]{2,1,0:T(8,128)(2,1)S(1)}, bf16[16,32,128]{2,1,0:T(8,128)(2,1)S(1)}, u32[]{:S(2)}, u32[]{:S(2)}) collective-permute-start(bf16[16,32,128]{2,1,0:T(8,128)(2,1)S(1)} %bitcast.11), channel_id=1, source_target_pairs={{0,4},{2,6},{4,8},{6,10},{8,12},{10,14},{12,0},{14,2},{1,5},{3,7},... | collective-permute-start | bytes 393224 | tf_op jit(solution)/shard_map/ppermute | solution.py:472
  10.9 26.6 %collective-permute-start = (bf16[16,32,128]{2,1,0:T(8,128)(2,1)S(1)}, bf16[16,32,128]{2,1,0:T(8,128)(2,1)S(1)}, u32[]{:S(2)}, u32[]{:S(2)}) collective-permute-start(bf16[16,32,128]{2,1,0:T(8,128)(2,1)S(1)} %bitcast.12), channel_id=1, source_target_pairs={{0,2},{2,4},{4,6},{6,8},{8,10},{10,12},{12,14},{14,0},{1,3},{3,5},... | collective-permute-start | bytes 393224 | tf_op jit(solution)/shard_map/ppermute | solution.py:472
  13.6 9.8 %all-to-all-start = ((s32[4,1,2]{2,1,0:T(1,128)}), s32[4,1,2]{2,1,0:T(1,128)S(1)}, u32[]{:S(2)}, u32[]{:S(2)}) async-start(s32[4,1,2]{2,1,0:T(1,128)} %codes.1), calls=%async_computation | async-start | bytes 4096 | tf_op jit(solution)/shard_map/all_to_all | solution.py:500
  18.0 19.5 %collective-permute-start.4 = (bf16[16,32,128]{2,1,0:T(8,128)(2,1)S(1)}, bf16[16,32,128]{2,1,0:T(8,128)(2,1)S(1)}, u32[]{:S(2)}, u32[]{:S(2)}) collective-permute-start(bf16[16,32,128]{2,1,0:T(8,128)(2,1)S(1)} %collective-permute-done.2.refs_4_), channel_id=1, source_target_pairs={{0,2},{2,4},{4,6},{6,8},{8,10},{10,12},{12,14},{14,0},{1,3},{3,5},... | collective-permute-start | bytes 393224 | tf_op jit(solution)/shard_map/ppermute | solution.py:472
  20.0 17.5 %collective-permute-start.3 = (bf16[16,32,128]{2,1,0:T(8,128)(2,1)S(1)}, bf16[16,32,128]{2,1,0:T(8,128)(2,1)S(1)}, u32[]{:S(2)}, u32[]{:S(2)}) collective-permute-start(bf16[16,32,128]{2,1,0:T(8,128)(2,1)S(1)} %collective-permute-done.2.refs_4_), channel_id=1, source_target_pairs={{0,14},{2,0},{4,2},{6,4},{8,6},{10,8},{12,10},{14,12},{1,15},{3,1}... | collective-permute-start | bytes 393224 | tf_op jit(solution)/shard_map/ppermute | solution.py:472
  22.7 14.7 %copy-start.6 = (s32[64,4]{1,0:T(8,128)}, s32[64,4]{1,0:T(8,128)S(1)}, u32[]{:S(2)}) copy-start(s32[64,4]{1,0:T(8,128)S(1)} %copy.10.fetch_ref) | copy-start | bytes 3076
  23.4 0.6 copy-start.9
  25.4 12.0 %all-to-all-start.1 = ((s32[8,1,40]{2,1,0:T(1,128)}), s32[8,1,40]{2,1,0:T(1,128)S(1)}, u32[]{:S(2)}, u32[]{:S(2)}) async-start(s32[8,1,40]{2,1,0:T(1,128)} %note.1), calls=%async_computation.1 | async-start | bytes 8192 | tf_op jit(solution)/shard_map/all_to_all | solution.py:503
  33.1 1.4 %copy-start = (bf16[16,64,704]{2,1,0:T(8,128)(2,1)S(1)}, bf16[16,64,704]{2,1,0:T(8,128)(2,1)}, u32[]{:S(2)}) copy-start(bf16[16,64,704]{2,1,0:T(8,128)(2,1)} %a_hbm.1) | copy-start | bytes 4325380
  37.5 29.7 %copy-start.4 = (s32[1,8]{1,0:T(1,128)S(1)}, s32[1,8]{1,0:T(1,128)}, u32[]{:S(2)}) copy-start(s32[1,8]{1,0:T(1,128)} %send_ref.5) | copy-start | bytes 100
  37.5 12.8 %copy-start.2 = (s32[8,1,40]{2,1,0:T(1,128)}, s32[8,1,40]{2,1,0:T(1,128)S(1)}, u32[]{:S(2)}) copy-start(s32[8,1,40]{2,1,0:T(1,128)S(1)} %all-to-all-done.1.note_ref.wanted_ref) | copy-start | bytes 3844
  38.8 7.0 %collective-permute-start.7 = (bf16[32,32,128]{2,1,0:T(8,128)(2,1)S(1)}, bf16[32,32,128]{2,1,0:T(8,128)(2,1)S(1)}, u32[]{:S(2)}, u32[]{:S(2)}) collective-permute-start(bf16[32,32,128]{2,1,0:T(8,128)(2,1)S(1)} %get-tuple-element.30), channel_id=1, source_target_pairs={{0,1},{1,0},{16,17},{17,16},{32,33},{33,32},{48,49},{49,48},{2,3},... | collective-permute-start | bytes 786440 | tf_op jit(solution)/shard_map/ppermute | solution.py:482
  39.2 8.4 %collective-permute-start.8 = (bf16[32,32,128]{2,1,0:T(8,128)(2,1)S(1)}, bf16[32,32,128]{2,1,0:T(8,128)(2,1)S(1)}, u32[]{:S(2)}, u32[]{:S(2)}) collective-permute-start(bf16[32,32,128]{2,1,0:T(8,128)(2,1)S(1)} %get-tuple-element.31), channel_id=1, source_target_pairs={{0,16},{1,17},{16,32},{17,33},{32,48},{33,49},{48,0},{49,1},{2,18}... | collective-permute-start | bytes 786440 | tf_op jit(solution)/shard_map/ppermute | solution.py:482
  40.4 21.8 %collective-permute-start.10 = (bf16[32,32,128]{2,1,0:T(8,128)(2,1)S(1)}, bf16[32,32,128]{2,1,0:T(8,128)(2,1)}, u32[]{:S(2)}, u32[]{:S(2)}) collective-permute-start(bf16[32,32,128]{2,1,0:T(8,128)(2,1)S(1)} %get-tuple-element.33), channel_id=1, source_target_pairs={{0,32},{1,33},{16,48},{17,49},{32,0},{33,1},{48,16},{49,17},{2,34}... | collective-permute-start | bytes 786440 | tf_op jit(solution)/shard_map/ppermute | solution.py:482
  41.6 20.7 %collective-permute-start.11 = (bf16[32,32,128]{2,1,0:T(8,128)(2,1)S(1)}, bf16[32,32,128]{2,1,0:T(8,128)(2,1)}, u32[]{:S(2)}, u32[]{:S(2)}) collective-permute-start(bf16[32,32,128]{2,1,0:T(8,128)(2,1)S(1)} %get-tuple-element.34), channel_id=1, source_target_pairs={{0,33},{1,32},{16,49},{17,48},{32,1},{33,0},{48,17},{49,16},{2,35}... | collective-permute-start | bytes 786440 | tf_op jit(solution)/shard_map/ppermute | solution.py:482
  44.0 18.3 %collective-permute-start.12 = (bf16[32,32,128]{2,1,0:T(8,128)(2,1)S(1)}, bf16[32,32,128]{2,1,0:T(8,128)(2,1)}, u32[]{:S(2)}, u32[]{:S(2)}) collective-permute-start(bf16[32,32,128]{2,1,0:T(8,128)(2,1)S(1)} %get-tuple-element.35), channel_id=1, source_target_pairs={{0,48},{1,49},{16,0},{17,1},{32,16},{33,17},{48,32},{49,33},{2,50}... | collective-permute-start | bytes 786440 | tf_op jit(solution)/shard_map/ppermute | solution.py:482
  45.8 1.9 %copy-start.7 = (bf16[32,32,128]{2,1,0:T(8,128)(2,1)}, bf16[32,32,128]{2,1,0:T(8,128)(2,1)S(1)}, u32[]{:S(2)}) copy-start(bf16[32,32,128]{2,1,0:T(8,128)(2,1)S(1)} %collective-permute-done.7.refs_1_) | copy-start | bytes 786436
  45.8 21.4 %collective-permute-start.13 = (bf16[32,32,128]{2,1,0:T(8,128)(2,1)}, bf16[32,32,128]{2,1,0:T(8,128)(2,1)}, u32[]{:S(2)}, u32[]{:S(2)}) collective-permute-start(bf16[32,32,128]{2,1,0:T(8,128)(2,1)} %get-tuple-element.36), channel_id=1, source_target_pairs={{0,49},{1,48},{16,1},{17,0},{32,17},{33,16},{48,33},{49,32},{2,51}... | collective-permute-start | bytes 786440 | tf_op jit(solution)/shard_map/ppermute | solution.py:482
  47.7 0.7 copy-start.8
  48.4 18.8 %collective-permute-start.9 = (bf16[32,32,128]{2,1,0:T(8,128)(2,1)}, bf16[32,32,128]{2,1,0:T(8,128)(2,1)}, u32[]{:S(2)}, u32[]{:S(2)}) collective-permute-start(bf16[32,32,128]{2,1,0:T(8,128)(2,1)} %get-tuple-element.32), channel_id=1, source_target_pairs={{0,17},{1,16},{16,33},{17,32},{32,49},{33,48},{48,1},{49,0},{2,19}... | collective-permute-start | bytes 786440 | tf_op jit(solution)/shard_map/ppermute | solution.py:482
  51.6 10.6 %all-to-all-start.2 = ((s32[8,1,64]{2,1,0:T(1,128)}), s32[8,1,64]{2,1,0:T(1,128)S(1)}, u32[]{:S(2)}, u32[]{:S(2)}) async-start(s32[8,1,64]{2,1,0:T(1,128)} %plane.1), calls=%async_computation.2 | async-start | bytes 8192 | tf_op jit(solution)/shard_map/all_to_all | solution.py:511
  60.1 0.7 copy-start.3
  61.5 0.7 copy-start.1
  70.1 8.3 %collective-permute-start.14 = (bf16[2,64,768]{2,1,0:T(8,128)(2,1)S(1)}, bf16[2,64,768]{2,1,0:T(8,128)(2,1)S(1)}, u32[]{:S(2)}, u32[]{:S(2)}) collective-permute-start(bf16[2,64,768]{2,1,0:T(8,128)(2,1)S(1)} %get-tuple-element.41), channel_id=1, source_target_pairs={{0,64},{64,128},{128,192},{192,0},{1,65},{65,129},{129,193},{193,1... | collective-permute-start | bytes 589832 | tf_op jit(solution)/shard_map/ppermute | solution.py:472
  71.4 7.3 %collective-permute-start.15 = (bf16[2,64,768]{2,1,0:T(8,128)(2,1)S(1)}, bf16[2,64,768]{2,1,0:T(8,128)(2,1)S(1)}, u32[]{:S(2)}, u32[]{:S(2)}) collective-permute-start(bf16[2,64,768]{2,1,0:T(8,128)(2,1)S(1)} %get-tuple-element.42), channel_id=1, source_target_pairs={{0,128},{64,192},{128,0},{192,64},{1,129},{65,193},{129,1},{193,65... | collective-permute-start | bytes 589832 | tf_op jit(solution)/shard_map/ppermute | solution.py:472
  73.4 10.5 %copy-start.5 = (s32[1,8]{1,0:T(1,128)S(1)}, s32[1,8]{1,0:T(1,128)}, u32[]{:S(2)}) copy-start(s32[1,8]{1,0:T(1,128)} %slots_ref.3) | copy-start | bytes 100
  73.4 10.5 %collective-permute-start.16 = (bf16[2,64,768]{2,1,0:T(8,128)(2,1)S(1)}, bf16[2,64,768]{2,1,0:T(8,128)(2,1)S(1)}, u32[]{:S(2)}, u32[]{:S(2)}) collective-permute-start(bf16[2,64,768]{2,1,0:T(8,128)(2,1)S(1)} %get-tuple-element.43), channel_id=1, source_target_pairs={{0,192},{64,0},{128,64},{192,128},{1,193},{65,1},{129,65},{193,129... | collective-permute-start | bytes 589832 | tf_op jit(solution)/shard_map/ppermute | solution.py:472
